TPU v7x, 256 devices: a whole 4x4x8 slice. The times are simulated.
256 devices in a mesh: dp: 4 (over x), space: 64 (over y, z, core).
Axes of the slice: x: 4, y: 4, z: 8, core: 2. Of those that a mesh axis runs over, the one named last changes fastest.
Arguments:
- volume: bfloat16 [4, 128, 128, 16, 256], P('dp', None, 'space'), may hold values from -6 to 6
- w_first: bfloat16 [3, 3, 3, 128, 256], replicated, may hold values from -0.109375 to 0.109375
- w_second: bfloat16 [3, 3, 3, 256, 512], P(None, None, None, 'space'), may hold values from -0.078125 to 0.078125
- cotangent: bfloat16 [4, 512, 32, 256], P('dp', 'space'), may hold values from -6 to 6
Outputs:
- grad_second: float32 [3, 3, 3, 256, 512], P(None, None, None, 'space')
- pre_grad: bfloat16 [4, 256, 64, 4, 256], P('dp', None, 'space')
All inputs are finite; a program needn't handle non-finite values.
Results may differ from a plain program's by a relative error of at most 0.0049.
Values may be sent and summed in bfloat16 or wider, within the bound.
No kernel may reach another device: no remote copies, remote signals or barrier semaphores. Data moves between devices by JAX's collectives and lax.ppermute only.
A program may use at most 128 MiB of HBM per device.

v0:
```python
import jax
import jax.numpy as jnp
from jax import lax
from jax.sharding import PartitionSpec as P

C3 = 512
WID = 128


leak_slope = 0.3


def from_behind(block, axis, distance):
    devices = range(lax.axis_size(axis))
    route = [(i - distance, i) for i in devices if i - distance in devices]
    return lax.ppermute(block, axis, route)


def activate(values):
    return leak_slope * values + (1.0 - leak_slope) * values * jax.nn.sigmoid(values)


def slope_of(values):
    sigmoid_value = jax.nn.sigmoid(values)
    return leak_slope + (1.0 - leak_slope) * (
        sigmoid_value + values * sigmoid_value * (1.0 - sigmoid_value)
    )


def stride_taps(values, along_dim):
    length = values.shape[along_dim] // 2
    paired = values.reshape(values.shape[:along_dim] + (length, 2) + values.shape[along_dim + 1 :])
    even_cells = lax.index_in_dim(paired, 0, along_dim + 1, keepdims=False)
    odd_cells = lax.index_in_dim(paired, 1, along_dim + 1, keepdims=False)
    before = jnp.concatenate(
        [
            jnp.zeros_like(lax.slice_in_dim(odd_cells, 0, 1, axis=along_dim)),
            lax.slice_in_dim(odd_cells, 0, length - 1, axis=along_dim),
        ],
        along_dim,
    )
    return [before, even_cells, odd_cells]


def step_cells(values, by_row, by_col, row_len):
    cells = values.shape[-1]
    if by_row:
        filler = jnp.zeros(values.shape[:-1] + (row_len,), values.dtype)
        values = jnp.concatenate([filler, values[..., : cells - row_len]], -1)
    if by_col:
        filler = jnp.zeros(values.shape[:-1] + (1,), values.dtype)
        moved = jnp.concatenate([filler, values[..., : cells - 1]], -1)
        keeper = lax.iota(jnp.int32, cells) % row_len != 0
        values = jnp.where(keeper, moved, jnp.zeros_like(moved))
    return values


def plane_taps(values, row_len):
    phases = values.shape[-2]
    out_phases = phases // 2
    collected = []
    for row_tap in range(3):
        for col_tap in range(3):
            rows_out = []
            for row_phase in range(out_phases):
                cols_out = []
                for col_phase in range(out_phases):
                    row_at = 2 * row_phase + row_tap - 1
                    col_at = 2 * col_phase + col_tap - 1
                    part = values[..., row_at % phases, col_at % phases, :]
                    cols_out.append(step_cells(part, row_at < 0, col_at < 0, row_len))
                rows_out.append(jnp.stack(cols_out, -2))
            collected.append(jnp.stack(rows_out, -3))
    return collected


def all_taps(values, row_len):
    collected = []
    for depth_part in stride_taps(values, 1):
        collected.extend(plane_taps(depth_part, row_len))
    return collected


def contract_first(left_side, right_side):
    return lax.dot_general(
        left_side, right_side, (((0,), (0,)), ((), ())), preferred_element_type=jnp.float32
    )


def contract_last(left_side, right_side):
    return lax.dot_general(
        left_side, right_side, (((1,), (1,)), ((), ())), preferred_element_type=jnp.float32
    )


def per_device(volume, w_first, w_second, cotangent):
    channels = volume.shape[1]
    depth_cells = volume.shape[2]
    cell_count = volume.shape[4]
    half_depth = depth_cells // 2
    out_channels = w_first.shape[4]
    row_len = WID // 4
    paired = volume[0].reshape(channels, half_depth, 2, 4, 4, cell_count)
    even_cells = paired[:, :, 0]
    odd_cells = paired[:, :, 1]
    w_flat = w_first.reshape(27 * channels, out_channels)
    rim_cells = from_behind(odd_cells, "space", 1)
    before = jnp.concatenate([rim_cells, odd_cells[:, : half_depth - 1]], 1)
    collected = []
    for depth_part in (before, even_cells, odd_cells):
        collected.extend(plane_taps(depth_part, row_len))
    stacked = jnp.stack(collected, 0).reshape(27 * channels, -1)
    pre_act = contract_first(w_flat, stacked).reshape(out_channels, half_depth, 4, cell_count)
    hidden = activate(pre_act).astype(jnp.bfloat16)
    by_channel = lax.all_to_all(hidden, "space", split_axis=0, concat_axis=1, tiled=True)
    own_channels = by_channel.shape[0]
    full_depth = by_channel.shape[1]
    hidden_cells = by_channel.reshape(own_channels, full_depth, 2, 2, cell_count)
    hidden_taps = jnp.stack(all_taps(hidden_cells, row_len), 0).reshape(27 * own_channels, -1)
    w_rows = w_second.reshape(27 * own_channels, C3)
    out_cells = hidden_taps.shape[1]
    gathered = lax.all_gather(cotangent[0], "space", axis=0, tiled=True)
    cot_flat = gathered.reshape(C3, out_cells)
    weight_grad = contract_last(hidden_taps, cot_flat)
    tap_terms = jnp.dot(w_rows, cot_flat, preferred_element_type=jnp.float32)
    grad_second = lax.psum(weight_grad, "dp").reshape(3, 3, 3, own_channels, C3)

    def spread(field):
        return jnp.stack(all_taps(field, row_len), 0).reshape(27 * own_channels, -1)

    unused, pull = jax.vjp(
        spread, jnp.zeros((own_channels, full_depth, 2, 2, cell_count), jnp.float32)
    )
    back_terms = pull(tap_terms)[0]
    back_terms = back_terms.astype(jnp.bfloat16).reshape(own_channels, full_depth, 4, cell_count)
    hidden_grad = lax.all_to_all(back_terms, "space", split_axis=1, concat_axis=0, tiled=True)
    pre_grad = (hidden_grad.astype(jnp.float32) * slope_of(pre_act)).astype(jnp.bfloat16)
    return (grad_second, pre_grad[None])


def solution(mesh):
    in_specs = (
        P("dp", None, "space", None, None),
        P(),
        P(None, None, None, "space", None),
        P("dp", "space", None, None),
    )
    out_specs = (P(None, None, None, "space", None), P("dp", None, "space", None, None))
    return jax.shard_map(
        per_device, mesh=mesh, in_specs=in_specs, out_specs=out_specs, check_vma=False
    )
```

profile of v0, /device:TPU:1, one launch (start us, length us, event | category | flops | bytes accessed | tf_op | source)
XLA Modules:
  0.0 216.6 jit_solution(14263887980538199394)
XLA Ops:
  7.2 0.7 all-gather.3.cloned.1.call-update
  7.9 2.8 %copy.103 = bf16[1,128,2,16,256]{4,1,3,2,0:T(8,128)(2,1)S(1)} copy(bf16[1,128,2,16,256]{4,3,2,1,0:T(8,128)(2,1)} %param.4) | data formatting | bytes 4194304 | tf_op args[0]
  10.9 4.9 %collective-permute-start = (bf16[128,1,4,4,256]{4,0,3,2,1:T(8,128)(2,1)S(1)}, bf16[128,1,4,4,256]{4,0,3,2,1:T(8,128)(2,1)S(1)}, u32[]{:S(2)}, u32[]{:S(2)}) collective-permute-start(bf16[128,1,4,4,256]{4,0,3,2,1:T(8,128)(2,1)S(1)} %get-tuple-element.34), channel_id=1, source_target_pairs={{0,1},{1,2},{2,3},{3,4},{4,5},{5,6},{6,7},{7,8},{8,9},{9,10},{10,1... | collective-permute-start | bytes 3145736 | tf_op jit(solution)/shard_map/ppermute | solution.py:16
  17.1 10.5 %collective-permute-done = bf16[128,1,4,4,256]{4,0,3,2,1:T(8,128)(2,1)S(1)} collective-permute-done((bf16[128,1,4,4,256]{4,0,3,2,1:T(8,128)(2,1)S(1)}, bf16[128,1,4,4,256]{4,0,3,2,1:T(8,128)(2,1)S(1)}, u32[]{:S(2)}, u32[]{:S(2)}) %collective-permute-start) | collective-permute-done | bytes 1048608 | tf_op jit(solution)/shard_map/ppermute | solution.py:16
  29.8 6.8 %copy.104 = bf16[27,128,1,2,2,256]{5,4,3,1,0,2:T(2,128)(2,1)} copy(bf16[27,128,1,2,2,256]{5,1,4,3,2,0:T(8,128)(2,1)S(1)} %fusion.33) | data formatting | bytes 14155776 | tf_op jit(solution)/shard_map/stack | solution.py:112
  36.6 16.2 %reshape.233 = bf16[3456,1024]{1,0:T(8,128)(2,1)} reshape(bf16[27,128,1,2,2,256]{5,4,3,1,0,2:T(2,128)(2,1)} %copy.104) | data formatting | bytes 14155776 | tf_op jit(solution)/shard_map/reshape | solution.py:112
  52.8 6.2 %fusion.2 = (bf16[256,1024]{0,1:T(8,128)(2,1)S(1)}, f32[1024,256]{1,0:T(8,128)}) fusion(bf16[3456,1024]{1,0:T(8,128)(2,1)} %reshape.233, bf16[3456,256]{1,0:T(8,128)(2,1)S(1)} %bitcast.641), kind=kOutput, calls=%fused_computation.9 | convolution fusion | flops 1814036480 | bytes 10420224 | tf_op jit(solution)/shard_map/dot_general | solution.py:85
  58.9 1.1 copy.105
  60.0 14.8 %all-to-all-start = ((bf16[256,1,4,256]{3,2,1,0:T(4,128)(2,1)}), bf16[256,1,4,256]{3,2,1,0:T(4,128)(2,1)S(1)}, u32[]{:S(2)}, u32[]{:S(2)}) async-start(bf16[256,1,4,256]{3,2,1,0:T(4,128)(2,1)} %copy.105), calls=%async_computation | async-start | bytes 1048576 | tf_op jit(solution)/shard_map/all_to_all | solution.py:115
  74.9 1.6 copy.142
  76.5 21.1 %all-to-all-done = bf16[256,1,4,256]{3,2,1,0:T(4,128)(2,1)S(1)} async-done(((bf16[256,1,4,256]{3,2,1,0:T(4,128)(2,1)}), bf16[256,1,4,256]{3,2,1,0:T(4,128)(2,1)S(1)}, u32[]{:S(2)}, u32[]{:S(2)}) %all-to-all-start) | async-done | bytes 524320 | tf_op jit(solution)/shard_map/all_to_all | solution.py:115
  98.4 0.7 constant_dynamic-update-slice_fusion.26
  99.2 0.7 constant_dynamic-update-slice_fusion.25
  99.9 0.7 constant_dynamic-update-slice_fusion.24
  100.6 0.7 constant_dynamic-update-slice_fusion.23
  101.3 0.7 constant_dynamic-update-slice_fusion.22
  102.0 0.6 constant_dynamic-update-slice_fusion.21
  102.7 0.7 constant_dynamic-update-slice_fusion.20
  103.4 0.7 constant_dynamic-update-slice_fusion.19
  104.1 0.7 constant_dynamic-update-slice_fusion.18
  104.9 0.7 constant_dynamic-update-slice_fusion.17
  105.6 0.7 constant_dynamic-update-slice_fusion.16
  106.4 0.7 constant_dynamic-update-slice_fusion.15
  107.3 0.7 constant_dynamic-update-slice_fusion.14
  108.0 0.7 constant_dynamic-update-slice_fusion.13
  108.7 0.6 constant_dynamic-update-slice_fusion.12
  109.3 0.7 constant_dynamic-update-slice_fusion.11
  110.1 0.7 constant_dynamic-update-slice_fusion.10
  111.4 0.7 constant_dynamic-update-slice_fusion.8
  112.1 0.7 constant_dynamic-update-slice_fusion.7
  112.8 0.7 constant_dynamic-update-slice_fusion.6
  113.6 0.7 constant_dynamic-update-slice_fusion.5
  114.3 0.6 constant_dynamic-update-slice_fusion.4
  115.6 0.7 constant_dynamic-update-slice_fusion.2
  116.3 16.7 %copy.149 = bf16[64,8,32,256]{3,1,2,0:T(8,128)(2,1)} copy(bf16[64,8,32,256]{3,2,1,0:T(8,128)(2,1)} %bitcast.644) | data formatting | bytes 16777216
  133.0 4.6 %fusion.42 = f32[108,8192]{1,0:T(8,128)S(1)} fusion(bf16[108,512]{1,0:T(8,128)(2,1)S(1)} %reshape.238, bf16[512,8192]{1,0:T(8,128)(2,1)} %bitcast.642), kind=kOutput, calls=%fused_computation.302 | convolution fusion | flops 905969664 | bytes 12038144 | tf_op jit(solution)/shard_map/dot_general | solution.py:125
  138.3 0.7 slice_select_fusion.8
  141.5 1.1 copy.140
  142.6 6.1 %all-to-all-start.1 = ((bf16[4,64,4,256]{3,0,2,1:T(4,128)(2,1)}), bf16[4,64,4,256]{3,0,2,1:T(4,128)(2,1)S(1)}, u32[]{:S(2)}, u32[]{:S(2)}) async-start(bf16[4,64,4,256]{3,0,2,1:T(4,128)(2,1)} %bitcast.260), calls=%async_computation.1 | async-start | bytes 1048576 | tf_op jit(solution)/shard_map/all_to_all | solution.py:136
  149.7 0.6 constant_dynamic-update-slice_fusion
  150.3 1.8 copy.111
  152.3 1.2 copy.150
  153.6 7.1 %fusion.41 = f32[108,512]{1,0:T(8,128)} fusion(bf16[108,8192]{1,0:T(8,128)(2,1)S(1)} %bitcast.646, bf16[512,8192]{1,0:T(8,128)(2,1)} %bitcast.643), kind=kOutput, calls=%fused_computation.301 | convolution fusion | flops 905969664 | bytes 10379264 | tf_op jit(solution)/shard_map/dot_general | solution.py:91
  160.7 1.7 reshape.237
  162.4 3.6 %all-to-all-done.1 = bf16[4,64,4,256]{3,0,2,1:T(4,128)(2,1)S(1)} async-done(((bf16[4,64,4,256]{3,0,2,1:T(4,128)(2,1)}), bf16[4,64,4,256]{3,0,2,1:T(4,128)(2,1)S(1)}, u32[]{:S(2)}, u32[]{:S(2)}) %all-to-all-start.1) | async-done | bytes 524320 | tf_op jit(solution)/shard_map/all_to_all | solution.py:136
  166.6 1.8 fusion
  168.4 39.8 %all-reduce.93.cloned.1.call-done = f32[3,3,3,4,512]{4,3,2,1,0:T(4,128)} async-done(((f32[3,3,3,4,512]{4,3,2,1,0:T(4,128)}), f32[3,3,3,4,512]{4,3,2,1,0:T(4,128)}) %all-reduce.93.cloned.1.call-update) | async-done | bytes 221200 | tf_op jit(solution)/shard_map/psum | solution.py:126
  208.2 1.6 copy.206
  (122 shorter events, 10.4 us)
Async XLA Ops:
  7.2 45.6 %copy-start = (bf16[3,3,3,128,256]{4,3,2,1,0:T(8,128)(2,1)S(1)}, bf16[3,3,3,128,256]{4,3,2,1,0:T(8,128)(2,1)}, u32[]{:S(2)}) copy-start(bf16[3,3,3,128,256]{4,3,2,1,0:T(8,128)(2,1)} %param.5) | copy-start | bytes 5308420
  7.2 109.2 %all-gather.3.cloned.1.call-start = ((), (), s32[]{:S(2)}) async-start(), calls=%async_computation.3 | async-start | bytes 8519680 | tf_op jit(solution)/shard_map/all_gather | solution.py:122
  10.9 16.7 %collective-permute-start = (bf16[128,1,4,4,256]{4,0,3,2,1:T(8,128)(2,1)S(1)}, bf16[128,1,4,4,256]{4,0,3,2,1:T(8,128)(2,1)S(1)}, u32[]{:S(2)}, u32[]{:S(2)}) collective-permute-start(bf16[128,1,4,4,256]{4,0,3,2,1:T(8,128)(2,1)S(1)} %get-tuple-element.34), channel_id=1, source_target_pairs={{0,1},{1,2},{2,3},{3,4},{4,5},{5,6},{6,7},{7,8},{8,9},{9,10},{10,1... | collective-permute-start | bytes 3145736 | tf_op jit(solution)/shard_map/ppermute | solution.py:16
  52.8 22.1 %copy-start.2 = (bf16[3,3,3,4,512]{4,3,2,1,0:T(4,128)(2,1)S(1)}, bf16[3,3,3,4,512]{4,3,2,1,0:T(4,128)(2,1)}, u32[]{:S(2)}) copy-start(bf16[3,3,3,4,512]{4,3,2,1,0:T(4,128)(2,1)} %param.6) | copy-start | bytes 331780
  60.0 37.6 %all-to-all-start = ((bf16[256,1,4,256]{3,2,1,0:T(4,128)(2,1)}), bf16[256,1,4,256]{3,2,1,0:T(4,128)(2,1)S(1)}, u32[]{:S(2)}, u32[]{:S(2)}) async-start(bf16[256,1,4,256]{3,2,1,0:T(4,128)(2,1)} %copy.105), calls=%async_computation | async-start | bytes 1048576 | tf_op jit(solution)/shard_map/all_to_all | solution.py:115
  142.6 23.4 %all-to-all-start.1 = ((bf16[4,64,4,256]{3,0,2,1:T(4,128)(2,1)}), bf16[4,64,4,256]{3,0,2,1:T(4,128)(2,1)S(1)}, u32[]{:S(2)}, u32[]{:S(2)}) async-start(bf16[4,64,4,256]{3,0,2,1:T(4,128)(2,1)} %bitcast.260), calls=%async_computation.1 | async-start | bytes 1048576 | tf_op jit(solution)/shard_map/all_to_all | solution.py:136
  148.7 59.4 %all-reduce.93.cloned.1.call-start = ((), (), s32[]{:S(2)}) async-start(), calls=%async_computation.2 | async-start | bytes 442368 | tf_op jit(solution)/shard_map/psum | solution.py:126
  153.6 56.2 %copy-start.1 = (bf16[3,3,3,128,256]{4,3,2,1,0:T(8,128)(2,1)S(1)}, bf16[3,3,3,128,256]{4,3,2,1,0:T(8,128)(2,1)}, u32[]{:S(2)}) copy-start(bf16[3,3,3,128,256]{4,3,2,1,0:T(8,128)(2,1)} %param.5) | copy-start | bytes 5308420
Sparse Core Ops, SparseCore 0:
  10.8 97.4 all-gather.2
  162.5 45.5 all-reduce.92
where the time goes:
time: 219 us; the launch traced here: 217 us
  waiting for transfers between devices  75.7 us (35%)
  local copies, waits for them, and re-layouts  70.2 us (32%)
  starting transfers between devices  26.2 us (12%)
  matrix products  18 us (8%)
  between operations  14.9 us (7%)
  other arithmetic  11.8 us (5%)
    psum x1, waiting for transfers between devices, per_device(): grad_second = lax.psum(weight_grad, 'dp').reshape(3, 3, 3, own_channels, C3)  39.8 us
    unnamed x29, local copies, waits for them, and re-layouts  34.1 us
    all_to_all x1, waiting for transfers between devices, per_device(): lax.all_to_all(hidden, 'space', split_axis=0, concat_axis=1, tiled=True)  21.1 us
    reshape x1, local copies, waits for them, and re-layouts, per_device(): stacked = jnp.stack(collected, 0).reshape(27 * channels, -1)  16.2 us
    all_to_all x1, starting transfers between devices, per_device(): lax.all_to_all(hidden, 'space', split_axis=0, concat_axis=1, tiled=True)  14.8 us
    ppermute x1, waiting for transfers between devices, from_behind(): return lax.ppermute(block, axis, route)  10.5 us
    unnamed x35, other arithmetic  7.14 us
    dot_general x1, matrix products, contract_last(): lax.dot_general(left_side, right_side, (((1,), (1,)), ((), ())), preferre...  7.13 us
  transfers between devices with their start and end apart: 5, of which 4 were waited for; matrix products, arithmetic and copies ran while one was open for 33% of the time, Pallas kernels for 0%

commit v1 on v0

v1 whole, which is shorter than its diff:
```python
import functools

import jax
import jax.numpy as jnp
from jax import lax
from jax.experimental import pallas as pl
from jax.experimental.pallas import tpu as pltpu
from jax.sharding import PartitionSpec as P

C3 = 512
WID = 128


leak_slope = 0.3


def from_behind(block, axis, distance):
    devices = range(lax.axis_size(axis))
    route = [(i - distance, i) for i in devices if i - distance in devices]
    return lax.ppermute(block, axis, route)


def from_side(block, axis, distance):
    size = lax.axis_size(axis)
    return lax.ppermute(block, axis, [(i, (i + distance) % size) for i in range(size)])


def activate(values):
    return leak_slope * values + (1.0 - leak_slope) * values * jax.nn.sigmoid(values)


def slope_of(values):
    sigmoid_value = jax.nn.sigmoid(values)
    return leak_slope + (1.0 - leak_slope) * (
        sigmoid_value + values * sigmoid_value * (1.0 - sigmoid_value)
    )


def shifted(block, by_row, by_col, row_len):
    moved = block.astype(jnp.float32)
    lane = lax.broadcasted_iota(jnp.int32, moved.shape, 1)
    moved = pltpu.roll(moved, by_row * row_len + by_col, 1)
    keep = None
    if by_row:
        keep = lane >= row_len
    if by_col:
        inner = lane % row_len != 0
        keep = inner if keep is None else jnp.logical_and(keep, inner)
    return jnp.where(keep, moved, 0.0).astype(block.dtype)


def conv_kernel(taps_of_plane, channels, row_len, w_ref, *refs):
    planes = refs[: len(taps_of_plane)]
    out_ref = refs[len(taps_of_plane)]
    cols_ref = refs[len(taps_of_plane) + 1]
    tap_rows = 9 * channels
    for at, plane in enumerate(planes):
        for row in range(-1, 4):
            for col in range(-1, 4):
                source = ((row % 4) * 4 + col % 4) * channels
                block = plane[source : source + channels, :]
                if row < 0 or col < 0:
                    block = shifted(block, int(row < 0), int(col < 0), row_len)
                for row_phase in range(2):
                    row_tap = row + 1 - 2 * row_phase
                    if not 0 <= row_tap <= 2:
                        continue
                    for col_phase in range(2):
                        col_tap = col + 1 - 2 * col_phase
                        if not 0 <= col_tap <= 2:
                            continue
                        start = at * tap_rows + (row_tap * 3 + col_tap) * channels
                        cols_ref[row_phase * 2 + col_phase, start : start + channels, :] = block
    for phase in range(4):
        out_ref[phase, :, :] = jnp.dot(
            w_ref[...], cols_ref[phase], preferred_element_type=jnp.float32
        ).astype(out_ref.dtype)


def conv(w_rows, planes, dtype, row_len):
    out_channels, depth = w_rows.shape
    count = len(planes)
    channels = depth // (9 * count)
    cells = planes[0].shape[1]
    return pl.pallas_call(
        functools.partial(conv_kernel, tuple(range(count)), channels, row_len),
        out_shape=jax.ShapeDtypeStruct((4, out_channels, cells), dtype),
        scratch_shapes=[pltpu.VMEM((4, depth, cells), jnp.bfloat16)],
        cost_estimate=pl.CostEstimate(
            flops=8 * out_channels * depth * cells, bytes_accessed=8 * depth * cells, transcendentals=0
        ),
    )(w_rows, *planes)


def spread(block, row_len):
    return jnp.concatenate(
        [block]
        + [shifted(block, by_row, by_col, row_len) for by_row, by_col in ((0, 1), (1, 0), (1, 1))],
        0,
    )


def gather_back(terms, row_len):
    rows = terms.shape[0] // 4
    lane = lax.broadcasted_iota(jnp.int32, (rows, terms.shape[1]), 1)
    cells = terms.shape[1]
    total = terms[:rows]
    for at, (by_row, by_col) in ((1, (0, 1)), (2, (1, 0)), (3, (1, 1))):
        moved = pltpu.roll(terms[at * rows : (at + 1) * rows], cells - by_row * row_len - by_col, 1)
        keep = lane < cells - row_len if by_row else None
        if by_col:
            inner = lane % row_len != row_len - 1
            keep = inner if keep is None else jnp.logical_and(keep, inner)
        total = total + jnp.where(keep, moved, 0.0)
    return total


def grad_kernel(row_len, hidden_ref, cot_ref, out_ref, rows_ref):
    planes, group, cells = hidden_ref.shape
    steps = planes // 2
    size = 4 * group
    rows_ref[0:size, 0:cells] = jnp.zeros((size, cells), rows_ref.dtype)

    def fill(s, carry):
        here = pl.ds(pl.multiple_of(s * cells, cells), cells)
        rows_ref[size : 2 * size, here] = spread(hidden_ref[2 * s], row_len)
        odd = spread(hidden_ref[2 * s + 1], row_len)
        rows_ref[2 * size : 3 * size, here] = odd

        @pl.when(s + 1 < steps)
        def _():
            rows_ref[0:size, pl.ds(pl.multiple_of((s + 1) * cells, cells), cells)] = odd

        return carry

    lax.fori_loop(0, steps, fill, 0)
    total = lax.dot_general(
        rows_ref[...], cot_ref[...], (((1,), (1,)), ((), ())), preferred_element_type=jnp.float32
    )
    own = group // 4
    for depth_tap in range(3):
        for row_tap in range(3):
            for col_tap in range(3):
                start = (
                    depth_tap * size
                    + (2 * int(row_tap == 0) + int(col_tap == 0)) * group
                    + (2 * int(row_tap != 1) + int(col_tap != 1)) * own
                )
                put = ((depth_tap * 3 + row_tap) * 3 + col_tap) * own
                out_ref[put : put + own, :] = total[start : start + own, :].astype(out_ref.dtype)


def grad(hidden, cot, dtype, row_len):
    planes, group, cells = hidden.shape
    outs = cot.shape[0]
    return pl.pallas_call(
        functools.partial(grad_kernel, row_len),
        out_shape=jax.ShapeDtypeStruct((27 * group // 4, outs), dtype),
        scratch_shapes=[pltpu.VMEM((12 * group, planes // 2 * cells), jnp.bfloat16)],
        cost_estimate=pl.CostEstimate(
            flops=12 * group * outs * planes * cells, bytes_accessed=2 * cot.size, transcendentals=0
        ),
    )(hidden, cot)


def back_kernel(row_len, w_ref, cot_ref, out_ref, terms_ref):
    planes, group, cells = out_ref.shape
    steps = planes // 2
    size = 4 * group

    def multiply(s, carry):
        here = pl.ds(pl.multiple_of(s * cells, cells), cells)
        terms_ref[:, here] = jnp.dot(
            w_ref[...], cot_ref[:, here], preferred_element_type=jnp.float32
        )
        return carry

    lax.fori_loop(0, steps, multiply, 0)

    def combine(s, carry):
        here = pl.ds(pl.multiple_of(s * cells, cells), cells)
        out_ref[2 * s] = gather_back(terms_ref[size : 2 * size, here], row_len).astype(out_ref.dtype)
        after = jnp.minimum(s + 1, steps - 1)
        next_one = pl.ds(pl.multiple_of(after * cells, cells), cells)
        extra = jnp.where(s + 1 < steps, terms_ref[0:size, next_one], 0.0)
        odd = terms_ref[2 * size : 3 * size, here] + extra
        out_ref[2 * s + 1] = gather_back(odd, row_len).astype(out_ref.dtype)
        return carry

    lax.fori_loop(0, steps, combine, 0)


def back(w_rows, cot, planes, row_len):
    rows, outs = w_rows.shape
    group = rows // 12
    cells = 2 * cot.shape[1] // planes
    return pl.pallas_call(
        functools.partial(back_kernel, row_len),
        out_shape=jax.ShapeDtypeStruct((planes, group, cells), jnp.bfloat16),
        scratch_shapes=[pltpu.VMEM((rows, cot.shape[1]), jnp.float32)],
        cost_estimate=pl.CostEstimate(
            flops=2 * rows * cot.size, bytes_accessed=2 * cot.size, transcendentals=0
        ),
    )(w_rows, cot)


def move_rows(w_second):
    nothing = jnp.zeros_like(w_second[:, 0])

    def halves(taps, gap):
        return [[taps[1], taps[2]], [gap, taps[0]]]

    by_row = halves([w_second[:, b] for b in range(3)], nothing)
    moved_rows = []
    for row in by_row:
        for_phase = []
        for part in row:
            by_col = halves([part[:, c] for c in range(3)], jnp.zeros_like(part[:, 0]))
            for_phase.append(jnp.stack([jnp.stack(col, 1) for col in by_col], 1))
        moved_rows.append(jnp.stack(for_phase, 2))
    rows = jnp.stack(moved_rows, 1)
    return rows.reshape(-1, w_second.shape[-1])


def per_device(volume, w_first, w_second, cotangent):
    channels = volume.shape[1]
    cell_count = volume.shape[4]
    out_channels = w_first.shape[4]
    row_len = WID // 4
    members = lax.axis_size("space")
    own_channels = out_channels // members
    planes = volume[0].reshape(channels, 2, 16, cell_count).transpose(1, 2, 0, 3)
    planes = planes.reshape(2, 16 * channels, cell_count)
    w_rows = w_first.reshape(27 * channels, out_channels)
    w_before = w_rows[: 9 * channels].T
    w_here = w_rows[9 * channels :].T
    ahead = conv(w_before, [planes[1]], jnp.bfloat16, row_len)
    behind = from_behind(ahead, "space", 1)
    gathered = lax.all_gather(cotangent[0], "space", axis=0, tiled=True)
    cot_flat = gathered.reshape(C3, -1)
    pre_act = conv(w_here, [planes[0], planes[1]], jnp.float32, row_len)
    pre_act = pre_act + behind.astype(jnp.float32)
    hidden = activate(pre_act).astype(jnp.bfloat16)
    blocks = hidden.reshape(4, members, own_channels, cell_count).transpose(1, 0, 2, 3)
    blocks = blocks.reshape(members, 4 * own_channels, cell_count)
    by_plane = lax.all_to_all(blocks, "space", split_axis=0, concat_axis=0, tiled=True)
    back_terms = back(move_rows(w_second), cot_flat, members, row_len)
    hidden_grad = lax.all_to_all(back_terms, "space", split_axis=0, concat_axis=0, tiled=True)
    partial = grad(by_plane, cot_flat, jnp.bfloat16, row_len)
    sides = [from_side(partial, "dp", distance) for distance in (1, 2, 3)]
    left, opposite, right = [side.astype(jnp.float32) for side in sides]
    grad_second = (partial.astype(jnp.float32) + opposite) + (left + right)
    grad_second = grad_second.reshape(3, 3, 3, own_channels, C3)
    hidden_grad = hidden_grad.reshape(members, 4, own_channels, cell_count).transpose(0, 2, 1, 3)
    hidden_grad = hidden_grad.reshape(out_channels, 4, cell_count).astype(jnp.float32)
    slopes = slope_of(pre_act.transpose(1, 0, 2))
    pre_grad = (hidden_grad * slopes).astype(jnp.bfloat16)
    return (grad_second, pre_grad[None, :, None])


def solution(mesh):
    in_specs = (
        P("dp", None, "space", None, None),
        P(),
        P(None, None, None, "space", None),
        P("dp", "space", None, None),
    )
    out_specs = (P(None, None, None, "space", None), P("dp", None, "space", None, None))
    return jax.shard_map(
        per_device, mesh=mesh, in_specs=in_specs, out_specs=out_specs, check_vma=False
    )
```

time: 219 us -> 170 us (0.78)
  local copies, waits for them, and re-layouts: 70.2 us -> 30.2 us
  Pallas kernels: 0 us -> 32.1 us
  matrix products: 18 us -> 0 us
  waiting for transfers between devices: 75.7 us -> 59.9 us
  other arithmetic: 11.8 us -> 4.56 us
    all_gather x1, waiting for transfers between devices: 0.01 us -> 52.7 us  [per_device(): gathered = lax.all_gather(cotangent[0], 'space', axis=0, tiled=True)]
    psum x1 -> x0, waiting for transfers between devices: 39.8 us -> none  [per_device(): grad_second = lax.psum(weight_grad, 'dp').reshape(3, 3, 3, own_channels, C3)]
    pallas_call x0 -> x4, Pallas kernels: none -> 32.1 us  [the longest x1 14.5 us: back(): pl.pallas_call(functools.partial(back_kernel, row_len), out_shape=jax.Sha...]
    all_to_all x2, waiting for transfers between devices: 24.7 us -> 0.01 us  [the longest x1 0.01 us: per_device(): lax.all_to_all(blocks, 'space', split_axis=0, concat_axis=0, tiled=True)]
    dot_general x3 -> x0, matrix products: 18 us -> none  [the longest x1 7.13 us: contract_last(): lax.dot_general(left_side, right_side, (((1,), (1,)), ((), ())), preferre...]
    reshape x4 -> x5, local copies, waits for them, and re-layouts: 19.5 us -> 2.7 us  [the longest x1 0.92 us: per_device(): blocks = blocks.reshape(members, 4 * own_channels, cell_count)]
    unnamed x29 -> x10, local copies, waits for them, and re-layouts: 34.1 us -> 18.3 us
    another operation x16 -> x6, local copies, waits for them, and re-layouts: 11 us -> 0.18 us  [the longest x2 0.11 us: move_rows(): rows = jnp.stack(moved_rows, 1)]
  transfers between devices with their start and end apart: 5 -> 7, of which waited for: 4 -> 3; matrix products, arithmetic and copies ran while one was open for 33% -> 18% of each run, Pallas kernels for 0% -> 19%
where the time goes in v1:
time: 170 us; the launch traced here: 169 us
  waiting for transfers between devices  59.9 us (35%)
  Pallas kernels  32.1 us (19%)
  local copies, waits for them, and re-layouts  30.2 us (18%)
  starting transfers between devices  28.3 us (17%)
  between operations  14.3 us (8%)
  other arithmetic  4.56 us (3%)
    all_gather x1, waiting for transfers between devices, per_device(): gathered = lax.all_gather(cotangent[0], 'space', axis=0, tiled=True)  52.7 us
    unnamed x10, local copies, waits for them, and re-layouts  18.3 us
    pallas_call x1, Pallas kernels, back(): pl.pallas_call(functools.partial(back_kernel, row_len), out_shape=jax.Sha...  14.5 us
    all_to_all x1, starting transfers between devices, per_device(): lax.all_to_all(blocks, 'space', split_axis=0, concat_axis=0, tiled=True)  13.4 us
    pallas_call x1, Pallas kernels, grad(): pl.pallas_call(functools.partial(grad_kernel, row_len), out_shape=jax.Sha...  9.99 us
    pallas_call x2, Pallas kernels, conv(): pl.pallas_call(functools.partial(conv_kernel, tuple(range(count)), channe...  7.63 us
    ppermute x3, waiting for transfers between devices, from_side(): lax.ppermute(block, axis, [(i, (i + distance) % size) for i in range(size)])  6.53 us
    all_to_all x1, starting transfers between devices, per_device(): lax.all_to_all(back_terms, 'space', split_axis=0, concat_axis=0, tiled=True)  5.76 us
  transfers between devices with their start and end apart: 7, of which 3 were waited for; matrix products, arithmetic and copies ran while one was open for 18% of the time, Pallas kernels for 19%

profile of v1, /device:TPU:1, one launch (start us, length us, event | category | flops | bytes accessed | tf_op | source)
XLA Modules:
  0.0 169.4 jit_solution(18362806694326293055)
XLA Ops:
  7.2 0.0 all-gather.3.cloned.1.call-start
  7.2 0.7 all-gather.3.cloned.1.call-update
  7.9 1.1 slice.52
  9.0 1.1 copy.29
  10.1 1.7 %fusion.10 = (bf16[1,16,128,256]{3,1,0,2:T(8,128)(2,1)S(1)}, bf16[1,16,128,256]{3,1,0,2:T(8,128)(2,1)S(1)}) fusion(bf16[2,16,128,256]{3,1,0,2:T(8,128)(2,1)} %bitcast.85), kind=kLoop, calls=%fused_computation.31 | loop fusion | bytes 4194304 | tf_op jit(solution)/shard_map/slice | solution.py:241
  11.8 1.3 copy.28
  13.2 3.3 %shard_map.60 = bf16[4,256,256]{2,1,0:T(8,128)(2,1)} custom-call(bf16[256,1152]{1,0:T(8,128)(2,1)} %bitcast.91, bf16[2048,256]{1,0:T(8,128)(2,1)} %bitcast.88), custom_call_target="tpu_custom_call" | custom-call | flops 603979776 | bytes 2359296 | tf_op jit(solution)/shard_map/pallas_call | solution.py:85
  16.4 4.9 %collective-permute-start = (bf16[4,256,256]{2,1,0:T(8,128)(2,1)}, bf16[4,256,256]{2,1,0:T(8,128)(2,1)S(1)}, u32[]{:S(2)}, u32[]{:S(2)}) collective-permute-start(bf16[4,256,256]{2,1,0:T(8,128)(2,1)} %shard_map.60), channel_id=1, source_target_pairs={{0,1},{1,2},{2,3},{3,4},{4,5},{5,6},{6,7},{7,8},{8,9},{9,10},{10,1... | collective-permute-start | bytes 1572872 | tf_op jit(solution)/shard_map/ppermute | solution.py:20
  21.4 0.0 copy-done.3
  21.5 0.0 slice-done
  21.5 1.6 copy.26
  23.1 1.3 copy.27
  24.4 4.4 %shard_map.59 = f32[4,256,256]{2,1,0:T(8,128)} custom-call(bf16[256,2304]{1,0:T(8,128)(2,1)} %bitcast.87, bf16[2048,256]{1,0:T(8,128)(2,1)} %bitcast.90, bf16[2048,256]{1,0:T(8,128)(2,1)} %bitcast.89), custom_call_target="tpu_custom_call" | custom-call | flops 1207959552 | bytes 4718592 | tf_op jit(solution)/shard_map/pallas_call | solution.py:85
  28.8 0.0 collective-permute-done
  28.8 0.0 copy-start.2
  28.9 1.8 %add_convert_fusion = bf16[4,256,256]{2,1,0:T(8,128)(2,1)S(1)} fusion(f32[4,256,256]{2,1,0:T(8,128)} %shard_map.59, bf16[4,256,256]{2,1,0:T(8,128)(2,1)S(1)} %collective-permute-done), kind=kLoop, calls=%fused_computation.11 | loop fusion | flops 2621440 | bytes 2097152 | tf_op jit(solution)/shard_map/convert_element_type | solution.py:243
  30.6 0.1 reshape.33
  30.8 0.2 copy.41
  31.0 0.0 copy-done.2
  31.0 0.9 reshape.34
  31.9 13.4 %all-to-all-start = ((bf16[64,16,256]{2,1,0:T(8,128)(2,1)}), bf16[64,16,256]{2,1,0:T(8,128)(2,1)S(1)}, u32[]{:S(2)}, u32[]{:S(2)}) async-start(bf16[64,16,256]{2,1,0:T(8,128)(2,1)} %reshape.34), calls=%async_computation | async-start | bytes 1048576 | tf_op jit(solution)/shard_map/all_to_all | solution.py:246
  45.5 0.1 maximum_bitcast_fusion
  45.6 0.1 pad_maximum_fusion
  45.7 0.1 copy.34
  45.8 0.7 reshape.37.w_ref
  46.6 52.7 %all-gather.3.cloned.1.call-done = bf16[1,512,32,256]{3,2,0,1:T(8,128)(2,1)} async-done(((bf16[1,8,32,256]{3,2,0,1:T(8,128)(2,1)}), bf16[1,512,32,256]{3,2,0,1:T(8,128)(2,1)}) %all-gather.3.cloned.1.call-update) | async-done | bytes 8388624 | tf_op jit(solution)/shard_map/all_gather | solution.py:239
  99.3 16.4 %copy.39 = bf16[64,8,32,256]{3,1,2,0:T(8,128)(2,1)} copy(bf16[64,8,32,256]{3,2,1,0:T(8,128)(2,1)} %bitcast.81) | data formatting | bytes 16777216
  115.7 14.5 %shard_map.62 = bf16[64,16,256]{2,1,0:T(8,128)(2,1)} custom-call(bf16[192,512]{1,0:T(8,128)(2,1)} %reshape.37.w_ref, bf16[512,8192]{1,0:T(8,128)(2,1)} %bitcast.79), custom_call_target="tpu_custom_call" | custom-call | flops 1610612736 | bytes 8388608 | tf_op jit(solution)/shard_map/pallas_call | solution.py:197
  130.2 0.0 all-to-all-done.hidden_ref
  130.2 5.8 %all-to-all-start.1 = ((bf16[64,16,256]{2,1,0:T(8,128)(2,1)}), bf16[64,16,256]{2,1,0:T(8,128)(2,1)S(1)}, u32[]{:S(2)}, u32[]{:S(2)}) async-start(bf16[64,16,256]{2,1,0:T(8,128)(2,1)} %shard_map.62), calls=%async_computation.1 | async-start | bytes 1048576 | tf_op jit(solution)/shard_map/all_to_all | solution.py:248
  136.0 0.0 copy-done.1
  136.0 10.0 %shard_map.61 = bf16[108,512]{1,0:T(8,128)(2,1)} custom-call(bf16[64,16,256]{2,1,0:T(8,128)(2,1)} %copy-done.1, bf16[512,8192]{1,0:T(8,128)(2,1)} %bitcast.80), custom_call_target="tpu_custom_call" | custom-call | flops 1610612736 | bytes 8388608 | tf_op jit(solution)/shard_map/pallas_call | solution.py:156
  146.0 2.4 %collective-permute-start.3 = (bf16[108,512]{1,0:T(8,128)(2,1)}, bf16[108,512]{1,0:T(8,128)(2,1)S(1)}, u32[]{:S(2)}, u32[]{:S(2)}) collective-permute-start(bf16[108,512]{1,0:T(8,128)(2,1)} %shard_map.61), channel_id=1, source_target_pairs={{0,192},{64,0},{128,64},{192,128},{1,193},{65,1},{129,65},{193,129... | collective-permute-start | bytes 331784 | tf_op jit(solution)/shard_map/ppermute | solution.py:25
  148.4 0.0 collective-permute-start.2
  148.4 1.7 %collective-permute-start.1 = (bf16[108,512]{1,0:T(8,128)(2,1)}, bf16[108,512]{1,0:T(8,128)(2,1)S(1)}, u32[]{:S(2)}, u32[]{:S(2)}) collective-permute-start(bf16[108,512]{1,0:T(8,128)(2,1)} %shard_map.61), channel_id=1, source_target_pairs={{0,128},{64,192},{128,0},{192,64},{1,129},{65,193},{129,1},{193,65... | collective-permute-start | bytes 331784 | tf_op jit(solution)/shard_map/ppermute | solution.py:25
  150.2 0.6 collective-permute-done.3
  150.8 5.9 %collective-permute-done.2 = bf16[108,512]{1,0:T(8,128)(2,1)S(1)} collective-permute-done((bf16[108,512]{1,0:T(8,128)(2,1)}, bf16[108,512]{1,0:T(8,128)(2,1)S(1)}, u32[]{:S(2)}, u32[]{:S(2)}) %collective-permute-start.2) | collective-permute-done | bytes 110624 | tf_op jit(solution)/shard_map/ppermute | solution.py:25
  156.7 0.0 collective-permute-done.1
  156.7 1.0 add_add_fusion
  157.6 0.7 reshape.36
  158.4 0.0 all-to-all-done.1
  158.4 0.2 reshape.39
  158.7 0.0 copy-start
  158.7 0.2 copy.35
  158.9 0.4 reshape.38
  159.2 0.7 copy-done
  159.9 1.5 fusion.9
  161.4 1.2 copy.36
  (15 shorter events, 0.3 us)
Async XLA Ops:
  7.2 92.1 %all-gather.3.cloned.1.call-start = ((), (), s32[]{:S(2)}) async-start(), calls=%async_computation.2 | async-start | bytes 8519680 | tf_op jit(solution)/shard_map/all_gather | solution.py:239
  13.2 8.2 %copy-start.3 = (bf16[3,3,3,4,512]{4,3,2,1,0:T(4,128)(2,1)S(1)}, bf16[3,3,3,4,512]{4,3,2,1,0:T(4,128)(2,1)}, u32[]{:S(2)}) copy-start(bf16[3,3,3,4,512]{4,3,2,1,0:T(4,128)(2,1)} %param.6) | copy-start | bytes 331780
  13.2 8.3 %slice-start = ((bf16[3,3,3,128,256]{4,3,2,1,0:T(8,128)(2,1)}), bf16[2,3,3,128,256]{4,3,2,1,0:T(8,128)(2,1)S(1)}, s32[]{:S(2)}) async-start(bf16[3,3,3,128,256]{4,3,2,1,0:T(8,128)(2,1)} %param.5), calls=%async_computation.3 | async-start | bytes 2359296 | tf_op jit(solution)/shard_map/slice | solution.py:236
  16.4 12.4 %collective-permute-start = (bf16[4,256,256]{2,1,0:T(8,128)(2,1)}, bf16[4,256,256]{2,1,0:T(8,128)(2,1)S(1)}, u32[]{:S(2)}, u32[]{:S(2)}) collective-permute-start(bf16[4,256,256]{2,1,0:T(8,128)(2,1)} %shard_map.60), channel_id=1, source_target_pairs={{0,1},{1,2},{2,3},{3,4},{4,5},{5,6},{6,7},{7,8},{8,9},{9,10},{10,1... | collective-permute-start | bytes 1572872 | tf_op jit(solution)/shard_map/ppermute | solution.py:20
  28.8 2.1 %copy-start.2 = (bf16[4,256,256]{2,1,0:T(8,128)(2,1)}, bf16[4,256,256]{2,1,0:T(8,128)(2,1)S(1)}, u32[]{:S(2)}) copy-start(bf16[4,256,256]{2,1,0:T(8,128)(2,1)S(1)} %collective-permute-done) | copy-start | bytes 1572868
  31.9 98.3 %all-to-all-start = ((bf16[64,16,256]{2,1,0:T(8,128)(2,1)}), bf16[64,16,256]{2,1,0:T(8,128)(2,1)S(1)}, u32[]{:S(2)}, u32[]{:S(2)}) async-start(bf16[64,16,256]{2,1,0:T(8,128)(2,1)} %reshape.34), calls=%async_computation | async-start | bytes 1048576 | tf_op jit(solution)/shard_map/all_to_all | solution.py:246
  130.2 5.8 %copy-start.1 = (bf16[64,16,256]{2,1,0:T(8,128)(2,1)}, bf16[64,16,256]{2,1,0:T(8,128)(2,1)S(1)}, u32[]{:S(2)}) copy-start(bf16[64,16,256]{2,1,0:T(8,128)(2,1)S(1)} %all-to-all-done.hidden_ref) | copy-start | bytes 1572868
  130.2 28.2 %all-to-all-start.1 = ((bf16[64,16,256]{2,1,0:T(8,128)(2,1)}), bf16[64,16,256]{2,1,0:T(8,128)(2,1)S(1)}, u32[]{:S(2)}, u32[]{:S(2)}) async-start(bf16[64,16,256]{2,1,0:T(8,128)(2,1)} %shard_map.62), calls=%async_computation.1 | async-start | bytes 1048576 | tf_op jit(solution)/shard_map/all_to_all | solution.py:248
  146.0 4.8 %collective-permute-start.3 = (bf16[108,512]{1,0:T(8,128)(2,1)}, bf16[108,512]{1,0:T(8,128)(2,1)S(1)}, u32[]{:S(2)}, u32[]{:S(2)}) collective-permute-start(bf16[108,512]{1,0:T(8,128)(2,1)} %shard_map.61), channel_id=1, source_target_pairs={{0,192},{64,0},{128,64},{192,128},{1,193},{65,1},{129,65},{193,129... | collective-permute-start | bytes 331784 | tf_op jit(solution)/shard_map/ppermute | solution.py:25
  148.4 8.3 %collective-permute-start.2 = (bf16[108,512]{1,0:T(8,128)(2,1)}, bf16[108,512]{1,0:T(8,128)(2,1)S(1)}, u32[]{:S(2)}, u32[]{:S(2)}) collective-permute-start(bf16[108,512]{1,0:T(8,128)(2,1)} %shard_map.61), channel_id=1, source_target_pairs={{0,64},{64,128},{128,192},{192,0},{1,65},{65,129},{129,193},{193,1... | collective-permute-start | bytes 331784 | tf_op jit(solution)/shard_map/ppermute | solution.py:25
  148.4 8.3 %collective-permute-start.1 = (bf16[108,512]{1,0:T(8,128)(2,1)}, bf16[108,512]{1,0:T(8,128)(2,1)S(1)}, u32[]{:S(2)}, u32[]{:S(2)}) collective-permute-start(bf16[108,512]{1,0:T(8,128)(2,1)} %shard_map.61), channel_id=1, source_target_pairs={{0,128},{64,192},{128,0},{192,64},{1,129},{65,193},{129,1},{193,65... | collective-permute-start | bytes 331784 | tf_op jit(solution)/shard_map/ppermute | solution.py:25
  158.7 1.2 copy-start
Sparse Core Ops, SparseCore 0:
  10.7 88.5 all-gather.2

commit v2 on v1

--- a/solution.py
+++ b/solution.py
@@ -115,93 +115,91 @@
     return total
 
 
-def grad_kernel(row_len, hidden_ref, cot_ref, out_ref, rows_ref):
+def grad_kernel(row_len, hidden_ref, cot_ref, out_ref, even_ref, odd_ref):
     planes, group, cells = hidden_ref.shape
     steps = planes // 2
-    size = 4 * group
-    rows_ref[0:size, 0:cells] = jnp.zeros((size, cells), rows_ref.dtype)
-
-    def fill(s, carry):
-        here = pl.ds(pl.multiple_of(s * cells, cells), cells)
-        rows_ref[size : 2 * size, here] = spread(hidden_ref[2 * s], row_len)
-        odd = spread(hidden_ref[2 * s + 1], row_len)
-        rows_ref[2 * size : 3 * size, here] = odd
-
-        @pl.when(s + 1 < steps)
-        def _():
-            rows_ref[0:size, pl.ds(pl.multiple_of((s + 1) * cells, cells), cells)] = odd
-
-        return carry
-
-    lax.fori_loop(0, steps, fill, 0)
-    total = lax.dot_general(
-        rows_ref[...], cot_ref[...], (((1,), (1,)), ((), ())), preferred_element_type=jnp.float32
-    )
     own = group // 4
-    for depth_tap in range(3):
+    for s in range(steps):
+        here = slice(s * cells, (s + 1) * cells)
+        even_ref[:, here] = spread(hidden_ref[2 * s], row_len)
+        odd_ref[:, here] = spread(hidden_ref[2 * s + 1], row_len)
+    over_cells = (((1,), (1,)), ((), ()))
+    sources = ((odd_ref, cells), (even_ref, 0), (odd_ref, 0))
+    for depth_tap, (rows_ref, start) in enumerate(sources):
+        total = lax.dot_general(
+            rows_ref[...],
+            cot_ref[:, start : start + steps * cells],
+            over_cells,
+            preferred_element_type=jnp.float32,
+        )
         for row_tap in range(3):
             for col_tap in range(3):
-                start = (
-                    depth_tap * size
-                    + (2 * int(row_tap == 0) + int(col_tap == 0)) * group
-                    + (2 * int(row_tap != 1) + int(col_tap != 1)) * own
-                )
-                put = ((depth_tap * 3 + row_tap) * 3 + col_tap) * own
-                out_ref[put : put + own, :] = total[start : start + own, :].astype(out_ref.dtype)
+                at = (2 * int(row_tap == 0) + int(col_tap == 0)) * group
+                at += (2 * int(row_tap != 1) + int(col_tap != 1)) * own
+                put = (depth_tap * 3 + row_tap) * 3 + col_tap
+                out_ref[put] = total[at : at + own, :].astype(out_ref.dtype)
 
 
 def grad(hidden, cot, dtype, row_len):
     planes, group, cells = hidden.shape
     outs = cot.shape[0]
+    rows = pltpu.VMEM((4 * group, planes // 2 * cells), jnp.bfloat16)
     return pl.pallas_call(
         functools.partial(grad_kernel, row_len),
-        out_shape=jax.ShapeDtypeStruct((27 * group // 4, outs), dtype),
-        scratch_shapes=[pltpu.VMEM((12 * group, planes // 2 * cells), jnp.bfloat16)],
+        out_shape=jax.ShapeDtypeStruct((27, group // 4, outs), dtype),
+        scratch_shapes=[rows, rows],
         cost_estimate=pl.CostEstimate(
             flops=12 * group * outs * planes * cells, bytes_accessed=2 * cot.size, transcendentals=0
         ),
     )(hidden, cot)
 
 
-def back_kernel(row_len, w_ref, cot_ref, out_ref, terms_ref):
+def back_kernel(row_len, place_ref, w_ref, mine_ref, theirs_ref, out_ref, cot_ref):
     planes, group, cells = out_ref.shape
-    steps = planes // 2
+    ring, rows_y, unit, half = mine_ref.shape
+    z, core = place_ref[0], place_ref[1]
+    here = pl.ds(pl.multiple_of(core * half, 128), half)
+    there = pl.ds(pl.multiple_of((1 - core) * half, 128), half)
+    for k in range(ring):
+        for y in range(rows_y):
+            row = y * ring * unit + lax.rem(z + k, ring) * unit
+            rows = pl.ds(pl.multiple_of(row, unit), unit)
+            cot_ref[rows, here] = mine_ref[k, y]
+            cot_ref[rows, there] = theirs_ref[k, y]
     size = 4 * group
 
-    def multiply(s, carry):
-        here = pl.ds(pl.multiple_of(s * cells, cells), cells)
-        terms_ref[:, here] = jnp.dot(
-            w_ref[...], cot_ref[:, here], preferred_element_type=jnp.float32
+    def one(at, start):
+        return jnp.dot(
+            w_ref[at * size : (at + 1) * size, :],
+            cot_ref[:, start : start + cells],
+            preferred_element_type=jnp.float32,
         )
-        return carry
-
-    lax.fori_loop(0, steps, multiply, 0)
-
-    def combine(s, carry):
-        here = pl.ds(pl.multiple_of(s * cells, cells), cells)
-        out_ref[2 * s] = gather_back(terms_ref[size : 2 * size, here], row_len).astype(out_ref.dtype)
-        after = jnp.minimum(s + 1, steps - 1)
-        next_one = pl.ds(pl.multiple_of(after * cells, cells), cells)
-        extra = jnp.where(s + 1 < steps, terms_ref[0:size, next_one], 0.0)
-        odd = terms_ref[2 * size : 3 * size, here] + extra
+
+    for s in range(planes // 2):
+        start = s * cells
+        out_ref[2 * s] = gather_back(one(1, start), row_len).astype(out_ref.dtype)
+        odd = one(2, start) + one(0, start + cells)
         out_ref[2 * s + 1] = gather_back(odd, row_len).astype(out_ref.dtype)
-        return carry
-
-    lax.fori_loop(0, steps, combine, 0)
-
-
-def back(w_rows, cot, planes, row_len):
+
+
+def back(place, w_rows, mine, theirs, planes, row_len):
     rows, outs = w_rows.shape
     group = rows // 12
-    cells = 2 * cot.shape[1] // planes
+    width = 2 * mine.shape[3]
+    cells = width // (planes // 2 + 1)
+    vmem = pl.BlockSpec(memory_space=pltpu.VMEM)
     return pl.pallas_call(
         functools.partial(back_kernel, row_len),
-        out_shape=jax.ShapeDtypeStruct((planes, group, cells), jnp.bfloat16),
-        scratch_shapes=[pltpu.VMEM((rows, cot.shape[1]), jnp.float32)],
+        out_shape=(
+            jax.ShapeDtypeStruct((planes, group, cells), jnp.bfloat16),
+            jax.ShapeDtypeStruct((outs, width), jnp.bfloat16),
+        ),
+        in_specs=[pl.BlockSpec(memory_space=pltpu.SMEM), vmem, vmem, vmem],
+        out_specs=(vmem, vmem),
         cost_estimate=pl.CostEstimate(
-            flops=2 * rows * cot.size, bytes_accessed=2 * cot.size, transcendentals=0
+            flops=rows * outs * planes * cells, bytes_accessed=4 * outs * width, transcendentals=0
         ),
-    )(w_rows, cot)
+    )(place, w_rows, mine, theirs)
 
 
 def move_rows(w_second):
@@ -222,37 +220,92 @@
     return rows.reshape(-1, w_second.shape[-1])
 
 
+ROWS, RING, CORES = 4, 8, 2
+
+
+def on_space(block, y_by=0, z_by=0, core_by=0):
+    route = []
+    for y in range(ROWS):
+        for z in range(RING):
+            for core in range(CORES):
+                to = ((y + y_by) % ROWS, (z + z_by) % RING, (core + core_by) % CORES)
+                route.append(((y * RING + z) * CORES + core, (to[0] * RING + to[1]) * CORES + to[2]))
+    return lax.ppermute(block, "space", route)
+
+
+COLUMNS = [[y * RING * CORES + g for y in range(ROWS)] for g in range(RING * CORES)]
+SLABS = [[y * RING * CORES + g for g in range(RING * CORES)] for y in range(ROWS)]
+
+
+def exchange(blocks, groups):
+    return lax.all_to_all(
+        blocks, "space", split_axis=0, concat_axis=0, axis_index_groups=groups, tiled=True
+    )
+
+
 def per_device(volume, w_first, w_second, cotangent):
     channels = volume.shape[1]
-    cell_count = volume.shape[4]
+    cells = volume.shape[4]
     out_channels = w_first.shape[4]
+    own = w_second.shape[3]
     row_len = WID // 4
-    members = lax.axis_size("space")
-    own_channels = out_channels // members
-    planes = volume[0].reshape(channels, 2, 16, cell_count).transpose(1, 2, 0, 3)
-    planes = planes.reshape(2, 16 * channels, cell_count)
+    me = lax.axis_index("space")
+    core, z = me % CORES, me // CORES % RING
+    group = RING * CORES
+
+    depth = cotangent.shape[2]
+    share = depth // ROWS
+    local = jnp.pad(cotangent[0], ((0, 0), (0, 1), (0, 0)))
+    parts = jnp.stack([local[:, y * share : (y + 1) * share + 1] for y in range(ROWS)])
+    parts = parts.reshape(ROWS, -1, (share + 1) * cells)
+    half = (share + 1) * cells // 2
+    low, high = parts[:, :, :half], parts[:, :, half:]
+    kept = jnp.where(core == 0, low, high)
+    other = on_space(jnp.where(core == 0, high, low), core_by=1)
+    unit = jnp.concatenate(
+        [jnp.where(core == 0, kept, other), jnp.where(core == 0, other, kept)], 1
+    )
+    first = exchange(unit, COLUMNS)
+    up, down = [first], [first]
+    for _ in range(3):
+        up.append(on_space(up[-1], z_by=1))
+        down.append(on_space(down[-1], z_by=-1))
+    far = jnp.concatenate(
+        [on_space(up[3][: ROWS // 2], z_by=1), on_space(down[3][ROWS // 2 :], z_by=-1)], 0
+    )
+    mine = jnp.stack(down + [far] + up[:0:-1])
+    theirs = on_space(mine, core_by=1)
+
+    w_all = exchange(jnp.broadcast_to(w_second, (ROWS,) + w_second.shape), COLUMNS)
+    w_group = w_all.transpose(1, 2, 3, 0, 4, 5).reshape(3, 3, 3, ROWS * own, C3)
+
+    planes = volume[0].reshape(channels, 2, 16, cells).transpose(1, 2, 0, 3)
+    planes = planes.reshape(2, 16 * channels, cells)
     w_rows = w_first.reshape(27 * channels, out_channels)
     w_before = w_rows[: 9 * channels].T
     w_here = w_rows[9 * channels :].T
     ahead = conv(w_before, [planes[1]], jnp.bfloat16, row_len)
     behind = from_behind(ahead, "space", 1)
-    gathered = lax.all_gather(cotangent[0], "space", axis=0, tiled=True)
-    cot_flat = gathered.reshape(C3, -1)
     pre_act = conv(w_here, [planes[0], planes[1]], jnp.float32, row_len)
     pre_act = pre_act + behind.astype(jnp.float32)
     hidden = activate(pre_act).astype(jnp.bfloat16)
-    blocks = hidden.reshape(4, members, own_channels, cell_count).transpose(1, 0, 2, 3)
-    blocks = blocks.reshape(members, 4 * own_channels, cell_count)
-    by_plane = lax.all_to_all(blocks, "space", split_axis=0, concat_axis=0, tiled=True)
-    back_terms = back(move_rows(w_second), cot_flat, members, row_len)
-    hidden_grad = lax.all_to_all(back_terms, "space", split_axis=0, concat_axis=0, tiled=True)
-    partial = grad(by_plane, cot_flat, jnp.bfloat16, row_len)
+    blocks = hidden.reshape(4, ROWS, group, own, cells).transpose(2, 0, 1, 3, 4)
+    by_plane = exchange(blocks.reshape(group, 4 * ROWS * own, cells), SLABS)
+
+    place = jnp.stack([z, core]).astype(jnp.int32)
+    back_terms, cot_row = back(place, move_rows(w_group), mine, theirs, group, row_len)
+    hidden_grad = exchange(back_terms, SLABS)
+
+    partial = grad(by_plane, cot_row, jnp.bfloat16, row_len)
+    partial = partial.reshape(27, ROWS, own, C3).transpose(1, 0, 2, 3).reshape(ROWS, 27 * own, C3)
+    partial = jnp.sum(exchange(partial, COLUMNS).astype(jnp.float32), 0).astype(jnp.bfloat16)
     sides = [from_side(partial, "dp", distance) for distance in (1, 2, 3)]
     left, opposite, right = [side.astype(jnp.float32) for side in sides]
     grad_second = (partial.astype(jnp.float32) + opposite) + (left + right)
-    grad_second = grad_second.reshape(3, 3, 3, own_channels, C3)
-    hidden_grad = hidden_grad.reshape(members, 4, own_channels, cell_count).transpose(0, 2, 1, 3)
-    hidden_grad = hidden_grad.reshape(out_channels, 4, cell_count).astype(jnp.float32)
+    grad_second = grad_second.reshape(3, 3, 3, own, C3)
+
+    hidden_grad = hidden_grad.reshape(group, 4, ROWS, own, cells).transpose(2, 0, 3, 1, 4)
+    hidden_grad = hidden_grad.reshape(out_channels, 4, cells).astype(jnp.float32)
     slopes = slope_of(pre_act.transpose(1, 0, 2))
     pre_grad = (hidden_grad * slopes).astype(jnp.bfloat16)
     return (grad_second, pre_grad[None, :, None])

time: 170 us -> 140 us (0.82)
  waiting for transfers between devices: 59.9 us -> 39.5 us
  starting transfers between devices: 28.3 us -> 44.7 us
  Pallas kernels: 32.1 us -> 16.8 us
  between operations: 14.3 us -> 1.03 us
  blocking collectives: 0 us -> 10.7 us
  local copies, waits for them, and re-layouts: 30.2 us -> 22.5 us
    all_gather x1 -> x0, waiting for transfers between devices: 52.7 us -> none  [per_device(): gathered = lax.all_gather(cotangent[0], 'space', axis=0, tiled=True)]
    all_to_all x2 -> x4, waiting for transfers between devices: 0.01 us -> 27.6 us  [exchange(): lax.all_to_all(blocks, 'space', split_axis=0, concat_axis=0, axis_index_g...]
    ppermute x0 -> x10, starting transfers between devices: none -> 20.5 us  [on_space(): return lax.ppermute(block, 'space', route)]
    all_to_all x0 -> x1, blocking collectives: none -> 10.7 us  [exchange(): lax.all_to_all(blocks, 'space', split_axis=0, concat_axis=0, axis_index_g...]
    unnamed x10 -> x17, local copies, waits for them, and re-layouts: 18.3 us -> 8.21 us
    pallas_call x1, Pallas kernels: 14.5 us -> 4.78 us  [back(): pl.pallas_call(functools.partial(back_kernel, row_len), out_shape=(jax.Sh...]
    ppermute x0 -> x10, waiting for transfers between devices: none -> 8.5 us  [on_space(): return lax.ppermute(block, 'space', route)]
    pallas_call x1, Pallas kernels: 9.99 us -> 4.47 us  [grad(): pl.pallas_call(functools.partial(grad_kernel, row_len), out_shape=jax.Sha...]
  transfers between devices with their start and end apart: 7 -> 18, of which waited for: 3 -> 9; matrix products, arithmetic and copies ran while one was open for 18% -> 13% of each run, Pallas kernels for 19% -> 9%
where the time goes in v2:
time: 140 us
  starting transfers between devices  44.7 us (32%)
  waiting for transfers between devices  39.5 us (28%)
  local copies, waits for them, and re-layouts  22.5 us (16%)
  Pallas kernels  16.8 us (12%)
  blocking collectives  10.7 us (8%)
  other arithmetic  4.25 us (3%)
    all_to_all x4, waiting for transfers between devices, exchange(): lax.all_to_all(blocks, 'space', split_axis=0, concat_axis=0, axis_index_g...  27.6 us
    ppermute x10, starting transfers between devices, on_space(): return lax.ppermute(block, 'space', route)  20.5 us
    all_to_all x4, starting transfers between devices, exchange(): lax.all_to_all(blocks, 'space', split_axis=0, concat_axis=0, axis_index_g...  16.8 us
    all_to_all x1, blocking collectives, exchange(): lax.all_to_all(blocks, 'space', split_axis=0, concat_axis=0, axis_index_g...  10.7 us
    ppermute x10, waiting for transfers between devices, on_space(): return lax.ppermute(block, 'space', route)  8.5 us
    unnamed x17, local copies, waits for them, and re-layouts  8.21 us
    pallas_call x2, Pallas kernels, conv(): pl.pallas_call(functools.partial(conv_kernel, tuple(range(count)), channe...  7.52 us
    ppermute x3, starting transfers between devices, from_side(): lax.ppermute(block, axis, [(i, (i + distance) % size) for i in range(size)])  5.5 us
  transfers between devices with their start and end apart: 18, of which 9 were waited for; matrix products, arithmetic and copies ran while one was open for 13% of the time, Pallas kernels for 9%

profile of v2, /device:TPU:1, one launch (start us, length us, event | category | flops | bytes accessed | tf_op | source)
XLA Modules:
  0.0 139.5 jit_solution(2308474585908567507)
XLA Ops:
  0.6 1.0 copy.61
  1.7 3.3 %collective-permute-start.1 = (bf16[4,8,1152]{2,1,0:T(8,128)(2,1)S(1)}, bf16[4,8,1152]{2,1,0:T(8,128)(2,1)S(1)}, u32[]{:S(2)}, u32[]{:S(2)}) collective-permute-start(bf16[4,8,1152]{2,1,0:T(8,128)(2,1)S(1)} %broadcast_select_fusion.2), channel_id=1, source_target_pairs={{0,1},{1,0},{2,3},{3,2},{4,5},{5,4},{6,7},{7,6},{8,9},{9,8},{10,11... | collective-permute-start | bytes 221192 | tf_op jit(solution)/shard_map/ppermute | solution.py:233
  5.0 1.7 %fusion.11 = (bf16[1,16,128,256]{3,1,0,2:T(8,128)(2,1)S(1)}, bf16[1,16,128,256]{3,1,0,2:T(8,128)(2,1)S(1)}) fusion(bf16[2,16,128,256]{3,1,0,2:T(8,128)(2,1)} %bitcast.109), kind=kLoop, calls=%fused_computation.49 | loop fusion | bytes 4194304 | tf_op jit(solution)/shard_map/slice | solution.py:289
  6.7 1.3 copy.43
  8.1 1.1 copy.44
  9.1 3.2 %shard_map.60 = bf16[4,256,256]{2,1,0:T(8,128)(2,1)} custom-call(bf16[256,1152]{1,0:T(8,128)(2,1)} %bitcast.119, bf16[2048,256]{1,0:T(8,128)(2,1)} %bitcast.115), custom_call_target="tpu_custom_call" | custom-call | flops 603979776 | bytes 2359296 | tf_op jit(solution)/shard_map/pallas_call | solution.py:85
  12.3 1.9 %collective-permute-start = (bf16[4,256,256]{2,1,0:T(8,128)(2,1)}, bf16[4,256,256]{2,1,0:T(8,128)(2,1)S(1)}, u32[]{:S(2)}, u32[]{:S(2)}) collective-permute-start(bf16[4,256,256]{2,1,0:T(8,128)(2,1)} %shard_map.60), channel_id=1, source_target_pairs={{0,1},{1,2},{2,3},{3,4},{4,5},{5,6},{6,7},{7,8},{8,9},{9,10},{10,1... | collective-permute-start | bytes 1572872 | tf_op jit(solution)/shard_map/ppermute | solution.py:20
  14.2 0.9 copy-done.3
  15.2 1.3 copy.42
  16.5 1.6 %copy.41 = bf16[2304,256]{0,1:T(8,128)(2,1)} copy(bf16[2304,256]{1,0:T(8,128)(2,1)S(1)} %bitcast.107) | data formatting | bytes 2359296 | tf_op jit(solution)/shard_map/slice | solution.py:286
  18.1 4.4 %shard_map.59 = f32[4,256,256]{2,1,0:T(8,128)} custom-call(bf16[256,2304]{1,0:T(8,128)(2,1)} %bitcast.113, bf16[2048,256]{1,0:T(8,128)(2,1)} %bitcast.117, bf16[2048,256]{1,0:T(8,128)(2,1)} %bitcast.116), custom_call_target="tpu_custom_call" | custom-call | flops 1207959552 | bytes 4718592 | tf_op jit(solution)/shard_map/pallas_call | solution.py:85
  22.5 0.7 pad_maximum_fusion.2
  23.1 4.0 %all-to-all-start.2 = ((bf16[4,16,1152]{2,1,0:T(8,128)(2,1)}), bf16[4,16,1152]{2,1,0:T(8,128)(2,1)S(1)}, u32[]{:S(2)}, u32[]{:S(2)}) async-start(bf16[4,16,1152]{2,1,0:T(8,128)(2,1)} %pad_maximum_fusion.2), calls=%async_computation.2 | async-start | bytes 294912 | tf_op jit(solution)/shard_map/all_to_all | solution.py:241
  27.8 5.0 %all-to-all-done.2 = bf16[4,16,1152]{2,1,0:T(8,128)(2,1)S(1)} async-done(((bf16[4,16,1152]{2,1,0:T(8,128)(2,1)}), bf16[4,16,1152]{2,1,0:T(8,128)(2,1)S(1)}, u32[]{:S(2)}, u32[]{:S(2)}) %all-to-all-start.2) | async-done | bytes 147488 | tf_op jit(solution)/shard_map/all_to_all | solution.py:241
  32.9 0.9 broadcast_in_dim.6
  33.7 3.5 %all-to-all-start.1 = ((bf16[4,3,3,3,4,512]{5,4,3,1,2,0:T(4,128)(2,1)}), bf16[4,3,3,3,4,512]{5,4,3,1,2,0:T(4,128)(2,1)S(1)}, u32[]{:S(2)}, u32[]{:S(2)}) async-start(bf16[4,3,3,3,4,512]{5,4,3,1,2,0:T(4,128)(2,1)} %broadcast_in_dim.6), calls=%async_computation.1 | async-start | bytes 884736 | tf_op jit(solution)/shard_map/all_to_all | solution.py:241
  37.2 3.3 %collective-permute-start.2 = (bf16[4,16,1152]{2,1,0:T(8,128)(2,1)S(1)}, bf16[4,16,1152]{2,1,0:T(8,128)(2,1)S(1)}, u32[]{:S(2)}, u32[]{:S(2)}) collective-permute-start(bf16[4,16,1152]{2,1,0:T(8,128)(2,1)S(1)} %all-to-all-done.2), channel_id=1, source_target_pairs={{0,14},{1,15},{2,0},{3,1},{4,2},{5,3},{6,4},{7,5},{8,6},{9,7},{10,... | collective-permute-start | bytes 442376 | tf_op jit(solution)/shard_map/ppermute | solution.py:233
  40.5 0.7 bitcast_dynamic-update-slice_fusion.6
  41.2 4.0 %all-to-all-done.1 = bf16[4,3,3,3,4,512]{5,4,3,1,2,0:T(4,128)(2,1)S(1)} async-done(((bf16[4,3,3,3,4,512]{5,4,3,1,2,0:T(4,128)(2,1)}), bf16[4,3,3,3,4,512]{5,4,3,1,2,0:T(4,128)(2,1)S(1)}, u32[]{:S(2)}, u32[]{:S(2)}) %all-to-all-start.1) | async-done | bytes 442400 | tf_op jit(solution)/shard_map/all_to_all | solution.py:241
  45.7 1.8 %collective-permute-start.3 = (bf16[4,16,1152]{2,1,0:T(8,128)(2,1)S(1)}, bf16[4,16,1152]{2,1,0:T(8,128)(2,1)S(1)}, u32[]{:S(2)}, u32[]{:S(2)}) collective-permute-start(bf16[4,16,1152]{2,1,0:T(8,128)(2,1)S(1)} %collective-permute-done.2), channel_id=1, source_target_pairs={{0,14},{1,15},{2,0},{3,1},{4,2},{5,3},{6,4},{7,5},{8,6},{9,7},{10,... | collective-permute-start | bytes 442376 | tf_op jit(solution)/shard_map/ppermute | solution.py:233
  48.2 1.7 %collective-permute-done.3 = bf16[4,16,1152]{2,1,0:T(8,128)(2,1)S(1)} collective-permute-done((bf16[4,16,1152]{2,1,0:T(8,128)(2,1)S(1)}, bf16[4,16,1152]{2,1,0:T(8,128)(2,1)S(1)}, u32[]{:S(2)}, u32[]{:S(2)}) %collective-permute-start.3) | collective-permute-done | bytes 147488 | tf_op jit(solution)/shard_map/ppermute | solution.py:233
  49.9 2.8 %collective-permute-start.4 = (bf16[4,16,1152]{2,1,0:T(8,128)(2,1)S(1)}, bf16[4,16,1152]{2,1,0:T(8,128)(2,1)S(1)}, u32[]{:S(2)}, u32[]{:S(2)}) collective-permute-start(bf16[4,16,1152]{2,1,0:T(8,128)(2,1)S(1)} %collective-permute-done.3), channel_id=1, source_target_pairs={{0,14},{1,15},{2,0},{3,1},{4,2},{5,3},{6,4},{7,5},{8,6},{9,7},{10,... | collective-permute-start | bytes 442376 | tf_op jit(solution)/shard_map/ppermute | solution.py:233
  53.4 4.7 %collective-permute-done.7 = bf16[4,16,1152]{2,1,0:T(8,128)(2,1)S(1)} collective-permute-done((bf16[4,16,1152]{2,1,0:T(8,128)(2,1)S(1)}, bf16[4,16,1152]{2,1,0:T(8,128)(2,1)S(1)}, u32[]{:S(2)}, u32[]{:S(2)}) %collective-permute-start.7) | collective-permute-done | bytes 147488 | tf_op jit(solution)/shard_map/ppermute | solution.py:233
  58.1 2.7 %collective-permute-start.9 = (bf16[2,16,1152]{2,1,0:T(8,128)(2,1)S(1)}, bf16[2,16,1152]{2,1,0:T(8,128)(2,1)S(1)}, u32[]{:S(2)}, u32[]{:S(2)}) collective-permute-start(bf16[2,16,1152]{2,1,0:T(8,128)(2,1)S(1)} %slice.109), channel_id=1, source_target_pairs={{0,14},{1,15},{2,0},{3,1},{4,2},{5,3},{6,4},{7,5},{8,6},{9,7},{10,... | collective-permute-start | bytes 221192 | tf_op jit(solution)/shard_map/ppermute | solution.py:233
  60.9 0.7 bitcast_dynamic-update-slice_fusion.3
  61.6 2.1 %collective-permute-done.8 = bf16[2,16,1152]{2,1,0:T(8,128)(2,1)S(1)} collective-permute-done((bf16[2,16,1152]{2,1,0:T(8,128)(2,1)S(1)}, bf16[2,16,1152]{2,1,0:T(8,128)(2,1)S(1)}, u32[]{:S(2)}, u32[]{:S(2)}) %collective-permute-start.8) | collective-permute-done | bytes 73760 | tf_op jit(solution)/shard_map/ppermute | solution.py:233
  63.6 0.7 fusion.10
  64.3 0.7 bitcast_dynamic-update-slice_fusion.2
  65.0 0.7 bitcast_dynamic-update-slice_fusion.1
  66.3 6.5 %collective-permute-start.10 = (bf16[8,4,16,1152]{3,2,1,0:T(8,128)(2,1)}, bf16[8,4,16,1152]{3,2,1,0:T(8,128)(2,1)}, u32[]{:S(2)}, u32[]{:S(2)}) collective-permute-start(bf16[8,4,16,1152]{3,2,1,0:T(8,128)(2,1)} %bitcast_dynamic-update-slice_fusion.mine_ref), channel_id=1, source_target_pairs={{0,1},{1,0},{2,3},{3,2},{4,5},{5,4},{6,7},{7,6},{8,9},{9,8},{10,11... | collective-permute-start | bytes 3538952 | tf_op jit(solution)/shard_map/ppermute | solution.py:233
  73.9 0.9 reshape.49
  74.8 5.3 %all-to-all-start = ((bf16[16,64,256]{2,1,0:T(8,128)(2,1)}), bf16[16,64,256]{2,1,0:T(8,128)(2,1)S(1)}, u32[]{:S(2)}, u32[]{:S(2)}) async-start(bf16[16,64,256]{2,1,0:T(8,128)(2,1)} %reshape.49), calls=%async_computation | async-start | bytes 1048576 | tf_op jit(solution)/shard_map/all_to_all | solution.py:241
  80.4 1.0 copy.50
  81.4 4.8 %shard_map.61 = (bf16[16,64,256]{2,1,0:T(8,128)(2,1)}, bf16[512,2304]{1,0:T(8,128)(2,1)}) custom-call(s32[2]{0:T(128)} %pad_add_fusion.place_ref, bf16[768,512]{1,0:T(8,128)(2,1)} %bitcast.118, bf16[8,4,16,1152]{3,2,1,0:T(8,128)(2,1)} %bitcast_dynamic-update-slice_fusion.mine_ref, bf16[8,4,16,1152]{3,2,1,0:T(8,128)(2,1)} %collective-permute-done.10.theirs_ref), custom_call_target="tpu_custom_call" | custom-call | flops 1610612736 | bytes 4718592 | tf_op jit(solution)/shard_map/pallas_call | solution.py:191
  86.1 11.2 %all-to-all-done.hidden_ref = bf16[16,64,256]{2,1,0:T(8,128)(2,1)S(1)} async-done(((bf16[16,64,256]{2,1,0:T(8,128)(2,1)}), bf16[16,64,256]{2,1,0:T(8,128)(2,1)S(1)}, u32[]{:S(2)}, u32[]{:S(2)}) %all-to-all-start) | async-done | bytes 524320 | tf_op jit(solution)/shard_map/all_to_all | solution.py:241
  97.3 0.8 copy-done.2
  98.1 4.5 %shard_map.62 = bf16[27,16,512]{2,1,0:T(8,128)(2,1)} custom-call(bf16[16,64,256]{2,1,0:T(8,128)(2,1)} %copy-done.2, bf16[512,2304]{1,0:T(8,128)(2,1)} %get-tuple-element.4.cot_ref), custom_call_target="tpu_custom_call" | custom-call | flops 1610612736 | bytes 2359296 | tf_op jit(solution)/shard_map/pallas_call | solution.py:147
  102.6 1.1 reshape.52
  104.0 10.7 %all_to_all.25 = bf16[4,108,512]{2,1,0:T(8,128)(2,1)S(1)} all-to-all(bf16[4,108,512]{2,1,0:T(8,128)(2,1)S(1)} %copy.53), channel_id=1, replica_groups={{0,16,32,48},{1,17,33,49},{2,18,34,50},{3,19,35,51},{4,20,36,52},{5,21,..., dimensions={0} | all-to-all | bytes 884736 | tf_op jit(solution)/shard_map/all_to_all | solution.py:241
  114.7 4.0 %all-to-all-start.4 = ((bf16[16,64,256]{2,1,0:T(8,128)(2,1)}), bf16[16,64,256]{2,1,0:T(8,128)(2,1)S(1)}, u32[]{:S(2)}, u32[]{:S(2)}) async-start(bf16[16,64,256]{2,1,0:T(8,128)(2,1)} %get-tuple-element.5), calls=%async_computation.4 | async-start | bytes 1048576 | tf_op jit(solution)/shard_map/all_to_all | solution.py:241
  118.8 2.8 %collective-permute-start.11 = (bf16[108,512]{1,0:T(8,128)(2,1)S(1)}, bf16[108,512]{1,0:T(8,128)(2,1)S(1)}, u32[]{:S(2)}, u32[]{:S(2)}) collective-permute-start(bf16[108,512]{1,0:T(8,128)(2,1)S(1)} %reduce_sum.12), channel_id=1, source_target_pairs={{0,128},{64,192},{128,0},{192,64},{1,129},{65,193},{129,1},{193,65... | collective-permute-start | bytes 331784 | tf_op jit(solution)/shard_map/ppermute | solution.py:25
  121.9 2.4 %collective-permute-start.13 = (bf16[108,512]{1,0:T(8,128)(2,1)S(1)}, bf16[108,512]{1,0:T(8,128)(2,1)S(1)}, u32[]{:S(2)}, u32[]{:S(2)}) collective-permute-start(bf16[108,512]{1,0:T(8,128)(2,1)S(1)} %reduce_sum.12), channel_id=1, source_target_pairs={{0,192},{64,0},{128,64},{192,128},{1,193},{65,1},{129,65},{193,129... | collective-permute-start | bytes 331784 | tf_op jit(solution)/shard_map/ppermute | solution.py:25
  124.3 0.7 collective-permute-done.11
  125.0 2.7 %collective-permute-done.12 = bf16[108,512]{1,0:T(8,128)(2,1)S(1)} collective-permute-done((bf16[108,512]{1,0:T(8,128)(2,1)S(1)}, bf16[108,512]{1,0:T(8,128)(2,1)S(1)}, u32[]{:S(2)}, u32[]{:S(2)}) %collective-permute-start.12) | collective-permute-done | bytes 110624 | tf_op jit(solution)/shard_map/ppermute | solution.py:25
  127.8 0.7 reshape.54
  128.5 7.4 %all-to-all-done.4 = bf16[16,64,256]{2,1,0:T(8,128)(2,1)S(1)} async-done(((bf16[16,64,256]{2,1,0:T(8,128)(2,1)}), bf16[16,64,256]{2,1,0:T(8,128)(2,1)S(1)}, u32[]{:S(2)}, u32[]{:S(2)}) %all-to-all-start.4) | async-done | bytes 524320 | tf_op jit(solution)/shard_map/all_to_all | solution.py:241
  136.8 1.5 %fusion.9 = bf16[1,256,1,4,256]{4,1,3,2,0:T(8,128)(2,1)S(1)} fusion(f32[256,4,256]{2,0,1:T(8,128)S(1)} %reshape.55, f32[4,256,256]{2,1,0:T(8,128)S(1)} %copy-done, bf16[4,256,256]{2,1,0:T(8,128)(2,1)} %copy-done.1), kind=kLoop, calls=%fused_computation.15 | loop fusion | flops 3407872 | bytes 3145728 | tf_op jit(solution)/shard_map/broadcast_in_dim | solution.py:311
  138.3 1.2 copy.55
  (61 shorter events, 6.1 us)
Async XLA Ops:
  1.7 20.7 %collective-permute-start.1 = (bf16[4,8,1152]{2,1,0:T(8,128)(2,1)S(1)}, bf16[4,8,1152]{2,1,0:T(8,128)(2,1)S(1)}, u32[]{:S(2)}, u32[]{:S(2)}) collective-permute-start(bf16[4,8,1152]{2,1,0:T(8,128)(2,1)S(1)} %broadcast_select_fusion.2), channel_id=1, source_target_pairs={{0,1},{1,0},{2,3},{3,2},{4,5},{5,4},{6,7},{7,6},{8,9},{9,8},{10,11... | collective-permute-start | bytes 221192 | tf_op jit(solution)/shard_map/ppermute | solution.py:233
  6.7 1.4 slice-start
  12.3 60.5 %collective-permute-start = (bf16[4,256,256]{2,1,0:T(8,128)(2,1)}, bf16[4,256,256]{2,1,0:T(8,128)(2,1)S(1)}, u32[]{:S(2)}, u32[]{:S(2)}) collective-permute-start(bf16[4,256,256]{2,1,0:T(8,128)(2,1)} %shard_map.60), channel_id=1, source_target_pairs={{0,1},{1,2},{2,3},{3,4},{4,5},{5,6},{6,7},{7,8},{8,9},{9,10},{10,1... | collective-permute-start | bytes 1572872 | tf_op jit(solution)/shard_map/ppermute | solution.py:20
  14.2 0.9 copy-start.3
  14.2 2.3 %slice-start.1 = ((bf16[3,3,3,128,256]{4,3,2,1,0:T(8,128)(2,1)}), bf16[2,3,3,128,256]{4,3,2,1,0:T(8,128)(2,1)S(1)}, s32[]{:S(2)}) async-start(bf16[3,3,3,128,256]{4,3,2,1,0:T(8,128)(2,1)} %param.5), calls=%async_computation.6 | async-start | bytes 2359296 | tf_op jit(solution)/shard_map/slice | solution.py:286
  23.1 9.7 %all-to-all-start.2 = ((bf16[4,16,1152]{2,1,0:T(8,128)(2,1)}), bf16[4,16,1152]{2,1,0:T(8,128)(2,1)S(1)}, u32[]{:S(2)}, u32[]{:S(2)}) async-start(bf16[4,16,1152]{2,1,0:T(8,128)(2,1)} %pad_maximum_fusion.2), calls=%async_computation.2 | async-start | bytes 294912 | tf_op jit(solution)/shard_map/all_to_all | solution.py:241
  33.7 11.5 %all-to-all-start.1 = ((bf16[4,3,3,3,4,512]{5,4,3,1,2,0:T(4,128)(2,1)}), bf16[4,3,3,3,4,512]{5,4,3,1,2,0:T(4,128)(2,1)S(1)}, u32[]{:S(2)}, u32[]{:S(2)}) async-start(bf16[4,3,3,3,4,512]{5,4,3,1,2,0:T(4,128)(2,1)} %broadcast_in_dim.6), calls=%async_computation.1 | async-start | bytes 884736 | tf_op jit(solution)/shard_map/all_to_all | solution.py:241
  37.2 8.5 %collective-permute-start.2 = (bf16[4,16,1152]{2,1,0:T(8,128)(2,1)S(1)}, bf16[4,16,1152]{2,1,0:T(8,128)(2,1)S(1)}, u32[]{:S(2)}, u32[]{:S(2)}) collective-permute-start(bf16[4,16,1152]{2,1,0:T(8,128)(2,1)S(1)} %all-to-all-done.2), channel_id=1, source_target_pairs={{0,14},{1,15},{2,0},{3,1},{4,2},{5,3},{6,4},{7,5},{8,6},{9,7},{10,... | collective-permute-start | bytes 442376 | tf_op jit(solution)/shard_map/ppermute | solution.py:233
  40.5 7.0 %collective-permute-start.5 = (bf16[4,16,1152]{2,1,0:T(8,128)(2,1)S(1)}, bf16[4,16,1152]{2,1,0:T(8,128)(2,1)S(1)}, u32[]{:S(2)}, u32[]{:S(2)}) collective-permute-start(bf16[4,16,1152]{2,1,0:T(8,128)(2,1)S(1)} %all-to-all-done.2), channel_id=1, source_target_pairs={{0,2},{1,3},{2,4},{3,5},{4,6},{5,7},{6,8},{7,9},{8,10},{9,11},{10,... | collective-permute-start | bytes 442376 | tf_op jit(solution)/shard_map/ppermute | solution.py:233
  45.7 27.1 %copy-start = (f32[4,256,256]{2,1,0:T(8,128)S(1)}, f32[4,256,256]{2,1,0:T(8,128)}, u32[]{:S(2)}) copy-start(f32[4,256,256]{2,1,0:T(8,128)} %shard_map.59) | copy-start | bytes 3145732
  45.7 4.2 %collective-permute-start.3 = (bf16[4,16,1152]{2,1,0:T(8,128)(2,1)S(1)}, bf16[4,16,1152]{2,1,0:T(8,128)(2,1)S(1)}, u32[]{:S(2)}, u32[]{:S(2)}) collective-permute-start(bf16[4,16,1152]{2,1,0:T(8,128)(2,1)S(1)} %collective-permute-done.2), channel_id=1, source_target_pairs={{0,14},{1,15},{2,0},{3,1},{4,2},{5,3},{6,4},{7,5},{8,6},{9,7},{10,... | collective-permute-start | bytes 442376 | tf_op jit(solution)/shard_map/ppermute | solution.py:233
  47.5 5.2 %collective-permute-start.6 = (bf16[4,16,1152]{2,1,0:T(8,128)(2,1)S(1)}, bf16[4,16,1152]{2,1,0:T(8,128)(2,1)S(1)}, u32[]{:S(2)}, u32[]{:S(2)}) collective-permute-start(bf16[4,16,1152]{2,1,0:T(8,128)(2,1)S(1)} %collective-permute-done.5), channel_id=1, source_target_pairs={{0,2},{1,3},{2,4},{3,5},{4,6},{5,7},{6,8},{7,9},{8,10},{9,11},{10,... | collective-permute-start | bytes 442376 | tf_op jit(solution)/shard_map/ppermute | solution.py:233
  49.9 8.2 %collective-permute-start.4 = (bf16[4,16,1152]{2,1,0:T(8,128)(2,1)S(1)}, bf16[4,16,1152]{2,1,0:T(8,128)(2,1)S(1)}, u32[]{:S(2)}, u32[]{:S(2)}) collective-permute-start(bf16[4,16,1152]{2,1,0:T(8,128)(2,1)S(1)} %collective-permute-done.3), channel_id=1, source_target_pairs={{0,14},{1,15},{2,0},{3,1},{4,2},{5,3},{6,4},{7,5},{8,6},{9,7},{10,... | collective-permute-start | bytes 442376 | tf_op jit(solution)/shard_map/ppermute | solution.py:233
  52.7 5.4 %collective-permute-start.7 = (bf16[4,16,1152]{2,1,0:T(8,128)(2,1)S(1)}, bf16[4,16,1152]{2,1,0:T(8,128)(2,1)S(1)}, u32[]{:S(2)}, u32[]{:S(2)}) collective-permute-start(bf16[4,16,1152]{2,1,0:T(8,128)(2,1)S(1)} %collective-permute-done.6), channel_id=1, source_target_pairs={{0,2},{1,3},{2,4},{3,5},{4,6},{5,7},{6,8},{7,9},{8,10},{9,11},{10,... | collective-permute-start | bytes 442376 | tf_op jit(solution)/shard_map/ppermute | solution.py:233
  58.1 5.5 %collective-permute-start.8 = (bf16[2,16,1152]{2,1,0:T(8,128)(2,1)S(1)}, bf16[2,16,1152]{2,1,0:T(8,128)(2,1)S(1)}, u32[]{:S(2)}, u32[]{:S(2)}) collective-permute-start(bf16[2,16,1152]{2,1,0:T(8,128)(2,1)S(1)} %slice.108), channel_id=1, source_target_pairs={{0,2},{1,3},{2,4},{3,5},{4,6},{5,7},{6,8},{7,9},{8,10},{9,11},{10,... | collective-permute-start | bytes 221192 | tf_op jit(solution)/shard_map/ppermute | solution.py:233
  58.1 5.5 %collective-permute-start.9 = (bf16[2,16,1152]{2,1,0:T(8,128)(2,1)S(1)}, bf16[2,16,1152]{2,1,0:T(8,128)(2,1)S(1)}, u32[]{:S(2)}, u32[]{:S(2)}) collective-permute-start(bf16[2,16,1152]{2,1,0:T(8,128)(2,1)S(1)} %slice.109), channel_id=1, source_target_pairs={{0,14},{1,15},{2,0},{3,1},{4,2},{5,3},{6,4},{7,5},{8,6},{9,7},{10,... | collective-permute-start | bytes 221192 | tf_op jit(solution)/shard_map/ppermute | solution.py:233
  66.3 15.1 %collective-permute-start.10 = (bf16[8,4,16,1152]{3,2,1,0:T(8,128)(2,1)}, bf16[8,4,16,1152]{3,2,1,0:T(8,128)(2,1)}, u32[]{:S(2)}, u32[]{:S(2)}) collective-permute-start(bf16[8,4,16,1152]{3,2,1,0:T(8,128)(2,1)} %bitcast_dynamic-update-slice_fusion.mine_ref), channel_id=1, source_target_pairs={{0,1},{1,0},{2,3},{3,2},{4,5},{5,4},{6,7},{7,6},{8,9},{9,8},{10,11... | collective-permute-start | bytes 3538952 | tf_op jit(solution)/shard_map/ppermute | solution.py:233
  72.8 0.8 copy-start.1
  74.8 22.6 %all-to-all-start = ((bf16[16,64,256]{2,1,0:T(8,128)(2,1)}), bf16[16,64,256]{2,1,0:T(8,128)(2,1)S(1)}, u32[]{:S(2)}, u32[]{:S(2)}) async-start(bf16[16,64,256]{2,1,0:T(8,128)(2,1)} %reshape.49), calls=%async_computation | async-start | bytes 1048576 | tf_op jit(solution)/shard_map/all_to_all | solution.py:241
  97.3 0.8 copy-start.2
  114.7 21.2 %all-to-all-start.4 = ((bf16[16,64,256]{2,1,0:T(8,128)(2,1)}), bf16[16,64,256]{2,1,0:T(8,128)(2,1)S(1)}, u32[]{:S(2)}, u32[]{:S(2)}) async-start(bf16[16,64,256]{2,1,0:T(8,128)(2,1)} %get-tuple-element.5), calls=%async_computation.4 | async-start | bytes 1048576 | tf_op jit(solution)/shard_map/all_to_all | solution.py:241
  118.8 6.2 %collective-permute-start.11 = (bf16[108,512]{1,0:T(8,128)(2,1)S(1)}, bf16[108,512]{1,0:T(8,128)(2,1)S(1)}, u32[]{:S(2)}, u32[]{:S(2)}) collective-permute-start(bf16[108,512]{1,0:T(8,128)(2,1)S(1)} %reduce_sum.12), channel_id=1, source_target_pairs={{0,128},{64,192},{128,0},{192,64},{1,129},{65,193},{129,1},{193,65... | collective-permute-start | bytes 331784 | tf_op jit(solution)/shard_map/ppermute | solution.py:25
  121.6 6.1 %collective-permute-start.12 = (bf16[108,512]{1,0:T(8,128)(2,1)S(1)}, bf16[108,512]{1,0:T(8,128)(2,1)S(1)}, u32[]{:S(2)}, u32[]{:S(2)}) collective-permute-start(bf16[108,512]{1,0:T(8,128)(2,1)S(1)} %reduce_sum.12), channel_id=1, source_target_pairs={{0,64},{64,128},{128,192},{192,0},{1,65},{65,129},{129,193},{193,1... | collective-permute-start | bytes 331784 | tf_op jit(solution)/shard_map/ppermute | solution.py:25
  121.9 5.8 %collective-permute-start.13 = (bf16[108,512]{1,0:T(8,128)(2,1)S(1)}, bf16[108,512]{1,0:T(8,128)(2,1)S(1)}, u32[]{:S(2)}, u32[]{:S(2)}) collective-permute-start(bf16[108,512]{1,0:T(8,128)(2,1)S(1)} %reduce_sum.12), channel_id=1, source_target_pairs={{0,192},{64,0},{128,64},{192,128},{1,193},{65,1},{129,65},{193,129... | collective-permute-start | bytes 331784 | tf_op jit(solution)/shard_map/ppermute | solution.py:25

commit v3 on v2

--- a/solution.py
+++ b/solution.py
@@ -7,6 +7,7 @@
 from jax.experimental.pallas import tpu as pltpu
 from jax.sharding import PartitionSpec as P
 
+
 C3 = 512
 WID = 128
 
@@ -23,17 +24,6 @@
 def from_side(block, axis, distance):
     size = lax.axis_size(axis)
     return lax.ppermute(block, axis, [(i, (i + distance) % size) for i in range(size)])
-
-
-def activate(values):
-    return leak_slope * values + (1.0 - leak_slope) * values * jax.nn.sigmoid(values)
-
-
-def slope_of(values):
-    sigmoid_value = jax.nn.sigmoid(values)
-    return leak_slope + (1.0 - leak_slope) * (
-        sigmoid_value + values * sigmoid_value * (1.0 - sigmoid_value)
-    )
 
 
 def shifted(block, by_row, by_col, row_len):
@@ -49,16 +39,13 @@
     return jnp.where(keep, moved, 0.0).astype(block.dtype)
 
 
-def conv_kernel(taps_of_plane, channels, row_len, w_ref, *refs):
-    planes = refs[: len(taps_of_plane)]
-    out_ref = refs[len(taps_of_plane)]
-    cols_ref = refs[len(taps_of_plane) + 1]
+def conv_kernel(use, channels, row_len, w_ref, planes_ref, out_ref, cols_ref):
     tap_rows = 9 * channels
-    for at, plane in enumerate(planes):
+    for at, (_, plane) in enumerate(use):
         for row in range(-1, 4):
             for col in range(-1, 4):
                 source = ((row % 4) * 4 + col % 4) * channels
-                block = plane[source : source + channels, :]
+                block = planes_ref[plane, source : source + channels, :]
                 if row < 0 or col < 0:
                     block = shifted(block, int(row < 0), int(col < 0), row_len)
                 for row_phase in range(2):
@@ -71,25 +58,74 @@
                             continue
                         start = at * tap_rows + (row_tap * 3 + col_tap) * channels
                         cols_ref[row_phase * 2 + col_phase, start : start + channels, :] = block
+    first = use[0][0] * tap_rows
+    weights = w_ref[:, first : first + len(use) * tap_rows]
     for phase in range(4):
         out_ref[phase, :, :] = jnp.dot(
-            w_ref[...], cols_ref[phase], preferred_element_type=jnp.float32
+            weights, cols_ref[phase], preferred_element_type=jnp.float32
         ).astype(out_ref.dtype)
 
 
-def conv(w_rows, planes, dtype, row_len):
-    out_channels, depth = w_rows.shape
-    count = len(planes)
-    channels = depth // (9 * count)
-    cells = planes[0].shape[1]
-    return pl.pallas_call(
-        functools.partial(conv_kernel, tuple(range(count)), channels, row_len),
-        out_shape=jax.ShapeDtypeStruct((4, out_channels, cells), dtype),
+def conv(w_rows, planes, use, dtype, row_len):
+    outs, depth = w_rows.shape
+    channels = depth // 27
+    cells = planes.shape[2]
+    depth = 9 * channels * len(use)
+    return pl.pallas_call(
+        functools.partial(conv_kernel, use, channels, row_len),
+        out_shape=jax.ShapeDtypeStruct((4, outs, cells), dtype),
         scratch_shapes=[pltpu.VMEM((4, depth, cells), jnp.bfloat16)],
         cost_estimate=pl.CostEstimate(
-            flops=8 * out_channels * depth * cells, bytes_accessed=8 * depth * cells, transcendentals=0
-        ),
-    )(w_rows, *planes)
+            flops=8 * outs * depth * cells, bytes_accessed=4 * depth * cells, transcendentals=0
+        ),
+    )(w_rows, planes)
+
+
+def act_kernel(part_ref, behind_ref, hidden_ref, slope_ref):
+    groups, rows, _ = hidden_ref.shape
+    unit = rows // 4
+    for phase in range(4):
+        for at in range(groups):
+            here = slice(at * unit, (at + 1) * unit)
+            values = part_ref[phase, here, :] + behind_ref[phase, here, :].astype(jnp.float32)
+            gate = jax.nn.sigmoid(values)
+            there = slice(phase * unit, (phase + 1) * unit)
+            gated = (1.0 - leak_slope) * gate
+            hidden_ref[at, there, :] = (leak_slope * values + gated * values).astype(
+                hidden_ref.dtype
+            )
+            slope_ref[at, there, :] = leak_slope + gated * (1.0 + values * (1.0 - gate))
+
+
+def act(part, behind, groups):
+    phases, outs, cells = part.shape
+    shape = (groups, phases * outs // groups, cells)
+    return pl.pallas_call(
+        act_kernel,
+        out_shape=(
+            jax.ShapeDtypeStruct(shape, jnp.bfloat16),
+            jax.ShapeDtypeStruct(shape, jnp.float32),
+        ),
+        cost_estimate=pl.CostEstimate(
+            flops=10 * part.size, bytes_accessed=12 * part.size, transcendentals=part.size
+        ),
+    )(part, behind)
+
+
+def pile_kernel(*refs):
+    for at, ref in enumerate(refs[:-1]):
+        refs[-1][at] = ref[...]
+
+
+def pile(blocks):
+    shape = (len(blocks),) + blocks[0].shape
+    return pl.pallas_call(
+        pile_kernel,
+        out_shape=jax.ShapeDtypeStruct(shape, blocks[0].dtype),
+        cost_estimate=pl.CostEstimate(
+            flops=0, bytes_accessed=4 * len(blocks) * blocks[0].size, transcendentals=0
+        ),
+    )(*blocks)
 
 
 def spread(block, row_len):
@@ -115,10 +151,12 @@
     return total
 
 
-def grad_kernel(row_len, hidden_ref, cot_ref, out_ref, even_ref, odd_ref):
+def grad_kernel(row_len, place_ref, hidden_ref, cot_ref, *refs):
+    outs_refs, (even_ref, odd_ref, sum_ref) = refs[:-3], refs[-3:]
     planes, group, cells = hidden_ref.shape
     steps = planes // 2
     own = group // 4
+    unit = own // len(outs_refs)
     for s in range(steps):
         here = slice(s * cells, (s + 1) * cells)
         even_ref[:, here] = spread(hidden_ref[2 * s], row_len)
@@ -136,28 +174,40 @@
             for col_tap in range(3):
                 at = (2 * int(row_tap == 0) + int(col_tap == 0)) * group
                 at += (2 * int(row_tap != 1) + int(col_tap != 1)) * own
-                put = (depth_tap * 3 + row_tap) * 3 + col_tap
-                out_ref[put] = total[at : at + own, :].astype(out_ref.dtype)
-
-
-def grad(hidden, cot, dtype, row_len):
+                put = ((depth_tap * 3 + row_tap) * 3 + col_tap) * unit
+                for y in range(len(outs_refs)):
+                    first = at + y * unit
+                    sum_ref[y, put : put + unit, :] = total[first : first + unit, :]
+    for away, out_ref in enumerate(outs_refs):
+        y = lax.rem(place_ref[0] + away, len(outs_refs))
+        out_ref[...] = sum_ref[y].astype(out_ref.dtype)
+
+
+def grad(place, hidden, cot, row_count, row_len):
     planes, group, cells = hidden.shape
     outs = cot.shape[0]
     rows = pltpu.VMEM((4 * group, planes // 2 * cells), jnp.bfloat16)
+    size = 27 * group // (4 * row_count)
+    vmem = pl.BlockSpec(memory_space=pltpu.VMEM)
     return pl.pallas_call(
         functools.partial(grad_kernel, row_len),
-        out_shape=jax.ShapeDtypeStruct((27, group // 4, outs), dtype),
-        scratch_shapes=[rows, rows],
+        out_shape=[
+            jax.ShapeDtypeStruct((size, outs), jnp.bfloat16 if away else jnp.float32)
+            for away in range(row_count)
+        ],
+        in_specs=[pl.BlockSpec(memory_space=pltpu.SMEM), vmem, vmem],
+        out_specs=[vmem] * row_count,
+        scratch_shapes=[rows, rows, pltpu.VMEM((row_count, size, outs), jnp.float32)],
         cost_estimate=pl.CostEstimate(
             flops=12 * group * outs * planes * cells, bytes_accessed=2 * cot.size, transcendentals=0
         ),
-    )(hidden, cot)
+    )(place, hidden, cot)
 
 
 def back_kernel(row_len, place_ref, w_ref, mine_ref, theirs_ref, out_ref, cot_ref):
     planes, group, cells = out_ref.shape
     ring, rows_y, unit, half = mine_ref.shape
-    z, core = place_ref[0], place_ref[1]
+    z, core = place_ref[1], place_ref[2]
     here = pl.ds(pl.multiple_of(core * half, 128), half)
     there = pl.ds(pl.multiple_of((1 - core) * half, 128), half)
     for k in range(ring):
@@ -233,8 +283,20 @@
     return lax.ppermute(block, "space", route)
 
 
-COLUMNS = [[y * RING * CORES + g for y in range(ROWS)] for g in range(RING * CORES)]
-SLABS = [[y * RING * CORES + g for g in range(RING * CORES)] for y in range(ROWS)]
+CHIPS = [(y, z) for y in range(ROWS) for z in range(RING)]
+
+
+def members(pick):
+    groups = {}
+    for y, z in CHIPS:
+        for core in range(CORES):
+            groups.setdefault(pick(y, z, core), []).append((y * RING + z) * CORES + core)
+    return list(groups.values())
+
+
+COLUMNS = members(lambda y, z, core: (z, core))
+PILLARS = members(lambda y, z, core: z)
+SLABS = members(lambda y, z, core: y)
 
 
 def exchange(blocks, groups):
@@ -243,72 +305,63 @@
     )
 
 
-def per_device(volume, w_first, w_second, cotangent):
+def section(volume, w_first, w_second, cotangent):
     channels = volume.shape[1]
     cells = volume.shape[4]
-    out_channels = w_first.shape[4]
+    outs = w_first.shape[4]
     own = w_second.shape[3]
     row_len = WID // 4
     me = lax.axis_index("space")
-    core, z = me % CORES, me // CORES % RING
+    y, z, core = me // (RING * CORES), me // CORES % RING, me % CORES
+    place = jnp.stack([y, z, core]).astype(jnp.int32)
     group = RING * CORES
 
-    depth = cotangent.shape[2]
-    share = depth // ROWS
+    share = cotangent.shape[2] // ROWS
     local = jnp.pad(cotangent[0], ((0, 0), (0, 1), (0, 0)))
-    parts = jnp.stack([local[:, y * share : (y + 1) * share + 1] for y in range(ROWS)])
-    parts = parts.reshape(ROWS, -1, (share + 1) * cells)
-    half = (share + 1) * cells // 2
-    low, high = parts[:, :, :half], parts[:, :, half:]
-    kept = jnp.where(core == 0, low, high)
-    other = on_space(jnp.where(core == 0, high, low), core_by=1)
-    unit = jnp.concatenate(
-        [jnp.where(core == 0, kept, other), jnp.where(core == 0, other, kept)], 1
-    )
-    first = exchange(unit, COLUMNS)
+    parts = jnp.stack([local[:, at * share : (at + 1) * share + 1] for at in range(ROWS)])
+    parts = parts.reshape(ROWS, -1, CORES, (share + 1) * cells // CORES).transpose(0, 2, 1, 3)
+    first = exchange(parts.reshape((ROWS * CORES,) + parts.shape[2:]), PILLARS)
+    first = first.reshape(ROWS, -1, first.shape[2])
     up, down = [first], [first]
     for _ in range(3):
         up.append(on_space(up[-1], z_by=1))
         down.append(on_space(down[-1], z_by=-1))
-    far = jnp.concatenate(
-        [on_space(up[3][: ROWS // 2], z_by=1), on_space(down[3][ROWS // 2 :], z_by=-1)], 0
-    )
-    mine = jnp.stack(down + [far] + up[:0:-1])
+    far = on_space(up[3], z_by=1)
+    mine = pile(down + [far] + up[:0:-1])
     theirs = on_space(mine, core_by=1)
 
-    w_all = exchange(jnp.broadcast_to(w_second, (ROWS,) + w_second.shape), COLUMNS)
-    w_group = w_all.transpose(1, 2, 3, 0, 4, 5).reshape(3, 3, 3, ROWS * own, C3)
-
-    planes = volume[0].reshape(channels, 2, 16, cells).transpose(1, 2, 0, 3)
-    planes = planes.reshape(2, 16 * channels, cells)
-    w_rows = w_first.reshape(27 * channels, out_channels)
-    w_before = w_rows[: 9 * channels].T
-    w_here = w_rows[9 * channels :].T
-    ahead = conv(w_before, [planes[1]], jnp.bfloat16, row_len)
+    w_rel = [w_second]
+    for step in range(1, ROWS):
+        w_rel.append(on_space(w_second, y_by=-step))
+    w_rel = jnp.stack(w_rel + w_rel, 3)
+    w_group = lax.dynamic_slice_in_dim(w_rel, (ROWS - y) % ROWS, ROWS, 3)
+    w_group = w_group.reshape(3, 3, 3, ROWS * own, C3)
+
+    planes = volume[0].transpose(1, 2, 0, 3).reshape(2, 16 * channels, cells)
+    w_rows = w_first.reshape(27 * channels, ROWS, group, own).transpose(2, 1, 3, 0)
+    w_rows = w_rows.reshape(outs, 27 * channels)
+    ahead = conv(w_rows, planes, ((0, 1),), jnp.bfloat16, row_len)
     behind = from_behind(ahead, "space", 1)
-    pre_act = conv(w_here, [planes[0], planes[1]], jnp.float32, row_len)
-    pre_act = pre_act + behind.astype(jnp.float32)
-    hidden = activate(pre_act).astype(jnp.bfloat16)
-    blocks = hidden.reshape(4, ROWS, group, own, cells).transpose(2, 0, 1, 3, 4)
-    by_plane = exchange(blocks.reshape(group, 4 * ROWS * own, cells), SLABS)
-
-    place = jnp.stack([z, core]).astype(jnp.int32)
+    part = conv(w_rows, planes, ((1, 0), (2, 1)), jnp.float32, row_len)
+    hidden, slopes = act(part, behind, group)
+    by_plane = exchange(hidden, SLABS)
+
     back_terms, cot_row = back(place, move_rows(w_group), mine, theirs, group, row_len)
     hidden_grad = exchange(back_terms, SLABS)
 
-    partial = grad(by_plane, cot_row, jnp.bfloat16, row_len)
-    partial = partial.reshape(27, ROWS, own, C3).transpose(1, 0, 2, 3).reshape(ROWS, 27 * own, C3)
-    partial = jnp.sum(exchange(partial, COLUMNS).astype(jnp.float32), 0).astype(jnp.bfloat16)
-    sides = [from_side(partial, "dp", distance) for distance in (1, 2, 3)]
-    left, opposite, right = [side.astype(jnp.float32) for side in sides]
-    grad_second = (partial.astype(jnp.float32) + opposite) + (left + right)
+    partial, *others = grad(place, by_plane, cot_row, ROWS, row_len)
+    for step, block in enumerate(others, 1):
+        partial = partial + on_space(block, y_by=step).astype(jnp.float32)
+    partial = partial.astype(jnp.bfloat16)
+    sides = []
+    for distance in (1, 2, 3):
+        sides.append(from_side(partial, "dp", distance).astype(jnp.float32))
+    grad_second = (partial.astype(jnp.float32) + sides[1]) + (sides[0] + sides[2])
     grad_second = grad_second.reshape(3, 3, 3, own, C3)
 
-    hidden_grad = hidden_grad.reshape(group, 4, ROWS, own, cells).transpose(2, 0, 3, 1, 4)
-    hidden_grad = hidden_grad.reshape(out_channels, 4, cells).astype(jnp.float32)
-    slopes = slope_of(pre_act.transpose(1, 0, 2))
-    pre_grad = (hidden_grad * slopes).astype(jnp.bfloat16)
-    return (grad_second, pre_grad[None, :, None])
+    pre_grad = (hidden_grad.astype(jnp.float32) * slopes).astype(jnp.bfloat16)
+    pre_grad = pre_grad.reshape(group, 4, ROWS, own, cells).transpose(2, 0, 3, 1, 4)
+    return (grad_second, pre_grad.reshape(1, outs, 1, 4, cells))
 
 
 def solution(mesh):
@@ -320,5 +373,5 @@
     )
     out_specs = (P(None, None, None, "space", None), P("dp", None, "space", None, None))
     return jax.shard_map(
-        per_device, mesh=mesh, in_specs=in_specs, out_specs=out_specs, check_vma=False
+        section, mesh=mesh, in_specs=in_specs, out_specs=out_specs, check_vma=False
     )

time: 140 us -> 136 us (0.971)
  blocking collectives: 10.7 us -> 0 us
  Pallas kernels: 16.8 us -> 23.3 us
  local copies, waits for them, and re-layouts: 22.5 us -> 27.7 us
  waiting for transfers between devices: 39.5 us -> 36.2 us
  other arithmetic: 4.25 us -> 2.25 us
    all_to_all x4 -> x3, waiting for transfers between devices: 27.6 us -> 10.2 us  [exchange(): lax.all_to_all(blocks, 'space', split_axis=0, concat_axis=0, axis_index_g...]
    ppermute x10 -> x14, waiting for transfers between devices: 8.5 us -> 19.6 us  [on_space(): return lax.ppermute(block, 'space', route)]
    all_to_all x1 -> x0, blocking collectives: 10.7 us -> none  [exchange(): lax.all_to_all(blocks, 'space', split_axis=0, concat_axis=0, axis_index_g...]
    transpose x1 -> x4, local copies, waits for them, and re-layouts: 0.22 us -> 7.95 us  [the longest x1 4.12 us: section(): planes = volume[0].transpose(1, 2, 0, 3).reshape(2, 16 * channels, cells)]
    slice x12 -> x1, local copies, waits for them, and re-layouts: 7.05 us -> 0.02 us  [section(): local[:, at * share:(at + 1) * share + 1]]
    pallas_call x3 -> x5, Pallas kernels: 12 us -> 18.6 us  [the longest x2 8.57 us: conv(): pl.pallas_call(functools.partial(conv_kernel, use, channels, row_len), ou...]
    all_to_all x4 -> x3, starting transfers between devices: 16.8 us -> 13.2 us  [exchange(): lax.all_to_all(blocks, 'space', split_axis=0, concat_axis=0, axis_index_g...]
    unnamed x17 -> x36, local copies, waits for them, and re-layouts: 8.21 us -> 11.3 us
  transfers between devices with their start and end apart: 18 -> 21, of which waited for: 9 -> 12; matrix products, arithmetic and copies ran while one was open for 13% -> 19% of each run, Pallas kernels for 9% -> 17%
where the time goes in v3:
time: 136 us; the launch traced here: 135 us
  starting transfers between devices  44.5 us (33%)
  waiting for transfers between devices  36.2 us (27%)
  local copies, waits for them, and re-layouts  27.7 us (20%)
  Pallas kernels  23.3 us (17%)
  other arithmetic  2.25 us (2%)
    ppermute x14, starting transfers between devices, on_space(): return lax.ppermute(block, 'space', route)  22 us
    ppermute x14, waiting for transfers between devices, on_space(): return lax.ppermute(block, 'space', route)  19.6 us
    all_to_all x3, starting transfers between devices, exchange(): lax.all_to_all(blocks, 'space', split_axis=0, concat_axis=0, axis_index_g...  13.2 us
    unnamed x36, local copies, waits for them, and re-layouts  11.3 us
    all_to_all x3, waiting for transfers between devices, exchange(): lax.all_to_all(blocks, 'space', split_axis=0, concat_axis=0, axis_index_g...  10.2 us
    pallas_call x2, Pallas kernels, conv(): pl.pallas_call(functools.partial(conv_kernel, use, channels, row_len), ou...  8.57 us
    ppermute x3, waiting for transfers between devices, from_side(): lax.ppermute(block, axis, [(i, (i + distance) % size) for i in range(size)])  6.35 us
    ppermute x1, starting transfers between devices, from_behind(): return lax.ppermute(block, axis, route)  4.93 us
  transfers between devices with their start and end apart: 21, of which 12 were waited for; matrix products, arithmetic and copies ran while one was open for 19% of the time, Pallas kernels for 17%

profile of v3, /device:TPU:1, one launch (start us, length us, event | category | flops | bytes accessed | tf_op | source)
XLA Modules:
  0.0 134.9 jit_solution(7120917163771022188)
XLA Ops:
  0.6 3.6 %collective-permute-start.1 = (bf16[3,3,3,4,512]{4,3,2,1,0:T(4,128)(2,1)}, bf16[3,3,3,4,512]{4,3,2,1,0:T(4,128)(2,1)S(1)}, u32[]{:S(2)}, u32[]{:S(2)}) collective-permute-start(bf16[3,3,3,4,512]{4,3,2,1,0:T(4,128)(2,1)} %param.6), channel_id=1, source_target_pairs={{0,48},{1,49},{2,50},{3,51},{4,52},{5,53},{6,54},{7,55},{8,56},{9,... | collective-permute-start | bytes 331784 | tf_op jit(solution)/shard_map/ppermute | solution.py:283
  4.6 0.7 collective-permute-start.3
  5.3 4.1 %copy.20 = bf16[3,3,3,128,256]{3,2,1,0,4:T(4,128)(2,1)S(1)} copy(bf16[3,3,3,128,256]{4,3,2,1,0:T(8,128)(2,1)} %param.5) | data formatting | bytes 3538944 | tf_op args[1]
  9.4 2.7 %reshape.43 = bf16[3456,4,16,4]{0,3,2,1:T(4,128)(2,1)} reshape(bf16[3,3,3,128,256]{3,2,1,0,4:T(4,128)(2,1)S(1)} %copy.20) | data formatting | bytes 3538944 | tf_op jit(solution)/shard_map/reshape | solution.py:341
  12.1 2.1 %copy.21 = bf16[16,4,4,3456]{3,2,1,0:T(4,128)(2,1)S(1)} copy(bf16[16,4,4,3456]{3,2,0,1:T(4,128)(2,1)} %bitcast.64) | data formatting | bytes 3538944 | tf_op jit(solution)/shard_map/transpose | solution.py:341
  14.2 1.4 %reshape.44.w_ref = bf16[256,3456]{1,0:T(8,128)(2,1)} reshape(bf16[16,4,4,3456]{3,2,1,0:T(4,128)(2,1)S(1)} %copy.21) | data formatting | bytes 3538944 | tf_op jit(solution)/shard_map/reshape | solution.py:342
  15.6 4.1 %copy.22 = bf16[2,16,128,256]{3,2,1,0:T(8,128)(2,1)} copy(bf16[2,16,128,256]{3,1,0,2:T(8,128)(2,1)} %bitcast.65) | data formatting | bytes 4194304 | tf_op jit(solution)/shard_map/transpose | solution.py:340
  19.7 3.9 %shard_map.60 = bf16[4,256,256]{2,1,0:T(8,128)(2,1)} custom-call(bf16[256,3456]{1,0:T(8,128)(2,1)} %reshape.44.w_ref, bf16[2,2048,256]{2,1,0:T(8,128)(2,1)} %bitcast.62), custom_call_target="tpu_custom_call" | custom-call | flops 603979776 | bytes 1179648 | tf_op jit(solution)/shard_map/pallas_call | solution.py:74
  23.6 4.9 %collective-permute-start = (bf16[4,256,256]{2,1,0:T(8,128)(2,1)}, bf16[4,256,256]{2,1,0:T(8,128)(2,1)S(1)}, u32[]{:S(2)}, u32[]{:S(2)}) collective-permute-start(bf16[4,256,256]{2,1,0:T(8,128)(2,1)} %shard_map.60), channel_id=1, source_target_pairs={{0,1},{1,2},{2,3},{3,4},{4,5},{5,6},{6,7},{7,8},{8,9},{9,10},{10,1... | collective-permute-start | bytes 1572872 | tf_op jit(solution)/shard_map/ppermute | solution.py:21
  29.7 3.6 %all-to-all-start.1 = ((bf16[8,8,1152]{2,1,0:T(8,128)(2,1)}), bf16[8,8,1152]{2,1,0:T(8,128)(2,1)S(1)}, u32[]{:S(2)}, u32[]{:S(2)}) async-start(bf16[8,8,1152]{2,1,0:T(8,128)(2,1)} %bitcast.28), calls=%async_computation.1 | async-start | bytes 294912 | tf_op jit(solution)/shard_map/all_to_all | solution.py:303
  33.4 4.7 %shard_map.59.part_ref = f32[4,256,256]{2,1,0:T(8,128)} custom-call(bf16[256,3456]{1,0:T(8,128)(2,1)} %reshape.44.w_ref, bf16[2,2048,256]{2,1,0:T(8,128)(2,1)} %bitcast.63), custom_call_target="tpu_custom_call" | custom-call | flops 1207959552 | bytes 2359296 | tf_op jit(solution)/shard_map/pallas_call | solution.py:74
  38.1 0.7 bitcast_dynamic-update-slice_fusion.6
  39.4 0.7 bitcast_dynamic-update-slice_fusion.4
  40.0 0.7 bitcast_dynamic-update-slice_fusion.2
  41.4 0.7 bitcast_dynamic-update-slice_fusion.7
  42.8 1.6 %collective-permute-start.7 = (bf16[4,16,1152]{2,1,0:T(8,128)(2,1)S(1)}, bf16[4,16,1152]{2,1,0:T(8,128)(2,1)S(1)}, u32[]{:S(2)}, u32[]{:S(2)}) collective-permute-start(bf16[4,16,1152]{2,1,0:T(8,128)(2,1)S(1)} %bitcast.69), channel_id=1, source_target_pairs={{0,2},{1,3},{2,4},{3,5},{4,6},{5,7},{6,8},{7,9},{8,10},{9,11},{10,... | collective-permute-start | bytes 442376 | tf_op jit(solution)/shard_map/ppermute | solution.py:283
  44.4 0.7 bitcast_dynamic-update-slice_fusion.3
  45.1 2.3 %collective-permute-start.4 = (bf16[4,16,1152]{2,1,0:T(8,128)(2,1)S(1)}, bf16[4,16,1152]{2,1,0:T(8,128)(2,1)S(1)}, u32[]{:S(2)}, u32[]{:S(2)}) collective-permute-start(bf16[4,16,1152]{2,1,0:T(8,128)(2,1)S(1)} %bitcast.70), channel_id=1, source_target_pairs={{0,14},{1,15},{2,0},{3,1},{4,2},{5,3},{6,4},{7,5},{8,6},{9,7},{10,... | collective-permute-start | bytes 442376 | tf_op jit(solution)/shard_map/ppermute | solution.py:283
  47.4 3.5 %collective-permute-done.7.refs_7_ = bf16[4,16,1152]{2,1,0:T(8,128)(2,1)S(1)} collective-permute-done((bf16[4,16,1152]{2,1,0:T(8,128)(2,1)S(1)}, bf16[4,16,1152]{2,1,0:T(8,128)(2,1)S(1)}, u32[]{:S(2)}, u32[]{:S(2)}) %collective-permute-start.7) | collective-permute-done | bytes 147488 | tf_op jit(solution)/shard_map/ppermute | solution.py:283
  51.0 0.7 bitcast_dynamic-update-slice_fusion.1
  51.6 1.2 constant_dynamic-slice_fusion
  53.2 2.7 %collective-permute-start.5 = (bf16[4,16,1152]{2,1,0:T(8,128)(2,1)S(1)}, bf16[4,16,1152]{2,1,0:T(8,128)(2,1)S(1)}, u32[]{:S(2)}, u32[]{:S(2)}) collective-permute-start(bf16[4,16,1152]{2,1,0:T(8,128)(2,1)S(1)} %collective-permute-done.4.refs_1_), channel_id=1, source_target_pairs={{0,14},{1,15},{2,0},{3,1},{4,2},{5,3},{6,4},{7,5},{8,6},{9,7},{10,... | collective-permute-start | bytes 442376 | tf_op jit(solution)/shard_map/ppermute | solution.py:283
  55.9 1.1 collective-permute-done.8.refs_6_
  57.1 1.2 collective-permute-done.5.refs_2_
  58.3 3.4 %collective-permute-start.6 = (bf16[4,16,1152]{2,1,0:T(8,128)(2,1)S(1)}, bf16[4,16,1152]{2,1,0:T(8,128)(2,1)S(1)}, u32[]{:S(2)}, u32[]{:S(2)}) collective-permute-start(bf16[4,16,1152]{2,1,0:T(8,128)(2,1)S(1)} %collective-permute-done.5.refs_2_), channel_id=1, source_target_pairs={{0,14},{1,15},{2,0},{3,1},{4,2},{5,3},{6,4},{7,5},{8,6},{9,7},{10,... | collective-permute-start | bytes 442376 | tf_op jit(solution)/shard_map/ppermute | solution.py:283
  62.3 1.5 %collective-permute-done.6.refs_3_ = bf16[4,16,1152]{2,1,0:T(8,128)(2,1)S(1)} collective-permute-done((bf16[4,16,1152]{2,1,0:T(8,128)(2,1)S(1)}, bf16[4,16,1152]{2,1,0:T(8,128)(2,1)S(1)}, u32[]{:S(2)}, u32[]{:S(2)}) %collective-permute-start.6) | collective-permute-done | bytes 147488 | tf_op jit(solution)/shard_map/ppermute | solution.py:283
  63.8 3.6 %collective-permute-done.10.refs_4_ = bf16[4,16,1152]{2,1,0:T(8,128)(2,1)S(1)} collective-permute-done((bf16[4,16,1152]{2,1,0:T(8,128)(2,1)S(1)}, bf16[4,16,1152]{2,1,0:T(8,128)(2,1)S(1)}, u32[]{:S(2)}, u32[]{:S(2)}) %collective-permute-start.10) | collective-permute-done | bytes 147488 | tf_op jit(solution)/shard_map/ppermute | solution.py:283
  68.1 2.4 %shard_map.62.mine_ref = bf16[8,4,16,1152]{3,2,1,0:T(8,128)(2,1)} custom-call(bf16[4,16,1152]{2,1,0:T(8,128)(2,1)} %bitcast.71, bf16[4,16,1152]{2,1,0:T(8,128)(2,1)} %copy-done.7, bf16[4,16,1152]{2,1,0:T(8,128)(2,1)} %copy-done.9, bf16[4,16,1152]{2,1,0:T(8,128)(2,1)} %copy-done.11, bf16[4,16,1152]{2,1,0:T(8,128)(2,1)} %copy-done.12, ...), custom_call_target="tpu_custom_call" | custom-call | bytes 2359296 | tf_op jit(solution)/shard_map/pallas_call | solution.py:122
  70.5 3.7 %collective-permute-start.11 = (bf16[8,4,16,1152]{3,2,1,0:T(8,128)(2,1)}, bf16[8,4,16,1152]{3,2,1,0:T(8,128)(2,1)S(1)}, u32[]{:S(2)}, u32[]{:S(2)}) collective-permute-start(bf16[8,4,16,1152]{3,2,1,0:T(8,128)(2,1)} %shard_map.62.mine_ref), channel_id=1, source_target_pairs={{0,1},{1,0},{2,3},{3,2},{4,5},{5,4},{6,7},{7,6},{8,9},{9,8},{10,11... | collective-permute-start | bytes 3538952 | tf_op jit(solution)/shard_map/ppermute | solution.py:283
  74.3 0.8 copy-done.3
  75.1 3.0 %shard_map.61 = (bf16[16,64,256]{2,1,0:T(8,128)(2,1)}, f32[16,64,256]{2,1,0:T(8,128)}) custom-call(f32[4,256,256]{2,1,0:T(8,128)} %shard_map.59.part_ref, bf16[4,256,256]{2,1,0:T(8,128)(2,1)} %copy-done.3), custom_call_target="tpu_custom_call" | custom-call | flops 2621440 | bytes 3145728 | tf_op jit(solution)/shard_map/pallas_call | solution.py:103
  78.2 6.1 %all-to-all-start = ((bf16[16,64,256]{2,1,0:T(8,128)(2,1)}), bf16[16,64,256]{2,1,0:T(8,128)(2,1)S(1)}, u32[]{:S(2)}, u32[]{:S(2)}) async-start(bf16[16,64,256]{2,1,0:T(8,128)(2,1)} %get-tuple-element.10), calls=%async_computation | async-start | bytes 1048576 | tf_op jit(solution)/shard_map/all_to_all | solution.py:303
  84.5 1.0 copy.26
  85.5 1.0 copy-done.13
  86.5 4.8 %shard_map.63 = (bf16[16,64,256]{2,1,0:T(8,128)(2,1)}, bf16[512,2304]{1,0:T(8,128)(2,1)}) custom-call(s32[3]{0:T(128)} %pad_add_fusion.place_ref, bf16[768,512]{1,0:T(8,128)(2,1)} %bitcast.68, bf16[8,4,16,1152]{3,2,1,0:T(8,128)(2,1)} %shard_map.62.mine_ref, bf16[8,4,16,1152]{3,2,1,0:T(8,128)(2,1)} %copy-done.13), custom_call_target="tpu_custom_call" | custom-call | flops 1610612736 | bytes 4718592 | tf_op jit(solution)/shard_map/pallas_call | solution.py:241
  91.3 10.2 %all-to-all-done.hidden_ref = bf16[16,64,256]{2,1,0:T(8,128)(2,1)S(1)} async-done(((bf16[16,64,256]{2,1,0:T(8,128)(2,1)}), bf16[16,64,256]{2,1,0:T(8,128)(2,1)S(1)}, u32[]{:S(2)}, u32[]{:S(2)}) %all-to-all-start) | async-done | bytes 524320 | tf_op jit(solution)/shard_map/all_to_all | solution.py:303
  101.5 3.5 %all-to-all-start.2 = ((bf16[16,64,256]{2,1,0:T(8,128)(2,1)}), bf16[16,64,256]{2,1,0:T(8,128)(2,1)S(1)}, u32[]{:S(2)}, u32[]{:S(2)}) async-start(bf16[16,64,256]{2,1,0:T(8,128)(2,1)} %get-tuple-element.16), calls=%async_computation.2 | async-start | bytes 1048576 | tf_op jit(solution)/shard_map/all_to_all | solution.py:303
  105.0 4.5 %shard_map.64 = (f32[108,512]{1,0:T(8,128)}, bf16[108,512]{1,0:T(8,128)(2,1)}, bf16[108,512]{1,0:T(8,128)(2,1)}, bf16[108,512]{1,0:T(8,128)(2,1)}) custom-call(s32[3]{0:T(128)} %pad_add_fusion.place_ref, bf16[16,64,256]{2,1,0:T(8,128)(2,1)} %copy-done.4, bf16[512,2304]{1,0:T(8,128)(2,1)} %get-tuple-element.11.cot_ref), custom_call_target="tpu_custom_call" | custom-call | flops 1610612736 | bytes 2359296 | tf_op jit(solution)/shard_map/pallas_call | solution.py:192
  109.5 2.3 %collective-permute-start.14 = (bf16[108,512]{1,0:T(8,128)(2,1)}, bf16[108,512]{1,0:T(8,128)(2,1)S(1)}, u32[]{:S(2)}, u32[]{:S(2)}) collective-permute-start(bf16[108,512]{1,0:T(8,128)(2,1)} %get-tuple-element.15), channel_id=1, source_target_pairs={{0,48},{1,49},{2,50},{3,51},{4,52},{5,53},{6,54},{7,55},{8,56},{9,... | collective-permute-start | bytes 331784 | tf_op jit(solution)/shard_map/ppermute | solution.py:283
  113.0 4.4 %collective-permute-done.14 = bf16[108,512]{1,0:T(8,128)(2,1)S(1)} collective-permute-done((bf16[108,512]{1,0:T(8,128)(2,1)}, bf16[108,512]{1,0:T(8,128)(2,1)S(1)}, u32[]{:S(2)}, u32[]{:S(2)}) %collective-permute-start.14) | collective-permute-done | bytes 110624 | tf_op jit(solution)/shard_map/ppermute | solution.py:283
  117.3 1.0 collective-permute-done.13
  118.4 2.7 %collective-permute-done.12 = bf16[108,512]{1,0:T(8,128)(2,1)S(1)} collective-permute-done((bf16[108,512]{1,0:T(8,128)(2,1)}, bf16[108,512]{1,0:T(8,128)(2,1)S(1)}, u32[]{:S(2)}, u32[]{:S(2)}) %collective-permute-start.12) | collective-permute-done | bytes 110624 | tf_op jit(solution)/shard_map/ppermute | solution.py:283
  121.1 1.0 add_convert_fusion
  122.1 2.6 %collective-permute-start.17 = (bf16[108,512]{1,0:T(8,128)(2,1)S(1)}, bf16[108,512]{1,0:T(8,128)(2,1)S(1)}, u32[]{:S(2)}, u32[]{:S(2)}) collective-permute-start(bf16[108,512]{1,0:T(8,128)(2,1)S(1)} %add_convert_fusion), channel_id=1, source_target_pairs={{0,192},{64,0},{128,64},{192,128},{1,193},{65,1},{129,65},{193,129... | collective-permute-start | bytes 331784 | tf_op jit(solution)/shard_map/ppermute | solution.py:26
  124.7 1.7 %collective-permute-start.15 = (bf16[108,512]{1,0:T(8,128)(2,1)S(1)}, bf16[108,512]{1,0:T(8,128)(2,1)S(1)}, u32[]{:S(2)}, u32[]{:S(2)}) collective-permute-start(bf16[108,512]{1,0:T(8,128)(2,1)S(1)} %add_convert_fusion), channel_id=1, source_target_pairs={{0,128},{64,192},{128,0},{192,64},{1,129},{65,193},{129,1},{193,65... | collective-permute-start | bytes 331784 | tf_op jit(solution)/shard_map/ppermute | solution.py:26
  126.7 6.0 %collective-permute-done.16 = bf16[108,512]{1,0:T(8,128)(2,1)S(1)} collective-permute-done((bf16[108,512]{1,0:T(8,128)(2,1)S(1)}, bf16[108,512]{1,0:T(8,128)(2,1)S(1)}, u32[]{:S(2)}, u32[]{:S(2)}) %collective-permute-start.16) | collective-permute-done | bytes 110624 | tf_op jit(solution)/shard_map/ppermute | solution.py:26
  132.8 0.7 reshape.50
  133.8 1.1 copy.28
  (73 shorter events, 7.1 us)
Async XLA Ops:
  0.6 38.7 %collective-permute-start.1 = (bf16[3,3,3,4,512]{4,3,2,1,0:T(4,128)(2,1)}, bf16[3,3,3,4,512]{4,3,2,1,0:T(4,128)(2,1)S(1)}, u32[]{:S(2)}, u32[]{:S(2)}) collective-permute-start(bf16[3,3,3,4,512]{4,3,2,1,0:T(4,128)(2,1)} %param.6), channel_id=1, source_target_pairs={{0,48},{1,49},{2,50},{3,51},{4,52},{5,53},{6,54},{7,55},{8,56},{9,... | collective-permute-start | bytes 331784 | tf_op jit(solution)/shard_map/ppermute | solution.py:283
  4.3 35.8 %collective-permute-start.2 = (bf16[3,3,3,4,512]{4,3,2,1,0:T(4,128)(2,1)}, bf16[3,3,3,4,512]{4,3,2,1,0:T(4,128)(2,1)S(1)}, u32[]{:S(2)}, u32[]{:S(2)}) collective-permute-start(bf16[3,3,3,4,512]{4,3,2,1,0:T(4,128)(2,1)} %param.6), channel_id=1, source_target_pairs={{0,32},{1,33},{2,34},{3,35},{4,36},{5,37},{6,38},{7,39},{8,40},{9,... | collective-permute-start | bytes 331784 | tf_op jit(solution)/shard_map/ppermute | solution.py:283
  4.6 36.1 %collective-permute-start.3 = (bf16[3,3,3,4,512]{4,3,2,1,0:T(4,128)(2,1)}, bf16[3,3,3,4,512]{4,3,2,1,0:T(4,128)(2,1)S(1)}, u32[]{:S(2)}, u32[]{:S(2)}) collective-permute-start(bf16[3,3,3,4,512]{4,3,2,1,0:T(4,128)(2,1)} %param.6), channel_id=1, source_target_pairs={{0,16},{1,17},{2,18},{3,19},{4,20},{5,21},{6,22},{7,23},{8,24},{9,... | collective-permute-start | bytes 331784 | tf_op jit(solution)/shard_map/ppermute | solution.py:283
  19.7 8.9 %copy-start.1 = (bf16[1,8,32,256]{3,2,1,0:T(8,128)(2,1)S(1)}, bf16[1,8,32,256]{3,2,1,0:T(8,128)(2,1)}, u32[]{:S(2)}) copy-start(bf16[1,8,32,256]{3,2,1,0:T(8,128)(2,1)} %param.7) | copy-start | bytes 393220
  23.6 50.7 %collective-permute-start = (bf16[4,256,256]{2,1,0:T(8,128)(2,1)}, bf16[4,256,256]{2,1,0:T(8,128)(2,1)S(1)}, u32[]{:S(2)}, u32[]{:S(2)}) collective-permute-start(bf16[4,256,256]{2,1,0:T(8,128)(2,1)} %shard_map.60), channel_id=1, source_target_pairs={{0,1},{1,2},{2,3},{3,4},{4,5},{5,6},{6,7},{7,8},{8,9},{9,10},{10,1... | collective-permute-start | bytes 1572872 | tf_op jit(solution)/shard_map/ppermute | solution.py:21
  29.7 13.0 %all-to-all-start.1 = ((bf16[8,8,1152]{2,1,0:T(8,128)(2,1)}), bf16[8,8,1152]{2,1,0:T(8,128)(2,1)S(1)}, u32[]{:S(2)}, u32[]{:S(2)}) async-start(bf16[8,8,1152]{2,1,0:T(8,128)(2,1)} %bitcast.28), calls=%async_computation.1 | async-start | bytes 294912 | tf_op jit(solution)/shard_map/all_to_all | solution.py:303
  33.4 4.7 %copy-start.5 = (bf16[3,3,3,4,512]{4,3,2,1,0:T(4,128)(2,1)S(1)}, bf16[3,3,3,4,512]{4,3,2,1,0:T(4,128)(2,1)}, u32[]{:S(2)}) copy-start(bf16[3,3,3,4,512]{4,3,2,1,0:T(4,128)(2,1)} %param.6) | copy-start | bytes 331780
  42.8 14.3 %copy-start.2 = (bf16[8,8,1152]{2,1,0:T(8,128)(2,1)}, bf16[8,8,1152]{2,1,0:T(8,128)(2,1)S(1)}, u32[]{:S(2)}) copy-start(bf16[8,8,1152]{2,1,0:T(8,128)(2,1)S(1)} %all-to-all-done.1) | copy-start | bytes 442372
  42.8 8.2 %collective-permute-start.7 = (bf16[4,16,1152]{2,1,0:T(8,128)(2,1)S(1)}, bf16[4,16,1152]{2,1,0:T(8,128)(2,1)S(1)}, u32[]{:S(2)}, u32[]{:S(2)}) collective-permute-start(bf16[4,16,1152]{2,1,0:T(8,128)(2,1)S(1)} %bitcast.69), channel_id=1, source_target_pairs={{0,2},{1,3},{2,4},{3,5},{4,6},{5,7},{6,8},{7,9},{8,10},{9,11},{10,... | collective-permute-start | bytes 442376 | tf_op jit(solution)/shard_map/ppermute | solution.py:283
  45.1 8.1 %collective-permute-start.4 = (bf16[4,16,1152]{2,1,0:T(8,128)(2,1)S(1)}, bf16[4,16,1152]{2,1,0:T(8,128)(2,1)S(1)}, u32[]{:S(2)}, u32[]{:S(2)}) collective-permute-start(bf16[4,16,1152]{2,1,0:T(8,128)(2,1)S(1)} %bitcast.70), channel_id=1, source_target_pairs={{0,14},{1,15},{2,0},{3,1},{4,2},{5,3},{6,4},{7,5},{8,6},{9,7},{10,... | collective-permute-start | bytes 442376 | tf_op jit(solution)/shard_map/ppermute | solution.py:283
  50.9 6.1 %copy-start.6 = (bf16[4,16,1152]{2,1,0:T(8,128)(2,1)}, bf16[4,16,1152]{2,1,0:T(8,128)(2,1)S(1)}, u32[]{:S(2)}) copy-start(bf16[4,16,1152]{2,1,0:T(8,128)(2,1)S(1)} %collective-permute-done.7.refs_7_) | copy-start | bytes 442372
  51.0 6.0 %collective-permute-start.8 = (bf16[4,16,1152]{2,1,0:T(8,128)(2,1)S(1)}, bf16[4,16,1152]{2,1,0:T(8,128)(2,1)S(1)}, u32[]{:S(2)}, u32[]{:S(2)}) collective-permute-start(bf16[4,16,1152]{2,1,0:T(8,128)(2,1)S(1)} %collective-permute-done.7.refs_7_), channel_id=1, source_target_pairs={{0,2},{1,3},{2,4},{3,5},{4,6},{5,7},{6,8},{7,9},{8,10},{9,11},{10,... | collective-permute-start | bytes 442376 | tf_op jit(solution)/shard_map/ppermute | solution.py:283
  53.2 14.2 %copy-start.7 = (bf16[4,16,1152]{2,1,0:T(8,128)(2,1)}, bf16[4,16,1152]{2,1,0:T(8,128)(2,1)S(1)}, u32[]{:S(2)}) copy-start(bf16[4,16,1152]{2,1,0:T(8,128)(2,1)S(1)} %collective-permute-done.4.refs_1_) | copy-start | bytes 442372
  53.2 5.1 %collective-permute-start.5 = (bf16[4,16,1152]{2,1,0:T(8,128)(2,1)S(1)}, bf16[4,16,1152]{2,1,0:T(8,128)(2,1)S(1)}, u32[]{:S(2)}, u32[]{:S(2)}) collective-permute-start(bf16[4,16,1152]{2,1,0:T(8,128)(2,1)S(1)} %collective-permute-done.4.refs_1_), channel_id=1, source_target_pairs={{0,14},{1,15},{2,0},{3,1},{4,2},{5,3},{6,4},{7,5},{8,6},{9,7},{10,... | collective-permute-start | bytes 442376 | tf_op jit(solution)/shard_map/ppermute | solution.py:283
  57.0 10.4 %copy-start.8 = (bf16[4,16,1152]{2,1,0:T(8,128)(2,1)}, bf16[4,16,1152]{2,1,0:T(8,128)(2,1)S(1)}, u32[]{:S(2)}) copy-start(bf16[4,16,1152]{2,1,0:T(8,128)(2,1)S(1)} %collective-permute-done.8.refs_6_) | copy-start | bytes 442372
  57.0 5.2 %collective-permute-start.9 = (bf16[4,16,1152]{2,1,0:T(8,128)(2,1)S(1)}, bf16[4,16,1152]{2,1,0:T(8,128)(2,1)S(1)}, u32[]{:S(2)}, u32[]{:S(2)}) collective-permute-start(bf16[4,16,1152]{2,1,0:T(8,128)(2,1)S(1)} %collective-permute-done.8.refs_6_), channel_id=1, source_target_pairs={{0,2},{1,3},{2,4},{3,5},{4,6},{5,7},{6,8},{7,9},{8,10},{9,11},{10,... | collective-permute-start | bytes 442376 | tf_op jit(solution)/shard_map/ppermute | solution.py:283
  58.3 9.2 %copy-start.9 = (bf16[4,16,1152]{2,1,0:T(8,128)(2,1)}, bf16[4,16,1152]{2,1,0:T(8,128)(2,1)S(1)}, u32[]{:S(2)}) copy-start(bf16[4,16,1152]{2,1,0:T(8,128)(2,1)S(1)} %collective-permute-done.5.refs_2_) | copy-start | bytes 442372
  58.3 5.5 %collective-permute-start.6 = (bf16[4,16,1152]{2,1,0:T(8,128)(2,1)S(1)}, bf16[4,16,1152]{2,1,0:T(8,128)(2,1)S(1)}, u32[]{:S(2)}, u32[]{:S(2)}) collective-permute-start(bf16[4,16,1152]{2,1,0:T(8,128)(2,1)S(1)} %collective-permute-done.5.refs_2_), channel_id=1, source_target_pairs={{0,14},{1,15},{2,0},{3,1},{4,2},{5,3},{6,4},{7,5},{8,6},{9,7},{10,... | collective-permute-start | bytes 442376 | tf_op jit(solution)/shard_map/ppermute | solution.py:283
  62.2 5.2 %copy-start.10 = (bf16[4,16,1152]{2,1,0:T(8,128)(2,1)}, bf16[4,16,1152]{2,1,0:T(8,128)(2,1)S(1)}, u32[]{:S(2)}) copy-start(bf16[4,16,1152]{2,1,0:T(8,128)(2,1)S(1)} %collective-permute-done.9.refs_5_) | copy-start | bytes 442372
  62.2 5.2 %collective-permute-start.10 = (bf16[4,16,1152]{2,1,0:T(8,128)(2,1)S(1)}, bf16[4,16,1152]{2,1,0:T(8,128)(2,1)S(1)}, u32[]{:S(2)}, u32[]{:S(2)}) collective-permute-start(bf16[4,16,1152]{2,1,0:T(8,128)(2,1)S(1)} %collective-permute-done.9.refs_5_), channel_id=1, source_target_pairs={{0,2},{1,3},{2,4},{3,5},{4,6},{5,7},{6,8},{7,9},{8,10},{9,11},{10,... | collective-permute-start | bytes 442376 | tf_op jit(solution)/shard_map/ppermute | solution.py:283
  63.8 3.6 %copy-start.11 = (bf16[4,16,1152]{2,1,0:T(8,128)(2,1)}, bf16[4,16,1152]{2,1,0:T(8,128)(2,1)S(1)}, u32[]{:S(2)}) copy-start(bf16[4,16,1152]{2,1,0:T(8,128)(2,1)S(1)} %collective-permute-done.6.refs_3_) | copy-start | bytes 442372
  67.4 0.6 copy-start.12
  70.5 15.0 %collective-permute-start.11 = (bf16[8,4,16,1152]{3,2,1,0:T(8,128)(2,1)}, bf16[8,4,16,1152]{3,2,1,0:T(8,128)(2,1)S(1)}, u32[]{:S(2)}, u32[]{:S(2)}) collective-permute-start(bf16[8,4,16,1152]{3,2,1,0:T(8,128)(2,1)} %shard_map.62.mine_ref), channel_id=1, source_target_pairs={{0,1},{1,0},{2,3},{3,2},{4,5},{5,4},{6,7},{7,6},{8,9},{9,8},{10,11... | collective-permute-start | bytes 3538952 | tf_op jit(solution)/shard_map/ppermute | solution.py:283
  74.3 0.8 copy-start.3
  78.2 23.3 %all-to-all-start = ((bf16[16,64,256]{2,1,0:T(8,128)(2,1)}), bf16[16,64,256]{2,1,0:T(8,128)(2,1)S(1)}, u32[]{:S(2)}, u32[]{:S(2)}) async-start(bf16[16,64,256]{2,1,0:T(8,128)(2,1)} %get-tuple-element.10), calls=%async_computation | async-start | bytes 1048576 | tf_op jit(solution)/shard_map/all_to_all | solution.py:303
  85.5 1.0 copy-start.13
  101.5 3.5 %copy-start.4 = (bf16[16,64,256]{2,1,0:T(8,128)(2,1)}, bf16[16,64,256]{2,1,0:T(8,128)(2,1)S(1)}, u32[]{:S(2)}) copy-start(bf16[16,64,256]{2,1,0:T(8,128)(2,1)S(1)} %all-to-all-done.hidden_ref) | copy-start | bytes 1572868
  101.5 32.1 %all-to-all-start.2 = ((bf16[16,64,256]{2,1,0:T(8,128)(2,1)}), bf16[16,64,256]{2,1,0:T(8,128)(2,1)S(1)}, u32[]{:S(2)}, u32[]{:S(2)}) async-start(bf16[16,64,256]{2,1,0:T(8,128)(2,1)} %get-tuple-element.16), calls=%async_computation.2 | async-start | bytes 1048576 | tf_op jit(solution)/shard_map/all_to_all | solution.py:303
  109.5 24.0 %copy-start = (f32[16,64,256]{2,1,0:T(8,128)S(1)}, f32[16,64,256]{2,1,0:T(8,128)}, u32[]{:S(2)}) copy-start(f32[16,64,256]{2,1,0:T(8,128)} %get-tuple-element.17) | copy-start | bytes 3145732
  109.5 7.8 %collective-permute-start.14 = (bf16[108,512]{1,0:T(8,128)(2,1)}, bf16[108,512]{1,0:T(8,128)(2,1)S(1)}, u32[]{:S(2)}, u32[]{:S(2)}) collective-permute-start(bf16[108,512]{1,0:T(8,128)(2,1)} %get-tuple-element.15), channel_id=1, source_target_pairs={{0,48},{1,49},{2,50},{3,51},{4,52},{5,53},{6,54},{7,55},{8,56},{9,... | collective-permute-start | bytes 331784 | tf_op jit(solution)/shard_map/ppermute | solution.py:283
  111.8 6.6 %collective-permute-start.13 = (bf16[108,512]{1,0:T(8,128)(2,1)}, bf16[108,512]{1,0:T(8,128)(2,1)S(1)}, u32[]{:S(2)}, u32[]{:S(2)}) collective-permute-start(bf16[108,512]{1,0:T(8,128)(2,1)} %get-tuple-element.14), channel_id=1, source_target_pairs={{0,32},{1,33},{2,34},{3,35},{4,36},{5,37},{6,38},{7,39},{8,40},{9,... | collective-permute-start | bytes 331784 | tf_op jit(solution)/shard_map/ppermute | solution.py:283
  112.4 8.7 %collective-permute-start.12 = (bf16[108,512]{1,0:T(8,128)(2,1)}, bf16[108,512]{1,0:T(8,128)(2,1)S(1)}, u32[]{:S(2)}, u32[]{:S(2)}) collective-permute-start(bf16[108,512]{1,0:T(8,128)(2,1)} %get-tuple-element.13), channel_id=1, source_target_pairs={{0,16},{1,17},{2,18},{3,19},{4,20},{5,21},{6,22},{7,23},{8,24},{9,... | collective-permute-start | bytes 331784 | tf_op jit(solution)/shard_map/ppermute | solution.py:283
  122.1 4.6 %collective-permute-start.17 = (bf16[108,512]{1,0:T(8,128)(2,1)S(1)}, bf16[108,512]{1,0:T(8,128)(2,1)S(1)}, u32[]{:S(2)}, u32[]{:S(2)}) collective-permute-start(bf16[108,512]{1,0:T(8,128)(2,1)S(1)} %add_convert_fusion), channel_id=1, source_target_pairs={{0,192},{64,0},{128,64},{192,128},{1,193},{65,1},{129,65},{193,129... | collective-permute-start | bytes 331784 | tf_op jit(solution)/shard_map/ppermute | solution.py:26
  124.7 8.1 %collective-permute-start.16 = (bf16[108,512]{1,0:T(8,128)(2,1)S(1)}, bf16[108,512]{1,0:T(8,128)(2,1)S(1)}, u32[]{:S(2)}, u32[]{:S(2)}) collective-permute-start(bf16[108,512]{1,0:T(8,128)(2,1)S(1)} %add_convert_fusion), channel_id=1, source_target_pairs={{0,64},{64,128},{128,192},{192,0},{1,65},{65,129},{129,193},{193,1... | collective-permute-start | bytes 331784 | tf_op jit(solution)/shard_map/ppermute | solution.py:26
  124.7 8.1 %collective-permute-start.15 = (bf16[108,512]{1,0:T(8,128)(2,1)S(1)}, bf16[108,512]{1,0:T(8,128)(2,1)S(1)}, u32[]{:S(2)}, u32[]{:S(2)}) collective-permute-start(bf16[108,512]{1,0:T(8,128)(2,1)S(1)} %add_convert_fusion), channel_id=1, source_target_pairs={{0,128},{64,192},{128,0},{192,64},{1,129},{65,193},{129,1},{193,65... | collective-permute-start | bytes 331784 | tf_op jit(solution)/shard_map/ppermute | solution.py:26

commit v4 on v3

--- a/solution.py
+++ b/solution.py
@@ -24,6 +24,10 @@
 def from_side(block, axis, distance):
     size = lax.axis_size(axis)
     return lax.ppermute(block, axis, [(i, (i + distance) % size) for i in range(size)])
+
+
+ROWS, RING, CORES = 4, 8, 2
+IN_VMEM = pl.BlockSpec(memory_space=pltpu.VMEM)
 
 
 def shifted(block, by_row, by_col, row_len):
@@ -74,6 +78,8 @@
     return pl.pallas_call(
         functools.partial(conv_kernel, use, channels, row_len),
         out_shape=jax.ShapeDtypeStruct((4, outs, cells), dtype),
+        in_specs=[IN_VMEM] * 2,
+        out_specs=IN_VMEM,
         scratch_shapes=[pltpu.VMEM((4, depth, cells), jnp.bfloat16)],
         cost_estimate=pl.CostEstimate(
             flops=8 * outs * depth * cells, bytes_accessed=4 * depth * cells, transcendentals=0
@@ -84,17 +90,20 @@
 def act_kernel(part_ref, behind_ref, hidden_ref, slope_ref):
     groups, rows, _ = hidden_ref.shape
     unit = rows // 4
+    outs = part_ref.shape[1]
+    own = unit // ROWS
     for phase in range(4):
+        values = part_ref[phase] + behind_ref[phase].astype(jnp.float32)
+        gate = jax.nn.sigmoid(values)
+        gated = (1.0 - leak_slope) * gate
+        active = leak_slope * values + gated * values
+        slope = leak_slope + gated * (1.0 + values * (1.0 - gate))
+        there = slice(phase * unit, (phase + 1) * unit)
         for at in range(groups):
-            here = slice(at * unit, (at + 1) * unit)
-            values = part_ref[phase, here, :] + behind_ref[phase, here, :].astype(jnp.float32)
-            gate = jax.nn.sigmoid(values)
-            there = slice(phase * unit, (phase + 1) * unit)
-            gated = (1.0 - leak_slope) * gate
-            hidden_ref[at, there, :] = (leak_slope * values + gated * values).astype(
-                hidden_ref.dtype
-            )
-            slope_ref[at, there, :] = leak_slope + gated * (1.0 + values * (1.0 - gate))
+            picks = [slice(first, first + own) for first in range(at * own, outs, outs // ROWS)]
+            block = jnp.concatenate([active[pick] for pick in picks], 0)
+            hidden_ref[at, there, :] = block.astype(hidden_ref.dtype)
+            slope_ref[at, there, :] = jnp.concatenate([slope[pick] for pick in picks], 0)
 
 
 def act(part, behind, groups):
@@ -106,6 +115,8 @@
             jax.ShapeDtypeStruct(shape, jnp.bfloat16),
             jax.ShapeDtypeStruct(shape, jnp.float32),
         ),
+        in_specs=[IN_VMEM] * 2,
+        out_specs=(IN_VMEM,) * 2,
         cost_estimate=pl.CostEstimate(
             flops=10 * part.size, bytes_accessed=12 * part.size, transcendentals=part.size
         ),
@@ -122,6 +133,8 @@
     return pl.pallas_call(
         pile_kernel,
         out_shape=jax.ShapeDtypeStruct(shape, blocks[0].dtype),
+        in_specs=[IN_VMEM] * len(blocks),
+        out_specs=IN_VMEM,
         cost_estimate=pl.CostEstimate(
             flops=0, bytes_accessed=4 * len(blocks) * blocks[0].size, transcendentals=0
         ),
@@ -188,15 +201,14 @@
     outs = cot.shape[0]
     rows = pltpu.VMEM((4 * group, planes // 2 * cells), jnp.bfloat16)
     size = 27 * group // (4 * row_count)
-    vmem = pl.BlockSpec(memory_space=pltpu.VMEM)
     return pl.pallas_call(
         functools.partial(grad_kernel, row_len),
         out_shape=[
             jax.ShapeDtypeStruct((size, outs), jnp.bfloat16 if away else jnp.float32)
             for away in range(row_count)
         ],
-        in_specs=[pl.BlockSpec(memory_space=pltpu.SMEM), vmem, vmem],
-        out_specs=[vmem] * row_count,
+        in_specs=[pl.BlockSpec(memory_space=pltpu.SMEM), IN_VMEM, IN_VMEM],
+        out_specs=[IN_VMEM] * row_count,
         scratch_shapes=[rows, rows, pltpu.VMEM((row_count, size, outs), jnp.float32)],
         cost_estimate=pl.CostEstimate(
             flops=12 * group * outs * planes * cells, bytes_accessed=2 * cot.size, transcendentals=0
@@ -204,23 +216,36 @@
     )(place, hidden, cot)
 
 
-def back_kernel(row_len, place_ref, w_ref, mine_ref, theirs_ref, out_ref, cot_ref):
+def back_kernel(row_len, place_ref, *refs):
+    w_refs, (mine_ref, theirs_ref, out_ref, cot_ref, rows_ref, moves_ref) = refs[:-6], refs[-6:]
     planes, group, cells = out_ref.shape
-    ring, rows_y, unit, half = mine_ref.shape
-    z, core = place_ref[1], place_ref[2]
+    ring, row_count, unit, half = mine_ref.shape
+    y, z, core = place_ref[0], place_ref[1], place_ref[2]
     here = pl.ds(pl.multiple_of(core * half, 128), half)
     there = pl.ds(pl.multiple_of((1 - core) * half, 128), half)
     for k in range(ring):
-        for y in range(rows_y):
-            row = y * ring * unit + lax.rem(z + k, ring) * unit
-            rows = pl.ds(pl.multiple_of(row, unit), unit)
-            cot_ref[rows, here] = mine_ref[k, y]
-            cot_ref[rows, there] = theirs_ref[k, y]
+        for row in range(row_count):
+            first = row * ring * unit + lax.rem(z + k, ring) * unit
+            rows = pl.ds(pl.multiple_of(first, unit), unit)
+            cot_ref[rows, here] = mine_ref[k, row]
+            cot_ref[rows, there] = theirs_ref[k, row]
+
+    for away, w_ref in enumerate(w_refs):
+        rows_ref[lax.rem(y + away, row_count)] = w_ref[...].astype(jnp.float32)
+    block = group // 4
+    own = block // row_count
     size = 4 * group
+    moves_ref[...] = jnp.zeros_like(moves_ref)
+    for tap in range(27):
+        depth_tap, row_tap, col_tap = tap // 9, tap // 3 % 3, tap % 3
+        at = depth_tap * size + (2 * int(row_tap == 0) + int(col_tap == 0)) * group
+        at += (2 * int(row_tap != 1) + int(col_tap != 1)) * block
+        pieces = [rows_ref[row, tap * own : (tap + 1) * own, :] for row in range(row_count)]
+        moves_ref[at : at + block, :] = jnp.concatenate(pieces, 0).astype(moves_ref.dtype)
 
     def one(at, start):
         return jnp.dot(
-            w_ref[at * size : (at + 1) * size, :],
+            moves_ref[at * size : (at + 1) * size, :],
             cot_ref[:, start : start + cells],
             preferred_element_type=jnp.float32,
         )
@@ -232,45 +257,28 @@
         out_ref[2 * s + 1] = gather_back(odd, row_len).astype(out_ref.dtype)
 
 
-def back(place, w_rows, mine, theirs, planes, row_len):
-    rows, outs = w_rows.shape
-    group = rows // 12
+def back(place, w_rel, mine, theirs, planes, row_len):
+    size, outs = w_rel[0].shape
+    row_count = len(w_rel)
+    group = 4 * row_count * size // 27
     width = 2 * mine.shape[3]
     cells = width // (planes // 2 + 1)
-    vmem = pl.BlockSpec(memory_space=pltpu.VMEM)
     return pl.pallas_call(
         functools.partial(back_kernel, row_len),
         out_shape=(
             jax.ShapeDtypeStruct((planes, group, cells), jnp.bfloat16),
             jax.ShapeDtypeStruct((outs, width), jnp.bfloat16),
         ),
-        in_specs=[pl.BlockSpec(memory_space=pltpu.SMEM), vmem, vmem, vmem],
-        out_specs=(vmem, vmem),
-        cost_estimate=pl.CostEstimate(
-            flops=rows * outs * planes * cells, bytes_accessed=4 * outs * width, transcendentals=0
-        ),
-    )(place, w_rows, mine, theirs)
-
-
-def move_rows(w_second):
-    nothing = jnp.zeros_like(w_second[:, 0])
-
-    def halves(taps, gap):
-        return [[taps[1], taps[2]], [gap, taps[0]]]
-
-    by_row = halves([w_second[:, b] for b in range(3)], nothing)
-    moved_rows = []
-    for row in by_row:
-        for_phase = []
-        for part in row:
-            by_col = halves([part[:, c] for c in range(3)], jnp.zeros_like(part[:, 0]))
-            for_phase.append(jnp.stack([jnp.stack(col, 1) for col in by_col], 1))
-        moved_rows.append(jnp.stack(for_phase, 2))
-    rows = jnp.stack(moved_rows, 1)
-    return rows.reshape(-1, w_second.shape[-1])
-
-
-ROWS, RING, CORES = 4, 8, 2
+        in_specs=[pl.BlockSpec(memory_space=pltpu.SMEM)] + [IN_VMEM] * (row_count + 2),
+        out_specs=(IN_VMEM,) * 2,
+        scratch_shapes=[
+            pltpu.VMEM((row_count, size, outs), jnp.float32),
+            pltpu.VMEM((12 * group, outs), jnp.bfloat16),
+        ],
+        cost_estimate=pl.CostEstimate(
+            flops=12 * group * outs * planes * cells, bytes_accessed=4 * outs * width, transcendentals=0
+        ),
+    )(place, *w_rel, mine, theirs)
 
 
 def on_space(block, y_by=0, z_by=0, core_by=0):
@@ -330,23 +338,19 @@
     mine = pile(down + [far] + up[:0:-1])
     theirs = on_space(mine, core_by=1)
 
-    w_rel = [w_second]
+    w_rel = [w_second.reshape(27 * own, C3)]
     for step in range(1, ROWS):
-        w_rel.append(on_space(w_second, y_by=-step))
-    w_rel = jnp.stack(w_rel + w_rel, 3)
-    w_group = lax.dynamic_slice_in_dim(w_rel, (ROWS - y) % ROWS, ROWS, 3)
-    w_group = w_group.reshape(3, 3, 3, ROWS * own, C3)
+        w_rel.append(on_space(w_rel[0], y_by=-step))
 
     planes = volume[0].transpose(1, 2, 0, 3).reshape(2, 16 * channels, cells)
-    w_rows = w_first.reshape(27 * channels, ROWS, group, own).transpose(2, 1, 3, 0)
-    w_rows = w_rows.reshape(outs, 27 * channels)
+    w_rows = w_first.reshape(27 * channels, outs).T
     ahead = conv(w_rows, planes, ((0, 1),), jnp.bfloat16, row_len)
     behind = from_behind(ahead, "space", 1)
     part = conv(w_rows, planes, ((1, 0), (2, 1)), jnp.float32, row_len)
     hidden, slopes = act(part, behind, group)
     by_plane = exchange(hidden, SLABS)
 
-    back_terms, cot_row = back(place, move_rows(w_group), mine, theirs, group, row_len)
+    back_terms, cot_row = back(place, w_rel, mine, theirs, group, row_len)
     hidden_grad = exchange(back_terms, SLABS)
 
     partial, *others = grad(place, by_plane, cot_row, ROWS, row_len)

time: 136 us -> 125 us (0.919)
  local copies, waits for them, and re-layouts: 27.7 us -> 12.8 us
  blocking collectives: 0 us -> 11.2 us
  starting transfers between devices: 44.5 us -> 37 us
    all_to_all x0 -> x1, blocking collectives: none -> 11.2 us  [exchange(): lax.all_to_all(blocks, 'space', split_axis=0, concat_axis=0, axis_index_g...]
    ppermute x14, waiting for transfers between devices: 19.6 us -> 30.3 us  [on_space(): return lax.ppermute(block, 'space', route)]
    all_to_all x3 -> x2, waiting for transfers between devices: 10.2 us -> 0.51 us  [exchange(): lax.all_to_all(blocks, 'space', split_axis=0, concat_axis=0, axis_index_g...]
    unnamed x36, local copies, waits for them, and re-layouts: 11.3 us -> 3.14 us
    ppermute x14, starting transfers between devices: 22 us -> 16.9 us  [on_space(): return lax.ppermute(block, 'space', route)]
    transpose x1 -> x0, local copies, waits for them, and re-layouts: 2.08 us -> none  [section(): w_first.reshape(27 * channels, ROWS, group, own).transpose(2, 1, 3, 0)]
    ppermute x1, starting transfers between devices: 4.93 us -> 2.91 us  [from_behind(): return lax.ppermute(block, axis, route)]
    another operation x7 -> x0, local copies, waits for them, and re-layouts: 1.74 us -> none  [the longest x2 1.01 us: move_rows(): rows = jnp.stack(moved_rows, 1)]
  transfers between devices with their start and end apart: 21 -> 20, of which waited for: 12 -> 13; matrix products, arithmetic and copies ran while one was open for 19% -> 7% of each run, Pallas kernels for 17% -> 19%
where the time goes in v4:
time: 125 us
  waiting for transfers between devices  37.1 us (30%)
  starting transfers between devices  37 us (30%)
  Pallas kernels  23.5 us (19%)
  local copies, waits for them, and re-layouts  12.8 us (10%)
  blocking collectives  11.2 us (9%)
  other arithmetic  2.04 us (2%)
    ppermute x14, waiting for transfers between devices, on_space(): return lax.ppermute(block, 'space', route)  30.3 us
    ppermute x14, starting transfers between devices, on_space(): return lax.ppermute(block, 'space', route)  16.9 us
    all_to_all x2, starting transfers between devices, exchange(): lax.all_to_all(blocks, 'space', split_axis=0, concat_axis=0, axis_index_g...  13 us
    all_to_all x1, blocking collectives, exchange(): lax.all_to_all(blocks, 'space', split_axis=0, concat_axis=0, axis_index_g...  11.2 us
    pallas_call x2, Pallas kernels, conv(): pl.pallas_call(functools.partial(conv_kernel, use, channels, row_len), ou...  8.46 us
    ppermute x3, waiting for transfers between devices, from_side(): lax.ppermute(block, axis, [(i, (i + distance) % size) for i in range(size)])  6.33 us
    pallas_call x1, Pallas kernels, back(): pl.pallas_call(functools.partial(back_kernel, row_len), out_shape=(jax.Sh...  4.88 us
    pallas_call x1, Pallas kernels, grad(): pl.pallas_call(functools.partial(grad_kernel, row_len), out_shape=[jax.Sh...  4.55 us
  transfers between devices with their start and end apart: 20, of which 13 were waited for; matrix products, arithmetic and copies ran while one was open for 7% of the time, Pallas kernels for 19%

profile of v4, /device:TPU:1, one launch (start us, length us, event | category | flops | bytes accessed | tf_op | source)
XLA Modules:
  0.0 124.5 jit_solution(14762492768595031873)
XLA Ops:
  0.6 1.0 fusion
  1.7 0.3 maximum_bitcast_fusion
  2.0 11.2 %all_to_all.15 = bf16[8,8,1152]{2,1,0:T(8,128)(2,1)S(1)} all-to-all(bf16[8,8,1152]{2,1,0:T(8,128)(2,1)S(1)} %bitcast.27), channel_id=1, replica_groups={{0,1,16,17,32,33,48,49},{2,3,18,19,34,35,50,51},{4,5,20,21,36,37,52,53}..., dimensions={0} | all-to-all | bytes 294912 | tf_op jit(solution)/shard_map/all_to_all | solution.py:311
  13.2 1.6 %collective-permute-start.7 = (bf16[4,16,1152]{2,1,0:T(8,128)(2,1)S(1)}, bf16[4,16,1152]{2,1,0:T(8,128)(2,1)S(1)}, u32[]{:S(2)}, u32[]{:S(2)}) collective-permute-start(bf16[4,16,1152]{2,1,0:T(8,128)(2,1)S(1)} %bitcast.24), channel_id=1, source_target_pairs={{0,2},{1,3},{2,4},{3,5},{4,6},{5,7},{6,8},{7,9},{8,10},{9,11},{10,... | collective-permute-start | bytes 442376 | tf_op jit(solution)/shard_map/ppermute | solution.py:291
  14.8 3.9 %collective-permute-start.4 = (bf16[4,16,1152]{2,1,0:T(8,128)(2,1)S(1)}, bf16[4,16,1152]{2,1,0:T(8,128)(2,1)S(1)}, u32[]{:S(2)}, u32[]{:S(2)}) collective-permute-start(bf16[4,16,1152]{2,1,0:T(8,128)(2,1)S(1)} %bitcast.25), channel_id=1, source_target_pairs={{0,14},{1,15},{2,0},{3,1},{4,2},{5,3},{6,4},{7,5},{8,6},{9,7},{10,... | collective-permute-start | bytes 442376 | tf_op jit(solution)/shard_map/ppermute | solution.py:291
  18.8 3.3 %collective-permute-done.7.refs_7_ = bf16[4,16,1152]{2,1,0:T(8,128)(2,1)S(1)} collective-permute-done((bf16[4,16,1152]{2,1,0:T(8,128)(2,1)S(1)}, bf16[4,16,1152]{2,1,0:T(8,128)(2,1)S(1)}, u32[]{:S(2)}, u32[]{:S(2)}) %collective-permute-start.7) | collective-permute-done | bytes 147488 | tf_op jit(solution)/shard_map/ppermute | solution.py:291
  22.1 2.7 %collective-permute-start.5 = (bf16[4,16,1152]{2,1,0:T(8,128)(2,1)S(1)}, bf16[4,16,1152]{2,1,0:T(8,128)(2,1)S(1)}, u32[]{:S(2)}, u32[]{:S(2)}) collective-permute-start(bf16[4,16,1152]{2,1,0:T(8,128)(2,1)S(1)} %collective-permute-done.4.refs_1_), channel_id=1, source_target_pairs={{0,14},{1,15},{2,0},{3,1},{4,2},{5,3},{6,4},{7,5},{8,6},{9,7},{10,... | collective-permute-start | bytes 442376 | tf_op jit(solution)/shard_map/ppermute | solution.py:291
  24.8 2.5 %collective-permute-done.8.refs_6_ = bf16[4,16,1152]{2,1,0:T(8,128)(2,1)S(1)} collective-permute-done((bf16[4,16,1152]{2,1,0:T(8,128)(2,1)S(1)}, bf16[4,16,1152]{2,1,0:T(8,128)(2,1)S(1)}, u32[]{:S(2)}, u32[]{:S(2)}) %collective-permute-start.8) | collective-permute-done | bytes 147488 | tf_op jit(solution)/shard_map/ppermute | solution.py:291
  27.3 4.1 %copy.13 = bf16[3456,256]{0,1:T(8,128)(2,1)} copy(bf16[3456,256]{1,0:T(8,128)(2,1)} %bitcast.22) | data formatting | bytes 3538944 | tf_op jit(solution)/shard_map/reshape | solution.py:346
  31.4 2.5 %copy.14 = bf16[2,16,128,256]{3,2,1,0:T(8,128)(2,1)} copy(bf16[2,16,128,256]{3,1,0,2:T(8,128)(2,1)S(1)} %bitcast.20) | data formatting | bytes 4194304 | tf_op jit(solution)/shard_map/transpose | solution.py:345
  33.9 3.9 %shard_map.60 = bf16[4,256,256]{2,1,0:T(8,128)(2,1)} custom-call(bf16[256,3456]{1,0:T(8,128)(2,1)} %bitcast.18, bf16[2,2048,256]{2,1,0:T(8,128)(2,1)} %bitcast.16), custom_call_target="tpu_custom_call" | custom-call | flops 603979776 | bytes 1179648 | tf_op jit(solution)/shard_map/pallas_call | solution.py:78
  37.8 2.9 %collective-permute-start = (bf16[4,256,256]{2,1,0:T(8,128)(2,1)}, bf16[4,256,256]{2,1,0:T(8,128)(2,1)S(1)}, u32[]{:S(2)}, u32[]{:S(2)}) collective-permute-start(bf16[4,256,256]{2,1,0:T(8,128)(2,1)} %shard_map.60), channel_id=1, source_target_pairs={{0,1},{1,2},{2,3},{3,4},{4,5},{5,6},{6,7},{7,8},{8,9},{9,10},{10,1... | collective-permute-start | bytes 1572872 | tf_op jit(solution)/shard_map/ppermute | solution.py:21
  40.7 4.2 %collective-permute-start.6 = (bf16[4,16,1152]{2,1,0:T(8,128)(2,1)S(1)}, bf16[4,16,1152]{2,1,0:T(8,128)(2,1)S(1)}, u32[]{:S(2)}, u32[]{:S(2)}) collective-permute-start(bf16[4,16,1152]{2,1,0:T(8,128)(2,1)S(1)} %collective-permute-done.5.refs_2_), channel_id=1, source_target_pairs={{0,14},{1,15},{2,0},{3,1},{4,2},{5,3},{6,4},{7,5},{8,6},{9,7},{10,... | collective-permute-start | bytes 442376 | tf_op jit(solution)/shard_map/ppermute | solution.py:291
  45.0 2.9 %collective-permute-done.6.refs_3_ = bf16[4,16,1152]{2,1,0:T(8,128)(2,1)S(1)} collective-permute-done((bf16[4,16,1152]{2,1,0:T(8,128)(2,1)S(1)}, bf16[4,16,1152]{2,1,0:T(8,128)(2,1)S(1)}, u32[]{:S(2)}, u32[]{:S(2)}) %collective-permute-start.6) | collective-permute-done | bytes 147488 | tf_op jit(solution)/shard_map/ppermute | solution.py:291
  47.9 6.9 %collective-permute-done.10.refs_4_ = bf16[4,16,1152]{2,1,0:T(8,128)(2,1)S(1)} collective-permute-done((bf16[4,16,1152]{2,1,0:T(8,128)(2,1)S(1)}, bf16[4,16,1152]{2,1,0:T(8,128)(2,1)S(1)}, u32[]{:S(2)}, u32[]{:S(2)}) %collective-permute-start.10) | collective-permute-done | bytes 147488 | tf_op jit(solution)/shard_map/ppermute | solution.py:291
  54.8 0.7 copy-done.11
  55.5 2.4 %shard_map.62.refs_4_ = bf16[8,4,16,1152]{3,2,1,0:T(8,128)(2,1)} custom-call(bf16[4,16,1152]{2,1,0:T(8,128)(2,1)} %bitcast.26, bf16[4,16,1152]{2,1,0:T(8,128)(2,1)} %copy-done.6, bf16[4,16,1152]{2,1,0:T(8,128)(2,1)} %copy-done.8, bf16[4,16,1152]{2,1,0:T(8,128)(2,1)} %copy-done.10, bf16[4,16,1152]{2,1,0:T(8,128)(2,1)} %copy-done.11, ...), custom_call_target="tpu_custom_call" | custom-call | bytes 2359296 | tf_op jit(solution)/shard_map/pallas_call | solution.py:133
  57.9 4.6 %shard_map.59.part_ref = f32[4,256,256]{2,1,0:T(8,128)} custom-call(bf16[256,3456]{1,0:T(8,128)(2,1)} %bitcast.19, bf16[2,2048,256]{2,1,0:T(8,128)(2,1)} %bitcast.17), custom_call_target="tpu_custom_call" | custom-call | flops 1207959552 | bytes 2359296 | tf_op jit(solution)/shard_map/pallas_call | solution.py:78
  62.5 0.8 copy-done.3
  63.3 3.1 %shard_map.61 = (bf16[16,64,256]{2,1,0:T(8,128)(2,1)}, f32[16,64,256]{2,1,0:T(8,128)}) custom-call(f32[4,256,256]{2,1,0:T(8,128)} %shard_map.59.part_ref, bf16[4,256,256]{2,1,0:T(8,128)(2,1)} %copy-done.3), custom_call_target="tpu_custom_call" | custom-call | flops 2621440 | bytes 3145728 | tf_op jit(solution)/shard_map/pallas_call | solution.py:112
  66.5 6.1 %all-to-all-start = ((bf16[16,64,256]{2,1,0:T(8,128)(2,1)}), bf16[16,64,256]{2,1,0:T(8,128)(2,1)S(1)}, u32[]{:S(2)}, u32[]{:S(2)}) async-start(bf16[16,64,256]{2,1,0:T(8,128)(2,1)} %get-tuple-element.10), calls=%async_computation | async-start | bytes 1048576 | tf_op jit(solution)/shard_map/all_to_all | solution.py:311
  72.6 1.2 collective-permute-start.1
  73.8 1.2 collective-permute-start.2
  74.9 0.6 pad_add_fusion.place_ref
  75.5 1.9 %collective-permute-done.1.refs_1_ = bf16[108,512]{1,0:T(8,128)(2,1)S(1)} collective-permute-done((bf16[108,512]{1,0:T(8,128)(2,1)S(1)}, bf16[108,512]{1,0:T(8,128)(2,1)S(1)}, u32[]{:S(2)}, u32[]{:S(2)}) %collective-permute-start.1) | collective-permute-done | bytes 110624 | tf_op jit(solution)/shard_map/ppermute | solution.py:291
  77.5 2.1 %collective-permute-done.2.refs_2_ = bf16[108,512]{1,0:T(8,128)(2,1)S(1)} collective-permute-done((bf16[108,512]{1,0:T(8,128)(2,1)S(1)}, bf16[108,512]{1,0:T(8,128)(2,1)S(1)}, u32[]{:S(2)}, u32[]{:S(2)}) %collective-permute-start.2) | collective-permute-done | bytes 110624 | tf_op jit(solution)/shard_map/ppermute | solution.py:291
  79.6 3.1 %collective-permute-done.3.refs_3_ = bf16[108,512]{1,0:T(8,128)(2,1)S(1)} collective-permute-done((bf16[108,512]{1,0:T(8,128)(2,1)S(1)}, bf16[108,512]{1,0:T(8,128)(2,1)S(1)}, u32[]{:S(2)}, u32[]{:S(2)}) %collective-permute-start.3) | collective-permute-done | bytes 110624 | tf_op jit(solution)/shard_map/ppermute | solution.py:291
  82.7 0.6 copy-done.17
  83.3 1.0 copy-done.14
  84.4 4.9 %shard_map.63 = (bf16[16,64,256]{2,1,0:T(8,128)(2,1)}, bf16[512,2304]{1,0:T(8,128)(2,1)}) custom-call(s32[3]{0:T(128)} %pad_add_fusion.place_ref, bf16[108,512]{1,0:T(8,128)(2,1)} %copy-done.12, bf16[108,512]{1,0:T(8,128)(2,1)} %copy-done.15, bf16[108,512]{1,0:T(8,128)(2,1)} %copy-done.16, bf16[108,512]{1,0:T(8,128)(2,1)} %copy-done.17, ...), custom_call_target="tpu_custom_call" | custom-call | flops 1610612736 | bytes 4718592 | tf_op jit(solution)/shard_map/pallas_call | solution.py:266
  89.2 0.5 all-to-all-done.hidden_ref
  89.8 6.9 %all-to-all-start.2 = ((bf16[16,64,256]{2,1,0:T(8,128)(2,1)}), bf16[16,64,256]{2,1,0:T(8,128)(2,1)S(1)}, u32[]{:S(2)}, u32[]{:S(2)}) async-start(bf16[16,64,256]{2,1,0:T(8,128)(2,1)} %get-tuple-element.16), calls=%async_computation.2 | async-start | bytes 1048576 | tf_op jit(solution)/shard_map/all_to_all | solution.py:311
  96.7 4.6 %shard_map.64 = (f32[108,512]{1,0:T(8,128)}, bf16[108,512]{1,0:T(8,128)(2,1)}, bf16[108,512]{1,0:T(8,128)(2,1)}, bf16[108,512]{1,0:T(8,128)(2,1)}) custom-call(s32[3]{0:T(128)} %pad_add_fusion.place_ref, bf16[16,64,256]{2,1,0:T(8,128)(2,1)} %copy-done.4, bf16[512,2304]{1,0:T(8,128)(2,1)} %get-tuple-element.11.cot_ref), custom_call_target="tpu_custom_call" | custom-call | flops 1610612736 | bytes 2359296 | tf_op jit(solution)/shard_map/pallas_call | solution.py:204
  101.2 0.3 collective-permute-start.14
  101.5 1.2 collective-permute-start.13
  102.7 0.6 collective-permute-start.12
  103.3 2.8 %collective-permute-done.14 = bf16[108,512]{1,0:T(8,128)(2,1)S(1)} collective-permute-done((bf16[108,512]{1,0:T(8,128)(2,1)}, bf16[108,512]{1,0:T(8,128)(2,1)S(1)}, u32[]{:S(2)}, u32[]{:S(2)}) %collective-permute-start.14) | collective-permute-done | bytes 110624 | tf_op jit(solution)/shard_map/ppermute | solution.py:291
  106.1 1.5 %collective-permute-done.13 = bf16[108,512]{1,0:T(8,128)(2,1)S(1)} collective-permute-done((bf16[108,512]{1,0:T(8,128)(2,1)}, bf16[108,512]{1,0:T(8,128)(2,1)S(1)}, u32[]{:S(2)}, u32[]{:S(2)}) %collective-permute-start.13) | collective-permute-done | bytes 110624 | tf_op jit(solution)/shard_map/ppermute | solution.py:291
  107.6 3.2 %collective-permute-done.12 = bf16[108,512]{1,0:T(8,128)(2,1)S(1)} collective-permute-done((bf16[108,512]{1,0:T(8,128)(2,1)}, bf16[108,512]{1,0:T(8,128)(2,1)S(1)}, u32[]{:S(2)}, u32[]{:S(2)}) %collective-permute-start.12) | collective-permute-done | bytes 110624 | tf_op jit(solution)/shard_map/ppermute | solution.py:291
  110.8 1.0 add_convert_fusion
  111.8 2.5 %collective-permute-start.17 = (bf16[108,512]{1,0:T(8,128)(2,1)S(1)}, bf16[108,512]{1,0:T(8,128)(2,1)S(1)}, u32[]{:S(2)}, u32[]{:S(2)}) collective-permute-start(bf16[108,512]{1,0:T(8,128)(2,1)S(1)} %add_convert_fusion), channel_id=1, source_target_pairs={{0,192},{64,0},{128,64},{192,128},{1,193},{65,1},{129,65},{193,129... | collective-permute-start | bytes 331784 | tf_op jit(solution)/shard_map/ppermute | solution.py:26
  114.3 1.7 %collective-permute-start.15 = (bf16[108,512]{1,0:T(8,128)(2,1)S(1)}, bf16[108,512]{1,0:T(8,128)(2,1)S(1)}, u32[]{:S(2)}, u32[]{:S(2)}) collective-permute-start(bf16[108,512]{1,0:T(8,128)(2,1)S(1)} %add_convert_fusion), channel_id=1, source_target_pairs={{0,128},{64,192},{128,0},{192,64},{1,129},{65,193},{129,1},{193,65... | collective-permute-start | bytes 331784 | tf_op jit(solution)/shard_map/ppermute | solution.py:26
  116.0 0.3 collective-permute-done.17
  116.3 6.1 %collective-permute-done.16 = bf16[108,512]{1,0:T(8,128)(2,1)S(1)} collective-permute-done((bf16[108,512]{1,0:T(8,128)(2,1)S(1)}, bf16[108,512]{1,0:T(8,128)(2,1)S(1)}, u32[]{:S(2)}, u32[]{:S(2)}) %collective-permute-start.16) | collective-permute-done | bytes 110624 | tf_op jit(solution)/shard_map/ppermute | solution.py:26
  122.4 0.7 reshape.42
  123.2 0.1 multiply_convert_fusion
  123.3 0.1 reshape.43
  123.4 1.1 copy.16
  (52 shorter events, 0.4 us)
Async XLA Ops:
  13.2 18.2 %copy-start.2 = (bf16[8,8,1152]{2,1,0:T(8,128)(2,1)}, bf16[8,8,1152]{2,1,0:T(8,128)(2,1)S(1)}, u32[]{:S(2)}) copy-start(bf16[8,8,1152]{2,1,0:T(8,128)(2,1)S(1)} %all_to_all.15) | copy-start | bytes 442372
  13.2 8.9 %collective-permute-start.7 = (bf16[4,16,1152]{2,1,0:T(8,128)(2,1)S(1)}, bf16[4,16,1152]{2,1,0:T(8,128)(2,1)S(1)}, u32[]{:S(2)}, u32[]{:S(2)}) collective-permute-start(bf16[4,16,1152]{2,1,0:T(8,128)(2,1)S(1)} %bitcast.24), channel_id=1, source_target_pairs={{0,2},{1,3},{2,4},{3,5},{4,6},{5,7},{6,8},{7,9},{8,10},{9,11},{10,... | collective-permute-start | bytes 442376 | tf_op jit(solution)/shard_map/ppermute | solution.py:291
  14.8 7.3 %collective-permute-start.4 = (bf16[4,16,1152]{2,1,0:T(8,128)(2,1)S(1)}, bf16[4,16,1152]{2,1,0:T(8,128)(2,1)S(1)}, u32[]{:S(2)}, u32[]{:S(2)}) collective-permute-start(bf16[4,16,1152]{2,1,0:T(8,128)(2,1)S(1)} %bitcast.25), channel_id=1, source_target_pairs={{0,14},{1,15},{2,0},{3,1},{4,2},{5,3},{6,4},{7,5},{8,6},{9,7},{10,... | collective-permute-start | bytes 442376 | tf_op jit(solution)/shard_map/ppermute | solution.py:291
  22.1 9.3 %copy-start.5 = (bf16[4,16,1152]{2,1,0:T(8,128)(2,1)}, bf16[4,16,1152]{2,1,0:T(8,128)(2,1)S(1)}, u32[]{:S(2)}) copy-start(bf16[4,16,1152]{2,1,0:T(8,128)(2,1)S(1)} %collective-permute-done.7.refs_7_) | copy-start | bytes 442372
  22.1 5.2 %collective-permute-start.8 = (bf16[4,16,1152]{2,1,0:T(8,128)(2,1)S(1)}, bf16[4,16,1152]{2,1,0:T(8,128)(2,1)S(1)}, u32[]{:S(2)}, u32[]{:S(2)}) collective-permute-start(bf16[4,16,1152]{2,1,0:T(8,128)(2,1)S(1)} %collective-permute-done.7.refs_7_), channel_id=1, source_target_pairs={{0,2},{1,3},{2,4},{3,5},{4,6},{5,7},{6,8},{7,9},{8,10},{9,11},{10,... | collective-permute-start | bytes 442376 | tf_op jit(solution)/shard_map/ppermute | solution.py:291
  22.1 9.3 %copy-start.6 = (bf16[4,16,1152]{2,1,0:T(8,128)(2,1)}, bf16[4,16,1152]{2,1,0:T(8,128)(2,1)S(1)}, u32[]{:S(2)}) copy-start(bf16[4,16,1152]{2,1,0:T(8,128)(2,1)S(1)} %collective-permute-done.4.refs_1_) | copy-start | bytes 442372
  22.1 18.6 %collective-permute-start.5 = (bf16[4,16,1152]{2,1,0:T(8,128)(2,1)S(1)}, bf16[4,16,1152]{2,1,0:T(8,128)(2,1)S(1)}, u32[]{:S(2)}, u32[]{:S(2)}) collective-permute-start(bf16[4,16,1152]{2,1,0:T(8,128)(2,1)S(1)} %collective-permute-done.4.refs_1_), channel_id=1, source_target_pairs={{0,14},{1,15},{2,0},{3,1},{4,2},{5,3},{6,4},{7,5},{8,6},{9,7},{10,... | collective-permute-start | bytes 442376 | tf_op jit(solution)/shard_map/ppermute | solution.py:291
  27.3 4.1 %copy-start.7 = (bf16[4,16,1152]{2,1,0:T(8,128)(2,1)}, bf16[4,16,1152]{2,1,0:T(8,128)(2,1)S(1)}, u32[]{:S(2)}) copy-start(bf16[4,16,1152]{2,1,0:T(8,128)(2,1)S(1)} %collective-permute-done.8.refs_6_) | copy-start | bytes 442372
  27.3 17.7 %collective-permute-start.9 = (bf16[4,16,1152]{2,1,0:T(8,128)(2,1)S(1)}, bf16[4,16,1152]{2,1,0:T(8,128)(2,1)S(1)}, u32[]{:S(2)}, u32[]{:S(2)}) collective-permute-start(bf16[4,16,1152]{2,1,0:T(8,128)(2,1)S(1)} %collective-permute-done.8.refs_6_), channel_id=1, source_target_pairs={{0,2},{1,3},{2,4},{3,5},{4,6},{5,7},{6,8},{7,9},{8,10},{9,11},{10,... | collective-permute-start | bytes 442376 | tf_op jit(solution)/shard_map/ppermute | solution.py:291
  27.3 4.1 %copy-start = (bf16[1,128,2,16,256]{4,3,2,1,0:T(8,128)(2,1)S(1)}, bf16[1,128,2,16,256]{4,3,2,1,0:T(8,128)(2,1)}, u32[]{:S(2)}) copy-start(bf16[1,128,2,16,256]{4,3,2,1,0:T(8,128)(2,1)} %param.4) | copy-start | bytes 6291460
  37.8 24.7 %collective-permute-start = (bf16[4,256,256]{2,1,0:T(8,128)(2,1)}, bf16[4,256,256]{2,1,0:T(8,128)(2,1)S(1)}, u32[]{:S(2)}, u32[]{:S(2)}) collective-permute-start(bf16[4,256,256]{2,1,0:T(8,128)(2,1)} %shard_map.60), channel_id=1, source_target_pairs={{0,1},{1,2},{2,3},{3,4},{4,5},{5,6},{6,7},{7,8},{8,9},{9,10},{10,1... | collective-permute-start | bytes 1572872 | tf_op jit(solution)/shard_map/ppermute | solution.py:21
  40.7 14.1 %copy-start.8 = (bf16[4,16,1152]{2,1,0:T(8,128)(2,1)}, bf16[4,16,1152]{2,1,0:T(8,128)(2,1)S(1)}, u32[]{:S(2)}) copy-start(bf16[4,16,1152]{2,1,0:T(8,128)(2,1)S(1)} %collective-permute-done.5.refs_2_) | copy-start | bytes 442372
  40.7 7.1 %collective-permute-start.6 = (bf16[4,16,1152]{2,1,0:T(8,128)(2,1)S(1)}, bf16[4,16,1152]{2,1,0:T(8,128)(2,1)S(1)}, u32[]{:S(2)}, u32[]{:S(2)}) collective-permute-start(bf16[4,16,1152]{2,1,0:T(8,128)(2,1)S(1)} %collective-permute-done.5.refs_2_), channel_id=1, source_target_pairs={{0,14},{1,15},{2,0},{3,1},{4,2},{5,3},{6,4},{7,5},{8,6},{9,7},{10,... | collective-permute-start | bytes 442376 | tf_op jit(solution)/shard_map/ppermute | solution.py:291
  45.0 9.8 %copy-start.9 = (bf16[4,16,1152]{2,1,0:T(8,128)(2,1)}, bf16[4,16,1152]{2,1,0:T(8,128)(2,1)S(1)}, u32[]{:S(2)}) copy-start(bf16[4,16,1152]{2,1,0:T(8,128)(2,1)S(1)} %collective-permute-done.9.refs_5_) | copy-start | bytes 442372
  45.0 9.8 %collective-permute-start.10 = (bf16[4,16,1152]{2,1,0:T(8,128)(2,1)S(1)}, bf16[4,16,1152]{2,1,0:T(8,128)(2,1)S(1)}, u32[]{:S(2)}, u32[]{:S(2)}) collective-permute-start(bf16[4,16,1152]{2,1,0:T(8,128)(2,1)S(1)} %collective-permute-done.9.refs_5_), channel_id=1, source_target_pairs={{0,2},{1,3},{2,4},{3,5},{4,6},{5,7},{6,8},{7,9},{8,10},{9,11},{10,... | collective-permute-start | bytes 442376 | tf_op jit(solution)/shard_map/ppermute | solution.py:291
  47.9 6.9 %copy-start.10 = (bf16[4,16,1152]{2,1,0:T(8,128)(2,1)}, bf16[4,16,1152]{2,1,0:T(8,128)(2,1)S(1)}, u32[]{:S(2)}) copy-start(bf16[4,16,1152]{2,1,0:T(8,128)(2,1)S(1)} %collective-permute-done.6.refs_3_) | copy-start | bytes 442372
  54.8 0.7 copy-start.11
  57.9 24.8 %collective-permute-start.11 = (bf16[8,4,16,1152]{3,2,1,0:T(8,128)(2,1)}, bf16[8,4,16,1152]{3,2,1,0:T(8,128)(2,1)S(1)}, u32[]{:S(2)}, u32[]{:S(2)}) collective-permute-start(bf16[8,4,16,1152]{3,2,1,0:T(8,128)(2,1)} %shard_map.62.refs_4_), channel_id=1, source_target_pairs={{0,1},{1,0},{2,3},{3,2},{4,5},{5,4},{6,7},{7,6},{8,9},{9,8},{10,11... | collective-permute-start | bytes 3538952 | tf_op jit(solution)/shard_map/ppermute | solution.py:291
  62.5 10.0 %copy-start.13 = (bf16[3,3,3,4,512]{4,3,2,1,0:T(4,128)(2,1)S(1)}, bf16[3,3,3,4,512]{4,3,2,1,0:T(4,128)(2,1)}, u32[]{:S(2)}) copy-start(bf16[3,3,3,4,512]{4,3,2,1,0:T(4,128)(2,1)} %param.6) | copy-start | bytes 331780
  62.5 0.8 copy-start.3
  66.5 23.3 %all-to-all-start = ((bf16[16,64,256]{2,1,0:T(8,128)(2,1)}), bf16[16,64,256]{2,1,0:T(8,128)(2,1)S(1)}, u32[]{:S(2)}, u32[]{:S(2)}) async-start(bf16[16,64,256]{2,1,0:T(8,128)(2,1)} %get-tuple-element.10), calls=%async_computation | async-start | bytes 1048576 | tf_op jit(solution)/shard_map/all_to_all | solution.py:311
  72.6 10.1 %copy-start.12 = (bf16[108,512]{1,0:T(8,128)(2,1)}, bf16[108,512]{1,0:T(8,128)(2,1)S(1)}, u32[]{:S(2)}) copy-start(bf16[108,512]{1,0:T(8,128)(2,1)S(1)} %reshape.39.refs_0_) | copy-start | bytes 331780
  72.6 4.9 %collective-permute-start.1 = (bf16[108,512]{1,0:T(8,128)(2,1)S(1)}, bf16[108,512]{1,0:T(8,128)(2,1)S(1)}, u32[]{:S(2)}, u32[]{:S(2)}) collective-permute-start(bf16[108,512]{1,0:T(8,128)(2,1)S(1)} %reshape.39.refs_0_), channel_id=1, source_target_pairs={{0,48},{1,49},{2,50},{3,51},{4,52},{5,53},{6,54},{7,55},{8,56},{9,... | collective-permute-start | bytes 331784 | tf_op jit(solution)/shard_map/ppermute | solution.py:291
  73.8 5.8 %collective-permute-start.2 = (bf16[108,512]{1,0:T(8,128)(2,1)S(1)}, bf16[108,512]{1,0:T(8,128)(2,1)S(1)}, u32[]{:S(2)}, u32[]{:S(2)}) collective-permute-start(bf16[108,512]{1,0:T(8,128)(2,1)S(1)} %reshape.39.refs_0_), channel_id=1, source_target_pairs={{0,32},{1,33},{2,34},{3,35},{4,36},{5,37},{6,38},{7,39},{8,40},{9,... | collective-permute-start | bytes 331784 | tf_op jit(solution)/shard_map/ppermute | solution.py:291
  74.9 7.8 %collective-permute-start.3 = (bf16[108,512]{1,0:T(8,128)(2,1)S(1)}, bf16[108,512]{1,0:T(8,128)(2,1)S(1)}, u32[]{:S(2)}, u32[]{:S(2)}) collective-permute-start(bf16[108,512]{1,0:T(8,128)(2,1)S(1)} %reshape.39.refs_0_), channel_id=1, source_target_pairs={{0,16},{1,17},{2,18},{3,19},{4,20},{5,21},{6,22},{7,23},{8,24},{9,... | collective-permute-start | bytes 331784 | tf_op jit(solution)/shard_map/ppermute | solution.py:291
  77.5 5.2 %copy-start.15 = (bf16[108,512]{1,0:T(8,128)(2,1)}, bf16[108,512]{1,0:T(8,128)(2,1)S(1)}, u32[]{:S(2)}) copy-start(bf16[108,512]{1,0:T(8,128)(2,1)S(1)} %collective-permute-done.1.refs_1_) | copy-start | bytes 331780
  79.6 3.1 %copy-start.16 = (bf16[108,512]{1,0:T(8,128)(2,1)}, bf16[108,512]{1,0:T(8,128)(2,1)S(1)}, u32[]{:S(2)}) copy-start(bf16[108,512]{1,0:T(8,128)(2,1)S(1)} %collective-permute-done.2.refs_2_) | copy-start | bytes 331780
  82.7 0.6 copy-start.17
  83.3 1.0 copy-start.14
  89.8 6.9 %copy-start.4 = (bf16[16,64,256]{2,1,0:T(8,128)(2,1)}, bf16[16,64,256]{2,1,0:T(8,128)(2,1)S(1)}, u32[]{:S(2)}) copy-start(bf16[16,64,256]{2,1,0:T(8,128)(2,1)S(1)} %all-to-all-done.hidden_ref) | copy-start | bytes 1572868
  89.8 33.4 %all-to-all-start.2 = ((bf16[16,64,256]{2,1,0:T(8,128)(2,1)}), bf16[16,64,256]{2,1,0:T(8,128)(2,1)S(1)}, u32[]{:S(2)}, u32[]{:S(2)}) async-start(bf16[16,64,256]{2,1,0:T(8,128)(2,1)} %get-tuple-element.16), calls=%async_computation.2 | async-start | bytes 1048576 | tf_op jit(solution)/shard_map/all_to_all | solution.py:311
  101.2 21.9 %copy-start.1 = (f32[16,64,256]{2,1,0:T(8,128)S(1)}, f32[16,64,256]{2,1,0:T(8,128)}, u32[]{:S(2)}) copy-start(f32[16,64,256]{2,1,0:T(8,128)} %get-tuple-element.17) | copy-start | bytes 3145732
  101.2 4.8 %collective-permute-start.14 = (bf16[108,512]{1,0:T(8,128)(2,1)}, bf16[108,512]{1,0:T(8,128)(2,1)S(1)}, u32[]{:S(2)}, u32[]{:S(2)}) collective-permute-start(bf16[108,512]{1,0:T(8,128)(2,1)} %get-tuple-element.15), channel_id=1, source_target_pairs={{0,48},{1,49},{2,50},{3,51},{4,52},{5,53},{6,54},{7,55},{8,56},{9,... | collective-permute-start | bytes 331784 | tf_op jit(solution)/shard_map/ppermute | solution.py:291
  101.5 6.0 %collective-permute-start.13 = (bf16[108,512]{1,0:T(8,128)(2,1)}, bf16[108,512]{1,0:T(8,128)(2,1)S(1)}, u32[]{:S(2)}, u32[]{:S(2)}) collective-permute-start(bf16[108,512]{1,0:T(8,128)(2,1)} %get-tuple-element.14), channel_id=1, source_target_pairs={{0,32},{1,33},{2,34},{3,35},{4,36},{5,37},{6,38},{7,39},{8,40},{9,... | collective-permute-start | bytes 331784 | tf_op jit(solution)/shard_map/ppermute | solution.py:291
  102.7 8.0 %collective-permute-start.12 = (bf16[108,512]{1,0:T(8,128)(2,1)}, bf16[108,512]{1,0:T(8,128)(2,1)S(1)}, u32[]{:S(2)}, u32[]{:S(2)}) collective-permute-start(bf16[108,512]{1,0:T(8,128)(2,1)} %get-tuple-element.13), channel_id=1, source_target_pairs={{0,16},{1,17},{2,18},{3,19},{4,20},{5,21},{6,22},{7,23},{8,24},{9,... | collective-permute-start | bytes 331784 | tf_op jit(solution)/shard_map/ppermute | solution.py:291
  111.8 4.5 %collective-permute-start.17 = (bf16[108,512]{1,0:T(8,128)(2,1)S(1)}, bf16[108,512]{1,0:T(8,128)(2,1)S(1)}, u32[]{:S(2)}, u32[]{:S(2)}) collective-permute-start(bf16[108,512]{1,0:T(8,128)(2,1)S(1)} %add_convert_fusion), channel_id=1, source_target_pairs={{0,192},{64,0},{128,64},{192,128},{1,193},{65,1},{129,65},{193,129... | collective-permute-start | bytes 331784 | tf_op jit(solution)/shard_map/ppermute | solution.py:26
  114.3 8.1 %collective-permute-start.16 = (bf16[108,512]{1,0:T(8,128)(2,1)S(1)}, bf16[108,512]{1,0:T(8,128)(2,1)S(1)}, u32[]{:S(2)}, u32[]{:S(2)}) collective-permute-start(bf16[108,512]{1,0:T(8,128)(2,1)S(1)} %add_convert_fusion), channel_id=1, source_target_pairs={{0,64},{64,128},{128,192},{192,0},{1,65},{65,129},{129,193},{193,1... | collective-permute-start | bytes 331784 | tf_op jit(solution)/shard_map/ppermute | solution.py:26
  114.3 8.1 %collective-permute-start.15 = (bf16[108,512]{1,0:T(8,128)(2,1)S(1)}, bf16[108,512]{1,0:T(8,128)(2,1)S(1)}, u32[]{:S(2)}, u32[]{:S(2)}) collective-permute-start(bf16[108,512]{1,0:T(8,128)(2,1)S(1)} %add_convert_fusion), channel_id=1, source_target_pairs={{0,128},{64,192},{128,0},{192,64},{1,129},{65,193},{129,1},{193,65... | collective-permute-start | bytes 331784 | tf_op jit(solution)/shard_map/ppermute | solution.py:26

commit v5 on v4

--- a/solution.py
+++ b/solution.py
@@ -45,6 +45,7 @@
 
 def conv_kernel(use, channels, row_len, w_ref, planes_ref, out_ref, cols_ref):
     tap_rows = 9 * channels
+    cells = planes_ref.shape[2]
     for at, (_, plane) in enumerate(use):
         for row in range(-1, 4):
             for col in range(-1, 4):
@@ -61,17 +62,22 @@
                         if not 0 <= col_tap <= 2:
                             continue
                         start = at * tap_rows + (row_tap * 3 + col_tap) * channels
-                        cols_ref[row_phase * 2 + col_phase, start : start + channels, :] = block
+                        phase = row_phase * 2 + col_phase
+                        put = slice(phase * cells, (phase + 1) * cells)
+                        cols_ref[start : start + channels, put] = block
     first = use[0][0] * tap_rows
-    weights = w_ref[:, first : first + len(use) * tap_rows]
+    total = lax.dot_general(
+        w_ref[first : first + len(use) * tap_rows, :],
+        cols_ref[...],
+        (((0,), (0,)), ((), ())),
+        preferred_element_type=jnp.float32,
+    )
     for phase in range(4):
-        out_ref[phase, :, :] = jnp.dot(
-            weights, cols_ref[phase], preferred_element_type=jnp.float32
-        ).astype(out_ref.dtype)
+        out_ref[phase] = total[:, phase * cells : (phase + 1) * cells].astype(out_ref.dtype)
 
 
 def conv(w_rows, planes, use, dtype, row_len):
-    outs, depth = w_rows.shape
+    depth, outs = w_rows.shape
     channels = depth // 27
     cells = planes.shape[2]
     depth = 9 * channels * len(use)
@@ -80,7 +86,7 @@
         out_shape=jax.ShapeDtypeStruct((4, outs, cells), dtype),
         in_specs=[IN_VMEM] * 2,
         out_specs=IN_VMEM,
-        scratch_shapes=[pltpu.VMEM((4, depth, cells), jnp.bfloat16)],
+        scratch_shapes=[pltpu.VMEM((depth, 4 * cells), jnp.bfloat16)],
         cost_estimate=pl.CostEstimate(
             flops=8 * outs * depth * cells, bytes_accessed=4 * depth * cells, transcendentals=0
         ),
@@ -330,12 +336,12 @@
     parts = parts.reshape(ROWS, -1, CORES, (share + 1) * cells // CORES).transpose(0, 2, 1, 3)
     first = exchange(parts.reshape((ROWS * CORES,) + parts.shape[2:]), PILLARS)
     first = first.reshape(ROWS, -1, first.shape[2])
-    up, down = [first], [first]
-    for _ in range(3):
-        up.append(on_space(up[-1], z_by=1))
-        down.append(on_space(down[-1], z_by=-1))
-    far = on_space(up[3], z_by=1)
-    mine = pile(down + [far] + up[:0:-1])
+    hops = {0: first}
+    for step in (1, -1, 2, -2):
+        hops[step] = on_space(first, z_by=-step)
+    for step, come in ((3, 2), (-3, -2), (4, 2)):
+        hops[step] = on_space(hops[come], z_by=come - step)
+    mine = pile([hops[step] for step in (0, 1, 2, 3, 4, -3, -2, -1)])
     theirs = on_space(mine, core_by=1)
 
     w_rel = [w_second.reshape(27 * own, C3)]
@@ -343,7 +349,7 @@
         w_rel.append(on_space(w_rel[0], y_by=-step))
 
     planes = volume[0].transpose(1, 2, 0, 3).reshape(2, 16 * channels, cells)
-    w_rows = w_first.reshape(27 * channels, outs).T
+    w_rows = w_first.reshape(27 * channels, outs)
     ahead = conv(w_rows, planes, ((0, 1),), jnp.bfloat16, row_len)
     behind = from_behind(ahead, "space", 1)
     part = conv(w_rows, planes, ((1, 0), (2, 1)), jnp.float32, row_len)

time: 125 us -> 119 us (0.952)
  waiting for transfers between devices: 37.1 us -> 30.2 us
  starting transfers between devices: 37 us -> 39.7 us
  local copies, waits for them, and re-layouts: 12.8 us -> 10.4 us
    ppermute x14, waiting for transfers between devices: 30.3 us -> 21.9 us  [on_space(): return lax.ppermute(block, 'space', route)]
    reshape x1 -> x0, local copies, waits for them, and re-layouts: 4.06 us -> none  [section(): w_rows = w_first.reshape(27 * channels, outs).T]
    transpose x1, local copies, waits for them, and re-layouts: 2.52 us -> 4.13 us  [section(): planes = volume[0].transpose(1, 2, 0, 3).reshape(2, 16 * channels, cells)]
    ppermute x14, starting transfers between devices: 16.9 us -> 18.4 us  [on_space(): return lax.ppermute(block, 'space', route)]
    all_to_all x2, waiting for transfers between devices: 0.51 us -> 1.92 us  [exchange(): lax.all_to_all(blocks, 'space', split_axis=0, concat_axis=0, axis_index_g...]
    unnamed x36 -> x34, local copies, waits for them, and re-layouts: 3.14 us -> 3.13 us
  transfers between devices with their start and end apart: 20 -> 20, of which waited for: 13 -> 11; matrix products, arithmetic and copies ran while one was open for 7% -> 6% of each run, Pallas kernels for 19% -> 20%
where the time goes in v5:
time: 119 us; the launch traced here: 118 us
  starting transfers between devices  39.7 us (33%)
  waiting for transfers between devices  30.2 us (25%)
  Pallas kernels  23.6 us (20%)
  blocking collectives  11.2 us (9%)
  local copies, waits for them, and re-layouts  10.4 us (9%)
  other arithmetic  2.07 us (2%)
    ppermute x14, waiting for transfers between devices, on_space(): return lax.ppermute(block, 'space', route)  21.9 us
    ppermute x14, starting transfers between devices, on_space(): return lax.ppermute(block, 'space', route)  18.4 us
    all_to_all x2, starting transfers between devices, exchange(): lax.all_to_all(blocks, 'space', split_axis=0, concat_axis=0, axis_index_g...  13.1 us
    all_to_all x1, blocking collectives, exchange(): lax.all_to_all(blocks, 'space', split_axis=0, concat_axis=0, axis_index_g...  11.2 us
    pallas_call x2, Pallas kernels, conv(): pl.pallas_call(functools.partial(conv_kernel, use, channels, row_len), ou...  8.59 us
    ppermute x3, waiting for transfers between devices, from_side(): lax.ppermute(block, axis, [(i, (i + distance) % size) for i in range(size)])  6.34 us
    pallas_call x1, Pallas kernels, back(): pl.pallas_call(functools.partial(back_kernel, row_len), out_shape=(jax.Sh...  4.89 us
    pallas_call x1, Pallas kernels, grad(): pl.pallas_call(functools.partial(grad_kernel, row_len), out_shape=[jax.Sh...  4.55 us
  transfers between devices with their start and end apart: 20, of which 11 were waited for; matrix products, arithmetic and copies ran while one was open for 6% of the time, Pallas kernels for 20%

profile of v5, /device:TPU:1, one launch (start us, length us, event | category | flops | bytes accessed | tf_op | source)
XLA Modules:
  0.0 117.9 jit_solution(1643679154696537149)
XLA Ops:
  0.6 1.0 fusion
  1.7 0.3 maximum_bitcast_fusion
  2.0 11.2 %all_to_all.15 = bf16[8,8,1152]{2,1,0:T(8,128)(2,1)S(1)} all-to-all(bf16[8,8,1152]{2,1,0:T(8,128)(2,1)S(1)} %bitcast.27), channel_id=1, replica_groups={{0,1,16,17,32,33,48,49},{2,3,18,19,34,35,50,51},{4,5,20,21,36,37,52,53}..., dimensions={0} | all-to-all | bytes 294912 | tf_op jit(solution)/shard_map/all_to_all | solution.py:317
  13.2 3.0 %collective-permute-start.8 = (bf16[4,16,1152]{2,1,0:T(8,128)(2,1)S(1)}, bf16[4,16,1152]{2,1,0:T(8,128)(2,1)S(1)}, u32[]{:S(2)}, u32[]{:S(2)}) collective-permute-start(bf16[4,16,1152]{2,1,0:T(8,128)(2,1)S(1)} %bitcast.22), channel_id=1, source_target_pairs={{0,4},{1,5},{2,6},{3,7},{4,8},{5,9},{6,10},{7,11},{8,12},{9,13},{1... | collective-permute-start | bytes 442376 | tf_op jit(solution)/shard_map/ppermute | solution.py:297
  16.2 3.0 %collective-permute-start.5 = (bf16[4,16,1152]{2,1,0:T(8,128)(2,1)S(1)}, bf16[4,16,1152]{2,1,0:T(8,128)(2,1)S(1)}, u32[]{:S(2)}, u32[]{:S(2)}) collective-permute-start(bf16[4,16,1152]{2,1,0:T(8,128)(2,1)S(1)} %bitcast.23), channel_id=1, source_target_pairs={{0,12},{1,13},{2,14},{3,15},{4,0},{5,1},{6,2},{7,3},{8,4},{9,5},{1... | collective-permute-start | bytes 442376 | tf_op jit(solution)/shard_map/ppermute | solution.py:297
  19.2 0.7 collective-permute-start.10
  20.0 4.1 %copy.11 = bf16[2,16,128,256]{3,2,1,0:T(8,128)(2,1)} copy(bf16[2,16,128,256]{3,1,0,2:T(8,128)(2,1)} %bitcast.19) | data formatting | bytes 4194304 | tf_op jit(solution)/shard_map/transpose | solution.py:351
  24.1 3.9 %shard_map.60 = bf16[4,256,256]{2,1,0:T(8,128)(2,1)} custom-call(bf16[3456,256]{1,0:T(8,128)(2,1)} %bitcast.17, bf16[2,2048,256]{2,1,0:T(8,128)(2,1)} %bitcast.15), custom_call_target="tpu_custom_call" | custom-call | flops 603979776 | bytes 1179648 | tf_op jit(solution)/shard_map/pallas_call | solution.py:84
  28.0 3.9 %collective-permute-start = (bf16[4,256,256]{2,1,0:T(8,128)(2,1)}, bf16[4,256,256]{2,1,0:T(8,128)(2,1)S(1)}, u32[]{:S(2)}, u32[]{:S(2)}) collective-permute-start(bf16[4,256,256]{2,1,0:T(8,128)(2,1)} %shard_map.60), channel_id=1, source_target_pairs={{0,1},{1,2},{2,3},{3,4},{4,5},{5,6},{6,7},{7,8},{8,9},{9,10},{10,1... | collective-permute-start | bytes 1572872 | tf_op jit(solution)/shard_map/ppermute | solution.py:21
  32.0 2.0 %collective-permute-start.4 = (bf16[4,16,1152]{2,1,0:T(8,128)(2,1)S(1)}, bf16[4,16,1152]{2,1,0:T(8,128)(2,1)S(1)}, u32[]{:S(2)}, u32[]{:S(2)}) collective-permute-start(bf16[4,16,1152]{2,1,0:T(8,128)(2,1)S(1)} %bitcast.25), channel_id=1, source_target_pairs={{0,14},{1,15},{2,0},{3,1},{4,2},{5,3},{6,4},{7,5},{8,6},{9,7},{10,... | collective-permute-start | bytes 442376 | tf_op jit(solution)/shard_map/ppermute | solution.py:297
  34.0 1.9 %collective-permute-start.7 = (bf16[4,16,1152]{2,1,0:T(8,128)(2,1)S(1)}, bf16[4,16,1152]{2,1,0:T(8,128)(2,1)S(1)}, u32[]{:S(2)}, u32[]{:S(2)}) collective-permute-start(bf16[4,16,1152]{2,1,0:T(8,128)(2,1)S(1)} %collective-permute-done.5.refs_2_), channel_id=1, source_target_pairs={{0,12},{1,13},{2,14},{3,15},{4,0},{5,1},{6,2},{7,3},{8,4},{9,5},{1... | collective-permute-start | bytes 442376 | tf_op jit(solution)/shard_map/ppermute | solution.py:297
  35.9 1.0 collective-permute-start.6
  36.9 0.8 collective-permute-done.4.refs_1_
  37.7 6.2 %collective-permute-done.9.refs_5_ = bf16[4,16,1152]{2,1,0:T(8,128)(2,1)S(1)} collective-permute-done((bf16[4,16,1152]{2,1,0:T(8,128)(2,1)S(1)}, bf16[4,16,1152]{2,1,0:T(8,128)(2,1)S(1)}, u32[]{:S(2)}, u32[]{:S(2)}) %collective-permute-start.9) | collective-permute-done | bytes 147488 | tf_op jit(solution)/shard_map/ppermute | solution.py:297
  43.8 1.8 %collective-permute-done.7.refs_4_ = bf16[4,16,1152]{2,1,0:T(8,128)(2,1)S(1)} collective-permute-done((bf16[4,16,1152]{2,1,0:T(8,128)(2,1)S(1)}, bf16[4,16,1152]{2,1,0:T(8,128)(2,1)S(1)}, u32[]{:S(2)}, u32[]{:S(2)}) %collective-permute-start.7) | collective-permute-done | bytes 147488 | tf_op jit(solution)/shard_map/ppermute | solution.py:297
  45.6 2.1 %collective-permute-done.6.refs_3_ = bf16[4,16,1152]{2,1,0:T(8,128)(2,1)S(1)} collective-permute-done((bf16[4,16,1152]{2,1,0:T(8,128)(2,1)S(1)}, bf16[4,16,1152]{2,1,0:T(8,128)(2,1)S(1)}, u32[]{:S(2)}, u32[]{:S(2)}) %collective-permute-start.6) | collective-permute-done | bytes 147488 | tf_op jit(solution)/shard_map/ppermute | solution.py:297
  47.8 0.6 copy-done.10
  48.5 2.5 %shard_map.62.refs_4_ = bf16[8,4,16,1152]{3,2,1,0:T(8,128)(2,1)} custom-call(bf16[4,16,1152]{2,1,0:T(8,128)(2,1)} %bitcast.26, bf16[4,16,1152]{2,1,0:T(8,128)(2,1)} %copy-done.7, bf16[4,16,1152]{2,1,0:T(8,128)(2,1)} %copy-done.5, bf16[4,16,1152]{2,1,0:T(8,128)(2,1)} %copy-done.10, bf16[4,16,1152]{2,1,0:T(8,128)(2,1)} %copy-done.9, ...), custom_call_target="tpu_custom_call" | custom-call | bytes 2359296 | tf_op jit(solution)/shard_map/pallas_call | solution.py:139
  50.9 0.6 collective-permute-start.11
  51.5 4.7 %shard_map.59.part_ref = f32[4,256,256]{2,1,0:T(8,128)} custom-call(bf16[3456,256]{1,0:T(8,128)(2,1)} %bitcast.18, bf16[2,2048,256]{2,1,0:T(8,128)(2,1)} %bitcast.16), custom_call_target="tpu_custom_call" | custom-call | flops 1207959552 | bytes 2359296 | tf_op jit(solution)/shard_map/pallas_call | solution.py:84
  56.2 0.8 copy-done.2
  57.0 3.2 %shard_map.61 = (bf16[16,64,256]{2,1,0:T(8,128)(2,1)}, f32[16,64,256]{2,1,0:T(8,128)}) custom-call(f32[4,256,256]{2,1,0:T(8,128)} %shard_map.59.part_ref, bf16[4,256,256]{2,1,0:T(8,128)(2,1)} %copy-done.2), custom_call_target="tpu_custom_call" | custom-call | flops 2621440 | bytes 3145728 | tf_op jit(solution)/shard_map/pallas_call | solution.py:118
  60.2 7.0 %all-to-all-start = ((bf16[16,64,256]{2,1,0:T(8,128)(2,1)}), bf16[16,64,256]{2,1,0:T(8,128)(2,1)S(1)}, u32[]{:S(2)}, u32[]{:S(2)}) async-start(bf16[16,64,256]{2,1,0:T(8,128)(2,1)} %get-tuple-element.10), calls=%async_computation | async-start | bytes 1048576 | tf_op jit(solution)/shard_map/all_to_all | solution.py:317
  67.2 0.1 collective-permute-start.3
  67.3 1.4 %collective-permute-start.2 = (bf16[108,512]{1,0:T(8,128)(2,1)S(1)}, bf16[108,512]{1,0:T(8,128)(2,1)S(1)}, u32[]{:S(2)}, u32[]{:S(2)}) collective-permute-start(bf16[108,512]{1,0:T(8,128)(2,1)S(1)} %reshape.39.refs_0_), channel_id=1, source_target_pairs={{0,32},{1,33},{2,34},{3,35},{4,36},{5,37},{6,38},{7,39},{8,40},{9,... | collective-permute-start | bytes 331784 | tf_op jit(solution)/shard_map/ppermute | solution.py:297
  68.7 1.3 %collective-permute-start.1 = (bf16[108,512]{1,0:T(8,128)(2,1)S(1)}, bf16[108,512]{1,0:T(8,128)(2,1)S(1)}, u32[]{:S(2)}, u32[]{:S(2)}) collective-permute-start(bf16[108,512]{1,0:T(8,128)(2,1)S(1)} %reshape.39.refs_0_), channel_id=1, source_target_pairs={{0,48},{1,49},{2,50},{3,51},{4,52},{5,53},{6,54},{7,55},{8,56},{9,... | collective-permute-start | bytes 331784 | tf_op jit(solution)/shard_map/ppermute | solution.py:297
  70.0 0.6 pad_add_fusion.place_ref
  70.6 4.9 %collective-permute-done.3.refs_3_ = bf16[108,512]{1,0:T(8,128)(2,1)S(1)} collective-permute-done((bf16[108,512]{1,0:T(8,128)(2,1)S(1)}, bf16[108,512]{1,0:T(8,128)(2,1)S(1)}, u32[]{:S(2)}, u32[]{:S(2)}) %collective-permute-start.3) | collective-permute-done | bytes 110624 | tf_op jit(solution)/shard_map/ppermute | solution.py:297
  75.5 0.3 collective-permute-done.1.refs_1_
  75.9 0.3 copy-done.14
  76.2 0.3 copy-done.16
  76.5 1.0 copy-done.13
  77.5 4.9 %shard_map.63 = (bf16[16,64,256]{2,1,0:T(8,128)(2,1)}, bf16[512,2304]{1,0:T(8,128)(2,1)}) custom-call(s32[3]{0:T(128)} %pad_add_fusion.place_ref, bf16[108,512]{1,0:T(8,128)(2,1)} %copy-done.11, bf16[108,512]{1,0:T(8,128)(2,1)} %copy-done.16, bf16[108,512]{1,0:T(8,128)(2,1)} %copy-done.15, bf16[108,512]{1,0:T(8,128)(2,1)} %copy-done.14, ...), custom_call_target="tpu_custom_call" | custom-call | flops 1610612736 | bytes 4718592 | tf_op jit(solution)/shard_map/pallas_call | solution.py:272
  82.4 1.9 %all-to-all-done.hidden_ref = bf16[16,64,256]{2,1,0:T(8,128)(2,1)S(1)} async-done(((bf16[16,64,256]{2,1,0:T(8,128)(2,1)}), bf16[16,64,256]{2,1,0:T(8,128)(2,1)S(1)}, u32[]{:S(2)}, u32[]{:S(2)}) %all-to-all-start) | async-done | bytes 524320 | tf_op jit(solution)/shard_map/all_to_all | solution.py:317
  84.3 6.2 %all-to-all-start.2 = ((bf16[16,64,256]{2,1,0:T(8,128)(2,1)}), bf16[16,64,256]{2,1,0:T(8,128)(2,1)S(1)}, u32[]{:S(2)}, u32[]{:S(2)}) async-start(bf16[16,64,256]{2,1,0:T(8,128)(2,1)} %get-tuple-element.16), calls=%async_computation.2 | async-start | bytes 1048576 | tf_op jit(solution)/shard_map/all_to_all | solution.py:317
  90.5 4.5 %shard_map.64 = (f32[108,512]{1,0:T(8,128)}, bf16[108,512]{1,0:T(8,128)(2,1)}, bf16[108,512]{1,0:T(8,128)(2,1)}, bf16[108,512]{1,0:T(8,128)(2,1)}) custom-call(s32[3]{0:T(128)} %pad_add_fusion.place_ref, bf16[16,64,256]{2,1,0:T(8,128)(2,1)} %copy-done.3, bf16[512,2304]{1,0:T(8,128)(2,1)} %get-tuple-element.11.cot_ref), custom_call_target="tpu_custom_call" | custom-call | flops 1610612736 | bytes 2359296 | tf_op jit(solution)/shard_map/pallas_call | solution.py:210
  95.1 3.3 %collective-permute-start.13 = (bf16[108,512]{1,0:T(8,128)(2,1)}, bf16[108,512]{1,0:T(8,128)(2,1)S(1)}, u32[]{:S(2)}, u32[]{:S(2)}) collective-permute-start(bf16[108,512]{1,0:T(8,128)(2,1)} %get-tuple-element.14), channel_id=1, source_target_pairs={{0,32},{1,33},{2,34},{3,35},{4,36},{5,37},{6,38},{7,39},{8,40},{9,... | collective-permute-start | bytes 331784 | tf_op jit(solution)/shard_map/ppermute | solution.py:297
  98.3 2.7 %collective-permute-done.12 = bf16[108,512]{1,0:T(8,128)(2,1)S(1)} collective-permute-done((bf16[108,512]{1,0:T(8,128)(2,1)}, bf16[108,512]{1,0:T(8,128)(2,1)S(1)}, u32[]{:S(2)}, u32[]{:S(2)}) %collective-permute-start.12) | collective-permute-done | bytes 110624 | tf_op jit(solution)/shard_map/ppermute | solution.py:297
  101.1 3.1 %collective-permute-done.13 = bf16[108,512]{1,0:T(8,128)(2,1)S(1)} collective-permute-done((bf16[108,512]{1,0:T(8,128)(2,1)}, bf16[108,512]{1,0:T(8,128)(2,1)S(1)}, u32[]{:S(2)}, u32[]{:S(2)}) %collective-permute-start.13) | collective-permute-done | bytes 110624 | tf_op jit(solution)/shard_map/ppermute | solution.py:297
  104.1 1.0 add_convert_fusion
  105.1 2.6 %collective-permute-start.17 = (bf16[108,512]{1,0:T(8,128)(2,1)S(1)}, bf16[108,512]{1,0:T(8,128)(2,1)S(1)}, u32[]{:S(2)}, u32[]{:S(2)}) collective-permute-start(bf16[108,512]{1,0:T(8,128)(2,1)S(1)} %add_convert_fusion), channel_id=1, source_target_pairs={{0,192},{64,0},{128,64},{192,128},{1,193},{65,1},{129,65},{193,129... | collective-permute-start | bytes 331784 | tf_op jit(solution)/shard_map/ppermute | solution.py:26
  107.7 1.7 %collective-permute-start.15 = (bf16[108,512]{1,0:T(8,128)(2,1)S(1)}, bf16[108,512]{1,0:T(8,128)(2,1)S(1)}, u32[]{:S(2)}, u32[]{:S(2)}) collective-permute-start(bf16[108,512]{1,0:T(8,128)(2,1)S(1)} %add_convert_fusion), channel_id=1, source_target_pairs={{0,128},{64,192},{128,0},{192,64},{1,129},{65,193},{129,1},{193,65... | collective-permute-start | bytes 331784 | tf_op jit(solution)/shard_map/ppermute | solution.py:26
  109.4 0.1 collective-permute-done.17
  109.5 6.3 %collective-permute-done.16 = bf16[108,512]{1,0:T(8,128)(2,1)S(1)} collective-permute-done((bf16[108,512]{1,0:T(8,128)(2,1)S(1)}, bf16[108,512]{1,0:T(8,128)(2,1)S(1)}, u32[]{:S(2)}, u32[]{:S(2)}) %collective-permute-start.16) | collective-permute-done | bytes 110624 | tf_op jit(solution)/shard_map/ppermute | solution.py:26
  115.8 0.7 reshape.42
  116.6 0.1 multiply_convert_fusion
  116.7 0.1 reshape.43
  116.9 1.1 copy.13
  (49 shorter events, 0.4 us)
Async XLA Ops:
  13.2 18.8 %copy-start.1 = (bf16[8,8,1152]{2,1,0:T(8,128)(2,1)}, bf16[8,8,1152]{2,1,0:T(8,128)(2,1)S(1)}, u32[]{:S(2)}) copy-start(bf16[8,8,1152]{2,1,0:T(8,128)(2,1)S(1)} %all_to_all.15) | copy-start | bytes 442372
  13.2 20.8 %collective-permute-start.8 = (bf16[4,16,1152]{2,1,0:T(8,128)(2,1)S(1)}, bf16[4,16,1152]{2,1,0:T(8,128)(2,1)S(1)}, u32[]{:S(2)}, u32[]{:S(2)}) collective-permute-start(bf16[4,16,1152]{2,1,0:T(8,128)(2,1)S(1)} %bitcast.22), channel_id=1, source_target_pairs={{0,4},{1,5},{2,6},{3,7},{4,8},{5,9},{6,10},{7,11},{8,12},{9,13},{1... | collective-permute-start | bytes 442376 | tf_op jit(solution)/shard_map/ppermute | solution.py:297
  16.2 17.8 %collective-permute-start.5 = (bf16[4,16,1152]{2,1,0:T(8,128)(2,1)S(1)}, bf16[4,16,1152]{2,1,0:T(8,128)(2,1)S(1)}, u32[]{:S(2)}, u32[]{:S(2)}) collective-permute-start(bf16[4,16,1152]{2,1,0:T(8,128)(2,1)S(1)} %bitcast.23), channel_id=1, source_target_pairs={{0,12},{1,13},{2,14},{3,15},{4,0},{5,1},{6,2},{7,3},{8,4},{9,5},{1... | collective-permute-start | bytes 442376 | tf_op jit(solution)/shard_map/ppermute | solution.py:297
  19.2 16.7 %collective-permute-start.10 = (bf16[4,16,1152]{2,1,0:T(8,128)(2,1)S(1)}, bf16[4,16,1152]{2,1,0:T(8,128)(2,1)S(1)}, u32[]{:S(2)}, u32[]{:S(2)}) collective-permute-start(bf16[4,16,1152]{2,1,0:T(8,128)(2,1)S(1)} %bitcast.24), channel_id=1, source_target_pairs={{0,2},{1,3},{2,4},{3,5},{4,6},{5,7},{6,8},{7,9},{8,10},{9,11},{10,... | collective-permute-start | bytes 442376 | tf_op jit(solution)/shard_map/ppermute | solution.py:297
  28.0 28.2 %collective-permute-start = (bf16[4,256,256]{2,1,0:T(8,128)(2,1)}, bf16[4,256,256]{2,1,0:T(8,128)(2,1)S(1)}, u32[]{:S(2)}, u32[]{:S(2)}) collective-permute-start(bf16[4,256,256]{2,1,0:T(8,128)(2,1)} %shard_map.60), channel_id=1, source_target_pairs={{0,1},{1,2},{2,3},{3,4},{4,5},{5,6},{6,7},{7,8},{8,9},{9,10},{10,1... | collective-permute-start | bytes 1572872 | tf_op jit(solution)/shard_map/ppermute | solution.py:21
  32.0 5.7 %collective-permute-start.4 = (bf16[4,16,1152]{2,1,0:T(8,128)(2,1)S(1)}, bf16[4,16,1152]{2,1,0:T(8,128)(2,1)S(1)}, u32[]{:S(2)}, u32[]{:S(2)}) collective-permute-start(bf16[4,16,1152]{2,1,0:T(8,128)(2,1)S(1)} %bitcast.25), channel_id=1, source_target_pairs={{0,14},{1,15},{2,0},{3,1},{4,2},{5,3},{6,4},{7,5},{8,6},{9,7},{10,... | collective-permute-start | bytes 442376 | tf_op jit(solution)/shard_map/ppermute | solution.py:297
  34.0 13.8 %copy-start.4 = (bf16[4,16,1152]{2,1,0:T(8,128)(2,1)}, bf16[4,16,1152]{2,1,0:T(8,128)(2,1)S(1)}, u32[]{:S(2)}) copy-start(bf16[4,16,1152]{2,1,0:T(8,128)(2,1)S(1)} %collective-permute-done.8.refs_6_) | copy-start | bytes 442372
  34.0 9.8 %collective-permute-start.9 = (bf16[4,16,1152]{2,1,0:T(8,128)(2,1)S(1)}, bf16[4,16,1152]{2,1,0:T(8,128)(2,1)S(1)}, u32[]{:S(2)}, u32[]{:S(2)}) collective-permute-start(bf16[4,16,1152]{2,1,0:T(8,128)(2,1)S(1)} %collective-permute-done.8.refs_6_), channel_id=1, source_target_pairs={{0,2},{1,3},{2,4},{3,5},{4,6},{5,7},{6,8},{7,9},{8,10},{9,11},{10,... | collective-permute-start | bytes 442376 | tf_op jit(solution)/shard_map/ppermute | solution.py:297
  34.0 13.7 %copy-start.5 = (bf16[4,16,1152]{2,1,0:T(8,128)(2,1)}, bf16[4,16,1152]{2,1,0:T(8,128)(2,1)S(1)}, u32[]{:S(2)}) copy-start(bf16[4,16,1152]{2,1,0:T(8,128)(2,1)S(1)} %collective-permute-done.5.refs_2_) | copy-start | bytes 442372
  34.0 11.6 %collective-permute-start.7 = (bf16[4,16,1152]{2,1,0:T(8,128)(2,1)S(1)}, bf16[4,16,1152]{2,1,0:T(8,128)(2,1)S(1)}, u32[]{:S(2)}, u32[]{:S(2)}) collective-permute-start(bf16[4,16,1152]{2,1,0:T(8,128)(2,1)S(1)} %collective-permute-done.5.refs_2_), channel_id=1, source_target_pairs={{0,12},{1,13},{2,14},{3,15},{4,0},{5,1},{6,2},{7,3},{8,4},{9,5},{1... | collective-permute-start | bytes 442376 | tf_op jit(solution)/shard_map/ppermute | solution.py:297
  35.9 11.8 %copy-start.6 = (bf16[4,16,1152]{2,1,0:T(8,128)(2,1)}, bf16[4,16,1152]{2,1,0:T(8,128)(2,1)S(1)}, u32[]{:S(2)}) copy-start(bf16[4,16,1152]{2,1,0:T(8,128)(2,1)S(1)} %collective-permute-done.10.refs_7_) | copy-start | bytes 442372
  35.9 11.8 %collective-permute-start.6 = (bf16[4,16,1152]{2,1,0:T(8,128)(2,1)S(1)}, bf16[4,16,1152]{2,1,0:T(8,128)(2,1)S(1)}, u32[]{:S(2)}, u32[]{:S(2)}) collective-permute-start(bf16[4,16,1152]{2,1,0:T(8,128)(2,1)S(1)} %collective-permute-done.5.refs_2_), channel_id=1, source_target_pairs={{0,14},{1,15},{2,0},{3,1},{4,2},{5,3},{6,4},{7,5},{8,6},{9,7},{10,... | collective-permute-start | bytes 442376 | tf_op jit(solution)/shard_map/ppermute | solution.py:297
  37.7 10.1 %copy-start.7 = (bf16[4,16,1152]{2,1,0:T(8,128)(2,1)}, bf16[4,16,1152]{2,1,0:T(8,128)(2,1)S(1)}, u32[]{:S(2)}) copy-start(bf16[4,16,1152]{2,1,0:T(8,128)(2,1)S(1)} %collective-permute-done.4.refs_1_) | copy-start | bytes 442372
  43.8 4.0 %copy-start.8 = (bf16[4,16,1152]{2,1,0:T(8,128)(2,1)}, bf16[4,16,1152]{2,1,0:T(8,128)(2,1)S(1)}, u32[]{:S(2)}) copy-start(bf16[4,16,1152]{2,1,0:T(8,128)(2,1)S(1)} %collective-permute-done.9.refs_5_) | copy-start | bytes 442372
  45.6 2.2 %copy-start.9 = (bf16[4,16,1152]{2,1,0:T(8,128)(2,1)}, bf16[4,16,1152]{2,1,0:T(8,128)(2,1)S(1)}, u32[]{:S(2)}) copy-start(bf16[4,16,1152]{2,1,0:T(8,128)(2,1)S(1)} %collective-permute-done.7.refs_4_) | copy-start | bytes 442372
  47.8 0.7 copy-start.10
  50.9 24.9 %collective-permute-start.11 = (bf16[8,4,16,1152]{3,2,1,0:T(8,128)(2,1)}, bf16[8,4,16,1152]{3,2,1,0:T(8,128)(2,1)S(1)}, u32[]{:S(2)}, u32[]{:S(2)}) collective-permute-start(bf16[8,4,16,1152]{3,2,1,0:T(8,128)(2,1)} %shard_map.62.refs_4_), channel_id=1, source_target_pairs={{0,1},{1,0},{2,3},{3,2},{4,5},{5,4},{6,7},{7,6},{8,9},{9,8},{10,11... | collective-permute-start | bytes 3538952 | tf_op jit(solution)/shard_map/ppermute | solution.py:297
  56.2 10.9 %copy-start.12 = (bf16[3,3,3,4,512]{4,3,2,1,0:T(4,128)(2,1)S(1)}, bf16[3,3,3,4,512]{4,3,2,1,0:T(4,128)(2,1)}, u32[]{:S(2)}) copy-start(bf16[3,3,3,4,512]{4,3,2,1,0:T(4,128)(2,1)} %param.6) | copy-start | bytes 331780
  56.2 0.8 copy-start.2
  60.2 24.2 %all-to-all-start = ((bf16[16,64,256]{2,1,0:T(8,128)(2,1)}), bf16[16,64,256]{2,1,0:T(8,128)(2,1)S(1)}, u32[]{:S(2)}, u32[]{:S(2)}) async-start(bf16[16,64,256]{2,1,0:T(8,128)(2,1)} %get-tuple-element.10), calls=%async_computation | async-start | bytes 1048576 | tf_op jit(solution)/shard_map/all_to_all | solution.py:317
  67.1 8.7 %copy-start.11 = (bf16[108,512]{1,0:T(8,128)(2,1)}, bf16[108,512]{1,0:T(8,128)(2,1)S(1)}, u32[]{:S(2)}) copy-start(bf16[108,512]{1,0:T(8,128)(2,1)S(1)} %reshape.39.refs_0_) | copy-start | bytes 331780
  67.2 8.3 %collective-permute-start.3 = (bf16[108,512]{1,0:T(8,128)(2,1)S(1)}, bf16[108,512]{1,0:T(8,128)(2,1)S(1)}, u32[]{:S(2)}, u32[]{:S(2)}) collective-permute-start(bf16[108,512]{1,0:T(8,128)(2,1)S(1)} %reshape.39.refs_0_), channel_id=1, source_target_pairs={{0,16},{1,17},{2,18},{3,19},{4,20},{5,21},{6,22},{7,23},{8,24},{9,... | collective-permute-start | bytes 331784 | tf_op jit(solution)/shard_map/ppermute | solution.py:297
  67.3 8.2 %collective-permute-start.2 = (bf16[108,512]{1,0:T(8,128)(2,1)S(1)}, bf16[108,512]{1,0:T(8,128)(2,1)S(1)}, u32[]{:S(2)}, u32[]{:S(2)}) collective-permute-start(bf16[108,512]{1,0:T(8,128)(2,1)S(1)} %reshape.39.refs_0_), channel_id=1, source_target_pairs={{0,32},{1,33},{2,34},{3,35},{4,36},{5,37},{6,38},{7,39},{8,40},{9,... | collective-permute-start | bytes 331784 | tf_op jit(solution)/shard_map/ppermute | solution.py:297
  68.7 7.2 %collective-permute-start.1 = (bf16[108,512]{1,0:T(8,128)(2,1)S(1)}, bf16[108,512]{1,0:T(8,128)(2,1)S(1)}, u32[]{:S(2)}, u32[]{:S(2)}) collective-permute-start(bf16[108,512]{1,0:T(8,128)(2,1)S(1)} %reshape.39.refs_0_), channel_id=1, source_target_pairs={{0,48},{1,49},{2,50},{3,51},{4,52},{5,53},{6,54},{7,55},{8,56},{9,... | collective-permute-start | bytes 331784 | tf_op jit(solution)/shard_map/ppermute | solution.py:297
  75.5 0.7 copy-start.14
  75.5 0.7 copy-start.15
  75.8 0.6 copy-start.16
  76.5 1.0 copy-start.13
  84.3 6.2 %copy-start.3 = (bf16[16,64,256]{2,1,0:T(8,128)(2,1)}, bf16[16,64,256]{2,1,0:T(8,128)(2,1)S(1)}, u32[]{:S(2)}) copy-start(bf16[16,64,256]{2,1,0:T(8,128)(2,1)S(1)} %all-to-all-done.hidden_ref) | copy-start | bytes 1572868
  84.3 32.3 %all-to-all-start.2 = ((bf16[16,64,256]{2,1,0:T(8,128)(2,1)}), bf16[16,64,256]{2,1,0:T(8,128)(2,1)S(1)}, u32[]{:S(2)}, u32[]{:S(2)}) async-start(bf16[16,64,256]{2,1,0:T(8,128)(2,1)} %get-tuple-element.16), calls=%async_computation.2 | async-start | bytes 1048576 | tf_op jit(solution)/shard_map/all_to_all | solution.py:317
  95.0 21.5 %copy-start = (f32[16,64,256]{2,1,0:T(8,128)S(1)}, f32[16,64,256]{2,1,0:T(8,128)}, u32[]{:S(2)}) copy-start(f32[16,64,256]{2,1,0:T(8,128)} %get-tuple-element.17) | copy-start | bytes 3145732
  95.0 6.0 %collective-permute-start.12 = (bf16[108,512]{1,0:T(8,128)(2,1)}, bf16[108,512]{1,0:T(8,128)(2,1)S(1)}, u32[]{:S(2)}, u32[]{:S(2)}) collective-permute-start(bf16[108,512]{1,0:T(8,128)(2,1)} %get-tuple-element.13), channel_id=1, source_target_pairs={{0,16},{1,17},{2,18},{3,19},{4,20},{5,21},{6,22},{7,23},{8,24},{9,... | collective-permute-start | bytes 331784 | tf_op jit(solution)/shard_map/ppermute | solution.py:297
  95.1 9.1 %collective-permute-start.13 = (bf16[108,512]{1,0:T(8,128)(2,1)}, bf16[108,512]{1,0:T(8,128)(2,1)S(1)}, u32[]{:S(2)}, u32[]{:S(2)}) collective-permute-start(bf16[108,512]{1,0:T(8,128)(2,1)} %get-tuple-element.14), channel_id=1, source_target_pairs={{0,32},{1,33},{2,34},{3,35},{4,36},{5,37},{6,38},{7,39},{8,40},{9,... | collective-permute-start | bytes 331784 | tf_op jit(solution)/shard_map/ppermute | solution.py:297
  98.3 5.8 %collective-permute-start.14 = (bf16[108,512]{1,0:T(8,128)(2,1)}, bf16[108,512]{1,0:T(8,128)(2,1)S(1)}, u32[]{:S(2)}, u32[]{:S(2)}) collective-permute-start(bf16[108,512]{1,0:T(8,128)(2,1)} %get-tuple-element.15), channel_id=1, source_target_pairs={{0,48},{1,49},{2,50},{3,51},{4,52},{5,53},{6,54},{7,55},{8,56},{9,... | collective-permute-start | bytes 331784 | tf_op jit(solution)/shard_map/ppermute | solution.py:297
  105.1 4.4 %collective-permute-start.17 = (bf16[108,512]{1,0:T(8,128)(2,1)S(1)}, bf16[108,512]{1,0:T(8,128)(2,1)S(1)}, u32[]{:S(2)}, u32[]{:S(2)}) collective-permute-start(bf16[108,512]{1,0:T(8,128)(2,1)S(1)} %add_convert_fusion), channel_id=1, source_target_pairs={{0,192},{64,0},{128,64},{192,128},{1,193},{65,1},{129,65},{193,129... | collective-permute-start | bytes 331784 | tf_op jit(solution)/shard_map/ppermute | solution.py:26
  107.7 8.1 %collective-permute-start.16 = (bf16[108,512]{1,0:T(8,128)(2,1)S(1)}, bf16[108,512]{1,0:T(8,128)(2,1)S(1)}, u32[]{:S(2)}, u32[]{:S(2)}) collective-permute-start(bf16[108,512]{1,0:T(8,128)(2,1)S(1)} %add_convert_fusion), channel_id=1, source_target_pairs={{0,64},{64,128},{128,192},{192,0},{1,65},{65,129},{129,193},{193,1... | collective-permute-start | bytes 331784 | tf_op jit(solution)/shard_map/ppermute | solution.py:26
  107.7 8.1 %collective-permute-start.15 = (bf16[108,512]{1,0:T(8,128)(2,1)S(1)}, bf16[108,512]{1,0:T(8,128)(2,1)S(1)}, u32[]{:S(2)}, u32[]{:S(2)}) collective-permute-start(bf16[108,512]{1,0:T(8,128)(2,1)S(1)} %add_convert_fusion), channel_id=1, source_target_pairs={{0,128},{64,192},{128,0},{192,64},{1,129},{65,193},{129,1},{193,65... | collective-permute-start | bytes 331784 | tf_op jit(solution)/shard_map/ppermute | solution.py:26

commit v6 on v5

--- a/solution.py
+++ b/solution.py
@@ -26,8 +26,20 @@
     return lax.ppermute(block, axis, [(i, (i + distance) % size) for i in range(size)])
 
 
+def activate(values):
+    return leak_slope * values + (1.0 - leak_slope) * values * jax.nn.sigmoid(values)
+
+
+def slope_of(values):
+    sigmoid_value = jax.nn.sigmoid(values)
+    return leak_slope + (1.0 - leak_slope) * (
+        sigmoid_value + values * sigmoid_value * (1.0 - sigmoid_value)
+    )
+
+
 ROWS, RING, CORES = 4, 8, 2
 IN_VMEM = pl.BlockSpec(memory_space=pltpu.VMEM)
+GRANT = pltpu.CompilerParams(vmem_limit_bytes=16 * 2**20)
 
 
 def shifted(block, by_row, by_col, row_len):
@@ -87,44 +99,39 @@
         in_specs=[IN_VMEM] * 2,
         out_specs=IN_VMEM,
         scratch_shapes=[pltpu.VMEM((depth, 4 * cells), jnp.bfloat16)],
+        compiler_params=GRANT,
         cost_estimate=pl.CostEstimate(
             flops=8 * outs * depth * cells, bytes_accessed=4 * depth * cells, transcendentals=0
         ),
     )(w_rows, planes)
 
 
-def act_kernel(part_ref, behind_ref, hidden_ref, slope_ref):
-    groups, rows, _ = hidden_ref.shape
+def regrouped(values, own, at):
+    outs = values.shape[0]
+    starts = range(at * own, outs, outs // ROWS)
+    return jnp.concatenate([values[start : start + own] for start in starts], 0)
+
+
+def pointwise_kernel(rule, part_ref, behind_ref, result_ref):
+    groups, rows, _ = result_ref.shape
     unit = rows // 4
-    outs = part_ref.shape[1]
-    own = unit // ROWS
     for phase in range(4):
-        values = part_ref[phase] + behind_ref[phase].astype(jnp.float32)
-        gate = jax.nn.sigmoid(values)
-        gated = (1.0 - leak_slope) * gate
-        active = leak_slope * values + gated * values
-        slope = leak_slope + gated * (1.0 + values * (1.0 - gate))
-        there = slice(phase * unit, (phase + 1) * unit)
+        values = rule(part_ref[phase] + behind_ref[phase].astype(jnp.float32))
         for at in range(groups):
-            picks = [slice(first, first + own) for first in range(at * own, outs, outs // ROWS)]
-            block = jnp.concatenate([active[pick] for pick in picks], 0)
-            hidden_ref[at, there, :] = block.astype(hidden_ref.dtype)
-            slope_ref[at, there, :] = jnp.concatenate([slope[pick] for pick in picks], 0)
-
-
-def act(part, behind, groups):
+            block = regrouped(values, unit // ROWS, at)
+            result_ref[at, phase * unit : (phase + 1) * unit, :] = block.astype(result_ref.dtype)
+
+
+def pointwise(rule, part, behind, groups, dtype):
     phases, outs, cells = part.shape
-    shape = (groups, phases * outs // groups, cells)
-    return pl.pallas_call(
-        act_kernel,
-        out_shape=(
-            jax.ShapeDtypeStruct(shape, jnp.bfloat16),
-            jax.ShapeDtypeStruct(shape, jnp.float32),
-        ),
+    return pl.pallas_call(
+        functools.partial(pointwise_kernel, rule),
+        out_shape=jax.ShapeDtypeStruct((groups, phases * outs // groups, cells), dtype),
         in_specs=[IN_VMEM] * 2,
-        out_specs=(IN_VMEM,) * 2,
-        cost_estimate=pl.CostEstimate(
-            flops=10 * part.size, bytes_accessed=12 * part.size, transcendentals=part.size
+        out_specs=IN_VMEM,
+        compiler_params=GRANT,
+        cost_estimate=pl.CostEstimate(
+            flops=10 * part.size, bytes_accessed=8 * part.size, transcendentals=part.size
         ),
     )(part, behind)
 
@@ -141,6 +148,7 @@
         out_shape=jax.ShapeDtypeStruct(shape, blocks[0].dtype),
         in_specs=[IN_VMEM] * len(blocks),
         out_specs=IN_VMEM,
+        compiler_params=GRANT,
         cost_estimate=pl.CostEstimate(
             flops=0, bytes_accessed=4 * len(blocks) * blocks[0].size, transcendentals=0
         ),
@@ -216,6 +224,7 @@
         in_specs=[pl.BlockSpec(memory_space=pltpu.SMEM), IN_VMEM, IN_VMEM],
         out_specs=[IN_VMEM] * row_count,
         scratch_shapes=[rows, rows, pltpu.VMEM((row_count, size, outs), jnp.float32)],
+        compiler_params=GRANT,
         cost_estimate=pl.CostEstimate(
             flops=12 * group * outs * planes * cells, bytes_accessed=2 * cot.size, transcendentals=0
         ),
@@ -281,6 +290,7 @@
             pltpu.VMEM((row_count, size, outs), jnp.float32),
             pltpu.VMEM((12 * group, outs), jnp.bfloat16),
         ],
+        compiler_params=GRANT,
         cost_estimate=pl.CostEstimate(
             flops=12 * group * outs * planes * cells, bytes_accessed=4 * outs * width, transcendentals=0
         ),
@@ -353,7 +363,8 @@
     ahead = conv(w_rows, planes, ((0, 1),), jnp.bfloat16, row_len)
     behind = from_behind(ahead, "space", 1)
     part = conv(w_rows, planes, ((1, 0), (2, 1)), jnp.float32, row_len)
-    hidden, slopes = act(part, behind, group)
+    hidden = pointwise(activate, part, behind, group, jnp.bfloat16)
+    slopes = pointwise(slope_of, part, behind, group, jnp.float32)
     by_plane = exchange(hidden, SLABS)
 
     back_terms, cot_row = back(place, w_rel, mine, theirs, group, row_len)

time: 119 us -> 104 us (0.87)
  Pallas kernels: 23.6 us -> 12.5 us
  other arithmetic: 2.07 us -> 0.59 us
  local copies, waits for them, and re-layouts: 10.4 us -> 9.1 us
    pallas_call x2, Pallas kernels: 8.59 us -> 2.6 us  [conv(): pl.pallas_call(functools.partial(conv_kernel, use, channels, row_len), ou...]
    pallas_call x1, Pallas kernels: 4.55 us -> 2.43 us  [grad(): pl.pallas_call(functools.partial(grad_kernel, row_len), out_shape=[jax.Sh...]
    pallas_call x1 -> x2, Pallas kernels: 3.16 us -> 1.57 us  [pointwise(): pl.pallas_call(functools.partial(pointwise_kernel, rule), out_shape=jax.S...]
    pallas_call x1, Pallas kernels: 2.45 us -> 1.13 us  [pile(): pl.pallas_call(pile_kernel, out_shape=jax.ShapeDtypeStruct(shape, blocks[...]
    transpose x1, local copies, waits for them, and re-layouts: 4.13 us -> 2.89 us  [section(): planes = volume[0].transpose(1, 2, 0, 3).reshape(2, 16 * channels, cells)]
    unnamed x34 -> x8, local copies, waits for them, and re-layouts: 3.13 us -> 3.11 us
  transfers between devices with their start and end apart: 20 -> 20, of which waited for: 11 -> 10; matrix products, arithmetic and copies ran while one was open for 6% -> 4% of each run, Pallas kernels for 20% -> 12%
where the time goes in v6:
time: 104 us
  starting transfers between devices  39.3 us (38%)
  waiting for transfers between devices  30.5 us (29%)
  Pallas kernels  12.5 us (12%)
  blocking collectives  11.2 us (11%)
  local copies, waits for them, and re-layouts  9.1 us (9%)
    ppermute x14, waiting for transfers between devices, on_space(): return lax.ppermute(block, 'space', route)  22.3 us
    ppermute x14, starting transfers between devices, on_space(): return lax.ppermute(block, 'space', route)  18.4 us
    all_to_all x2, starting transfers between devices, exchange(): lax.all_to_all(blocks, 'space', split_axis=0, concat_axis=0, axis_index_g...  12.7 us
    all_to_all x1, blocking collectives, exchange(): lax.all_to_all(blocks, 'space', split_axis=0, concat_axis=0, axis_index_g...  11.2 us
    ppermute x3, waiting for transfers between devices, from_side(): lax.ppermute(block, axis, [(i, (i + distance) % size) for i in range(size)])  5.92 us
    pallas_call x1, Pallas kernels, back(): pl.pallas_call(functools.partial(back_kernel, row_len), out_shape=(jax.Sh...  4.72 us
    ppermute x3, starting transfers between devices, from_side(): lax.ppermute(block, axis, [(i, (i + distance) % size) for i in range(size)])  4.28 us
    ppermute x1, starting transfers between devices, from_behind(): return lax.ppermute(block, axis, route)  3.96 us
  transfers between devices with their start and end apart: 20, of which 10 were waited for; matrix products, arithmetic and copies ran while one was open for 4% of the time, Pallas kernels for 12%

profile of v6, /device:TPU:1, one launch (start us, length us, event | category | flops | bytes accessed | tf_op | source)
XLA Modules:
  0.0 103.9 jit_solution(13426452847272604185)
XLA Ops:
  0.6 1.0 fusion
  1.7 0.3 maximum_bitcast_fusion
  2.0 11.2 %all_to_all.15 = bf16[8,8,1152]{2,1,0:T(8,128)(2,1)S(1)} all-to-all(bf16[8,8,1152]{2,1,0:T(8,128)(2,1)S(1)} %bitcast.27), channel_id=1, replica_groups={{0,1,16,17,32,33,48,49},{2,3,18,19,34,35,50,51},{4,5,20,21,36,37,52,53}..., dimensions={0} | all-to-all | bytes 294912 | tf_op jit(solution)/shard_map/all_to_all | solution.py:327
  13.2 3.0 %collective-permute-start.8 = (bf16[4,16,1152]{2,1,0:T(8,128)(2,1)S(1)}, bf16[4,16,1152]{2,1,0:T(8,128)(2,1)S(1)}, u32[]{:S(2)}, u32[]{:S(2)}) collective-permute-start(bf16[4,16,1152]{2,1,0:T(8,128)(2,1)S(1)} %bitcast.19), channel_id=1, source_target_pairs={{0,4},{1,5},{2,6},{3,7},{4,8},{5,9},{6,10},{7,11},{8,12},{9,13},{1... | collective-permute-start | bytes 442376 | tf_op jit(solution)/shard_map/ppermute | solution.py:307
  16.2 3.0 %collective-permute-start.5 = (bf16[4,16,1152]{2,1,0:T(8,128)(2,1)S(1)}, bf16[4,16,1152]{2,1,0:T(8,128)(2,1)S(1)}, u32[]{:S(2)}, u32[]{:S(2)}) collective-permute-start(bf16[4,16,1152]{2,1,0:T(8,128)(2,1)S(1)} %bitcast.20), channel_id=1, source_target_pairs={{0,12},{1,13},{2,14},{3,15},{4,0},{5,1},{6,2},{7,3},{8,4},{9,5},{1... | collective-permute-start | bytes 442376 | tf_op jit(solution)/shard_map/ppermute | solution.py:307
  19.2 0.7 collective-permute-start.10
  20.0 2.9 %copy.11 = bf16[2,16,128,256]{3,2,1,0:T(8,128)(2,1)S(1)} copy(bf16[2,16,128,256]{3,1,0,2:T(8,128)(2,1)} %bitcast.24) | data formatting | bytes 4194304 | tf_op jit(solution)/shard_map/transpose | solution.py:361
  22.9 1.0 shard_map.60
  23.9 4.0 %collective-permute-start = (bf16[4,256,256]{2,1,0:T(8,128)(2,1)S(1)}, bf16[4,256,256]{2,1,0:T(8,128)(2,1)S(1)}, u32[]{:S(2)}, u32[]{:S(2)}) collective-permute-start(bf16[4,256,256]{2,1,0:T(8,128)(2,1)S(1)} %shard_map.60), channel_id=1, source_target_pairs={{0,1},{1,2},{2,3},{3,4},{4,5},{5,6},{6,7},{7,8},{8,9},{9,10},{10,1... | collective-permute-start | bytes 1572872 | tf_op jit(solution)/shard_map/ppermute | solution.py:21
  27.8 2.0 %collective-permute-start.4 = (bf16[4,16,1152]{2,1,0:T(8,128)(2,1)S(1)}, bf16[4,16,1152]{2,1,0:T(8,128)(2,1)S(1)}, u32[]{:S(2)}, u32[]{:S(2)}) collective-permute-start(bf16[4,16,1152]{2,1,0:T(8,128)(2,1)S(1)} %bitcast.22), channel_id=1, source_target_pairs={{0,14},{1,15},{2,0},{3,1},{4,2},{5,3},{6,4},{7,5},{8,6},{9,7},{10,... | collective-permute-start | bytes 442376 | tf_op jit(solution)/shard_map/ppermute | solution.py:307
  29.9 1.9 %collective-permute-start.7 = (bf16[4,16,1152]{2,1,0:T(8,128)(2,1)S(1)}, bf16[4,16,1152]{2,1,0:T(8,128)(2,1)S(1)}, u32[]{:S(2)}, u32[]{:S(2)}) collective-permute-start(bf16[4,16,1152]{2,1,0:T(8,128)(2,1)S(1)} %collective-permute-done.5.refs_2_), channel_id=1, source_target_pairs={{0,12},{1,13},{2,14},{3,15},{4,0},{5,1},{6,2},{7,3},{8,4},{9,5},{1... | collective-permute-start | bytes 442376 | tf_op jit(solution)/shard_map/ppermute | solution.py:307
  31.8 1.0 collective-permute-start.6
  32.8 0.8 collective-permute-done.4.refs_1_
  33.6 6.0 %collective-permute-done.9.refs_5_ = bf16[4,16,1152]{2,1,0:T(8,128)(2,1)S(1)} collective-permute-done((bf16[4,16,1152]{2,1,0:T(8,128)(2,1)S(1)}, bf16[4,16,1152]{2,1,0:T(8,128)(2,1)S(1)}, u32[]{:S(2)}, u32[]{:S(2)}) %collective-permute-start.9) | collective-permute-done | bytes 147488 | tf_op jit(solution)/shard_map/ppermute | solution.py:307
  39.6 1.9 %collective-permute-done.7.refs_4_ = bf16[4,16,1152]{2,1,0:T(8,128)(2,1)S(1)} collective-permute-done((bf16[4,16,1152]{2,1,0:T(8,128)(2,1)S(1)}, bf16[4,16,1152]{2,1,0:T(8,128)(2,1)S(1)}, u32[]{:S(2)}, u32[]{:S(2)}) %collective-permute-start.7) | collective-permute-done | bytes 147488 | tf_op jit(solution)/shard_map/ppermute | solution.py:307
  41.5 2.1 %collective-permute-done.6.refs_3_ = bf16[4,16,1152]{2,1,0:T(8,128)(2,1)S(1)} collective-permute-done((bf16[4,16,1152]{2,1,0:T(8,128)(2,1)S(1)}, bf16[4,16,1152]{2,1,0:T(8,128)(2,1)S(1)}, u32[]{:S(2)}, u32[]{:S(2)}) %collective-permute-start.6) | collective-permute-done | bytes 147488 | tf_op jit(solution)/shard_map/ppermute | solution.py:307
  43.6 1.1 %shard_map.62.refs_4_ = bf16[8,4,16,1152]{3,2,1,0:T(8,128)(2,1)} custom-call(bf16[4,16,1152]{2,1,0:T(8,128)(2,1)S(1)} %bitcast.23, bf16[4,16,1152]{2,1,0:T(8,128)(2,1)S(1)} %collective-permute-done.4.refs_1_, bf16[4,16,1152]{2,1,0:T(8,128)(2,1)S(1)} %collective-permute-done.5.refs_2_, bf16[4,16,1152]{2,1,0:T(8,128)(2,1)S(1)} %collective-permute-done.6.refs_3_, ...), custom_call_target="tpu_custom_call" | custom-call | bytes 2359296 | tf_op jit(solution)/shard_map/pallas_call | solution.py:146
  44.8 0.6 collective-permute-start.11
  45.4 1.6 %shard_map.59.part_ref = f32[4,256,256]{2,1,0:T(8,128)S(1)} custom-call(bf16[3456,256]{1,0:T(8,128)(2,1)S(1)} %bitcast.18, bf16[2,2048,256]{2,1,0:T(8,128)(2,1)S(1)} %bitcast.16), custom_call_target="tpu_custom_call" | custom-call | flops 1207959552 | bytes 2359296 | tf_op jit(solution)/shard_map/pallas_call | solution.py:96
  47.0 0.0 copy-start.3
  47.0 1.2 %shard_map.61 = bf16[16,64,256]{2,1,0:T(8,128)(2,1)} custom-call(f32[4,256,256]{2,1,0:T(8,128)S(1)} %shard_map.59.part_ref, bf16[4,256,256]{2,1,0:T(8,128)(2,1)S(1)} %collective-permute-done.behind_ref), custom_call_target="tpu_custom_call" | custom-call | flops 2621440 | bytes 2097152 | tf_op jit(solution)/shard_map/pallas_call | solution.py:127
  48.1 6.9 %all-to-all-start = ((bf16[16,64,256]{2,1,0:T(8,128)(2,1)}), bf16[16,64,256]{2,1,0:T(8,128)(2,1)S(1)}, u32[]{:S(2)}, u32[]{:S(2)}) async-start(bf16[16,64,256]{2,1,0:T(8,128)(2,1)} %shard_map.61), calls=%async_computation | async-start | bytes 1048576 | tf_op jit(solution)/shard_map/all_to_all | solution.py:327
  55.1 0.2 collective-permute-start.3
  55.3 1.4 %collective-permute-start.2 = (bf16[108,512]{1,0:T(8,128)(2,1)S(1)}, bf16[108,512]{1,0:T(8,128)(2,1)S(1)}, u32[]{:S(2)}, u32[]{:S(2)}) collective-permute-start(bf16[108,512]{1,0:T(8,128)(2,1)S(1)} %reshape.39.refs_0_), channel_id=1, source_target_pairs={{0,32},{1,33},{2,34},{3,35},{4,36},{5,37},{6,38},{7,39},{8,40},{9,... | collective-permute-start | bytes 331784 | tf_op jit(solution)/shard_map/ppermute | solution.py:307
  56.7 1.2 %collective-permute-start.1 = (bf16[108,512]{1,0:T(8,128)(2,1)S(1)}, bf16[108,512]{1,0:T(8,128)(2,1)S(1)}, u32[]{:S(2)}, u32[]{:S(2)}) collective-permute-start(bf16[108,512]{1,0:T(8,128)(2,1)S(1)} %reshape.39.refs_0_), channel_id=1, source_target_pairs={{0,48},{1,49},{2,50},{3,51},{4,52},{5,53},{6,54},{7,55},{8,56},{9,... | collective-permute-start | bytes 331784 | tf_op jit(solution)/shard_map/ppermute | solution.py:307
  57.9 0.1 pad_add_fusion.place_ref
  58.0 5.5 %collective-permute-done.3.refs_3_ = bf16[108,512]{1,0:T(8,128)(2,1)S(1)} collective-permute-done((bf16[108,512]{1,0:T(8,128)(2,1)S(1)}, bf16[108,512]{1,0:T(8,128)(2,1)S(1)}, u32[]{:S(2)}, u32[]{:S(2)}) %collective-permute-start.3) | collective-permute-done | bytes 110624 | tf_op jit(solution)/shard_map/ppermute | solution.py:307
  63.5 0.3 collective-permute-done.1.refs_1_
  63.8 4.7 %shard_map.63 = (bf16[16,64,256]{2,1,0:T(8,128)(2,1)}, bf16[512,2304]{1,0:T(8,128)(2,1)S(1)}) custom-call(s32[3]{0:T(128)S(1)} %pad_add_fusion.place_ref, bf16[108,512]{1,0:T(8,128)(2,1)S(1)} %reshape.39.refs_0_, bf16[108,512]{1,0:T(8,128)(2,1)S(1)} %collective-permute-done.1.refs_1_, bf16[108,512]{1,0:T(8,128)(2,1)S(1)} %collective-permute-done.2.refs_2_, ...), custom_call_target="tpu_custom_call" | custom-call | flops 1610612736 | bytes 4718592 | tf_op jit(solution)/shard_map/pallas_call | solution.py:281
  68.6 1.4 %copy-done.1 = bf16[512,2304]{1,0:T(8,128)(2,1)} copy-done((bf16[512,2304]{1,0:T(8,128)(2,1)}, bf16[512,2304]{1,0:T(8,128)(2,1)S(1)}, u32[]{:S(2)}) %copy-start.1) | copy-done | bytes 2359320
  70.0 2.3 %all-to-all-done.hidden_ref = bf16[16,64,256]{2,1,0:T(8,128)(2,1)S(1)} async-done(((bf16[16,64,256]{2,1,0:T(8,128)(2,1)}), bf16[16,64,256]{2,1,0:T(8,128)(2,1)S(1)}, u32[]{:S(2)}, u32[]{:S(2)}) %all-to-all-start) | async-done | bytes 524320 | tf_op jit(solution)/shard_map/all_to_all | solution.py:327
  72.3 5.8 %all-to-all-start.2 = ((bf16[16,64,256]{2,1,0:T(8,128)(2,1)}), bf16[16,64,256]{2,1,0:T(8,128)(2,1)S(1)}, u32[]{:S(2)}, u32[]{:S(2)}) async-start(bf16[16,64,256]{2,1,0:T(8,128)(2,1)} %get-tuple-element.13), calls=%async_computation.2 | async-start | bytes 1048576 | tf_op jit(solution)/shard_map/all_to_all | solution.py:327
  78.1 1.7 %copy-done.2 = bf16[512,2304]{1,0:T(8,128)(2,1)S(1)} copy-done((bf16[512,2304]{1,0:T(8,128)(2,1)S(1)}, bf16[512,2304]{1,0:T(8,128)(2,1)}, u32[]{:S(2)}) %copy-start.2) | copy-done | bytes 2359320
  79.7 2.4 %shard_map.64 = (f32[108,512]{1,0:T(8,128)S(1)}, bf16[108,512]{1,0:T(8,128)(2,1)S(1)}, bf16[108,512]{1,0:T(8,128)(2,1)S(1)}, bf16[108,512]{1,0:T(8,128)(2,1)S(1)}) custom-call(s32[3]{0:T(128)S(1)} %pad_add_fusion.place_ref, bf16[16,64,256]{2,1,0:T(8,128)(2,1)S(1)} %all-to-all-done.hidden_ref, bf16[512,2304]{1,0:T(8,128)(2,1)S(1)} %copy-done.2), custom_call_target="tpu_custom_call" | custom-call | flops 1610612736 | bytes 2359296 | tf_op jit(solution)/shard_map/pallas_call | solution.py:218
  82.2 0.1 collective-permute-start.12
  82.2 3.2 %collective-permute-start.13 = (bf16[108,512]{1,0:T(8,128)(2,1)S(1)}, bf16[108,512]{1,0:T(8,128)(2,1)S(1)}, u32[]{:S(2)}, u32[]{:S(2)}) collective-permute-start(bf16[108,512]{1,0:T(8,128)(2,1)S(1)} %get-tuple-element.11), channel_id=1, source_target_pairs={{0,32},{1,33},{2,34},{3,35},{4,36},{5,37},{6,38},{7,39},{8,40},{9,... | collective-permute-start | bytes 331784 | tf_op jit(solution)/shard_map/ppermute | solution.py:307
  85.5 2.6 %collective-permute-done.12 = bf16[108,512]{1,0:T(8,128)(2,1)S(1)} collective-permute-done((bf16[108,512]{1,0:T(8,128)(2,1)S(1)}, bf16[108,512]{1,0:T(8,128)(2,1)S(1)}, u32[]{:S(2)}, u32[]{:S(2)}) %collective-permute-start.12) | collective-permute-done | bytes 110624 | tf_op jit(solution)/shard_map/ppermute | solution.py:307
  88.0 3.0 %collective-permute-done.13 = bf16[108,512]{1,0:T(8,128)(2,1)S(1)} collective-permute-done((bf16[108,512]{1,0:T(8,128)(2,1)S(1)}, bf16[108,512]{1,0:T(8,128)(2,1)S(1)}, u32[]{:S(2)}, u32[]{:S(2)}) %collective-permute-start.13) | collective-permute-done | bytes 110624 | tf_op jit(solution)/shard_map/ppermute | solution.py:307
  91.1 0.1 add_convert_fusion
  91.1 2.6 %collective-permute-start.17 = (bf16[108,512]{1,0:T(8,128)(2,1)S(1)}, bf16[108,512]{1,0:T(8,128)(2,1)S(1)}, u32[]{:S(2)}, u32[]{:S(2)}) collective-permute-start(bf16[108,512]{1,0:T(8,128)(2,1)S(1)} %add_convert_fusion), channel_id=1, source_target_pairs={{0,192},{64,0},{128,64},{192,128},{1,193},{65,1},{129,65},{193,129... | collective-permute-start | bytes 331784 | tf_op jit(solution)/shard_map/ppermute | solution.py:26
  93.7 1.7 %collective-permute-start.15 = (bf16[108,512]{1,0:T(8,128)(2,1)S(1)}, bf16[108,512]{1,0:T(8,128)(2,1)S(1)}, u32[]{:S(2)}, u32[]{:S(2)}) collective-permute-start(bf16[108,512]{1,0:T(8,128)(2,1)S(1)} %add_convert_fusion), channel_id=1, source_target_pairs={{0,128},{64,192},{128,0},{192,64},{1,129},{65,193},{129,1},{193,65... | collective-permute-start | bytes 331784 | tf_op jit(solution)/shard_map/ppermute | solution.py:26
  95.4 0.4 shard_map.65
  95.8 5.9 %collective-permute-done.16 = bf16[108,512]{1,0:T(8,128)(2,1)S(1)} collective-permute-done((bf16[108,512]{1,0:T(8,128)(2,1)S(1)}, bf16[108,512]{1,0:T(8,128)(2,1)S(1)}, u32[]{:S(2)}, u32[]{:S(2)}) %collective-permute-start.16) | collective-permute-done | bytes 110624 | tf_op jit(solution)/shard_map/ppermute | solution.py:26
  101.8 0.1 add_add_fusion
  101.8 0.7 reshape.42
  102.6 0.1 multiply_convert_fusion
  102.7 0.1 reshape.43
  102.9 1.1 %copy.13 = bf16[4,16,4,4,256]{4,3,2,1,0:T(4,128)(2,1)} copy(bf16[4,16,4,4,256]{4,2,0,3,1:T(4,128)(2,1)S(1)} %bitcast.25) | data formatting | bytes 1048576 | tf_op jit(solution)/shard_map/transpose | solution.py:384
  (24 shorter events, 0.2 us)
Async XLA Ops:
  13.2 16.7 %collective-permute-start.8 = (bf16[4,16,1152]{2,1,0:T(8,128)(2,1)S(1)}, bf16[4,16,1152]{2,1,0:T(8,128)(2,1)S(1)}, u32[]{:S(2)}, u32[]{:S(2)}) collective-permute-start(bf16[4,16,1152]{2,1,0:T(8,128)(2,1)S(1)} %bitcast.19), channel_id=1, source_target_pairs={{0,4},{1,5},{2,6},{3,7},{4,8},{5,9},{6,10},{7,11},{8,12},{9,13},{1... | collective-permute-start | bytes 442376 | tf_op jit(solution)/shard_map/ppermute | solution.py:307
  16.2 13.7 %collective-permute-start.5 = (bf16[4,16,1152]{2,1,0:T(8,128)(2,1)S(1)}, bf16[4,16,1152]{2,1,0:T(8,128)(2,1)S(1)}, u32[]{:S(2)}, u32[]{:S(2)}) collective-permute-start(bf16[4,16,1152]{2,1,0:T(8,128)(2,1)S(1)} %bitcast.20), channel_id=1, source_target_pairs={{0,12},{1,13},{2,14},{3,15},{4,0},{5,1},{6,2},{7,3},{8,4},{9,5},{1... | collective-permute-start | bytes 442376 | tf_op jit(solution)/shard_map/ppermute | solution.py:307
  19.2 12.6 %collective-permute-start.10 = (bf16[4,16,1152]{2,1,0:T(8,128)(2,1)S(1)}, bf16[4,16,1152]{2,1,0:T(8,128)(2,1)S(1)}, u32[]{:S(2)}, u32[]{:S(2)}) collective-permute-start(bf16[4,16,1152]{2,1,0:T(8,128)(2,1)S(1)} %bitcast.21), channel_id=1, source_target_pairs={{0,2},{1,3},{2,4},{3,5},{4,6},{5,7},{6,8},{7,9},{8,10},{9,11},{10,... | collective-permute-start | bytes 442376 | tf_op jit(solution)/shard_map/ppermute | solution.py:307
  20.0 2.9 %copy-start = (bf16[3,3,3,128,256]{4,3,2,1,0:T(8,128)(2,1)S(1)}, bf16[3,3,3,128,256]{4,3,2,1,0:T(8,128)(2,1)}, u32[]{:S(2)}) copy-start(bf16[3,3,3,128,256]{4,3,2,1,0:T(8,128)(2,1)} %param.5) | copy-start | bytes 5308420
  23.9 23.1 %collective-permute-start = (bf16[4,256,256]{2,1,0:T(8,128)(2,1)S(1)}, bf16[4,256,256]{2,1,0:T(8,128)(2,1)S(1)}, u32[]{:S(2)}, u32[]{:S(2)}) collective-permute-start(bf16[4,256,256]{2,1,0:T(8,128)(2,1)S(1)} %shard_map.60), channel_id=1, source_target_pairs={{0,1},{1,2},{2,3},{3,4},{4,5},{5,6},{6,7},{7,8},{8,9},{9,10},{10,1... | collective-permute-start | bytes 1572872 | tf_op jit(solution)/shard_map/ppermute | solution.py:21
  27.8 5.7 %collective-permute-start.4 = (bf16[4,16,1152]{2,1,0:T(8,128)(2,1)S(1)}, bf16[4,16,1152]{2,1,0:T(8,128)(2,1)S(1)}, u32[]{:S(2)}, u32[]{:S(2)}) collective-permute-start(bf16[4,16,1152]{2,1,0:T(8,128)(2,1)S(1)} %bitcast.22), channel_id=1, source_target_pairs={{0,14},{1,15},{2,0},{3,1},{4,2},{5,3},{6,4},{7,5},{8,6},{9,7},{10,... | collective-permute-start | bytes 442376 | tf_op jit(solution)/shard_map/ppermute | solution.py:307
  29.9 9.7 %collective-permute-start.9 = (bf16[4,16,1152]{2,1,0:T(8,128)(2,1)S(1)}, bf16[4,16,1152]{2,1,0:T(8,128)(2,1)S(1)}, u32[]{:S(2)}, u32[]{:S(2)}) collective-permute-start(bf16[4,16,1152]{2,1,0:T(8,128)(2,1)S(1)} %collective-permute-done.8.refs_6_), channel_id=1, source_target_pairs={{0,2},{1,3},{2,4},{3,5},{4,6},{5,7},{6,8},{7,9},{8,10},{9,11},{10,... | collective-permute-start | bytes 442376 | tf_op jit(solution)/shard_map/ppermute | solution.py:307
  29.9 11.6 %collective-permute-start.7 = (bf16[4,16,1152]{2,1,0:T(8,128)(2,1)S(1)}, bf16[4,16,1152]{2,1,0:T(8,128)(2,1)S(1)}, u32[]{:S(2)}, u32[]{:S(2)}) collective-permute-start(bf16[4,16,1152]{2,1,0:T(8,128)(2,1)S(1)} %collective-permute-done.5.refs_2_), channel_id=1, source_target_pairs={{0,12},{1,13},{2,14},{3,15},{4,0},{5,1},{6,2},{7,3},{8,4},{9,5},{1... | collective-permute-start | bytes 442376 | tf_op jit(solution)/shard_map/ppermute | solution.py:307
  31.8 11.8 %collective-permute-start.6 = (bf16[4,16,1152]{2,1,0:T(8,128)(2,1)S(1)}, bf16[4,16,1152]{2,1,0:T(8,128)(2,1)S(1)}, u32[]{:S(2)}, u32[]{:S(2)}) collective-permute-start(bf16[4,16,1152]{2,1,0:T(8,128)(2,1)S(1)} %collective-permute-done.5.refs_2_), channel_id=1, source_target_pairs={{0,14},{1,15},{2,0},{3,1},{4,2},{5,3},{6,4},{7,5},{8,6},{9,7},{10,... | collective-permute-start | bytes 442376 | tf_op jit(solution)/shard_map/ppermute | solution.py:307
  44.8 19.1 %collective-permute-start.11 = (bf16[8,4,16,1152]{3,2,1,0:T(8,128)(2,1)}, bf16[8,4,16,1152]{3,2,1,0:T(8,128)(2,1)}, u32[]{:S(2)}, u32[]{:S(2)}) collective-permute-start(bf16[8,4,16,1152]{3,2,1,0:T(8,128)(2,1)} %shard_map.62.refs_4_), channel_id=1, source_target_pairs={{0,1},{1,0},{2,3},{3,2},{4,5},{5,4},{6,7},{7,6},{8,9},{9,8},{10,11... | collective-permute-start | bytes 3538952 | tf_op jit(solution)/shard_map/ppermute | solution.py:307
  47.0 8.1 %copy-start.3 = (bf16[3,3,3,4,512]{4,3,2,1,0:T(4,128)(2,1)S(1)}, bf16[3,3,3,4,512]{4,3,2,1,0:T(4,128)(2,1)}, u32[]{:S(2)}) copy-start(bf16[3,3,3,4,512]{4,3,2,1,0:T(4,128)(2,1)} %param.6) | copy-start | bytes 331780
  48.1 24.2 %all-to-all-start = ((bf16[16,64,256]{2,1,0:T(8,128)(2,1)}), bf16[16,64,256]{2,1,0:T(8,128)(2,1)S(1)}, u32[]{:S(2)}, u32[]{:S(2)}) async-start(bf16[16,64,256]{2,1,0:T(8,128)(2,1)} %shard_map.61), calls=%async_computation | async-start | bytes 1048576 | tf_op jit(solution)/shard_map/all_to_all | solution.py:327
  55.1 8.3 %collective-permute-start.3 = (bf16[108,512]{1,0:T(8,128)(2,1)S(1)}, bf16[108,512]{1,0:T(8,128)(2,1)S(1)}, u32[]{:S(2)}, u32[]{:S(2)}) collective-permute-start(bf16[108,512]{1,0:T(8,128)(2,1)S(1)} %reshape.39.refs_0_), channel_id=1, source_target_pairs={{0,16},{1,17},{2,18},{3,19},{4,20},{5,21},{6,22},{7,23},{8,24},{9,... | collective-permute-start | bytes 331784 | tf_op jit(solution)/shard_map/ppermute | solution.py:307
  55.3 8.2 %collective-permute-start.2 = (bf16[108,512]{1,0:T(8,128)(2,1)S(1)}, bf16[108,512]{1,0:T(8,128)(2,1)S(1)}, u32[]{:S(2)}, u32[]{:S(2)}) collective-permute-start(bf16[108,512]{1,0:T(8,128)(2,1)S(1)} %reshape.39.refs_0_), channel_id=1, source_target_pairs={{0,32},{1,33},{2,34},{3,35},{4,36},{5,37},{6,38},{7,39},{8,40},{9,... | collective-permute-start | bytes 331784 | tf_op jit(solution)/shard_map/ppermute | solution.py:307
  56.7 7.2 %collective-permute-start.1 = (bf16[108,512]{1,0:T(8,128)(2,1)S(1)}, bf16[108,512]{1,0:T(8,128)(2,1)S(1)}, u32[]{:S(2)}, u32[]{:S(2)}) collective-permute-start(bf16[108,512]{1,0:T(8,128)(2,1)S(1)} %reshape.39.refs_0_), channel_id=1, source_target_pairs={{0,48},{1,49},{2,50},{3,51},{4,52},{5,53},{6,54},{7,55},{8,56},{9,... | collective-permute-start | bytes 331784 | tf_op jit(solution)/shard_map/ppermute | solution.py:307
  68.6 1.4 %copy-start.1 = (bf16[512,2304]{1,0:T(8,128)(2,1)}, bf16[512,2304]{1,0:T(8,128)(2,1)S(1)}, u32[]{:S(2)}) copy-start(bf16[512,2304]{1,0:T(8,128)(2,1)S(1)} %get-tuple-element.8.cot_ref) | copy-start | bytes 7077892
  72.3 30.3 %all-to-all-start.2 = ((bf16[16,64,256]{2,1,0:T(8,128)(2,1)}), bf16[16,64,256]{2,1,0:T(8,128)(2,1)S(1)}, u32[]{:S(2)}, u32[]{:S(2)}) async-start(bf16[16,64,256]{2,1,0:T(8,128)(2,1)} %get-tuple-element.13), calls=%async_computation.2 | async-start | bytes 1048576 | tf_op jit(solution)/shard_map/all_to_all | solution.py:327
  78.1 1.7 %copy-start.2 = (bf16[512,2304]{1,0:T(8,128)(2,1)S(1)}, bf16[512,2304]{1,0:T(8,128)(2,1)}, u32[]{:S(2)}) copy-start(bf16[512,2304]{1,0:T(8,128)(2,1)} %copy-done.1) | copy-start | bytes 7077892
  82.2 5.9 %collective-permute-start.12 = (bf16[108,512]{1,0:T(8,128)(2,1)S(1)}, bf16[108,512]{1,0:T(8,128)(2,1)S(1)}, u32[]{:S(2)}, u32[]{:S(2)}) collective-permute-start(bf16[108,512]{1,0:T(8,128)(2,1)S(1)} %get-tuple-element.10), channel_id=1, source_target_pairs={{0,16},{1,17},{2,18},{3,19},{4,20},{5,21},{6,22},{7,23},{8,24},{9,... | collective-permute-start | bytes 331784 | tf_op jit(solution)/shard_map/ppermute | solution.py:307
  82.2 8.8 %collective-permute-start.13 = (bf16[108,512]{1,0:T(8,128)(2,1)S(1)}, bf16[108,512]{1,0:T(8,128)(2,1)S(1)}, u32[]{:S(2)}, u32[]{:S(2)}) collective-permute-start(bf16[108,512]{1,0:T(8,128)(2,1)S(1)} %get-tuple-element.11), channel_id=1, source_target_pairs={{0,32},{1,33},{2,34},{3,35},{4,36},{5,37},{6,38},{7,39},{8,40},{9,... | collective-permute-start | bytes 331784 | tf_op jit(solution)/shard_map/ppermute | solution.py:307
  85.5 5.6 %collective-permute-start.14 = (bf16[108,512]{1,0:T(8,128)(2,1)S(1)}, bf16[108,512]{1,0:T(8,128)(2,1)S(1)}, u32[]{:S(2)}, u32[]{:S(2)}) collective-permute-start(bf16[108,512]{1,0:T(8,128)(2,1)S(1)} %get-tuple-element.12), channel_id=1, source_target_pairs={{0,48},{1,49},{2,50},{3,51},{4,52},{5,53},{6,54},{7,55},{8,56},{9,... | collective-permute-start | bytes 331784 | tf_op jit(solution)/shard_map/ppermute | solution.py:307
  91.1 4.7 %collective-permute-start.17 = (bf16[108,512]{1,0:T(8,128)(2,1)S(1)}, bf16[108,512]{1,0:T(8,128)(2,1)S(1)}, u32[]{:S(2)}, u32[]{:S(2)}) collective-permute-start(bf16[108,512]{1,0:T(8,128)(2,1)S(1)} %add_convert_fusion), channel_id=1, source_target_pairs={{0,192},{64,0},{128,64},{192,128},{1,193},{65,1},{129,65},{193,129... | collective-permute-start | bytes 331784 | tf_op jit(solution)/shard_map/ppermute | solution.py:26
  93.7 8.1 %collective-permute-start.16 = (bf16[108,512]{1,0:T(8,128)(2,1)S(1)}, bf16[108,512]{1,0:T(8,128)(2,1)S(1)}, u32[]{:S(2)}, u32[]{:S(2)}) collective-permute-start(bf16[108,512]{1,0:T(8,128)(2,1)S(1)} %add_convert_fusion), channel_id=1, source_target_pairs={{0,64},{64,128},{128,192},{192,0},{1,65},{65,129},{129,193},{193,1... | collective-permute-start | bytes 331784 | tf_op jit(solution)/shard_map/ppermute | solution.py:26
  93.7 8.1 %collective-permute-start.15 = (bf16[108,512]{1,0:T(8,128)(2,1)S(1)}, bf16[108,512]{1,0:T(8,128)(2,1)S(1)}, u32[]{:S(2)}, u32[]{:S(2)}) collective-permute-start(bf16[108,512]{1,0:T(8,128)(2,1)S(1)} %add_convert_fusion), channel_id=1, source_target_pairs={{0,128},{64,192},{128,0},{192,64},{1,129},{65,193},{129,1},{193,65... | collective-permute-start | bytes 331784 | tf_op jit(solution)/shard_map/ppermute | solution.py:26

commit v7 on v6

--- a/solution.py
+++ b/solution.py
@@ -39,6 +39,7 @@
 
 ROWS, RING, CORES = 4, 8, 2
 IN_VMEM = pl.BlockSpec(memory_space=pltpu.VMEM)
+ANYWHERE = pl.BlockSpec(memory_space=pl.ANY)
 GRANT = pltpu.CompilerParams(vmem_limit_bytes=16 * 2**20)
 
 
@@ -55,10 +56,20 @@
     return jnp.where(keep, moved, 0.0).astype(block.dtype)
 
 
-def conv_kernel(use, channels, row_len, w_ref, planes_ref, out_ref, cols_ref):
+def conv_kernel(row_len, w_from, planes_from, ahead_ref, part_ref, *scratch):
+    cols_ref, w_ref, planes_ref, sems = scratch
+    copies = [
+        pltpu.make_async_copy(planes_from.at[0], planes_ref.at[0], sems.at[0]),
+        pltpu.make_async_copy(planes_from.at[1], planes_ref.at[1], sems.at[1]),
+        pltpu.make_async_copy(w_from, w_ref, sems.at[2]),
+    ]
+    for copy in copies:
+        copy.start()
+    cells = planes_ref.shape[2]
+    channels = planes_ref.shape[1] // 16
     tap_rows = 9 * channels
-    cells = planes_ref.shape[2]
-    for at, (_, plane) in enumerate(use):
+    for plane in range(2):
+        copies[plane].wait()
         for row in range(-1, 4):
             for col in range(-1, 4):
                 source = ((row % 4) * 4 + col % 4) * channels
@@ -73,32 +84,38 @@
                         col_tap = col + 1 - 2 * col_phase
                         if not 0 <= col_tap <= 2:
                             continue
-                        start = at * tap_rows + (row_tap * 3 + col_tap) * channels
+                        start = plane * tap_rows + (row_tap * 3 + col_tap) * channels
                         phase = row_phase * 2 + col_phase
                         put = slice(phase * cells, (phase + 1) * cells)
                         cols_ref[start : start + channels, put] = block
-    first = use[0][0] * tap_rows
-    total = lax.dot_general(
-        w_ref[first : first + len(use) * tap_rows, :],
-        cols_ref[...],
-        (((0,), (0,)), ((), ())),
-        preferred_element_type=jnp.float32,
-    )
-    for phase in range(4):
-        out_ref[phase] = total[:, phase * cells : (phase + 1) * cells].astype(out_ref.dtype)
-
-
-def conv(w_rows, planes, use, dtype, row_len):
+    copies[2].wait()
+    over_rows = (((0,), (0,)), ((), ()))
+    for out_ref, weights, cols in (
+        (ahead_ref, w_ref[:tap_rows, :], cols_ref[tap_rows:, :]),
+        (part_ref, w_ref[tap_rows:, :], cols_ref[...]),
+    ):
+        total = lax.dot_general(weights, cols, over_rows, preferred_element_type=jnp.float32)
+        for phase in range(4):
+            out_ref[phase] = total[:, phase * cells : (phase + 1) * cells].astype(out_ref.dtype)
+
+
+def conv(w_rows, planes, row_len):
     depth, outs = w_rows.shape
-    channels = depth // 27
     cells = planes.shape[2]
-    depth = 9 * channels * len(use)
     return pl.pallas_call(
-        functools.partial(conv_kernel, use, channels, row_len),
-        out_shape=jax.ShapeDtypeStruct((4, outs, cells), dtype),
-        in_specs=[IN_VMEM] * 2,
-        out_specs=IN_VMEM,
-        scratch_shapes=[pltpu.VMEM((depth, 4 * cells), jnp.bfloat16)],
+        functools.partial(conv_kernel, row_len),
+        out_shape=(
+            jax.ShapeDtypeStruct((4, outs, cells), jnp.bfloat16),
+            jax.ShapeDtypeStruct((4, outs, cells), jnp.float32),
+        ),
+        in_specs=[ANYWHERE] * 2,
+        out_specs=(IN_VMEM,) * 2,
+        scratch_shapes=[
+            pltpu.VMEM((2 * depth // 3, 4 * cells), jnp.bfloat16),
+            pltpu.VMEM(w_rows.shape, jnp.bfloat16),
+            pltpu.VMEM(planes.shape, jnp.bfloat16),
+            pltpu.SemaphoreType.DMA((3,)),
+        ],
         compiler_params=GRANT,
         cost_estimate=pl.CostEstimate(
             flops=8 * outs * depth * cells, bytes_accessed=4 * depth * cells, transcendentals=0
@@ -137,8 +154,14 @@
 
 
 def pile_kernel(*refs):
-    for at, ref in enumerate(refs[:-1]):
-        refs[-1][at] = ref[...]
+    blocks, out_ref, sems = refs[:-2], refs[-2], refs[-1]
+    copies = [
+        pltpu.make_async_copy(block, out_ref.at[at], sems.at[at]) for at, block in enumerate(blocks)
+    ]
+    for copy in copies:
+        copy.start()
+    for copy in copies:
+        copy.wait()
 
 
 def pile(blocks):
@@ -146,8 +169,9 @@
     return pl.pallas_call(
         pile_kernel,
         out_shape=jax.ShapeDtypeStruct(shape, blocks[0].dtype),
-        in_specs=[IN_VMEM] * len(blocks),
+        in_specs=[ANYWHERE] * len(blocks),
         out_specs=IN_VMEM,
+        scratch_shapes=[pltpu.SemaphoreType.DMA((len(blocks),))],
         compiler_params=GRANT,
         cost_estimate=pl.CostEstimate(
             flops=0, bytes_accessed=4 * len(blocks) * blocks[0].size, transcendentals=0
@@ -178,8 +202,28 @@
     return total
 
 
-def grad_kernel(row_len, place_ref, hidden_ref, cot_ref, *refs):
-    outs_refs, (even_ref, odd_ref, sum_ref) = refs[:-3], refs[-3:]
+def cot_copies(place_ref, mine, theirs_ref, cot_ref, sems):
+    ring = len(mine)
+    half = cot_ref.shape[3] // 2
+    z, core = place_ref[1], place_ref[2]
+    here = pl.ds(pl.multiple_of(core * half, 128), half)
+    there = pl.ds(pl.multiple_of((1 - core) * half, 128), half)
+    copies = []
+    for k in range(ring):
+        to = lax.rem(z + k, ring)
+        for side, (source, part) in enumerate(((mine[k], here), (theirs_ref.at[k], there))):
+            copies.append(
+                pltpu.make_async_copy(source, cot_ref.at[:, to, :, part], sems.at[2 * k + side])
+            )
+    return copies
+
+
+def grad_kernel(row_len, place_ref, hidden_ref, *refs):
+    mine, theirs_ref, refs = refs[:RING], refs[RING], refs[RING + 1 :]
+    outs_refs, (cot_ref, sems, even_ref, odd_ref, sum_ref) = refs[:-5], refs[-5:]
+    copies = cot_copies(place_ref, mine, theirs_ref, cot_ref, sems)
+    for copy in copies:
+        copy.start()
     planes, group, cells = hidden_ref.shape
     steps = planes // 2
     own = group // 4
@@ -188,12 +232,14 @@
         here = slice(s * cells, (s + 1) * cells)
         even_ref[:, here] = spread(hidden_ref[2 * s], row_len)
         odd_ref[:, here] = spread(hidden_ref[2 * s + 1], row_len)
+    for copy in copies:
+        copy.wait()
     over_cells = (((1,), (1,)), ((), ()))
     sources = ((odd_ref, cells), (even_ref, 0), (odd_ref, 0))
     for depth_tap, (rows_ref, start) in enumerate(sources):
         total = lax.dot_general(
             rows_ref[...],
-            cot_ref[:, start : start + steps * cells],
+            cot_ref[:, :, :, start : start + steps * cells].reshape(-1, steps * cells),
             over_cells,
             preferred_element_type=jnp.float32,
         )
@@ -210,40 +256,43 @@
         out_ref[...] = sum_ref[y].astype(out_ref.dtype)
 
 
-def grad(place, hidden, cot, row_count, row_len):
+def grad(place, hidden, mine, theirs, row_len):
     planes, group, cells = hidden.shape
-    outs = cot.shape[0]
+    cot_shape = mine[0].shape[:1] + (RING,) + mine[0].shape[1:2] + (2 * mine[0].shape[2],)
+    outs = cot_shape[0] * cot_shape[1] * cot_shape[2]
     rows = pltpu.VMEM((4 * group, planes // 2 * cells), jnp.bfloat16)
-    size = 27 * group // (4 * row_count)
+    size = 27 * group // (4 * ROWS)
     return pl.pallas_call(
         functools.partial(grad_kernel, row_len),
         out_shape=[
             jax.ShapeDtypeStruct((size, outs), jnp.bfloat16 if away else jnp.float32)
-            for away in range(row_count)
+            for away in range(ROWS)
         ],
-        in_specs=[pl.BlockSpec(memory_space=pltpu.SMEM), IN_VMEM, IN_VMEM],
-        out_specs=[IN_VMEM] * row_count,
-        scratch_shapes=[rows, rows, pltpu.VMEM((row_count, size, outs), jnp.float32)],
+        in_specs=[pl.BlockSpec(memory_space=pltpu.SMEM), IN_VMEM] + [ANYWHERE] * (RING + 1),
+        out_specs=[IN_VMEM] * ROWS,
+        scratch_shapes=[
+            pltpu.VMEM(cot_shape, jnp.bfloat16),
+            pltpu.SemaphoreType.DMA((2 * RING,)),
+            rows,
+            rows,
+            pltpu.VMEM((ROWS, size, outs), jnp.float32),
+        ],
         compiler_params=GRANT,
         cost_estimate=pl.CostEstimate(
-            flops=12 * group * outs * planes * cells, bytes_accessed=2 * cot.size, transcendentals=0
-        ),
-    )(place, hidden, cot)
+            flops=12 * group * outs * planes * cells, bytes_accessed=2**22, transcendentals=0
+        ),
+    )(place, hidden, *mine, theirs)
 
 
 def back_kernel(row_len, place_ref, *refs):
-    w_refs, (mine_ref, theirs_ref, out_ref, cot_ref, rows_ref, moves_ref) = refs[:-6], refs[-6:]
+    w_refs, mine, theirs_ref = refs[:ROWS], refs[ROWS : ROWS + RING], refs[ROWS + RING]
+    out_ref, cot_ref, sems, rows_ref, moves_ref = refs[ROWS + RING + 1 :]
     planes, group, cells = out_ref.shape
-    ring, row_count, unit, half = mine_ref.shape
-    y, z, core = place_ref[0], place_ref[1], place_ref[2]
-    here = pl.ds(pl.multiple_of(core * half, 128), half)
-    there = pl.ds(pl.multiple_of((1 - core) * half, 128), half)
-    for k in range(ring):
-        for row in range(row_count):
-            first = row * ring * unit + lax.rem(z + k, ring) * unit
-            rows = pl.ds(pl.multiple_of(first, unit), unit)
-            cot_ref[rows, here] = mine_ref[k, row]
-            cot_ref[rows, there] = theirs_ref[k, row]
+    row_count = ROWS
+    y = place_ref[0]
+    copies = cot_copies(place_ref, mine, theirs_ref, cot_ref, sems)
+    for copy in copies:
+        copy.start()
 
     for away, w_ref in enumerate(w_refs):
         rows_ref[lax.rem(y + away, row_count)] = w_ref[...].astype(jnp.float32)
@@ -258,10 +307,13 @@
         pieces = [rows_ref[row, tap * own : (tap + 1) * own, :] for row in range(row_count)]
         moves_ref[at : at + block, :] = jnp.concatenate(pieces, 0).astype(moves_ref.dtype)
 
+    for copy in copies:
+        copy.wait()
+
     def one(at, start):
         return jnp.dot(
             moves_ref[at * size : (at + 1) * size, :],
-            cot_ref[:, start : start + cells],
+            cot_ref[:, :, :, start : start + cells].reshape(-1, cells),
             preferred_element_type=jnp.float32,
         )
 
@@ -274,27 +326,25 @@
 
 def back(place, w_rel, mine, theirs, planes, row_len):
     size, outs = w_rel[0].shape
-    row_count = len(w_rel)
-    group = 4 * row_count * size // 27
-    width = 2 * mine.shape[3]
-    cells = width // (planes // 2 + 1)
+    group = 4 * ROWS * size // 27
+    cot_shape = mine[0].shape[:1] + (RING,) + mine[0].shape[1:2] + (2 * mine[0].shape[2],)
+    cells = cot_shape[3] // (planes // 2 + 1)
     return pl.pallas_call(
         functools.partial(back_kernel, row_len),
-        out_shape=(
-            jax.ShapeDtypeStruct((planes, group, cells), jnp.bfloat16),
-            jax.ShapeDtypeStruct((outs, width), jnp.bfloat16),
-        ),
-        in_specs=[pl.BlockSpec(memory_space=pltpu.SMEM)] + [IN_VMEM] * (row_count + 2),
-        out_specs=(IN_VMEM,) * 2,
+        out_shape=jax.ShapeDtypeStruct((planes, group, cells), jnp.bfloat16),
+        in_specs=[pl.BlockSpec(memory_space=pltpu.SMEM)] + [IN_VMEM] * ROWS + [ANYWHERE] * (RING + 1),
+        out_specs=IN_VMEM,
         scratch_shapes=[
-            pltpu.VMEM((row_count, size, outs), jnp.float32),
+            pltpu.VMEM(cot_shape, jnp.bfloat16),
+            pltpu.SemaphoreType.DMA((2 * RING,)),
+            pltpu.VMEM((ROWS, size, outs), jnp.float32),
             pltpu.VMEM((12 * group, outs), jnp.bfloat16),
         ],
         compiler_params=GRANT,
         cost_estimate=pl.CostEstimate(
-            flops=12 * group * outs * planes * cells, bytes_accessed=4 * outs * width, transcendentals=0
-        ),
-    )(place, *w_rel, mine, theirs)
+            flops=12 * group * outs * planes * cells, bytes_accessed=2**22, transcendentals=0
+        ),
+    )(place, *w_rel, *mine, theirs)
 
 
 def on_space(block, y_by=0, z_by=0, core_by=0):
@@ -346,13 +396,14 @@
     parts = parts.reshape(ROWS, -1, CORES, (share + 1) * cells // CORES).transpose(0, 2, 1, 3)
     first = exchange(parts.reshape((ROWS * CORES,) + parts.shape[2:]), PILLARS)
     first = first.reshape(ROWS, -1, first.shape[2])
-    hops = {0: first}
-    for step in (1, -1, 2, -2):
-        hops[step] = on_space(first, z_by=-step)
-    for step, come in ((3, 2), (-3, -2), (4, 2)):
-        hops[step] = on_space(hops[come], z_by=come - step)
-    mine = pile([hops[step] for step in (0, 1, 2, 3, 4, -3, -2, -1)])
-    theirs = on_space(mine, core_by=1)
+    up, down = [first], [first]
+    for _ in range(3):
+        up.append(on_space(up[-1], z_by=1))
+        down.append(on_space(down[-1], z_by=-1))
+    far = on_space(up[3], z_by=1)
+    mine = down + [far] + up[:0:-1]
+    piled = pile(mine)
+    theirs = on_space(piled, core_by=1)
 
     w_rel = [w_second.reshape(27 * own, C3)]
     for step in range(1, ROWS):
@@ -360,17 +411,16 @@
 
     planes = volume[0].transpose(1, 2, 0, 3).reshape(2, 16 * channels, cells)
     w_rows = w_first.reshape(27 * channels, outs)
-    ahead = conv(w_rows, planes, ((0, 1),), jnp.bfloat16, row_len)
+    ahead, part = conv(w_rows, planes, row_len)
     behind = from_behind(ahead, "space", 1)
-    part = conv(w_rows, planes, ((1, 0), (2, 1)), jnp.float32, row_len)
     hidden = pointwise(activate, part, behind, group, jnp.bfloat16)
     slopes = pointwise(slope_of, part, behind, group, jnp.float32)
     by_plane = exchange(hidden, SLABS)
 
-    back_terms, cot_row = back(place, w_rel, mine, theirs, group, row_len)
+    back_terms = back(place, w_rel, mine, theirs, group, row_len)
     hidden_grad = exchange(back_terms, SLABS)
 
-    partial, *others = grad(place, by_plane, cot_row, ROWS, row_len)
+    partial, *others = grad(place, by_plane, mine, theirs, row_len)
     for step, block in enumerate(others, 1):
         partial = partial + on_space(block, y_by=step).astype(jnp.float32)
     partial = partial.astype(jnp.bfloat16)

time: 104 us -> 109 us (1.048)
  waiting for transfers between devices: 30.5 us -> 34.8 us
  Pallas kernels: 12.5 us -> 16.7 us
  starting transfers between devices: 39.3 us -> 36.2 us
  local copies, waits for them, and re-layouts: 9.1 us -> 6.89 us
    ppermute x14, waiting for transfers between devices: 22.3 us -> 27.9 us  [on_space(): return lax.ppermute(block, 'space', route)]
    unnamed x8 -> x2, local copies, waits for them, and re-layouts: 3.11 us -> 0.01 us
    ppermute x14, starting transfers between devices: 18.4 us -> 16.7 us  [on_space(): return lax.ppermute(block, 'space', route)]
    pallas_call x1, Pallas kernels: 2.43 us -> 4.01 us  [grad(): pl.pallas_call(functools.partial(grad_kernel, row_len), out_shape=[jax.Sh...]
    pallas_call x1, Pallas kernels: 1.13 us -> 2.58 us  [pile(): pl.pallas_call(pile_kernel, out_shape=jax.ShapeDtypeStruct(shape, blocks[...]
    all_to_all x2, waiting for transfers between devices: 2.31 us -> 0.96 us  [exchange(): lax.all_to_all(blocks, 'space', split_axis=0, concat_axis=0, axis_index_g...]
    ppermute x1, starting transfers between devices: 3.96 us -> 2.67 us  [from_behind(): return lax.ppermute(block, axis, route)]
    pallas_call x3 -> x2, Pallas kernels: 7.33 us -> 8.5 us  [the longest x1 5.31 us: back(): pl.pallas_call(functools.partial(back_kernel, row_len), out_shape=jax.Sha...]
  transfers between devices with their start and end apart: 20 -> 20, of which waited for: 10 -> 11; matrix products, arithmetic and copies ran while one was open for 4% -> 4% of each run, Pallas kernels for 12% -> 15%
where the time goes in v7:
time: 109 us; the launch traced here: 108 us
  starting transfers between devices  36.2 us (33%)
  waiting for transfers between devices  34.8 us (32%)
  Pallas kernels  16.7 us (15%)
  blocking collectives  11.2 us (10%)
  local copies, waits for them, and re-layouts  6.89 us (6%)
  other arithmetic  1.64 us (2%)
    ppermute x14, waiting for transfers between devices, on_space(): return lax.ppermute(block, 'space', route)  27.9 us
    ppermute x14, starting transfers between devices, on_space(): return lax.ppermute(block, 'space', route)  16.7 us
    all_to_all x2, starting transfers between devices, exchange(): lax.all_to_all(blocks, 'space', split_axis=0, concat_axis=0, axis_index_g...  12.6 us
    all_to_all x1, blocking collectives, exchange(): lax.all_to_all(blocks, 'space', split_axis=0, concat_axis=0, axis_index_g...  11.2 us
    ppermute x3, waiting for transfers between devices, from_side(): lax.ppermute(block, axis, [(i, (i + distance) % size) for i in range(size)])  5.9 us
    pallas_call x1, Pallas kernels, back(): pl.pallas_call(functools.partial(back_kernel, row_len), out_shape=jax.Sha...  5.31 us
    ppermute x3, starting transfers between devices, from_side(): lax.ppermute(block, axis, [(i, (i + distance) % size) for i in range(size)])  4.28 us
    pallas_call x1, Pallas kernels, grad(): pl.pallas_call(functools.partial(grad_kernel, row_len), out_shape=[jax.Sh...  4.01 us
  transfers between devices with their start and end apart: 20, of which 11 were waited for; matrix products, arithmetic and copies ran while one was open for 4% of the time, Pallas kernels for 15%

profile of v7, /device:TPU:1, one launch (start us, length us, event | category | flops | bytes accessed | tf_op | source)
XLA Modules:
  0.0 108.2 jit_solution(17314661637066730510)
XLA Ops:
  0.6 1.0 fusion
  1.7 0.3 maximum_bitcast_fusion
  2.0 11.2 %all_to_all.15 = bf16[8,8,1152]{2,1,0:T(8,128)(2,1)S(1)} all-to-all(bf16[8,8,1152]{2,1,0:T(8,128)(2,1)S(1)} %bitcast.25), channel_id=1, replica_groups={{0,1,16,17,32,33,48,49},{2,3,18,19,34,35,50,51},{4,5,20,21,36,37,52,53}..., dimensions={0} | all-to-all | bytes 294912 | tf_op jit(solution)/shard_map/all_to_all | solution.py:377
  13.2 1.6 %collective-permute-start.4 = (bf16[4,16,1152]{2,1,0:T(8,128)(2,1)S(1)}, bf16[4,16,1152]{2,1,0:T(8,128)(2,1)S(1)}, u32[]{:S(2)}, u32[]{:S(2)}) collective-permute-start(bf16[4,16,1152]{2,1,0:T(8,128)(2,1)S(1)} %bitcast.16), channel_id=1, source_target_pairs={{0,2},{1,3},{2,4},{3,5},{4,6},{5,7},{6,8},{7,9},{8,10},{9,11},{10,... | collective-permute-start | bytes 442376 | tf_op jit(solution)/shard_map/ppermute | solution.py:357
  14.8 3.9 %collective-permute-start.1 = (bf16[4,16,1152]{2,1,0:T(8,128)(2,1)S(1)}, bf16[4,16,1152]{2,1,0:T(8,128)(2,1)S(1)}, u32[]{:S(2)}, u32[]{:S(2)}) collective-permute-start(bf16[4,16,1152]{2,1,0:T(8,128)(2,1)S(1)} %bitcast.17), channel_id=1, source_target_pairs={{0,14},{1,15},{2,0},{3,1},{4,2},{5,3},{6,4},{7,5},{8,6},{9,7},{10,... | collective-permute-start | bytes 442376 | tf_op jit(solution)/shard_map/ppermute | solution.py:357
  18.8 3.3 %collective-permute-done.4.refs_7_.refs_11_ = bf16[4,16,1152]{2,1,0:T(8,128)(2,1)S(1)} collective-permute-done((bf16[4,16,1152]{2,1,0:T(8,128)(2,1)S(1)}, bf16[4,16,1152]{2,1,0:T(8,128)(2,1)S(1)}, u32[]{:S(2)}, u32[]{:S(2)}) %collective-permute-start.4) | collective-permute-done | bytes 147488 | tf_op jit(solution)/shard_map/ppermute | solution.py:357
  22.1 0.0 collective-permute-start.5
  22.1 2.9 %copy.11 = bf16[2,16,128,256]{3,2,1,0:T(8,128)(2,1)S(1)} copy(bf16[2,16,128,256]{3,1,0,2:T(8,128)(2,1)} %bitcast.22) | data formatting | bytes 4194304 | tf_op jit(solution)/shard_map/transpose | solution.py:412
  25.0 0.0 collective-permute-done.1.refs_1_.refs_5_
  25.0 2.7 %collective-permute-start.2 = (bf16[4,16,1152]{2,1,0:T(8,128)(2,1)S(1)}, bf16[4,16,1152]{2,1,0:T(8,128)(2,1)S(1)}, u32[]{:S(2)}, u32[]{:S(2)}) collective-permute-start(bf16[4,16,1152]{2,1,0:T(8,128)(2,1)S(1)} %collective-permute-done.1.refs_1_.refs_5_), channel_id=1, source_target_pairs={{0,14},{1,15},{2,0},{3,1},{4,2},{5,3},{6,4},{7,5},{8,6},{9,7},{10,... | collective-permute-start | bytes 442376 | tf_op jit(solution)/shard_map/ppermute | solution.py:357
  27.8 0.0 collective-permute-done.5.refs_6_.refs_10_
  27.8 3.2 %shard_map.59 = (bf16[4,256,256]{2,1,0:T(8,128)(2,1)S(1)}, f32[4,256,256]{2,1,0:T(8,128)S(1)}) custom-call(bf16[3456,256]{1,0:T(8,128)(2,1)S(1)} %bitcast.21, bf16[2,2048,256]{2,1,0:T(8,128)(2,1)S(1)} %bitcast.15), custom_call_target="tpu_custom_call" | custom-call | flops 1811939328 | bytes 3538944 | tf_op jit(solution)/shard_map/pallas_call | solution.py:105
  31.0 2.7 %collective-permute-start = (bf16[4,256,256]{2,1,0:T(8,128)(2,1)S(1)}, bf16[4,256,256]{2,1,0:T(8,128)(2,1)S(1)}, u32[]{:S(2)}, u32[]{:S(2)}) collective-permute-start(bf16[4,256,256]{2,1,0:T(8,128)(2,1)S(1)} %get-tuple-element.9), channel_id=1, source_target_pairs={{0,1},{1,2},{2,3},{3,4},{4,5},{5,6},{6,7},{7,8},{8,9},{9,10},{10,1... | collective-permute-start | bytes 1572872 | tf_op jit(solution)/shard_map/ppermute | solution.py:21
  33.7 4.0 %collective-permute-start.3 = (bf16[4,16,1152]{2,1,0:T(8,128)(2,1)S(1)}, bf16[4,16,1152]{2,1,0:T(8,128)(2,1)S(1)}, u32[]{:S(2)}, u32[]{:S(2)}) collective-permute-start(bf16[4,16,1152]{2,1,0:T(8,128)(2,1)S(1)} %collective-permute-done.2.refs_2_.refs_6_), channel_id=1, source_target_pairs={{0,14},{1,15},{2,0},{3,1},{4,2},{5,3},{6,4},{7,5},{8,6},{9,7},{10,... | collective-permute-start | bytes 442376 | tf_op jit(solution)/shard_map/ppermute | solution.py:357
  37.7 2.9 %collective-permute-done.3.refs_3_.refs_7_ = bf16[4,16,1152]{2,1,0:T(8,128)(2,1)S(1)} collective-permute-done((bf16[4,16,1152]{2,1,0:T(8,128)(2,1)S(1)}, bf16[4,16,1152]{2,1,0:T(8,128)(2,1)S(1)}, u32[]{:S(2)}, u32[]{:S(2)}) %collective-permute-start.3) | collective-permute-done | bytes 147488 | tf_op jit(solution)/shard_map/ppermute | solution.py:357
  40.6 6.7 %collective-permute-done.7.refs_4_.refs_8_ = bf16[4,16,1152]{2,1,0:T(8,128)(2,1)S(1)} collective-permute-done((bf16[4,16,1152]{2,1,0:T(8,128)(2,1)S(1)}, bf16[4,16,1152]{2,1,0:T(8,128)(2,1)S(1)}, u32[]{:S(2)}, u32[]{:S(2)}) %collective-permute-start.7) | collective-permute-done | bytes 147488 | tf_op jit(solution)/shard_map/ppermute | solution.py:357
  47.3 2.6 %shard_map.61 = bf16[8,4,16,1152]{3,2,1,0:T(8,128)(2,1)} custom-call(bf16[4,16,1152]{2,1,0:T(8,128)(2,1)S(1)} %bitcast.18, bf16[4,16,1152]{2,1,0:T(8,128)(2,1)S(1)} %collective-permute-done.1.refs_1_.refs_5_, bf16[4,16,1152]{2,1,0:T(8,128)(2,1)S(1)} %collective-permute-done.2.refs_2_.refs_6_, ...), custom_call_target="tpu_custom_call" | custom-call | bytes 2359296 | tf_op jit(solution)/shard_map/pallas_call | solution.py:169
  49.9 0.1 collective-permute-start.8
  50.0 1.2 %shard_map.60 = bf16[16,64,256]{2,1,0:T(8,128)(2,1)} custom-call(f32[4,256,256]{2,1,0:T(8,128)S(1)} %get-tuple-element.8.part_ref, bf16[4,256,256]{2,1,0:T(8,128)(2,1)S(1)} %collective-permute-done.behind_ref), custom_call_target="tpu_custom_call" | custom-call | flops 2621440 | bytes 2097152 | tf_op jit(solution)/shard_map/pallas_call | solution.py:144
  51.2 6.1 %all-to-all-start = ((bf16[16,64,256]{2,1,0:T(8,128)(2,1)}), bf16[16,64,256]{2,1,0:T(8,128)(2,1)S(1)}, u32[]{:S(2)}, u32[]{:S(2)}) async-start(bf16[16,64,256]{2,1,0:T(8,128)(2,1)} %shard_map.60), calls=%async_computation | async-start | bytes 1048576 | tf_op jit(solution)/shard_map/all_to_all | solution.py:377
  57.2 0.9 reshape.42.refs_0_
  58.2 1.0 collective-permute-start.15
  59.1 1.2 %collective-permute-start.16 = (bf16[108,512]{1,0:T(8,128)(2,1)S(1)}, bf16[108,512]{1,0:T(8,128)(2,1)}, u32[]{:S(2)}, u32[]{:S(2)}) collective-permute-start(bf16[108,512]{1,0:T(8,128)(2,1)S(1)} %reshape.42.refs_0_), channel_id=1, source_target_pairs={{0,32},{1,33},{2,34},{3,35},{4,36},{5,37},{6,38},{7,39},{8,40},{9,... | collective-permute-start | bytes 331784 | tf_op jit(solution)/shard_map/ppermute | solution.py:357
  60.3 0.0 collective-permute-start.17
  60.3 0.1 pad_add_fusion.place_ref
  60.4 2.6 %collective-permute-done.15.refs_1_ = bf16[108,512]{1,0:T(8,128)(2,1)} collective-permute-done((bf16[108,512]{1,0:T(8,128)(2,1)S(1)}, bf16[108,512]{1,0:T(8,128)(2,1)}, u32[]{:S(2)}, u32[]{:S(2)}) %collective-permute-start.15) | collective-permute-done | bytes 110624 | tf_op jit(solution)/shard_map/ppermute | solution.py:357
  62.9 2.1 %collective-permute-done.16.refs_2_ = bf16[108,512]{1,0:T(8,128)(2,1)} collective-permute-done((bf16[108,512]{1,0:T(8,128)(2,1)S(1)}, bf16[108,512]{1,0:T(8,128)(2,1)}, u32[]{:S(2)}, u32[]{:S(2)}) %collective-permute-start.16) | collective-permute-done | bytes 110624 | tf_op jit(solution)/shard_map/ppermute | solution.py:357
  65.0 3.1 %collective-permute-done.17.refs_3_ = bf16[108,512]{1,0:T(8,128)(2,1)} collective-permute-done((bf16[108,512]{1,0:T(8,128)(2,1)S(1)}, bf16[108,512]{1,0:T(8,128)(2,1)}, u32[]{:S(2)}, u32[]{:S(2)}) %collective-permute-start.17) | collective-permute-done | bytes 110624 | tf_op jit(solution)/shard_map/ppermute | solution.py:357
  68.1 5.3 %shard_map.63 = bf16[16,64,256]{2,1,0:T(8,128)(2,1)} custom-call(s32[3]{0:T(128)S(1)} %pad_add_fusion.place_ref, bf16[108,512]{1,0:T(8,128)(2,1)S(1)} %reshape.42.refs_0_, bf16[108,512]{1,0:T(8,128)(2,1)} %collective-permute-done.15.refs_1_, bf16[108,512]{1,0:T(8,128)(2,1)} %collective-permute-done.16.refs_2_, ...), custom_call_target="tpu_custom_call" | custom-call | flops 1610612736 | bytes 4194304 | tf_op jit(solution)/shard_map/pallas_call | solution.py:332
  73.5 1.0 all-to-all-done.hidden_ref
  74.4 6.5 %all-to-all-start.2 = ((bf16[16,64,256]{2,1,0:T(8,128)(2,1)}), bf16[16,64,256]{2,1,0:T(8,128)(2,1)}, u32[]{:S(2)}, u32[]{:S(2)}) async-start(bf16[16,64,256]{2,1,0:T(8,128)(2,1)} %shard_map.63), calls=%async_computation.2 | async-start | bytes 1048576 | tf_op jit(solution)/shard_map/all_to_all | solution.py:377
  80.9 4.0 %shard_map.62 = (f32[108,512]{1,0:T(8,128)S(1)}, bf16[108,512]{1,0:T(8,128)(2,1)S(1)}, bf16[108,512]{1,0:T(8,128)(2,1)S(1)}, bf16[108,512]{1,0:T(8,128)(2,1)S(1)}) custom-call(s32[3]{0:T(128)S(1)} %pad_add_fusion.place_ref, bf16[16,64,256]{2,1,0:T(8,128)(2,1)S(1)} %all-to-all-done.hidden_ref, bf16[4,16,1152]{2,1,0:T(8,128)(2,1)S(1)} %bitcast.20, ...), custom_call_target="tpu_custom_call" | custom-call | flops 1610612736 | bytes 4194304 | tf_op jit(solution)/shard_map/pallas_call | solution.py:265
  84.9 0.4 collective-permute-start.11
  85.3 1.2 %collective-permute-start.10 = (bf16[108,512]{1,0:T(8,128)(2,1)S(1)}, bf16[108,512]{1,0:T(8,128)(2,1)S(1)}, u32[]{:S(2)}, u32[]{:S(2)}) collective-permute-start(bf16[108,512]{1,0:T(8,128)(2,1)S(1)} %get-tuple-element.12), channel_id=1, source_target_pairs={{0,32},{1,33},{2,34},{3,35},{4,36},{5,37},{6,38},{7,39},{8,40},{9,... | collective-permute-start | bytes 331784 | tf_op jit(solution)/shard_map/ppermute | solution.py:357
  86.5 0.6 collective-permute-start.9
  87.1 2.6 %collective-permute-done.11 = bf16[108,512]{1,0:T(8,128)(2,1)S(1)} collective-permute-done((bf16[108,512]{1,0:T(8,128)(2,1)S(1)}, bf16[108,512]{1,0:T(8,128)(2,1)S(1)}, u32[]{:S(2)}, u32[]{:S(2)}) %collective-permute-start.11) | collective-permute-done | bytes 110624 | tf_op jit(solution)/shard_map/ppermute | solution.py:357
  89.7 1.5 %collective-permute-done.10 = bf16[108,512]{1,0:T(8,128)(2,1)S(1)} collective-permute-done((bf16[108,512]{1,0:T(8,128)(2,1)S(1)}, bf16[108,512]{1,0:T(8,128)(2,1)S(1)}, u32[]{:S(2)}, u32[]{:S(2)}) %collective-permute-start.10) | collective-permute-done | bytes 110624 | tf_op jit(solution)/shard_map/ppermute | solution.py:357
  91.2 3.1 %collective-permute-done.9 = bf16[108,512]{1,0:T(8,128)(2,1)S(1)} collective-permute-done((bf16[108,512]{1,0:T(8,128)(2,1)S(1)}, bf16[108,512]{1,0:T(8,128)(2,1)S(1)}, u32[]{:S(2)}, u32[]{:S(2)}) %collective-permute-start.9) | collective-permute-done | bytes 110624 | tf_op jit(solution)/shard_map/ppermute | solution.py:357
  94.3 0.1 add_convert_fusion
  94.4 2.5 %collective-permute-start.14 = (bf16[108,512]{1,0:T(8,128)(2,1)S(1)}, bf16[108,512]{1,0:T(8,128)(2,1)S(1)}, u32[]{:S(2)}, u32[]{:S(2)}) collective-permute-start(bf16[108,512]{1,0:T(8,128)(2,1)S(1)} %add_convert_fusion), channel_id=1, source_target_pairs={{0,192},{64,0},{128,64},{192,128},{1,193},{65,1},{129,65},{193,129... | collective-permute-start | bytes 331784 | tf_op jit(solution)/shard_map/ppermute | solution.py:26
  96.9 1.7 %collective-permute-start.12 = (bf16[108,512]{1,0:T(8,128)(2,1)S(1)}, bf16[108,512]{1,0:T(8,128)(2,1)S(1)}, u32[]{:S(2)}, u32[]{:S(2)}) collective-permute-start(bf16[108,512]{1,0:T(8,128)(2,1)S(1)} %add_convert_fusion), channel_id=1, source_target_pairs={{0,128},{64,192},{128,0},{192,64},{1,129},{65,193},{129,1},{193,65... | collective-permute-start | bytes 331784 | tf_op jit(solution)/shard_map/ppermute | solution.py:26
  98.6 0.4 shard_map.64
  99.1 5.9 %collective-permute-done.13 = bf16[108,512]{1,0:T(8,128)(2,1)S(1)} collective-permute-done((bf16[108,512]{1,0:T(8,128)(2,1)S(1)}, bf16[108,512]{1,0:T(8,128)(2,1)S(1)}, u32[]{:S(2)}, u32[]{:S(2)}) %collective-permute-start.13) | collective-permute-done | bytes 110624 | tf_op jit(solution)/shard_map/ppermute | solution.py:26
  105.0 0.1 add_add_fusion
  105.0 0.7 reshape.41
  105.8 1.2 %multiply_convert_fusion = bf16[16,64,256]{2,1,0:T(8,128)(2,1)S(1)} fusion(f32[16,64,256]{2,1,0:T(8,128)S(1)} %shard_map.64, bf16[16,64,256]{2,1,0:T(8,128)(2,1)} %all-to-all-done.2), kind=kLoop, calls=%fused_computation | loop fusion | flops 786432 | bytes 2097152 | tf_op jit(solution)/shard_map/convert_element_type | solution.py:433
  107.0 0.1 reshape.43
  107.1 1.1 copy.13
  (17 shorter events, 0.2 us)
Async XLA Ops:
  13.2 8.9 %collective-permute-start.4 = (bf16[4,16,1152]{2,1,0:T(8,128)(2,1)S(1)}, bf16[4,16,1152]{2,1,0:T(8,128)(2,1)S(1)}, u32[]{:S(2)}, u32[]{:S(2)}) collective-permute-start(bf16[4,16,1152]{2,1,0:T(8,128)(2,1)S(1)} %bitcast.16), channel_id=1, source_target_pairs={{0,2},{1,3},{2,4},{3,5},{4,6},{5,7},{6,8},{7,9},{8,10},{9,11},{10,... | collective-permute-start | bytes 442376 | tf_op jit(solution)/shard_map/ppermute | solution.py:357
  14.8 10.2 %collective-permute-start.1 = (bf16[4,16,1152]{2,1,0:T(8,128)(2,1)S(1)}, bf16[4,16,1152]{2,1,0:T(8,128)(2,1)S(1)}, u32[]{:S(2)}, u32[]{:S(2)}) collective-permute-start(bf16[4,16,1152]{2,1,0:T(8,128)(2,1)S(1)} %bitcast.17), channel_id=1, source_target_pairs={{0,14},{1,15},{2,0},{3,1},{4,2},{5,3},{6,4},{7,5},{8,6},{9,7},{10,... | collective-permute-start | bytes 442376 | tf_op jit(solution)/shard_map/ppermute | solution.py:357
  22.1 5.7 %collective-permute-start.5 = (bf16[4,16,1152]{2,1,0:T(8,128)(2,1)S(1)}, bf16[4,16,1152]{2,1,0:T(8,128)(2,1)S(1)}, u32[]{:S(2)}, u32[]{:S(2)}) collective-permute-start(bf16[4,16,1152]{2,1,0:T(8,128)(2,1)S(1)} %collective-permute-done.4.refs_7_.refs_11_), channel_id=1, source_target_pairs={{0,2},{1,3},{2,4},{3,5},{4,6},{5,7},{6,8},{7,9},{8,10},{9,11},{10,... | collective-permute-start | bytes 442376 | tf_op jit(solution)/shard_map/ppermute | solution.py:357
  22.1 5.7 %copy-start = (bf16[3,3,3,128,256]{4,3,2,1,0:T(8,128)(2,1)S(1)}, bf16[3,3,3,128,256]{4,3,2,1,0:T(8,128)(2,1)}, u32[]{:S(2)}) copy-start(bf16[3,3,3,128,256]{4,3,2,1,0:T(8,128)(2,1)} %param.5) | copy-start | bytes 5308420
  25.0 8.6 %collective-permute-start.2 = (bf16[4,16,1152]{2,1,0:T(8,128)(2,1)S(1)}, bf16[4,16,1152]{2,1,0:T(8,128)(2,1)S(1)}, u32[]{:S(2)}, u32[]{:S(2)}) collective-permute-start(bf16[4,16,1152]{2,1,0:T(8,128)(2,1)S(1)} %collective-permute-done.1.refs_1_.refs_5_), channel_id=1, source_target_pairs={{0,14},{1,15},{2,0},{3,1},{4,2},{5,3},{6,4},{7,5},{8,6},{9,7},{10,... | collective-permute-start | bytes 442376 | tf_op jit(solution)/shard_map/ppermute | solution.py:357
  27.8 9.9 %collective-permute-start.6 = (bf16[4,16,1152]{2,1,0:T(8,128)(2,1)S(1)}, bf16[4,16,1152]{2,1,0:T(8,128)(2,1)S(1)}, u32[]{:S(2)}, u32[]{:S(2)}) collective-permute-start(bf16[4,16,1152]{2,1,0:T(8,128)(2,1)S(1)} %collective-permute-done.5.refs_6_.refs_10_), channel_id=1, source_target_pairs={{0,2},{1,3},{2,4},{3,5},{4,6},{5,7},{6,8},{7,9},{8,10},{9,11},{10,... | collective-permute-start | bytes 442376 | tf_op jit(solution)/shard_map/ppermute | solution.py:357
  31.0 19.0 %collective-permute-start = (bf16[4,256,256]{2,1,0:T(8,128)(2,1)S(1)}, bf16[4,256,256]{2,1,0:T(8,128)(2,1)S(1)}, u32[]{:S(2)}, u32[]{:S(2)}) collective-permute-start(bf16[4,256,256]{2,1,0:T(8,128)(2,1)S(1)} %get-tuple-element.9), channel_id=1, source_target_pairs={{0,1},{1,2},{2,3},{3,4},{4,5},{5,6},{6,7},{7,8},{8,9},{9,10},{10,1... | collective-permute-start | bytes 1572872 | tf_op jit(solution)/shard_map/ppermute | solution.py:21
  33.7 6.9 %collective-permute-start.3 = (bf16[4,16,1152]{2,1,0:T(8,128)(2,1)S(1)}, bf16[4,16,1152]{2,1,0:T(8,128)(2,1)S(1)}, u32[]{:S(2)}, u32[]{:S(2)}) collective-permute-start(bf16[4,16,1152]{2,1,0:T(8,128)(2,1)S(1)} %collective-permute-done.2.refs_2_.refs_6_), channel_id=1, source_target_pairs={{0,14},{1,15},{2,0},{3,1},{4,2},{5,3},{6,4},{7,5},{8,6},{9,7},{10,... | collective-permute-start | bytes 442376 | tf_op jit(solution)/shard_map/ppermute | solution.py:357
  37.7 9.6 %collective-permute-start.7 = (bf16[4,16,1152]{2,1,0:T(8,128)(2,1)S(1)}, bf16[4,16,1152]{2,1,0:T(8,128)(2,1)S(1)}, u32[]{:S(2)}, u32[]{:S(2)}) collective-permute-start(bf16[4,16,1152]{2,1,0:T(8,128)(2,1)S(1)} %collective-permute-done.6.refs_5_.refs_9_), channel_id=1, source_target_pairs={{0,2},{1,3},{2,4},{3,5},{4,6},{5,7},{6,8},{7,9},{8,10},{9,11},{10,... | collective-permute-start | bytes 442376 | tf_op jit(solution)/shard_map/ppermute | solution.py:357
  49.9 18.3 %collective-permute-start.8 = (bf16[8,4,16,1152]{3,2,1,0:T(8,128)(2,1)}, bf16[8,4,16,1152]{3,2,1,0:T(8,128)(2,1)}, u32[]{:S(2)}, u32[]{:S(2)}) collective-permute-start(bf16[8,4,16,1152]{3,2,1,0:T(8,128)(2,1)} %shard_map.61), channel_id=1, source_target_pairs={{0,1},{1,0},{2,3},{3,2},{4,5},{5,4},{6,7},{7,6},{8,9},{9,8},{10,11... | collective-permute-start | bytes 3538952 | tf_op jit(solution)/shard_map/ppermute | solution.py:357
  51.2 23.3 %all-to-all-start = ((bf16[16,64,256]{2,1,0:T(8,128)(2,1)}), bf16[16,64,256]{2,1,0:T(8,128)(2,1)S(1)}, u32[]{:S(2)}, u32[]{:S(2)}) async-start(bf16[16,64,256]{2,1,0:T(8,128)(2,1)} %shard_map.60), calls=%async_computation | async-start | bytes 1048576 | tf_op jit(solution)/shard_map/all_to_all | solution.py:377
  58.2 4.8 %collective-permute-start.15 = (bf16[108,512]{1,0:T(8,128)(2,1)S(1)}, bf16[108,512]{1,0:T(8,128)(2,1)}, u32[]{:S(2)}, u32[]{:S(2)}) collective-permute-start(bf16[108,512]{1,0:T(8,128)(2,1)S(1)} %reshape.42.refs_0_), channel_id=1, source_target_pairs={{0,48},{1,49},{2,50},{3,51},{4,52},{5,53},{6,54},{7,55},{8,56},{9,... | collective-permute-start | bytes 331784 | tf_op jit(solution)/shard_map/ppermute | solution.py:357
  59.1 5.9 %collective-permute-start.16 = (bf16[108,512]{1,0:T(8,128)(2,1)S(1)}, bf16[108,512]{1,0:T(8,128)(2,1)}, u32[]{:S(2)}, u32[]{:S(2)}) collective-permute-start(bf16[108,512]{1,0:T(8,128)(2,1)S(1)} %reshape.42.refs_0_), channel_id=1, source_target_pairs={{0,32},{1,33},{2,34},{3,35},{4,36},{5,37},{6,38},{7,39},{8,40},{9,... | collective-permute-start | bytes 331784 | tf_op jit(solution)/shard_map/ppermute | solution.py:357
  60.3 7.8 %collective-permute-start.17 = (bf16[108,512]{1,0:T(8,128)(2,1)S(1)}, bf16[108,512]{1,0:T(8,128)(2,1)}, u32[]{:S(2)}, u32[]{:S(2)}) collective-permute-start(bf16[108,512]{1,0:T(8,128)(2,1)S(1)} %reshape.42.refs_0_), channel_id=1, source_target_pairs={{0,16},{1,17},{2,18},{3,19},{4,20},{5,21},{6,22},{7,23},{8,24},{9,... | collective-permute-start | bytes 331784 | tf_op jit(solution)/shard_map/ppermute | solution.py:357
  74.4 31.4 %all-to-all-start.2 = ((bf16[16,64,256]{2,1,0:T(8,128)(2,1)}), bf16[16,64,256]{2,1,0:T(8,128)(2,1)}, u32[]{:S(2)}, u32[]{:S(2)}) async-start(bf16[16,64,256]{2,1,0:T(8,128)(2,1)} %shard_map.63), calls=%async_computation.2 | async-start | bytes 1048576 | tf_op jit(solution)/shard_map/all_to_all | solution.py:377
  84.9 4.7 %collective-permute-start.11 = (bf16[108,512]{1,0:T(8,128)(2,1)S(1)}, bf16[108,512]{1,0:T(8,128)(2,1)S(1)}, u32[]{:S(2)}, u32[]{:S(2)}) collective-permute-start(bf16[108,512]{1,0:T(8,128)(2,1)S(1)} %get-tuple-element.13), channel_id=1, source_target_pairs={{0,48},{1,49},{2,50},{3,51},{4,52},{5,53},{6,54},{7,55},{8,56},{9,... | collective-permute-start | bytes 331784 | tf_op jit(solution)/shard_map/ppermute | solution.py:357
  85.3 5.9 %collective-permute-start.10 = (bf16[108,512]{1,0:T(8,128)(2,1)S(1)}, bf16[108,512]{1,0:T(8,128)(2,1)S(1)}, u32[]{:S(2)}, u32[]{:S(2)}) collective-permute-start(bf16[108,512]{1,0:T(8,128)(2,1)S(1)} %get-tuple-element.12), channel_id=1, source_target_pairs={{0,32},{1,33},{2,34},{3,35},{4,36},{5,37},{6,38},{7,39},{8,40},{9,... | collective-permute-start | bytes 331784 | tf_op jit(solution)/shard_map/ppermute | solution.py:357
  86.5 7.8 %collective-permute-start.9 = (bf16[108,512]{1,0:T(8,128)(2,1)S(1)}, bf16[108,512]{1,0:T(8,128)(2,1)S(1)}, u32[]{:S(2)}, u32[]{:S(2)}) collective-permute-start(bf16[108,512]{1,0:T(8,128)(2,1)S(1)} %get-tuple-element.11), channel_id=1, source_target_pairs={{0,16},{1,17},{2,18},{3,19},{4,20},{5,21},{6,22},{7,23},{8,24},{9,... | collective-permute-start | bytes 331784 | tf_op jit(solution)/shard_map/ppermute | solution.py:357
  94.4 4.7 %collective-permute-start.14 = (bf16[108,512]{1,0:T(8,128)(2,1)S(1)}, bf16[108,512]{1,0:T(8,128)(2,1)S(1)}, u32[]{:S(2)}, u32[]{:S(2)}) collective-permute-start(bf16[108,512]{1,0:T(8,128)(2,1)S(1)} %add_convert_fusion), channel_id=1, source_target_pairs={{0,192},{64,0},{128,64},{192,128},{1,193},{65,1},{129,65},{193,129... | collective-permute-start | bytes 331784 | tf_op jit(solution)/shard_map/ppermute | solution.py:26
  96.9 8.1 %collective-permute-start.13 = (bf16[108,512]{1,0:T(8,128)(2,1)S(1)}, bf16[108,512]{1,0:T(8,128)(2,1)S(1)}, u32[]{:S(2)}, u32[]{:S(2)}) collective-permute-start(bf16[108,512]{1,0:T(8,128)(2,1)S(1)} %add_convert_fusion), channel_id=1, source_target_pairs={{0,64},{64,128},{128,192},{192,0},{1,65},{65,129},{129,193},{193,1... | collective-permute-start | bytes 331784 | tf_op jit(solution)/shard_map/ppermute | solution.py:26
  96.9 8.1 %collective-permute-start.12 = (bf16[108,512]{1,0:T(8,128)(2,1)S(1)}, bf16[108,512]{1,0:T(8,128)(2,1)S(1)}, u32[]{:S(2)}, u32[]{:S(2)}) collective-permute-start(bf16[108,512]{1,0:T(8,128)(2,1)S(1)} %add_convert_fusion), channel_id=1, source_target_pairs={{0,128},{64,192},{128,0},{192,64},{1,129},{65,193},{129,1},{193,65... | collective-permute-start | bytes 331784 | tf_op jit(solution)/shard_map/ppermute | solution.py:26

commit v8 on v7

--- a/solution.py
+++ b/solution.py
@@ -39,7 +39,7 @@
 
 ROWS, RING, CORES = 4, 8, 2
 IN_VMEM = pl.BlockSpec(memory_space=pltpu.VMEM)
-ANYWHERE = pl.BlockSpec(memory_space=pl.ANY)
+IN_HBM = pl.BlockSpec(memory_space=pltpu.HBM)
 GRANT = pltpu.CompilerParams(vmem_limit_bytes=16 * 2**20)
 
 
@@ -56,20 +56,13 @@
     return jnp.where(keep, moved, 0.0).astype(block.dtype)
 
 
-def conv_kernel(row_len, w_from, planes_from, ahead_ref, part_ref, *scratch):
-    cols_ref, w_ref, planes_ref, sems = scratch
-    copies = [
-        pltpu.make_async_copy(planes_from.at[0], planes_ref.at[0], sems.at[0]),
-        pltpu.make_async_copy(planes_from.at[1], planes_ref.at[1], sems.at[1]),
-        pltpu.make_async_copy(w_from, w_ref, sems.at[2]),
-    ]
-    for copy in copies:
-        copy.start()
+def conv_kernel(row_len, w_from, planes_ref, ahead_ref, part_ref, cols_ref, w_ref, sem):
+    copy = pltpu.make_async_copy(w_from, w_ref, sem)
+    copy.start()
     cells = planes_ref.shape[2]
     channels = planes_ref.shape[1] // 16
     tap_rows = 9 * channels
     for plane in range(2):
-        copies[plane].wait()
         for row in range(-1, 4):
             for col in range(-1, 4):
                 source = ((row % 4) * 4 + col % 4) * channels
@@ -88,7 +81,7 @@
                         phase = row_phase * 2 + col_phase
                         put = slice(phase * cells, (phase + 1) * cells)
                         cols_ref[start : start + channels, put] = block
-    copies[2].wait()
+    copy.wait()
     over_rows = (((0,), (0,)), ((), ()))
     for out_ref, weights, cols in (
         (ahead_ref, w_ref[:tap_rows, :], cols_ref[tap_rows:, :]),
@@ -108,13 +101,12 @@
             jax.ShapeDtypeStruct((4, outs, cells), jnp.bfloat16),
             jax.ShapeDtypeStruct((4, outs, cells), jnp.float32),
         ),
-        in_specs=[ANYWHERE] * 2,
+        in_specs=[IN_HBM, IN_VMEM],
         out_specs=(IN_VMEM,) * 2,
         scratch_shapes=[
             pltpu.VMEM((2 * depth // 3, 4 * cells), jnp.bfloat16),
             pltpu.VMEM(w_rows.shape, jnp.bfloat16),
-            pltpu.VMEM(planes.shape, jnp.bfloat16),
-            pltpu.SemaphoreType.DMA((3,)),
+            pltpu.SemaphoreType.DMA(()),
         ],
         compiler_params=GRANT,
         cost_estimate=pl.CostEstimate(
@@ -169,7 +161,7 @@
     return pl.pallas_call(
         pile_kernel,
         out_shape=jax.ShapeDtypeStruct(shape, blocks[0].dtype),
-        in_specs=[ANYWHERE] * len(blocks),
+        in_specs=[IN_HBM] * len(blocks),
         out_specs=IN_VMEM,
         scratch_shapes=[pltpu.SemaphoreType.DMA((len(blocks),))],
         compiler_params=GRANT,
@@ -268,7 +260,7 @@
             jax.ShapeDtypeStruct((size, outs), jnp.bfloat16 if away else jnp.float32)
             for away in range(ROWS)
         ],
-        in_specs=[pl.BlockSpec(memory_space=pltpu.SMEM), IN_VMEM] + [ANYWHERE] * (RING + 1),
+        in_specs=[pl.BlockSpec(memory_space=pltpu.SMEM), IN_VMEM] + [IN_HBM] * (RING + 1),
         out_specs=[IN_VMEM] * ROWS,
         scratch_shapes=[
             pltpu.VMEM(cot_shape, jnp.bfloat16),
@@ -332,7 +324,7 @@
     return pl.pallas_call(
         functools.partial(back_kernel, row_len),
         out_shape=jax.ShapeDtypeStruct((planes, group, cells), jnp.bfloat16),
-        in_specs=[pl.BlockSpec(memory_space=pltpu.SMEM)] + [IN_VMEM] * ROWS + [ANYWHERE] * (RING + 1),
+        in_specs=[pl.BlockSpec(memory_space=pltpu.SMEM)] + [IN_VMEM] * ROWS + [IN_HBM] * (RING + 1),
         out_specs=IN_VMEM,
         scratch_shapes=[
             pltpu.VMEM(cot_shape, jnp.bfloat16),
@@ -396,12 +388,12 @@
     parts = parts.reshape(ROWS, -1, CORES, (share + 1) * cells // CORES).transpose(0, 2, 1, 3)
     first = exchange(parts.reshape((ROWS * CORES,) + parts.shape[2:]), PILLARS)
     first = first.reshape(ROWS, -1, first.shape[2])
-    up, down = [first], [first]
-    for _ in range(3):
-        up.append(on_space(up[-1], z_by=1))
-        down.append(on_space(down[-1], z_by=-1))
-    far = on_space(up[3], z_by=1)
-    mine = down + [far] + up[:0:-1]
+    hops = {0: first}
+    for step in (1, -1, 2, -2):
+        hops[step] = on_space(first, z_by=-step)
+    for step, come in ((3, 2), (-3, -2), (4, 2)):
+        hops[step] = on_space(hops[come], z_by=come - step)
+    mine = [hops[step] for step in (0, 1, 2, 3, 4, -3, -2, -1)]
     piled = pile(mine)
     theirs = on_space(piled, core_by=1)
 

time: 109 us -> 106 us (0.972)
  blocking collectives: 11.2 us -> 0 us
  starting transfers between devices: 36.2 us -> 42.8 us
  local copies, waits for them, and re-layouts: 6.89 us -> 10.5 us
  waiting for transfers between devices: 34.8 us -> 33.6 us
    all_to_all x1 -> x0, blocking collectives: 11.2 us -> none  [exchange(): lax.all_to_all(blocks, 'space', split_axis=0, concat_axis=0, axis_index_g...]
    all_to_all x2 -> x3, starting transfers between devices: 12.6 us -> 17.8 us  [exchange(): lax.all_to_all(blocks, 'space', split_axis=0, concat_axis=0, axis_index_g...]
    unnamed x2 -> x18, local copies, waits for them, and re-layouts: 0.01 us -> 3.94 us
    ppermute x14, waiting for transfers between devices: 27.9 us -> 24.9 us  [on_space(): return lax.ppermute(block, 'space', route)]
    all_to_all x2 -> x3, waiting for transfers between devices: 0.96 us -> 2.75 us  [exchange(): lax.all_to_all(blocks, 'space', split_axis=0, concat_axis=0, axis_index_g...]
    ppermute x14, starting transfers between devices: 16.7 us -> 17.9 us  [on_space(): return lax.ppermute(block, 'space', route)]
  transfers between devices with their start and end apart: 20 -> 21, of which waited for: 11 -> 11; matrix products, arithmetic and copies ran while one was open for 4% -> 4% of each run, Pallas kernels for 15% -> 16%
where the time goes in v8:
time: 106 us
  starting transfers between devices  42.8 us (40%)
  waiting for transfers between devices  33.6 us (32%)
  Pallas kernels  16.4 us (15%)
  local copies, waits for them, and re-layouts  10.5 us (10%)
  other arithmetic  1.64 us (2%)
    ppermute x14, waiting for transfers between devices, on_space(): return lax.ppermute(block, 'space', route)  24.9 us
    ppermute x14, starting transfers between devices, on_space(): return lax.ppermute(block, 'space', route)  17.9 us
    all_to_all x3, starting transfers between devices, exchange(): lax.all_to_all(blocks, 'space', split_axis=0, concat_axis=0, axis_index_g...  17.8 us
    ppermute x3, waiting for transfers between devices, from_side(): lax.ppermute(block, axis, [(i, (i + distance) % size) for i in range(size)])  5.94 us
    pallas_call x1, Pallas kernels, back(): pl.pallas_call(functools.partial(back_kernel, row_len), out_shape=jax.Sha...  5.23 us
    ppermute x3, starting transfers between devices, from_side(): lax.ppermute(block, axis, [(i, (i + distance) % size) for i in range(size)])  4.28 us
    pallas_call x1, Pallas kernels, grad(): pl.pallas_call(functools.partial(grad_kernel, row_len), out_shape=[jax.Sh...  4.03 us
    unnamed x18, local copies, waits for them, and re-layouts  3.94 us
  transfers between devices with their start and end apart: 21, of which 11 were waited for; matrix products, arithmetic and copies ran while one was open for 4% of the time, Pallas kernels for 16%

profile of v8, /device:TPU:1, one launch (start us, length us, event | category | flops | bytes accessed | tf_op | source)
XLA Modules:
  0.0 105.6 jit_solution(12267416993312952524)
XLA Ops:
  0.6 1.0 fusion
  1.7 0.3 maximum_bitcast_fusion
  2.0 0.7 copy.12
  2.7 6.5 %all-to-all-start.1 = ((bf16[8,8,1152]{2,1,0:T(8,128)(2,1)}), bf16[8,8,1152]{2,1,0:T(8,128)(2,1)S(1)}, u32[]{:S(2)}, u32[]{:S(2)}) async-start(bf16[8,8,1152]{2,1,0:T(8,128)(2,1)} %bitcast.9), calls=%async_computation.1 | async-start | bytes 294912 | tf_op jit(solution)/shard_map/all_to_all | solution.py:369
  9.2 2.8 %copy.11 = bf16[2,16,128,256]{3,2,1,0:T(8,128)(2,1)S(1)} copy(bf16[2,16,128,256]{3,1,0,2:T(8,128)(2,1)} %bitcast.24) | data formatting | bytes 4194304 | tf_op jit(solution)/shard_map/transpose | solution.py:404
  11.9 2.7 %all-to-all-done.1 = bf16[8,8,1152]{2,1,0:T(8,128)(2,1)S(1)} async-done(((bf16[8,8,1152]{2,1,0:T(8,128)(2,1)}), bf16[8,8,1152]{2,1,0:T(8,128)(2,1)S(1)}, u32[]{:S(2)}, u32[]{:S(2)}) %all-to-all-start.1) | async-done | bytes 147488 | tf_op jit(solution)/shard_map/all_to_all | solution.py:369
  14.6 5.0 %collective-permute-start.1 = (bf16[4,16,1152]{2,1,0:T(8,128)(2,1)S(1)}, bf16[4,16,1152]{2,1,0:T(8,128)(2,1)S(1)}, u32[]{:S(2)}, u32[]{:S(2)}) collective-permute-start(bf16[4,16,1152]{2,1,0:T(8,128)(2,1)S(1)} %bitcast.16), channel_id=1, source_target_pairs={{0,14},{1,15},{2,0},{3,1},{4,2},{5,3},{6,4},{7,5},{8,6},{9,7},{10,... | collective-permute-start | bytes 442376 | tf_op jit(solution)/shard_map/ppermute | solution.py:349
  19.6 1.2 %collective-permute-start.2 = (bf16[4,16,1152]{2,1,0:T(8,128)(2,1)S(1)}, bf16[4,16,1152]{2,1,0:T(8,128)(2,1)S(1)}, u32[]{:S(2)}, u32[]{:S(2)}) collective-permute-start(bf16[4,16,1152]{2,1,0:T(8,128)(2,1)S(1)} %bitcast.17), channel_id=1, source_target_pairs={{0,12},{1,13},{2,14},{3,15},{4,0},{5,1},{6,2},{7,3},{8,4},{9,5},{1... | collective-permute-start | bytes 442376 | tf_op jit(solution)/shard_map/ppermute | solution.py:349
  20.8 1.2 %collective-permute-start.5 = (bf16[4,16,1152]{2,1,0:T(8,128)(2,1)S(1)}, bf16[4,16,1152]{2,1,0:T(8,128)(2,1)S(1)}, u32[]{:S(2)}, u32[]{:S(2)}) collective-permute-start(bf16[4,16,1152]{2,1,0:T(8,128)(2,1)S(1)} %bitcast.18), channel_id=1, source_target_pairs={{0,4},{1,5},{2,6},{3,7},{4,8},{5,9},{6,10},{7,11},{8,12},{9,13},{1... | collective-permute-start | bytes 442376 | tf_op jit(solution)/shard_map/ppermute | solution.py:349
  22.0 1.5 %copy-done.5 = bf16[3,3,3,128,256]{4,3,2,1,0:T(8,128)(2,1)S(1)} copy-done((bf16[3,3,3,128,256]{4,3,2,1,0:T(8,128)(2,1)S(1)}, bf16[3,3,3,128,256]{4,3,2,1,0:T(8,128)(2,1)}, u32[]{:S(2)}) %copy-start.5) | copy-done | bytes 1769496
  23.5 3.0 %shard_map.59 = (bf16[4,256,256]{2,1,0:T(8,128)(2,1)S(1)}, f32[4,256,256]{2,1,0:T(8,128)S(1)}) custom-call(bf16[3456,256]{1,0:T(8,128)(2,1)S(1)} %bitcast.23, bf16[2,2048,256]{2,1,0:T(8,128)(2,1)S(1)} %bitcast.15), custom_call_target="tpu_custom_call" | custom-call | flops 1811939328 | bytes 3538944 | tf_op jit(solution)/shard_map/pallas_call | solution.py:98
  26.4 2.8 %collective-permute-start = (bf16[4,256,256]{2,1,0:T(8,128)(2,1)S(1)}, bf16[4,256,256]{2,1,0:T(8,128)(2,1)S(1)}, u32[]{:S(2)}, u32[]{:S(2)}) collective-permute-start(bf16[4,256,256]{2,1,0:T(8,128)(2,1)S(1)} %get-tuple-element.9), channel_id=1, source_target_pairs={{0,1},{1,2},{2,3},{3,4},{4,5},{5,6},{6,7},{7,8},{8,9},{9,10},{10,1... | collective-permute-start | bytes 1572872 | tf_op jit(solution)/shard_map/ppermute | solution.py:21
  29.2 0.8 collective-permute-start.7
  30.1 2.8 %collective-permute-start.3 = (bf16[4,16,1152]{2,1,0:T(8,128)(2,1)S(1)}, bf16[4,16,1152]{2,1,0:T(8,128)(2,1)S(1)}, u32[]{:S(2)}, u32[]{:S(2)}) collective-permute-start(bf16[4,16,1152]{2,1,0:T(8,128)(2,1)S(1)} %collective-permute-done.2.refs_2_.refs_6_), channel_id=1, source_target_pairs={{0,14},{1,15},{2,0},{3,1},{4,2},{5,3},{6,4},{7,5},{8,6},{9,7},{10,... | collective-permute-start | bytes 442376 | tf_op jit(solution)/shard_map/ppermute | solution.py:349
  32.8 1.8 %collective-permute-start.4 = (bf16[4,16,1152]{2,1,0:T(8,128)(2,1)S(1)}, bf16[4,16,1152]{2,1,0:T(8,128)(2,1)S(1)}, u32[]{:S(2)}, u32[]{:S(2)}) collective-permute-start(bf16[4,16,1152]{2,1,0:T(8,128)(2,1)S(1)} %collective-permute-done.2.refs_2_.refs_6_), channel_id=1, source_target_pairs={{0,12},{1,13},{2,14},{3,15},{4,0},{5,1},{6,2},{7,3},{8,4},{9,5},{1... | collective-permute-start | bytes 442376 | tf_op jit(solution)/shard_map/ppermute | solution.py:349
  34.6 0.7 collective-permute-start.6
  35.4 8.5 %collective-permute-done.7.refs_7_.refs_11_ = bf16[4,16,1152]{2,1,0:T(8,128)(2,1)S(1)} collective-permute-done((bf16[4,16,1152]{2,1,0:T(8,128)(2,1)S(1)}, bf16[4,16,1152]{2,1,0:T(8,128)(2,1)S(1)}, u32[]{:S(2)}, u32[]{:S(2)}) %collective-permute-start.7) | collective-permute-done | bytes 147488 | tf_op jit(solution)/shard_map/ppermute | solution.py:349
  43.9 1.6 %collective-permute-done.6.refs_5_.refs_9_ = bf16[4,16,1152]{2,1,0:T(8,128)(2,1)S(1)} collective-permute-done((bf16[4,16,1152]{2,1,0:T(8,128)(2,1)S(1)}, bf16[4,16,1152]{2,1,0:T(8,128)(2,1)S(1)}, u32[]{:S(2)}, u32[]{:S(2)}) %collective-permute-start.6) | collective-permute-done | bytes 147488 | tf_op jit(solution)/shard_map/ppermute | solution.py:349
  45.5 2.6 %shard_map.61 = bf16[8,4,16,1152]{3,2,1,0:T(8,128)(2,1)} custom-call(bf16[4,16,1152]{2,1,0:T(8,128)(2,1)S(1)} %bitcast.20, bf16[4,16,1152]{2,1,0:T(8,128)(2,1)S(1)} %collective-permute-done.1.refs_1_.refs_5_, bf16[4,16,1152]{2,1,0:T(8,128)(2,1)S(1)} %collective-permute-done.2.refs_2_.refs_6_, ...), custom_call_target="tpu_custom_call" | custom-call | bytes 2359296 | tf_op jit(solution)/shard_map/pallas_call | solution.py:161
  48.1 0.1 collective-permute-start.8
  48.3 1.2 %shard_map.60 = bf16[16,64,256]{2,1,0:T(8,128)(2,1)} custom-call(f32[4,256,256]{2,1,0:T(8,128)S(1)} %get-tuple-element.8.part_ref, bf16[4,256,256]{2,1,0:T(8,128)(2,1)S(1)} %collective-permute-done.behind_ref), custom_call_target="tpu_custom_call" | custom-call | flops 2621440 | bytes 2097152 | tf_op jit(solution)/shard_map/pallas_call | solution.py:136
  49.4 4.0 %all-to-all-start = ((bf16[16,64,256]{2,1,0:T(8,128)(2,1)}), bf16[16,64,256]{2,1,0:T(8,128)(2,1)S(1)}, u32[]{:S(2)}, u32[]{:S(2)}) async-start(bf16[16,64,256]{2,1,0:T(8,128)(2,1)} %shard_map.60), calls=%async_computation | async-start | bytes 1048576 | tf_op jit(solution)/shard_map/all_to_all | solution.py:369
  53.5 1.0 collective-permute-start.15
  54.4 1.2 %collective-permute-start.16 = (bf16[108,512]{1,0:T(8,128)(2,1)S(1)}, bf16[108,512]{1,0:T(8,128)(2,1)S(1)}, u32[]{:S(2)}, u32[]{:S(2)}) collective-permute-start(bf16[108,512]{1,0:T(8,128)(2,1)S(1)} %reshape.42.refs_0_), channel_id=1, source_target_pairs={{0,32},{1,33},{2,34},{3,35},{4,36},{5,37},{6,38},{7,39},{8,40},{9,... | collective-permute-start | bytes 331784 | tf_op jit(solution)/shard_map/ppermute | solution.py:349
  55.7 2.4 %collective-permute-done.15.refs_1_ = bf16[108,512]{1,0:T(8,128)(2,1)S(1)} collective-permute-done((bf16[108,512]{1,0:T(8,128)(2,1)S(1)}, bf16[108,512]{1,0:T(8,128)(2,1)S(1)}, u32[]{:S(2)}, u32[]{:S(2)}) %collective-permute-start.15) | collective-permute-done | bytes 110624 | tf_op jit(solution)/shard_map/ppermute | solution.py:349
  58.1 2.1 %collective-permute-done.16.refs_2_ = bf16[108,512]{1,0:T(8,128)(2,1)S(1)} collective-permute-done((bf16[108,512]{1,0:T(8,128)(2,1)S(1)}, bf16[108,512]{1,0:T(8,128)(2,1)S(1)}, u32[]{:S(2)}, u32[]{:S(2)}) %collective-permute-start.16) | collective-permute-done | bytes 110624 | tf_op jit(solution)/shard_map/ppermute | solution.py:349
  60.3 0.6 copy-done.6
  60.9 2.6 %collective-permute-done.17.refs_3_ = bf16[108,512]{1,0:T(8,128)(2,1)} collective-permute-done((bf16[108,512]{1,0:T(8,128)(2,1)S(1)}, bf16[108,512]{1,0:T(8,128)(2,1)}, u32[]{:S(2)}, u32[]{:S(2)}) %collective-permute-start.17) | collective-permute-done | bytes 110624 | tf_op jit(solution)/shard_map/ppermute | solution.py:349
  63.5 0.9 copy-done.3
  64.4 0.9 copy-done.7
  65.3 5.2 %shard_map.63 = bf16[16,64,256]{2,1,0:T(8,128)(2,1)} custom-call(s32[3]{0:T(128)S(1)} %pad_add_fusion.place_ref, bf16[108,512]{1,0:T(8,128)(2,1)S(1)} %reshape.42.refs_0_, bf16[108,512]{1,0:T(8,128)(2,1)S(1)} %collective-permute-done.15.refs_1_, bf16[108,512]{1,0:T(8,128)(2,1)S(1)} %copy-done.7, bf16[108,512]{1,0:T(8,128)(2,1)} %collective-permute-done.17.refs_3_, ...), custom_call_target="tpu_custom_call" | custom-call | flops 1610612736 | bytes 4194304 | tf_op jit(solution)/shard_map/pallas_call | solution.py:324
  70.5 0.1 all-to-all-done.hidden_ref
  70.6 7.3 %all-to-all-start.2 = ((bf16[16,64,256]{2,1,0:T(8,128)(2,1)}), bf16[16,64,256]{2,1,0:T(8,128)(2,1)}, u32[]{:S(2)}, u32[]{:S(2)}) async-start(bf16[16,64,256]{2,1,0:T(8,128)(2,1)} %shard_map.63), calls=%async_computation.2 | async-start | bytes 1048576 | tf_op jit(solution)/shard_map/all_to_all | solution.py:369
  78.0 4.0 %shard_map.62 = (f32[108,512]{1,0:T(8,128)S(1)}, bf16[108,512]{1,0:T(8,128)(2,1)S(1)}, bf16[108,512]{1,0:T(8,128)(2,1)S(1)}, bf16[108,512]{1,0:T(8,128)(2,1)S(1)}) custom-call(s32[3]{0:T(128)S(1)} %pad_add_fusion.place_ref, bf16[16,64,256]{2,1,0:T(8,128)(2,1)S(1)} %all-to-all-done.hidden_ref, bf16[4,16,1152]{2,1,0:T(8,128)(2,1)S(1)} %bitcast.22, ...), custom_call_target="tpu_custom_call" | custom-call | flops 1610612736 | bytes 4194304 | tf_op jit(solution)/shard_map/pallas_call | solution.py:257
  82.0 0.6 collective-permute-start.11
  82.6 0.9 collective-permute-start.10
  83.6 0.6 collective-permute-start.9
  84.1 2.6 %collective-permute-done.11 = bf16[108,512]{1,0:T(8,128)(2,1)S(1)} collective-permute-done((bf16[108,512]{1,0:T(8,128)(2,1)S(1)}, bf16[108,512]{1,0:T(8,128)(2,1)S(1)}, u32[]{:S(2)}, u32[]{:S(2)}) %collective-permute-start.11) | collective-permute-done | bytes 110624 | tf_op jit(solution)/shard_map/ppermute | solution.py:349
  86.8 1.8 %collective-permute-done.10 = bf16[108,512]{1,0:T(8,128)(2,1)S(1)} collective-permute-done((bf16[108,512]{1,0:T(8,128)(2,1)S(1)}, bf16[108,512]{1,0:T(8,128)(2,1)S(1)}, u32[]{:S(2)}, u32[]{:S(2)}) %collective-permute-start.10) | collective-permute-done | bytes 110624 | tf_op jit(solution)/shard_map/ppermute | solution.py:349
  88.5 3.2 %collective-permute-done.9 = bf16[108,512]{1,0:T(8,128)(2,1)S(1)} collective-permute-done((bf16[108,512]{1,0:T(8,128)(2,1)S(1)}, bf16[108,512]{1,0:T(8,128)(2,1)S(1)}, u32[]{:S(2)}, u32[]{:S(2)}) %collective-permute-start.9) | collective-permute-done | bytes 110624 | tf_op jit(solution)/shard_map/ppermute | solution.py:349
  91.8 2.6 %collective-permute-start.14 = (bf16[108,512]{1,0:T(8,128)(2,1)S(1)}, bf16[108,512]{1,0:T(8,128)(2,1)S(1)}, u32[]{:S(2)}, u32[]{:S(2)}) collective-permute-start(bf16[108,512]{1,0:T(8,128)(2,1)S(1)} %add_convert_fusion), channel_id=1, source_target_pairs={{0,192},{64,0},{128,64},{192,128},{1,193},{65,1},{129,65},{193,129... | collective-permute-start | bytes 331784 | tf_op jit(solution)/shard_map/ppermute | solution.py:26
  94.4 1.7 %collective-permute-start.12 = (bf16[108,512]{1,0:T(8,128)(2,1)S(1)}, bf16[108,512]{1,0:T(8,128)(2,1)S(1)}, u32[]{:S(2)}, u32[]{:S(2)}) collective-permute-start(bf16[108,512]{1,0:T(8,128)(2,1)S(1)} %add_convert_fusion), channel_id=1, source_target_pairs={{0,128},{64,192},{128,0},{192,64},{1,129},{65,193},{129,1},{193,65... | collective-permute-start | bytes 331784 | tf_op jit(solution)/shard_map/ppermute | solution.py:26
  96.1 0.4 shard_map.64
  96.5 5.9 %collective-permute-done.13 = bf16[108,512]{1,0:T(8,128)(2,1)S(1)} collective-permute-done((bf16[108,512]{1,0:T(8,128)(2,1)S(1)}, bf16[108,512]{1,0:T(8,128)(2,1)S(1)}, u32[]{:S(2)}, u32[]{:S(2)}) %collective-permute-start.13) | collective-permute-done | bytes 110624 | tf_op jit(solution)/shard_map/ppermute | solution.py:26
  102.5 0.7 reshape.41
  103.3 1.2 %multiply_convert_fusion = bf16[16,64,256]{2,1,0:T(8,128)(2,1)S(1)} fusion(f32[16,64,256]{2,1,0:T(8,128)S(1)} %shard_map.64, bf16[16,64,256]{2,1,0:T(8,128)(2,1)} %all-to-all-done.2), kind=kLoop, calls=%fused_computation | loop fusion | flops 786432 | bytes 2097152 | tf_op jit(solution)/shard_map/convert_element_type | solution.py:425
  104.5 0.1 reshape.43
  104.6 1.1 %copy.13 = bf16[4,16,4,4,256]{4,3,2,1,0:T(4,128)(2,1)} copy(bf16[4,16,4,4,256]{4,2,0,3,1:T(4,128)(2,1)S(1)} %bitcast.25) | data formatting | bytes 1048576 | tf_op jit(solution)/shard_map/transpose | solution.py:426
  (34 shorter events, 0.4 us)
Async XLA Ops:
  2.7 11.9 %all-to-all-start.1 = ((bf16[8,8,1152]{2,1,0:T(8,128)(2,1)}), bf16[8,8,1152]{2,1,0:T(8,128)(2,1)S(1)}, u32[]{:S(2)}, u32[]{:S(2)}) async-start(bf16[8,8,1152]{2,1,0:T(8,128)(2,1)} %bitcast.9), calls=%async_computation.1 | async-start | bytes 294912 | tf_op jit(solution)/shard_map/all_to_all | solution.py:369
  14.6 18.2 %collective-permute-start.1 = (bf16[4,16,1152]{2,1,0:T(8,128)(2,1)S(1)}, bf16[4,16,1152]{2,1,0:T(8,128)(2,1)S(1)}, u32[]{:S(2)}, u32[]{:S(2)}) collective-permute-start(bf16[4,16,1152]{2,1,0:T(8,128)(2,1)S(1)} %bitcast.16), channel_id=1, source_target_pairs={{0,14},{1,15},{2,0},{3,1},{4,2},{5,3},{6,4},{7,5},{8,6},{9,7},{10,... | collective-permute-start | bytes 442376 | tf_op jit(solution)/shard_map/ppermute | solution.py:349
  19.6 10.4 %collective-permute-start.2 = (bf16[4,16,1152]{2,1,0:T(8,128)(2,1)S(1)}, bf16[4,16,1152]{2,1,0:T(8,128)(2,1)S(1)}, u32[]{:S(2)}, u32[]{:S(2)}) collective-permute-start(bf16[4,16,1152]{2,1,0:T(8,128)(2,1)S(1)} %bitcast.17), channel_id=1, source_target_pairs={{0,12},{1,13},{2,14},{3,15},{4,0},{5,1},{6,2},{7,3},{8,4},{9,5},{1... | collective-permute-start | bytes 442376 | tf_op jit(solution)/shard_map/ppermute | solution.py:349
  20.8 13.8 %collective-permute-start.5 = (bf16[4,16,1152]{2,1,0:T(8,128)(2,1)S(1)}, bf16[4,16,1152]{2,1,0:T(8,128)(2,1)S(1)}, u32[]{:S(2)}, u32[]{:S(2)}) collective-permute-start(bf16[4,16,1152]{2,1,0:T(8,128)(2,1)S(1)} %bitcast.18), channel_id=1, source_target_pairs={{0,4},{1,5},{2,6},{3,7},{4,8},{5,9},{6,10},{7,11},{8,12},{9,13},{1... | collective-permute-start | bytes 442376 | tf_op jit(solution)/shard_map/ppermute | solution.py:349
  22.0 1.5 %copy-start.5 = (bf16[3,3,3,128,256]{4,3,2,1,0:T(8,128)(2,1)S(1)}, bf16[3,3,3,128,256]{4,3,2,1,0:T(8,128)(2,1)}, u32[]{:S(2)}) copy-start(bf16[3,3,3,128,256]{4,3,2,1,0:T(8,128)(2,1)} %param.5) | copy-start | bytes 5308420
  26.4 21.8 %collective-permute-start = (bf16[4,256,256]{2,1,0:T(8,128)(2,1)S(1)}, bf16[4,256,256]{2,1,0:T(8,128)(2,1)S(1)}, u32[]{:S(2)}, u32[]{:S(2)}) collective-permute-start(bf16[4,256,256]{2,1,0:T(8,128)(2,1)S(1)} %get-tuple-element.9), channel_id=1, source_target_pairs={{0,1},{1,2},{2,3},{3,4},{4,5},{5,6},{6,7},{7,8},{8,9},{9,10},{10,1... | collective-permute-start | bytes 1572872 | tf_op jit(solution)/shard_map/ppermute | solution.py:21
  29.2 14.7 %collective-permute-start.7 = (bf16[4,16,1152]{2,1,0:T(8,128)(2,1)S(1)}, bf16[4,16,1152]{2,1,0:T(8,128)(2,1)S(1)}, u32[]{:S(2)}, u32[]{:S(2)}) collective-permute-start(bf16[4,16,1152]{2,1,0:T(8,128)(2,1)S(1)} %bitcast.19), channel_id=1, source_target_pairs={{0,2},{1,3},{2,4},{3,5},{4,6},{5,7},{6,8},{7,9},{8,10},{9,11},{10,... | collective-permute-start | bytes 442376 | tf_op jit(solution)/shard_map/ppermute | solution.py:349
  30.1 18.2 %copy-start = (bf16[4,16,1152]{2,1,0:T(8,128)(2,1)}, bf16[4,16,1152]{2,1,0:T(8,128)(2,1)S(1)}, u32[]{:S(2)}) copy-start(bf16[4,16,1152]{2,1,0:T(8,128)(2,1)S(1)} %collective-permute-done.2.refs_2_.refs_6_) | copy-start | bytes 442372
  30.1 13.9 %collective-permute-start.3 = (bf16[4,16,1152]{2,1,0:T(8,128)(2,1)S(1)}, bf16[4,16,1152]{2,1,0:T(8,128)(2,1)S(1)}, u32[]{:S(2)}, u32[]{:S(2)}) collective-permute-start(bf16[4,16,1152]{2,1,0:T(8,128)(2,1)S(1)} %collective-permute-done.2.refs_2_.refs_6_), channel_id=1, source_target_pairs={{0,14},{1,15},{2,0},{3,1},{4,2},{5,3},{6,4},{7,5},{8,6},{9,7},{10,... | collective-permute-start | bytes 442376 | tf_op jit(solution)/shard_map/ppermute | solution.py:349
  32.8 11.1 %collective-permute-start.4 = (bf16[4,16,1152]{2,1,0:T(8,128)(2,1)S(1)}, bf16[4,16,1152]{2,1,0:T(8,128)(2,1)S(1)}, u32[]{:S(2)}, u32[]{:S(2)}) collective-permute-start(bf16[4,16,1152]{2,1,0:T(8,128)(2,1)S(1)} %collective-permute-done.2.refs_2_.refs_6_), channel_id=1, source_target_pairs={{0,12},{1,13},{2,14},{3,15},{4,0},{5,1},{6,2},{7,3},{8,4},{9,5},{1... | collective-permute-start | bytes 442376 | tf_op jit(solution)/shard_map/ppermute | solution.py:349
  34.6 13.6 %copy-start.2 = (bf16[4,16,1152]{2,1,0:T(8,128)(2,1)}, bf16[4,16,1152]{2,1,0:T(8,128)(2,1)S(1)}, u32[]{:S(2)}) copy-start(bf16[4,16,1152]{2,1,0:T(8,128)(2,1)S(1)} %collective-permute-done.5.refs_6_.refs_10_) | copy-start | bytes 442372
  34.6 10.9 %collective-permute-start.6 = (bf16[4,16,1152]{2,1,0:T(8,128)(2,1)S(1)}, bf16[4,16,1152]{2,1,0:T(8,128)(2,1)S(1)}, u32[]{:S(2)}, u32[]{:S(2)}) collective-permute-start(bf16[4,16,1152]{2,1,0:T(8,128)(2,1)S(1)} %collective-permute-done.5.refs_6_.refs_10_), channel_id=1, source_target_pairs={{0,2},{1,3},{2,4},{3,5},{4,6},{5,7},{6,8},{7,9},{8,10},{9,11},{10,... | collective-permute-start | bytes 442376 | tf_op jit(solution)/shard_map/ppermute | solution.py:349
  48.1 5.3 %copy-start.8 = (bf16[3,3,3,4,512]{4,3,2,1,0:T(4,128)(2,1)S(1)}, bf16[3,3,3,4,512]{4,3,2,1,0:T(4,128)(2,1)}, u32[]{:S(2)}) copy-start(bf16[3,3,3,4,512]{4,3,2,1,0:T(4,128)(2,1)} %param.6) | copy-start | bytes 331780
  48.1 15.3 %collective-permute-start.8 = (bf16[8,4,16,1152]{3,2,1,0:T(8,128)(2,1)}, bf16[8,4,16,1152]{3,2,1,0:T(8,128)(2,1)}, u32[]{:S(2)}, u32[]{:S(2)}) collective-permute-start(bf16[8,4,16,1152]{3,2,1,0:T(8,128)(2,1)} %shard_map.61), channel_id=1, source_target_pairs={{0,1},{1,0},{2,3},{3,2},{4,5},{5,4},{6,7},{7,6},{8,9},{9,8},{10,11... | collective-permute-start | bytes 3538952 | tf_op jit(solution)/shard_map/ppermute | solution.py:349
  48.3 15.2 %copy-start.1 = (bf16[4,16,1152]{2,1,0:T(8,128)(2,1)S(1)}, bf16[4,16,1152]{2,1,0:T(8,128)(2,1)}, u32[]{:S(2)}) copy-start(bf16[4,16,1152]{2,1,0:T(8,128)(2,1)} %copy-done) | copy-start | bytes 442372
  49.4 21.2 %all-to-all-start = ((bf16[16,64,256]{2,1,0:T(8,128)(2,1)}), bf16[16,64,256]{2,1,0:T(8,128)(2,1)S(1)}, u32[]{:S(2)}, u32[]{:S(2)}) async-start(bf16[16,64,256]{2,1,0:T(8,128)(2,1)} %shard_map.60), calls=%async_computation | async-start | bytes 1048576 | tf_op jit(solution)/shard_map/all_to_all | solution.py:369
  53.5 4.7 %collective-permute-start.15 = (bf16[108,512]{1,0:T(8,128)(2,1)S(1)}, bf16[108,512]{1,0:T(8,128)(2,1)S(1)}, u32[]{:S(2)}, u32[]{:S(2)}) collective-permute-start(bf16[108,512]{1,0:T(8,128)(2,1)S(1)} %reshape.42.refs_0_), channel_id=1, source_target_pairs={{0,48},{1,49},{2,50},{3,51},{4,52},{5,53},{6,54},{7,55},{8,56},{9,... | collective-permute-start | bytes 331784 | tf_op jit(solution)/shard_map/ppermute | solution.py:349
  54.4 5.8 %collective-permute-start.16 = (bf16[108,512]{1,0:T(8,128)(2,1)S(1)}, bf16[108,512]{1,0:T(8,128)(2,1)S(1)}, u32[]{:S(2)}, u32[]{:S(2)}) collective-permute-start(bf16[108,512]{1,0:T(8,128)(2,1)S(1)} %reshape.42.refs_0_), channel_id=1, source_target_pairs={{0,32},{1,33},{2,34},{3,35},{4,36},{5,37},{6,38},{7,39},{8,40},{9,... | collective-permute-start | bytes 331784 | tf_op jit(solution)/shard_map/ppermute | solution.py:349
  55.6 7.9 %collective-permute-start.17 = (bf16[108,512]{1,0:T(8,128)(2,1)S(1)}, bf16[108,512]{1,0:T(8,128)(2,1)}, u32[]{:S(2)}, u32[]{:S(2)}) collective-permute-start(bf16[108,512]{1,0:T(8,128)(2,1)S(1)} %reshape.42.refs_0_), channel_id=1, source_target_pairs={{0,16},{1,17},{2,18},{3,19},{4,20},{5,21},{6,22},{7,23},{8,24},{9,... | collective-permute-start | bytes 331784 | tf_op jit(solution)/shard_map/ppermute | solution.py:349
  60.3 0.6 copy-start.6
  63.5 0.9 copy-start.3
  64.4 0.9 copy-start.7
  65.3 12.7 %copy-start.4 = (bf16[4,16,1152]{2,1,0:T(8,128)(2,1)S(1)}, bf16[4,16,1152]{2,1,0:T(8,128)(2,1)}, u32[]{:S(2)}) copy-start(bf16[4,16,1152]{2,1,0:T(8,128)(2,1)} %copy-done.2) | copy-start | bytes 442372
  70.6 32.6 %all-to-all-start.2 = ((bf16[16,64,256]{2,1,0:T(8,128)(2,1)}), bf16[16,64,256]{2,1,0:T(8,128)(2,1)}, u32[]{:S(2)}, u32[]{:S(2)}) async-start(bf16[16,64,256]{2,1,0:T(8,128)(2,1)} %shard_map.63), calls=%async_computation.2 | async-start | bytes 1048576 | tf_op jit(solution)/shard_map/all_to_all | solution.py:369
  82.0 4.7 %collective-permute-start.11 = (bf16[108,512]{1,0:T(8,128)(2,1)S(1)}, bf16[108,512]{1,0:T(8,128)(2,1)S(1)}, u32[]{:S(2)}, u32[]{:S(2)}) collective-permute-start(bf16[108,512]{1,0:T(8,128)(2,1)S(1)} %get-tuple-element.13), channel_id=1, source_target_pairs={{0,48},{1,49},{2,50},{3,51},{4,52},{5,53},{6,54},{7,55},{8,56},{9,... | collective-permute-start | bytes 331784 | tf_op jit(solution)/shard_map/ppermute | solution.py:349
  82.6 5.9 %collective-permute-start.10 = (bf16[108,512]{1,0:T(8,128)(2,1)S(1)}, bf16[108,512]{1,0:T(8,128)(2,1)S(1)}, u32[]{:S(2)}, u32[]{:S(2)}) collective-permute-start(bf16[108,512]{1,0:T(8,128)(2,1)S(1)} %get-tuple-element.12), channel_id=1, source_target_pairs={{0,32},{1,33},{2,34},{3,35},{4,36},{5,37},{6,38},{7,39},{8,40},{9,... | collective-permute-start | bytes 331784 | tf_op jit(solution)/shard_map/ppermute | solution.py:349
  83.6 8.2 %collective-permute-start.9 = (bf16[108,512]{1,0:T(8,128)(2,1)S(1)}, bf16[108,512]{1,0:T(8,128)(2,1)S(1)}, u32[]{:S(2)}, u32[]{:S(2)}) collective-permute-start(bf16[108,512]{1,0:T(8,128)(2,1)S(1)} %get-tuple-element.11), channel_id=1, source_target_pairs={{0,16},{1,17},{2,18},{3,19},{4,20},{5,21},{6,22},{7,23},{8,24},{9,... | collective-permute-start | bytes 331784 | tf_op jit(solution)/shard_map/ppermute | solution.py:349
  91.8 4.7 %collective-permute-start.14 = (bf16[108,512]{1,0:T(8,128)(2,1)S(1)}, bf16[108,512]{1,0:T(8,128)(2,1)S(1)}, u32[]{:S(2)}, u32[]{:S(2)}) collective-permute-start(bf16[108,512]{1,0:T(8,128)(2,1)S(1)} %add_convert_fusion), channel_id=1, source_target_pairs={{0,192},{64,0},{128,64},{192,128},{1,193},{65,1},{129,65},{193,129... | collective-permute-start | bytes 331784 | tf_op jit(solution)/shard_map/ppermute | solution.py:26
  94.4 8.1 %collective-permute-start.13 = (bf16[108,512]{1,0:T(8,128)(2,1)S(1)}, bf16[108,512]{1,0:T(8,128)(2,1)S(1)}, u32[]{:S(2)}, u32[]{:S(2)}) collective-permute-start(bf16[108,512]{1,0:T(8,128)(2,1)S(1)} %add_convert_fusion), channel_id=1, source_target_pairs={{0,64},{64,128},{128,192},{192,0},{1,65},{65,129},{129,193},{193,1... | collective-permute-start | bytes 331784 | tf_op jit(solution)/shard_map/ppermute | solution.py:26
  94.4 8.1 %collective-permute-start.12 = (bf16[108,512]{1,0:T(8,128)(2,1)S(1)}, bf16[108,512]{1,0:T(8,128)(2,1)S(1)}, u32[]{:S(2)}, u32[]{:S(2)}) collective-permute-start(bf16[108,512]{1,0:T(8,128)(2,1)S(1)} %add_convert_fusion), channel_id=1, source_target_pairs={{0,128},{64,192},{128,0},{192,64},{1,129},{65,193},{129,1},{193,65... | collective-permute-start | bytes 331784 | tf_op jit(solution)/shard_map/ppermute | solution.py:26

commit v9 on v8

--- a/solution.py
+++ b/solution.py
@@ -276,29 +276,42 @@
     )(place, hidden, *mine, theirs)
 
 
-def back_kernel(row_len, place_ref, *refs):
-    w_refs, mine, theirs_ref = refs[:ROWS], refs[ROWS : ROWS + RING], refs[ROWS + RING]
-    out_ref, cot_ref, sems, rows_ref, moves_ref = refs[ROWS + RING + 1 :]
-    planes, group, cells = out_ref.shape
-    row_count = ROWS
-    y = place_ref[0]
-    copies = cot_copies(place_ref, mine, theirs_ref, cot_ref, sems)
-    for copy in copies:
-        copy.start()
-
+def moves_kernel(place_ref, *refs):
+    w_refs, (moves_ref, rows_ref) = refs[:-2], refs[-2:]
     for away, w_ref in enumerate(w_refs):
-        rows_ref[lax.rem(y + away, row_count)] = w_ref[...].astype(jnp.float32)
-    block = group // 4
-    own = block // row_count
-    size = 4 * group
+        rows_ref[lax.rem(place_ref[0] + away, ROWS)] = w_ref[...].astype(jnp.float32)
+    own = w_refs[0].shape[0] // 27
+    block = ROWS * own
+    group = 4 * block
     moves_ref[...] = jnp.zeros_like(moves_ref)
     for tap in range(27):
         depth_tap, row_tap, col_tap = tap // 9, tap // 3 % 3, tap % 3
-        at = depth_tap * size + (2 * int(row_tap == 0) + int(col_tap == 0)) * group
+        at = (4 * depth_tap + 2 * int(row_tap == 0) + int(col_tap == 0)) * group
         at += (2 * int(row_tap != 1) + int(col_tap != 1)) * block
-        pieces = [rows_ref[row, tap * own : (tap + 1) * own, :] for row in range(row_count)]
+        pieces = [rows_ref[row, tap * own : (tap + 1) * own, :] for row in range(ROWS)]
         moves_ref[at : at + block, :] = jnp.concatenate(pieces, 0).astype(moves_ref.dtype)
 
+
+def moves_of(place, w_rel):
+    size, outs = w_rel[0].shape
+    return pl.pallas_call(
+        moves_kernel,
+        out_shape=jax.ShapeDtypeStruct((48 * ROWS * size // 27, outs), jnp.bfloat16),
+        in_specs=[pl.BlockSpec(memory_space=pltpu.SMEM)] + [IN_VMEM] * ROWS,
+        out_specs=IN_VMEM,
+        scratch_shapes=[pltpu.VMEM((ROWS, size, outs), jnp.float32)],
+        compiler_params=GRANT,
+        cost_estimate=pl.CostEstimate(flops=0, bytes_accessed=2**20, transcendentals=0),
+    )(place, *w_rel)
+
+
+def back_kernel(row_len, place_ref, moves_ref, *refs):
+    mine, theirs_ref, (out_ref, cot_ref, sems) = refs[:RING], refs[RING], refs[RING + 1 :]
+    planes, group, cells = out_ref.shape
+    size = 4 * group
+    copies = cot_copies(place_ref, mine, theirs_ref, cot_ref, sems)
+    for copy in copies:
+        copy.start()
     for copy in copies:
         copy.wait()
 
@@ -316,27 +329,25 @@
         out_ref[2 * s + 1] = gather_back(odd, row_len).astype(out_ref.dtype)
 
 
-def back(place, w_rel, mine, theirs, planes, row_len):
-    size, outs = w_rel[0].shape
-    group = 4 * ROWS * size // 27
+def back(place, moves, mine, theirs, planes, row_len):
+    rows, outs = moves.shape
+    group = rows // 12
     cot_shape = mine[0].shape[:1] + (RING,) + mine[0].shape[1:2] + (2 * mine[0].shape[2],)
     cells = cot_shape[3] // (planes // 2 + 1)
     return pl.pallas_call(
         functools.partial(back_kernel, row_len),
         out_shape=jax.ShapeDtypeStruct((planes, group, cells), jnp.bfloat16),
-        in_specs=[pl.BlockSpec(memory_space=pltpu.SMEM)] + [IN_VMEM] * ROWS + [IN_HBM] * (RING + 1),
+        in_specs=[pl.BlockSpec(memory_space=pltpu.SMEM), IN_VMEM] + [IN_HBM] * (RING + 1),
         out_specs=IN_VMEM,
         scratch_shapes=[
             pltpu.VMEM(cot_shape, jnp.bfloat16),
             pltpu.SemaphoreType.DMA((2 * RING,)),
-            pltpu.VMEM((ROWS, size, outs), jnp.float32),
-            pltpu.VMEM((12 * group, outs), jnp.bfloat16),
         ],
         compiler_params=GRANT,
         cost_estimate=pl.CostEstimate(
             flops=12 * group * outs * planes * cells, bytes_accessed=2**22, transcendentals=0
         ),
-    )(place, *w_rel, *mine, theirs)
+    )(place, moves, *mine, theirs)
 
 
 def on_space(block, y_by=0, z_by=0, core_by=0):
@@ -409,7 +420,8 @@
     slopes = pointwise(slope_of, part, behind, group, jnp.float32)
     by_plane = exchange(hidden, SLABS)
 
-    back_terms = back(place, w_rel, mine, theirs, group, row_len)
+    moves = moves_of(place, w_rel)
+    back_terms = back(place, moves, mine, theirs, group, row_len)
     hidden_grad = exchange(back_terms, SLABS)
 
     partial, *others = grad(place, by_plane, mine, theirs, row_len)
@@ -424,7 +436,8 @@
 
     pre_grad = (hidden_grad.astype(jnp.float32) * slopes).astype(jnp.bfloat16)
     pre_grad = pre_grad.reshape(group, 4, ROWS, own, cells).transpose(2, 0, 3, 1, 4)
-    return (grad_second, pre_grad.reshape(1, outs, 1, 4, cells))
+    pre_grad = pre_grad.reshape(1, outs, 1, 4, cells)
+    return (grad_second, pre_grad)
 
 
 def solution(mesh):

time: 106 us -> 105 us (level)
  local copies, waits for them, and re-layouts: 10.5 us -> 8.02 us
  waiting for transfers between devices: 33.6 us -> 34.8 us
    unnamed x18 -> x12, local copies, waits for them, and re-layouts: 3.94 us -> 1.5 us
    pallas_call x0 -> x1, Pallas kernels: none -> 1.16 us  [moves_of(): pl.pallas_call(moves_kernel, out_shape=jax.ShapeDtypeStruct((48 * ROWS *...]
where the time goes in v9:
time: 105 us; the launch traced here: 104 us
  starting transfers between devices  41.9 us (40%)
  waiting for transfers between devices  34.8 us (33%)
  Pallas kernels  17.2 us (16%)
  local copies, waits for them, and re-layouts  8.02 us (8%)
  other arithmetic  1.64 us (2%)
    ppermute x14, waiting for transfers between devices, on_space(): return lax.ppermute(block, 'space', route)  25.1 us
    ppermute x14, starting transfers between devices, on_space(): return lax.ppermute(block, 'space', route)  17.9 us
    all_to_all x3, starting transfers between devices, exchange(): lax.all_to_all(blocks, 'space', split_axis=0, concat_axis=0, axis_index_g...  17 us
    ppermute x3, waiting for transfers between devices, from_side(): lax.ppermute(block, axis, [(i, (i + distance) % size) for i in range(size)])  5.91 us
    pallas_call x1, Pallas kernels, back(): pl.pallas_call(functools.partial(back_kernel, row_len), out_shape=jax.Sha...  4.86 us
    ppermute x3, starting transfers between devices, from_side(): lax.ppermute(block, axis, [(i, (i + distance) % size) for i in range(size)])  4.28 us
    pallas_call x1, Pallas kernels, grad(): pl.pallas_call(functools.partial(grad_kernel, row_len), out_shape=[jax.Sh...  4 us
    all_to_all x3, waiting for transfers between devices, exchange(): lax.all_to_all(blocks, 'space', split_axis=0, concat_axis=0, axis_index_g...  3.75 us
  transfers between devices with their start and end apart: 21, of which 11 were waited for; matrix products, arithmetic and copies ran while one was open for 4% of the time, Pallas kernels for 16%

profile of v9, /device:TPU:1, one launch (start us, length us, event | category | flops | bytes accessed | tf_op | source)
XLA Modules:
  0.0 104.4 jit_solution(5629394292559621221)
XLA Ops:
  0.6 1.0 fusion
  1.7 0.3 maximum_bitcast_fusion
  2.0 0.7 copy.12
  2.7 6.5 %all-to-all-start.1 = ((bf16[8,8,1152]{2,1,0:T(8,128)(2,1)}), bf16[8,8,1152]{2,1,0:T(8,128)(2,1)S(1)}, u32[]{:S(2)}, u32[]{:S(2)}) async-start(bf16[8,8,1152]{2,1,0:T(8,128)(2,1)} %bitcast.9), calls=%async_computation.1 | async-start | bytes 294912 | tf_op jit(solution)/shard_map/all_to_all | solution.py:380
  9.2 2.8 %copy.11 = bf16[2,16,128,256]{3,2,1,0:T(8,128)(2,1)S(1)} copy(bf16[2,16,128,256]{3,1,0,2:T(8,128)(2,1)} %bitcast.24) | data formatting | bytes 4194304 | tf_op jit(solution)/shard_map/transpose | solution.py:415
  11.9 2.7 %all-to-all-done.1 = bf16[8,8,1152]{2,1,0:T(8,128)(2,1)S(1)} async-done(((bf16[8,8,1152]{2,1,0:T(8,128)(2,1)}), bf16[8,8,1152]{2,1,0:T(8,128)(2,1)S(1)}, u32[]{:S(2)}, u32[]{:S(2)}) %all-to-all-start.1) | async-done | bytes 147488 | tf_op jit(solution)/shard_map/all_to_all | solution.py:380
  14.6 5.0 %collective-permute-start.1 = (bf16[4,16,1152]{2,1,0:T(8,128)(2,1)S(1)}, bf16[4,16,1152]{2,1,0:T(8,128)(2,1)S(1)}, u32[]{:S(2)}, u32[]{:S(2)}) collective-permute-start(bf16[4,16,1152]{2,1,0:T(8,128)(2,1)S(1)} %bitcast.16), channel_id=1, source_target_pairs={{0,14},{1,15},{2,0},{3,1},{4,2},{5,3},{6,4},{7,5},{8,6},{9,7},{10,... | collective-permute-start | bytes 442376 | tf_op jit(solution)/shard_map/ppermute | solution.py:360
  19.6 1.2 %collective-permute-start.2 = (bf16[4,16,1152]{2,1,0:T(8,128)(2,1)S(1)}, bf16[4,16,1152]{2,1,0:T(8,128)(2,1)S(1)}, u32[]{:S(2)}, u32[]{:S(2)}) collective-permute-start(bf16[4,16,1152]{2,1,0:T(8,128)(2,1)S(1)} %bitcast.17), channel_id=1, source_target_pairs={{0,12},{1,13},{2,14},{3,15},{4,0},{5,1},{6,2},{7,3},{8,4},{9,5},{1... | collective-permute-start | bytes 442376 | tf_op jit(solution)/shard_map/ppermute | solution.py:360
  20.8 1.2 %collective-permute-start.5 = (bf16[4,16,1152]{2,1,0:T(8,128)(2,1)S(1)}, bf16[4,16,1152]{2,1,0:T(8,128)(2,1)S(1)}, u32[]{:S(2)}, u32[]{:S(2)}) collective-permute-start(bf16[4,16,1152]{2,1,0:T(8,128)(2,1)S(1)} %bitcast.18), channel_id=1, source_target_pairs={{0,4},{1,5},{2,6},{3,7},{4,8},{5,9},{6,10},{7,11},{8,12},{9,13},{1... | collective-permute-start | bytes 442376 | tf_op jit(solution)/shard_map/ppermute | solution.py:360
  22.0 1.5 %copy-done.4 = bf16[3,3,3,128,256]{4,3,2,1,0:T(8,128)(2,1)S(1)} copy-done((bf16[3,3,3,128,256]{4,3,2,1,0:T(8,128)(2,1)S(1)}, bf16[3,3,3,128,256]{4,3,2,1,0:T(8,128)(2,1)}, u32[]{:S(2)}) %copy-start.4) | copy-done | bytes 1769496
  23.5 3.0 %shard_map.59 = (bf16[4,256,256]{2,1,0:T(8,128)(2,1)S(1)}, f32[4,256,256]{2,1,0:T(8,128)S(1)}) custom-call(bf16[3456,256]{1,0:T(8,128)(2,1)S(1)} %bitcast.23, bf16[2,2048,256]{2,1,0:T(8,128)(2,1)S(1)} %bitcast.15), custom_call_target="tpu_custom_call" | custom-call | flops 1811939328 | bytes 3538944 | tf_op jit(solution)/shard_map/pallas_call | solution.py:98
  26.4 2.8 %collective-permute-start = (bf16[4,256,256]{2,1,0:T(8,128)(2,1)S(1)}, bf16[4,256,256]{2,1,0:T(8,128)(2,1)S(1)}, u32[]{:S(2)}, u32[]{:S(2)}) collective-permute-start(bf16[4,256,256]{2,1,0:T(8,128)(2,1)S(1)} %get-tuple-element.9), channel_id=1, source_target_pairs={{0,1},{1,2},{2,3},{3,4},{4,5},{5,6},{6,7},{7,8},{8,9},{9,10},{10,1... | collective-permute-start | bytes 1572872 | tf_op jit(solution)/shard_map/ppermute | solution.py:21
  29.2 0.8 collective-permute-start.7
  30.1 2.8 %collective-permute-start.3 = (bf16[4,16,1152]{2,1,0:T(8,128)(2,1)S(1)}, bf16[4,16,1152]{2,1,0:T(8,128)(2,1)S(1)}, u32[]{:S(2)}, u32[]{:S(2)}) collective-permute-start(bf16[4,16,1152]{2,1,0:T(8,128)(2,1)S(1)} %collective-permute-done.2.refs_2_), channel_id=1, source_target_pairs={{0,14},{1,15},{2,0},{3,1},{4,2},{5,3},{6,4},{7,5},{8,6},{9,7},{10,... | collective-permute-start | bytes 442376 | tf_op jit(solution)/shard_map/ppermute | solution.py:360
  32.8 1.8 %collective-permute-start.4 = (bf16[4,16,1152]{2,1,0:T(8,128)(2,1)S(1)}, bf16[4,16,1152]{2,1,0:T(8,128)(2,1)S(1)}, u32[]{:S(2)}, u32[]{:S(2)}) collective-permute-start(bf16[4,16,1152]{2,1,0:T(8,128)(2,1)S(1)} %collective-permute-done.2.refs_2_), channel_id=1, source_target_pairs={{0,12},{1,13},{2,14},{3,15},{4,0},{5,1},{6,2},{7,3},{8,4},{9,5},{1... | collective-permute-start | bytes 442376 | tf_op jit(solution)/shard_map/ppermute | solution.py:360
  34.6 0.7 collective-permute-start.6
  35.4 8.5 %collective-permute-done.7.refs_7_ = bf16[4,16,1152]{2,1,0:T(8,128)(2,1)S(1)} collective-permute-done((bf16[4,16,1152]{2,1,0:T(8,128)(2,1)S(1)}, bf16[4,16,1152]{2,1,0:T(8,128)(2,1)S(1)}, u32[]{:S(2)}, u32[]{:S(2)}) %collective-permute-start.7) | collective-permute-done | bytes 147488 | tf_op jit(solution)/shard_map/ppermute | solution.py:360
  43.9 1.6 %collective-permute-done.6.refs_5_ = bf16[4,16,1152]{2,1,0:T(8,128)(2,1)S(1)} collective-permute-done((bf16[4,16,1152]{2,1,0:T(8,128)(2,1)S(1)}, bf16[4,16,1152]{2,1,0:T(8,128)(2,1)S(1)}, u32[]{:S(2)}, u32[]{:S(2)}) %collective-permute-start.6) | collective-permute-done | bytes 147488 | tf_op jit(solution)/shard_map/ppermute | solution.py:360
  45.5 2.6 %shard_map.61 = bf16[8,4,16,1152]{3,2,1,0:T(8,128)(2,1)} custom-call(bf16[4,16,1152]{2,1,0:T(8,128)(2,1)S(1)} %bitcast.20, bf16[4,16,1152]{2,1,0:T(8,128)(2,1)S(1)} %collective-permute-done.1.refs_1_, bf16[4,16,1152]{2,1,0:T(8,128)(2,1)S(1)} %collective-permute-done.2.refs_2_, bf16[4,16,1152]{2,1,0:T(8,128)(2,1)S(1)} %collective-permute-done.3.refs_3_, ...), custom_call_target="tpu_custom_call" | custom-call | bytes 2359296 | tf_op jit(solution)/shard_map/pallas_call | solution.py:161
  48.1 0.1 collective-permute-start.8
  48.3 1.2 %shard_map.60 = bf16[16,64,256]{2,1,0:T(8,128)(2,1)} custom-call(f32[4,256,256]{2,1,0:T(8,128)S(1)} %get-tuple-element.8.part_ref, bf16[4,256,256]{2,1,0:T(8,128)(2,1)S(1)} %collective-permute-done.behind_ref), custom_call_target="tpu_custom_call" | custom-call | flops 2621440 | bytes 2097152 | tf_op jit(solution)/shard_map/pallas_call | solution.py:136
  49.4 4.1 %all-to-all-start = ((bf16[16,64,256]{2,1,0:T(8,128)(2,1)}), bf16[16,64,256]{2,1,0:T(8,128)(2,1)S(1)}, u32[]{:S(2)}, u32[]{:S(2)}) async-start(bf16[16,64,256]{2,1,0:T(8,128)(2,1)} %shard_map.60), calls=%async_computation | async-start | bytes 1048576 | tf_op jit(solution)/shard_map/all_to_all | solution.py:380
  53.6 1.0 collective-permute-start.15
  54.6 1.2 %collective-permute-start.16 = (bf16[108,512]{1,0:T(8,128)(2,1)S(1)}, bf16[108,512]{1,0:T(8,128)(2,1)}, u32[]{:S(2)}, u32[]{:S(2)}) collective-permute-start(bf16[108,512]{1,0:T(8,128)(2,1)S(1)} %reshape.42.refs_0_), channel_id=1, source_target_pairs={{0,32},{1,33},{2,34},{3,35},{4,36},{5,37},{6,38},{7,39},{8,40},{9,... | collective-permute-start | bytes 331784 | tf_op jit(solution)/shard_map/ppermute | solution.py:360
  55.8 0.1 pad_add_fusion.place_ref
  55.8 2.4 %collective-permute-done.15.refs_1_ = bf16[108,512]{1,0:T(8,128)(2,1)S(1)} collective-permute-done((bf16[108,512]{1,0:T(8,128)(2,1)S(1)}, bf16[108,512]{1,0:T(8,128)(2,1)S(1)}, u32[]{:S(2)}, u32[]{:S(2)}) %collective-permute-start.15) | collective-permute-done | bytes 110624 | tf_op jit(solution)/shard_map/ppermute | solution.py:360
  58.3 2.2 %collective-permute-done.16.refs_2_ = bf16[108,512]{1,0:T(8,128)(2,1)} collective-permute-done((bf16[108,512]{1,0:T(8,128)(2,1)S(1)}, bf16[108,512]{1,0:T(8,128)(2,1)}, u32[]{:S(2)}, u32[]{:S(2)}) %collective-permute-start.16) | collective-permute-done | bytes 110624 | tf_op jit(solution)/shard_map/ppermute | solution.py:360
  60.5 3.1 %collective-permute-done.17.refs_3_ = bf16[108,512]{1,0:T(8,128)(2,1)} collective-permute-done((bf16[108,512]{1,0:T(8,128)(2,1)S(1)}, bf16[108,512]{1,0:T(8,128)(2,1)}, u32[]{:S(2)}, u32[]{:S(2)}) %collective-permute-start.17) | collective-permute-done | bytes 110624 | tf_op jit(solution)/shard_map/ppermute | solution.py:360
  63.6 1.2 %shard_map.63.moves_ref = bf16[768,512]{1,0:T(8,128)(2,1)S(1)} custom-call(s32[3]{0:T(128)S(1)} %pad_add_fusion.place_ref, bf16[108,512]{1,0:T(8,128)(2,1)S(1)} %reshape.42.refs_0_, bf16[108,512]{1,0:T(8,128)(2,1)S(1)} %collective-permute-done.15.refs_1_, bf16[108,512]{1,0:T(8,128)(2,1)} %collective-permute-done.16.refs_2_, ...), custom_call_target="tpu_custom_call" | custom-call | bytes 1048576 | tf_op jit(solution)/shard_map/pallas_call | solution.py:297
  64.8 4.9 %shard_map.64 = bf16[16,64,256]{2,1,0:T(8,128)(2,1)} custom-call(s32[3]{0:T(128)S(1)} %pad_add_fusion.place_ref, bf16[768,512]{1,0:T(8,128)(2,1)S(1)} %shard_map.63.moves_ref, bf16[4,16,1152]{2,1,0:T(8,128)(2,1)S(1)} %bitcast.21, bf16[4,16,1152]{2,1,0:T(8,128)(2,1)S(1)} %collective-permute-done.1.refs_1_, bf16[4,16,1152]{2,1,0:T(8,128)(2,1)S(1)} %copy-done.1, ...), custom_call_target="tpu_custom_call" | custom-call | flops 1610612736 | bytes 4194304 | tf_op jit(solution)/shard_map/pallas_call | solution.py:337
  69.7 1.1 %all-to-all-done.hidden_ref = bf16[16,64,256]{2,1,0:T(8,128)(2,1)S(1)} async-done(((bf16[16,64,256]{2,1,0:T(8,128)(2,1)}), bf16[16,64,256]{2,1,0:T(8,128)(2,1)S(1)}, u32[]{:S(2)}, u32[]{:S(2)}) %all-to-all-start) | async-done | bytes 524320 | tf_op jit(solution)/shard_map/all_to_all | solution.py:380
  70.8 6.4 %all-to-all-start.2 = ((bf16[16,64,256]{2,1,0:T(8,128)(2,1)}), bf16[16,64,256]{2,1,0:T(8,128)(2,1)}, u32[]{:S(2)}, u32[]{:S(2)}) async-start(bf16[16,64,256]{2,1,0:T(8,128)(2,1)} %shard_map.64), calls=%async_computation.2 | async-start | bytes 1048576 | tf_op jit(solution)/shard_map/all_to_all | solution.py:380
  77.1 4.0 %shard_map.62 = (f32[108,512]{1,0:T(8,128)S(1)}, bf16[108,512]{1,0:T(8,128)(2,1)S(1)}, bf16[108,512]{1,0:T(8,128)(2,1)S(1)}, bf16[108,512]{1,0:T(8,128)(2,1)S(1)}) custom-call(s32[3]{0:T(128)S(1)} %pad_add_fusion.place_ref, bf16[16,64,256]{2,1,0:T(8,128)(2,1)S(1)} %all-to-all-done.hidden_ref, bf16[4,16,1152]{2,1,0:T(8,128)(2,1)S(1)} %bitcast.22, ...), custom_call_target="tpu_custom_call" | custom-call | flops 1610612736 | bytes 4194304 | tf_op jit(solution)/shard_map/pallas_call | solution.py:257
  81.1 0.4 collective-permute-start.11
  81.5 1.2 %collective-permute-start.10 = (bf16[108,512]{1,0:T(8,128)(2,1)S(1)}, bf16[108,512]{1,0:T(8,128)(2,1)S(1)}, u32[]{:S(2)}, u32[]{:S(2)}) collective-permute-start(bf16[108,512]{1,0:T(8,128)(2,1)S(1)} %get-tuple-element.12), channel_id=1, source_target_pairs={{0,32},{1,33},{2,34},{3,35},{4,36},{5,37},{6,38},{7,39},{8,40},{9,... | collective-permute-start | bytes 331784 | tf_op jit(solution)/shard_map/ppermute | solution.py:360
  82.7 0.6 collective-permute-start.9
  83.3 2.6 %collective-permute-done.11 = bf16[108,512]{1,0:T(8,128)(2,1)S(1)} collective-permute-done((bf16[108,512]{1,0:T(8,128)(2,1)S(1)}, bf16[108,512]{1,0:T(8,128)(2,1)S(1)}, u32[]{:S(2)}, u32[]{:S(2)}) %collective-permute-start.11) | collective-permute-done | bytes 110624 | tf_op jit(solution)/shard_map/ppermute | solution.py:360
  85.9 1.5 %collective-permute-done.10 = bf16[108,512]{1,0:T(8,128)(2,1)S(1)} collective-permute-done((bf16[108,512]{1,0:T(8,128)(2,1)S(1)}, bf16[108,512]{1,0:T(8,128)(2,1)S(1)}, u32[]{:S(2)}, u32[]{:S(2)}) %collective-permute-start.10) | collective-permute-done | bytes 110624 | tf_op jit(solution)/shard_map/ppermute | solution.py:360
  87.4 3.1 %collective-permute-done.9 = bf16[108,512]{1,0:T(8,128)(2,1)S(1)} collective-permute-done((bf16[108,512]{1,0:T(8,128)(2,1)S(1)}, bf16[108,512]{1,0:T(8,128)(2,1)S(1)}, u32[]{:S(2)}, u32[]{:S(2)}) %collective-permute-start.9) | collective-permute-done | bytes 110624 | tf_op jit(solution)/shard_map/ppermute | solution.py:360
  90.5 0.1 add_convert_fusion
  90.5 2.6 %collective-permute-start.14 = (bf16[108,512]{1,0:T(8,128)(2,1)S(1)}, bf16[108,512]{1,0:T(8,128)(2,1)S(1)}, u32[]{:S(2)}, u32[]{:S(2)}) collective-permute-start(bf16[108,512]{1,0:T(8,128)(2,1)S(1)} %add_convert_fusion), channel_id=1, source_target_pairs={{0,192},{64,0},{128,64},{192,128},{1,193},{65,1},{129,65},{193,129... | collective-permute-start | bytes 331784 | tf_op jit(solution)/shard_map/ppermute | solution.py:26
  93.1 1.7 %collective-permute-start.12 = (bf16[108,512]{1,0:T(8,128)(2,1)S(1)}, bf16[108,512]{1,0:T(8,128)(2,1)S(1)}, u32[]{:S(2)}, u32[]{:S(2)}) collective-permute-start(bf16[108,512]{1,0:T(8,128)(2,1)S(1)} %add_convert_fusion), channel_id=1, source_target_pairs={{0,128},{64,192},{128,0},{192,64},{1,129},{65,193},{129,1},{193,65... | collective-permute-start | bytes 331784 | tf_op jit(solution)/shard_map/ppermute | solution.py:26
  94.8 0.4 shard_map.65
  95.3 5.9 %collective-permute-done.13 = bf16[108,512]{1,0:T(8,128)(2,1)S(1)} collective-permute-done((bf16[108,512]{1,0:T(8,128)(2,1)S(1)}, bf16[108,512]{1,0:T(8,128)(2,1)S(1)}, u32[]{:S(2)}, u32[]{:S(2)}) %collective-permute-start.13) | collective-permute-done | bytes 110624 | tf_op jit(solution)/shard_map/ppermute | solution.py:26
  101.2 0.7 reshape.41
  102.0 1.2 %multiply_convert_fusion = bf16[16,64,256]{2,1,0:T(8,128)(2,1)S(1)} fusion(f32[16,64,256]{2,1,0:T(8,128)S(1)} %shard_map.65, bf16[16,64,256]{2,1,0:T(8,128)(2,1)} %all-to-all-done.2), kind=kLoop, calls=%fused_computation | loop fusion | flops 786432 | bytes 2097152 | tf_op jit(solution)/shard_map/convert_element_type | solution.py:437
  103.2 0.1 reshape.43
  103.3 1.1 %copy.13 = bf16[4,16,4,4,256]{4,3,2,1,0:T(4,128)(2,1)} copy(bf16[4,16,4,4,256]{4,2,0,3,1:T(4,128)(2,1)S(1)} %bitcast.25) | data formatting | bytes 1048576 | tf_op jit(solution)/shard_map/transpose | solution.py:438
  (29 shorter events, 0.3 us)
Async XLA Ops:
  2.7 11.9 %all-to-all-start.1 = ((bf16[8,8,1152]{2,1,0:T(8,128)(2,1)}), bf16[8,8,1152]{2,1,0:T(8,128)(2,1)S(1)}, u32[]{:S(2)}, u32[]{:S(2)}) async-start(bf16[8,8,1152]{2,1,0:T(8,128)(2,1)} %bitcast.9), calls=%async_computation.1 | async-start | bytes 294912 | tf_op jit(solution)/shard_map/all_to_all | solution.py:380
  14.6 18.2 %collective-permute-start.1 = (bf16[4,16,1152]{2,1,0:T(8,128)(2,1)S(1)}, bf16[4,16,1152]{2,1,0:T(8,128)(2,1)S(1)}, u32[]{:S(2)}, u32[]{:S(2)}) collective-permute-start(bf16[4,16,1152]{2,1,0:T(8,128)(2,1)S(1)} %bitcast.16), channel_id=1, source_target_pairs={{0,14},{1,15},{2,0},{3,1},{4,2},{5,3},{6,4},{7,5},{8,6},{9,7},{10,... | collective-permute-start | bytes 442376 | tf_op jit(solution)/shard_map/ppermute | solution.py:360
  19.6 10.4 %collective-permute-start.2 = (bf16[4,16,1152]{2,1,0:T(8,128)(2,1)S(1)}, bf16[4,16,1152]{2,1,0:T(8,128)(2,1)S(1)}, u32[]{:S(2)}, u32[]{:S(2)}) collective-permute-start(bf16[4,16,1152]{2,1,0:T(8,128)(2,1)S(1)} %bitcast.17), channel_id=1, source_target_pairs={{0,12},{1,13},{2,14},{3,15},{4,0},{5,1},{6,2},{7,3},{8,4},{9,5},{1... | collective-permute-start | bytes 442376 | tf_op jit(solution)/shard_map/ppermute | solution.py:360
  20.8 13.8 %collective-permute-start.5 = (bf16[4,16,1152]{2,1,0:T(8,128)(2,1)S(1)}, bf16[4,16,1152]{2,1,0:T(8,128)(2,1)S(1)}, u32[]{:S(2)}, u32[]{:S(2)}) collective-permute-start(bf16[4,16,1152]{2,1,0:T(8,128)(2,1)S(1)} %bitcast.18), channel_id=1, source_target_pairs={{0,4},{1,5},{2,6},{3,7},{4,8},{5,9},{6,10},{7,11},{8,12},{9,13},{1... | collective-permute-start | bytes 442376 | tf_op jit(solution)/shard_map/ppermute | solution.py:360
  22.0 1.5 %copy-start.4 = (bf16[3,3,3,128,256]{4,3,2,1,0:T(8,128)(2,1)S(1)}, bf16[3,3,3,128,256]{4,3,2,1,0:T(8,128)(2,1)}, u32[]{:S(2)}) copy-start(bf16[3,3,3,128,256]{4,3,2,1,0:T(8,128)(2,1)} %param.5) | copy-start | bytes 5308420
  26.4 21.8 %collective-permute-start = (bf16[4,256,256]{2,1,0:T(8,128)(2,1)S(1)}, bf16[4,256,256]{2,1,0:T(8,128)(2,1)S(1)}, u32[]{:S(2)}, u32[]{:S(2)}) collective-permute-start(bf16[4,256,256]{2,1,0:T(8,128)(2,1)S(1)} %get-tuple-element.9), channel_id=1, source_target_pairs={{0,1},{1,2},{2,3},{3,4},{4,5},{5,6},{6,7},{7,8},{8,9},{9,10},{10,1... | collective-permute-start | bytes 1572872 | tf_op jit(solution)/shard_map/ppermute | solution.py:21
  29.2 14.7 %collective-permute-start.7 = (bf16[4,16,1152]{2,1,0:T(8,128)(2,1)S(1)}, bf16[4,16,1152]{2,1,0:T(8,128)(2,1)S(1)}, u32[]{:S(2)}, u32[]{:S(2)}) collective-permute-start(bf16[4,16,1152]{2,1,0:T(8,128)(2,1)S(1)} %bitcast.19), channel_id=1, source_target_pairs={{0,2},{1,3},{2,4},{3,5},{4,6},{5,7},{6,8},{7,9},{8,10},{9,11},{10,... | collective-permute-start | bytes 442376 | tf_op jit(solution)/shard_map/ppermute | solution.py:360
  30.1 18.2 %copy-start = (bf16[4,16,1152]{2,1,0:T(8,128)(2,1)}, bf16[4,16,1152]{2,1,0:T(8,128)(2,1)S(1)}, u32[]{:S(2)}) copy-start(bf16[4,16,1152]{2,1,0:T(8,128)(2,1)S(1)} %collective-permute-done.2.refs_2_) | copy-start | bytes 442372
  30.1 13.9 %collective-permute-start.3 = (bf16[4,16,1152]{2,1,0:T(8,128)(2,1)S(1)}, bf16[4,16,1152]{2,1,0:T(8,128)(2,1)S(1)}, u32[]{:S(2)}, u32[]{:S(2)}) collective-permute-start(bf16[4,16,1152]{2,1,0:T(8,128)(2,1)S(1)} %collective-permute-done.2.refs_2_), channel_id=1, source_target_pairs={{0,14},{1,15},{2,0},{3,1},{4,2},{5,3},{6,4},{7,5},{8,6},{9,7},{10,... | collective-permute-start | bytes 442376 | tf_op jit(solution)/shard_map/ppermute | solution.py:360
  32.8 11.1 %collective-permute-start.4 = (bf16[4,16,1152]{2,1,0:T(8,128)(2,1)S(1)}, bf16[4,16,1152]{2,1,0:T(8,128)(2,1)S(1)}, u32[]{:S(2)}, u32[]{:S(2)}) collective-permute-start(bf16[4,16,1152]{2,1,0:T(8,128)(2,1)S(1)} %collective-permute-done.2.refs_2_), channel_id=1, source_target_pairs={{0,12},{1,13},{2,14},{3,15},{4,0},{5,1},{6,2},{7,3},{8,4},{9,5},{1... | collective-permute-start | bytes 442376 | tf_op jit(solution)/shard_map/ppermute | solution.py:360
  34.6 13.6 %copy-start.2 = (bf16[4,16,1152]{2,1,0:T(8,128)(2,1)}, bf16[4,16,1152]{2,1,0:T(8,128)(2,1)S(1)}, u32[]{:S(2)}) copy-start(bf16[4,16,1152]{2,1,0:T(8,128)(2,1)S(1)} %collective-permute-done.5.refs_6_) | copy-start | bytes 442372
  34.6 10.9 %collective-permute-start.6 = (bf16[4,16,1152]{2,1,0:T(8,128)(2,1)S(1)}, bf16[4,16,1152]{2,1,0:T(8,128)(2,1)S(1)}, u32[]{:S(2)}, u32[]{:S(2)}) collective-permute-start(bf16[4,16,1152]{2,1,0:T(8,128)(2,1)S(1)} %collective-permute-done.5.refs_6_), channel_id=1, source_target_pairs={{0,2},{1,3},{2,4},{3,5},{4,6},{5,7},{6,8},{7,9},{8,10},{9,11},{10,... | collective-permute-start | bytes 442376 | tf_op jit(solution)/shard_map/ppermute | solution.py:360
  48.1 5.4 %copy-start.5 = (bf16[3,3,3,4,512]{4,3,2,1,0:T(4,128)(2,1)S(1)}, bf16[3,3,3,4,512]{4,3,2,1,0:T(4,128)(2,1)}, u32[]{:S(2)}) copy-start(bf16[3,3,3,4,512]{4,3,2,1,0:T(4,128)(2,1)} %param.6) | copy-start | bytes 331780
  48.1 16.6 %collective-permute-start.8 = (bf16[8,4,16,1152]{3,2,1,0:T(8,128)(2,1)}, bf16[8,4,16,1152]{3,2,1,0:T(8,128)(2,1)}, u32[]{:S(2)}, u32[]{:S(2)}) collective-permute-start(bf16[8,4,16,1152]{3,2,1,0:T(8,128)(2,1)} %shard_map.61), channel_id=1, source_target_pairs={{0,1},{1,0},{2,3},{3,2},{4,5},{5,4},{6,7},{7,6},{8,9},{9,8},{10,11... | collective-permute-start | bytes 3538952 | tf_op jit(solution)/shard_map/ppermute | solution.py:360
  49.4 15.3 %copy-start.1 = (bf16[4,16,1152]{2,1,0:T(8,128)(2,1)S(1)}, bf16[4,16,1152]{2,1,0:T(8,128)(2,1)}, u32[]{:S(2)}) copy-start(bf16[4,16,1152]{2,1,0:T(8,128)(2,1)} %copy-done) | copy-start | bytes 442372
  49.4 15.4 %copy-start.3 = (bf16[4,16,1152]{2,1,0:T(8,128)(2,1)S(1)}, bf16[4,16,1152]{2,1,0:T(8,128)(2,1)}, u32[]{:S(2)}) copy-start(bf16[4,16,1152]{2,1,0:T(8,128)(2,1)} %copy-done.2) | copy-start | bytes 442372
  49.4 21.3 %all-to-all-start = ((bf16[16,64,256]{2,1,0:T(8,128)(2,1)}), bf16[16,64,256]{2,1,0:T(8,128)(2,1)S(1)}, u32[]{:S(2)}, u32[]{:S(2)}) async-start(bf16[16,64,256]{2,1,0:T(8,128)(2,1)} %shard_map.60), calls=%async_computation | async-start | bytes 1048576 | tf_op jit(solution)/shard_map/all_to_all | solution.py:380
  53.6 4.7 %collective-permute-start.15 = (bf16[108,512]{1,0:T(8,128)(2,1)S(1)}, bf16[108,512]{1,0:T(8,128)(2,1)S(1)}, u32[]{:S(2)}, u32[]{:S(2)}) collective-permute-start(bf16[108,512]{1,0:T(8,128)(2,1)S(1)} %reshape.42.refs_0_), channel_id=1, source_target_pairs={{0,48},{1,49},{2,50},{3,51},{4,52},{5,53},{6,54},{7,55},{8,56},{9,... | collective-permute-start | bytes 331784 | tf_op jit(solution)/shard_map/ppermute | solution.py:360
  54.6 5.9 %collective-permute-start.16 = (bf16[108,512]{1,0:T(8,128)(2,1)S(1)}, bf16[108,512]{1,0:T(8,128)(2,1)}, u32[]{:S(2)}, u32[]{:S(2)}) collective-permute-start(bf16[108,512]{1,0:T(8,128)(2,1)S(1)} %reshape.42.refs_0_), channel_id=1, source_target_pairs={{0,32},{1,33},{2,34},{3,35},{4,36},{5,37},{6,38},{7,39},{8,40},{9,... | collective-permute-start | bytes 331784 | tf_op jit(solution)/shard_map/ppermute | solution.py:360
  55.8 7.9 %collective-permute-start.17 = (bf16[108,512]{1,0:T(8,128)(2,1)S(1)}, bf16[108,512]{1,0:T(8,128)(2,1)}, u32[]{:S(2)}, u32[]{:S(2)}) collective-permute-start(bf16[108,512]{1,0:T(8,128)(2,1)S(1)} %reshape.42.refs_0_), channel_id=1, source_target_pairs={{0,16},{1,17},{2,18},{3,19},{4,20},{5,21},{6,22},{7,23},{8,24},{9,... | collective-permute-start | bytes 331784 | tf_op jit(solution)/shard_map/ppermute | solution.py:360
  70.8 31.2 %all-to-all-start.2 = ((bf16[16,64,256]{2,1,0:T(8,128)(2,1)}), bf16[16,64,256]{2,1,0:T(8,128)(2,1)}, u32[]{:S(2)}, u32[]{:S(2)}) async-start(bf16[16,64,256]{2,1,0:T(8,128)(2,1)} %shard_map.64), calls=%async_computation.2 | async-start | bytes 1048576 | tf_op jit(solution)/shard_map/all_to_all | solution.py:380
  81.1 4.7 %collective-permute-start.11 = (bf16[108,512]{1,0:T(8,128)(2,1)S(1)}, bf16[108,512]{1,0:T(8,128)(2,1)S(1)}, u32[]{:S(2)}, u32[]{:S(2)}) collective-permute-start(bf16[108,512]{1,0:T(8,128)(2,1)S(1)} %get-tuple-element.13), channel_id=1, source_target_pairs={{0,48},{1,49},{2,50},{3,51},{4,52},{5,53},{6,54},{7,55},{8,56},{9,... | collective-permute-start | bytes 331784 | tf_op jit(solution)/shard_map/ppermute | solution.py:360
  81.5 5.9 %collective-permute-start.10 = (bf16[108,512]{1,0:T(8,128)(2,1)S(1)}, bf16[108,512]{1,0:T(8,128)(2,1)S(1)}, u32[]{:S(2)}, u32[]{:S(2)}) collective-permute-start(bf16[108,512]{1,0:T(8,128)(2,1)S(1)} %get-tuple-element.12), channel_id=1, source_target_pairs={{0,32},{1,33},{2,34},{3,35},{4,36},{5,37},{6,38},{7,39},{8,40},{9,... | collective-permute-start | bytes 331784 | tf_op jit(solution)/shard_map/ppermute | solution.py:360
  82.7 7.8 %collective-permute-start.9 = (bf16[108,512]{1,0:T(8,128)(2,1)S(1)}, bf16[108,512]{1,0:T(8,128)(2,1)S(1)}, u32[]{:S(2)}, u32[]{:S(2)}) collective-permute-start(bf16[108,512]{1,0:T(8,128)(2,1)S(1)} %get-tuple-element.11), channel_id=1, source_target_pairs={{0,16},{1,17},{2,18},{3,19},{4,20},{5,21},{6,22},{7,23},{8,24},{9,... | collective-permute-start | bytes 331784 | tf_op jit(solution)/shard_map/ppermute | solution.py:360
  90.5 4.7 %collective-permute-start.14 = (bf16[108,512]{1,0:T(8,128)(2,1)S(1)}, bf16[108,512]{1,0:T(8,128)(2,1)S(1)}, u32[]{:S(2)}, u32[]{:S(2)}) collective-permute-start(bf16[108,512]{1,0:T(8,128)(2,1)S(1)} %add_convert_fusion), channel_id=1, source_target_pairs={{0,192},{64,0},{128,64},{192,128},{1,193},{65,1},{129,65},{193,129... | collective-permute-start | bytes 331784 | tf_op jit(solution)/shard_map/ppermute | solution.py:26
  93.1 8.1 %collective-permute-start.13 = (bf16[108,512]{1,0:T(8,128)(2,1)S(1)}, bf16[108,512]{1,0:T(8,128)(2,1)S(1)}, u32[]{:S(2)}, u32[]{:S(2)}) collective-permute-start(bf16[108,512]{1,0:T(8,128)(2,1)S(1)} %add_convert_fusion), channel_id=1, source_target_pairs={{0,64},{64,128},{128,192},{192,0},{1,65},{65,129},{129,193},{193,1... | collective-permute-start | bytes 331784 | tf_op jit(solution)/shard_map/ppermute | solution.py:26
  93.1 8.1 %collective-permute-start.12 = (bf16[108,512]{1,0:T(8,128)(2,1)S(1)}, bf16[108,512]{1,0:T(8,128)(2,1)S(1)}, u32[]{:S(2)}, u32[]{:S(2)}) collective-permute-start(bf16[108,512]{1,0:T(8,128)(2,1)S(1)} %add_convert_fusion), channel_id=1, source_target_pairs={{0,128},{64,192},{128,0},{192,64},{1,129},{65,193},{129,1},{193,65... | collective-permute-start | bytes 331784 | tf_op jit(solution)/shard_map/ppermute | solution.py:26

commit v10 on v9

--- a/solution.py
+++ b/solution.py
@@ -56,9 +56,23 @@
     return jnp.where(keep, moved, 0.0).astype(block.dtype)
 
 
-def conv_kernel(row_len, w_from, planes_ref, ahead_ref, part_ref, cols_ref, w_ref, sem):
-    copy = pltpu.make_async_copy(w_from, w_ref, sem)
+def conv_kernel(row_len, w_from, volume_from, ahead_ref, part_ref, *scratch):
+    cols_ref, w_ref, volume_ref, planes_ref, sems = scratch
+    moves = [
+        pltpu.make_async_copy(volume_from.at[:, at * 16 : at * 16 + 16], volume_ref.at[at], sems.at[at])
+        for at in range(2)
+    ]
+    copy = pltpu.make_async_copy(w_from, w_ref, sems.at[2])
+    for move in moves:
+        move.start()
     copy.start()
+    for at in range(2):
+        moves[at].wait()
+        for first in range(0, volume_ref.shape[1], 16):
+            turned = jnp.swapaxes(volume_ref[at, first : first + 16], 0, 1)
+            for phase in range(16):
+                row = phase * volume_ref.shape[1] + first
+                planes_ref[at, row : row + 16, :] = turned[phase]
     cells = planes_ref.shape[2]
     channels = planes_ref.shape[1] // 16
     tap_rows = 9 * channels
@@ -92,27 +106,29 @@
             out_ref[phase] = total[:, phase * cells : (phase + 1) * cells].astype(out_ref.dtype)
 
 
-def conv(w_rows, planes, row_len):
+def conv(w_rows, volume, row_len):
     depth, outs = w_rows.shape
-    cells = planes.shape[2]
+    channels, _, cells = volume.shape
     return pl.pallas_call(
         functools.partial(conv_kernel, row_len),
         out_shape=(
             jax.ShapeDtypeStruct((4, outs, cells), jnp.bfloat16),
             jax.ShapeDtypeStruct((4, outs, cells), jnp.float32),
         ),
-        in_specs=[IN_HBM, IN_VMEM],
+        in_specs=[IN_HBM] * 2,
         out_specs=(IN_VMEM,) * 2,
         scratch_shapes=[
             pltpu.VMEM((2 * depth // 3, 4 * cells), jnp.bfloat16),
             pltpu.VMEM(w_rows.shape, jnp.bfloat16),
-            pltpu.SemaphoreType.DMA(()),
+            pltpu.VMEM((2, channels, 16, cells), jnp.bfloat16),
+            pltpu.VMEM((2, 16 * channels, cells), jnp.bfloat16),
+            pltpu.SemaphoreType.DMA((3,)),
         ],
         compiler_params=GRANT,
         cost_estimate=pl.CostEstimate(
             flops=8 * outs * depth * cells, bytes_accessed=4 * depth * cells, transcendentals=0
         ),
-    )(w_rows, planes)
+    )(w_rows, volume)
 
 
 def regrouped(values, own, at):
@@ -350,6 +366,59 @@
     )(place, moves, *mine, theirs)
 
 
+def parts_kernel(cot_ref, out_ref):
+    channels, depth, cells = cot_ref.shape
+    share = depth // ROWS
+    half = out_ref.shape[2]
+    turned = jnp.swapaxes(cot_ref[...].astype(jnp.float32), 0, 1)
+    for row in range(ROWS):
+        for at in range(share + 1):
+            s = row * share + at
+            for lane in range(0, cells, 128):
+                put = at * cells + lane
+                if s < depth:
+                    block = turned[s, :, lane : lane + 128].astype(out_ref.dtype)
+                else:
+                    block = jnp.zeros((channels, 128), out_ref.dtype)
+                out_ref[row * CORES + put // half, :, put % half : put % half + 128] = block
+
+
+def parts_of(cot):
+    channels, depth, cells = cot.shape
+    half = (depth // ROWS + 1) * cells // CORES
+    return pl.pallas_call(
+        parts_kernel,
+        out_shape=jax.ShapeDtypeStruct((ROWS * CORES, channels, half), cot.dtype),
+        in_specs=[IN_VMEM],
+        out_specs=IN_VMEM,
+        compiler_params=GRANT,
+        cost_estimate=pl.CostEstimate(flops=0, bytes_accessed=4 * cot.size, transcendentals=0),
+    )(cot)
+
+
+def total_kernel(own_ref, left_ref, opposite_ref, right_ref, out_ref):
+    f32 = jnp.float32
+    across = own_ref[...].astype(f32) + opposite_ref[...].astype(f32)
+    total = across + (left_ref[...].astype(f32) + right_ref[...].astype(f32))
+    taps, own, _ = out_ref.shape
+    for tap in range(taps):
+        out_ref[tap] = total[tap * own : (tap + 1) * own, :]
+
+
+def total_of(own, left, opposite, right):
+    rows, outs = own.shape
+    return pl.pallas_call(
+        total_kernel,
+        out_shape=jax.ShapeDtypeStruct((27, rows // 27, outs), jnp.float32),
+        in_specs=[IN_VMEM] * 4,
+        out_specs=IN_VMEM,
+        compiler_params=GRANT,
+        cost_estimate=pl.CostEstimate(
+            flops=3 * own.size, bytes_accessed=12 * own.size, transcendentals=0
+        ),
+    )(own, left, opposite, right)
+
+
 def on_space(block, y_by=0, z_by=0, core_by=0):
     route = []
     for y in range(ROWS):
@@ -393,11 +462,8 @@
     place = jnp.stack([y, z, core]).astype(jnp.int32)
     group = RING * CORES
 
-    share = cotangent.shape[2] // ROWS
-    local = jnp.pad(cotangent[0], ((0, 0), (0, 1), (0, 0)))
-    parts = jnp.stack([local[:, at * share : (at + 1) * share + 1] for at in range(ROWS)])
-    parts = parts.reshape(ROWS, -1, CORES, (share + 1) * cells // CORES).transpose(0, 2, 1, 3)
-    first = exchange(parts.reshape((ROWS * CORES,) + parts.shape[2:]), PILLARS)
+    parts = parts_of(cotangent[0])
+    first = exchange(parts, PILLARS)
     first = first.reshape(ROWS, -1, first.shape[2])
     hops = {0: first}
     for step in (1, -1, 2, -2):
@@ -412,9 +478,8 @@
     for step in range(1, ROWS):
         w_rel.append(on_space(w_rel[0], y_by=-step))
 
-    planes = volume[0].transpose(1, 2, 0, 3).reshape(2, 16 * channels, cells)
     w_rows = w_first.reshape(27 * channels, outs)
-    ahead, part = conv(w_rows, planes, row_len)
+    ahead, part = conv(w_rows, volume[0].reshape(channels, 32, cells), row_len)
     behind = from_behind(ahead, "space", 1)
     hidden = pointwise(activate, part, behind, group, jnp.bfloat16)
     slopes = pointwise(slope_of, part, behind, group, jnp.float32)
@@ -430,8 +495,8 @@
     partial = partial.astype(jnp.bfloat16)
     sides = []
     for distance in (1, 2, 3):
-        sides.append(from_side(partial, "dp", distance).astype(jnp.float32))
-    grad_second = (partial.astype(jnp.float32) + sides[1]) + (sides[0] + sides[2])
+        sides.append(from_side(partial, "dp", distance))
+    grad_second = total_of(partial, *sides)
     grad_second = grad_second.reshape(3, 3, 3, own, C3)
 
     pre_grad = (hidden_grad.astype(jnp.float32) * slopes).astype(jnp.bfloat16)

time: 105 us -> 104 us (level)
  blocking collectives: 0 us -> 11.2 us
  starting transfers between devices: 41.9 us -> 36.4 us
  waiting for transfers between devices: 34.8 us -> 29.9 us
  local copies, waits for them, and re-layouts: 8.02 us -> 5.19 us
  Pallas kernels: 17.2 us -> 18.6 us
    all_to_all x0 -> x1, blocking collectives: none -> 11.2 us  [exchange(): lax.all_to_all(blocks, 'space', split_axis=0, concat_axis=0, axis_index_g...]
    all_to_all x3 -> x2, starting transfers between devices: 17 us -> 10.3 us  [exchange(): lax.all_to_all(blocks, 'space', split_axis=0, concat_axis=0, axis_index_g...]
    transpose x2 -> x0, local copies, waits for them, and re-layouts: 3.44 us -> none  [the longest x1 2.76 us: section(): planes = volume[0].transpose(1, 2, 0, 3).reshape(2, 16 * channels, cells)]
    all_to_all x3 -> x2, waiting for transfers between devices: 3.75 us -> 1.13 us  [exchange(): lax.all_to_all(blocks, 'space', split_axis=0, concat_axis=0, axis_index_g...]
    unnamed x12 -> x8, local copies, waits for them, and re-layouts: 1.5 us -> 3.97 us
    ppermute x3, waiting for transfers between devices: 5.91 us -> 3.58 us  [from_side(): lax.ppermute(block, axis, [(i, (i + distance) % size) for i in range(size)])]
  transfers between devices with their start and end apart: 21 -> 20, of which waited for: 11 -> 11; matrix products, arithmetic and copies ran while one was open for 4% -> 0% of each run, Pallas kernels for 16% -> 18%
where the time goes in v10:
time: 104 us; the launch traced here: 103 us
  starting transfers between devices  36.4 us (35%)
  waiting for transfers between devices  29.9 us (29%)
  Pallas kernels  18.6 us (18%)
  blocking collectives  11.2 us (11%)
  local copies, waits for them, and re-layouts  5.19 us (5%)
  other arithmetic  1.32 us (1%)
    ppermute x14, waiting for transfers between devices, on_space(): return lax.ppermute(block, 'space', route)  25.1 us
    ppermute x14, starting transfers between devices, on_space(): return lax.ppermute(block, 'space', route)  18.4 us
    all_to_all x1, blocking collectives, exchange(): lax.all_to_all(blocks, 'space', split_axis=0, concat_axis=0, axis_index_g...  11.2 us
    all_to_all x2, starting transfers between devices, exchange(): lax.all_to_all(blocks, 'space', split_axis=0, concat_axis=0, axis_index_g...  10.3 us
    ppermute x3, starting transfers between devices, from_side(): lax.ppermute(block, axis, [(i, (i + distance) % size) for i in range(size)])  4.88 us
    pallas_call x1, Pallas kernels, back(): pl.pallas_call(functools.partial(back_kernel, row_len), out_shape=jax.Sha...  4.85 us
    pallas_call x1, Pallas kernels, grad(): pl.pallas_call(functools.partial(grad_kernel, row_len), out_shape=[jax.Sh...  4.02 us
    unnamed x8, local copies, waits for them, and re-layouts  3.97 us
  transfers between devices with their start and end apart: 20, of which 11 were waited for; matrix products, arithmetic and copies ran while one was open for 0% of the time, Pallas kernels for 18%

profile of v10, /device:TPU:1, one launch (start us, length us, event | category | flops | bytes accessed | tf_op | source)
XLA Modules:
  0.0 103.3 jit_solution(11765810347655171810)
XLA Ops:
  0.6 0.9 copy-done
  1.5 0.1 shard_map.61
  1.6 11.2 %all_to_all.15 = bf16[8,8,1152]{2,1,0:T(8,128)(2,1)S(1)} all-to-all(bf16[8,8,1152]{2,1,0:T(8,128)(2,1)S(1)} %shard_map.61), channel_id=1, replica_groups={{0,1,16,17,32,33,48,49},{2,3,18,19,34,35,50,51},{4,5,20,21,36,37,52,53}..., dimensions={0} | all-to-all | bytes 294912 | tf_op jit(solution)/shard_map/all_to_all | solution.py:449
  12.8 5.6 %collective-permute-start.1 = (bf16[4,16,1152]{2,1,0:T(8,128)(2,1)S(1)}, bf16[4,16,1152]{2,1,0:T(8,128)(2,1)S(1)}, u32[]{:S(2)}, u32[]{:S(2)}) collective-permute-start(bf16[4,16,1152]{2,1,0:T(8,128)(2,1)S(1)} %bitcast.10), channel_id=1, source_target_pairs={{0,14},{1,15},{2,0},{3,1},{4,2},{5,3},{6,4},{7,5},{8,6},{9,7},{10,... | collective-permute-start | bytes 442376 | tf_op jit(solution)/shard_map/ppermute | solution.py:429
  18.3 1.2 %collective-permute-start.2 = (bf16[4,16,1152]{2,1,0:T(8,128)(2,1)S(1)}, bf16[4,16,1152]{2,1,0:T(8,128)(2,1)S(1)}, u32[]{:S(2)}, u32[]{:S(2)}) collective-permute-start(bf16[4,16,1152]{2,1,0:T(8,128)(2,1)S(1)} %bitcast.11), channel_id=1, source_target_pairs={{0,12},{1,13},{2,14},{3,15},{4,0},{5,1},{6,2},{7,3},{8,4},{9,5},{1... | collective-permute-start | bytes 442376 | tf_op jit(solution)/shard_map/ppermute | solution.py:429
  19.5 1.2 %collective-permute-start.5 = (bf16[4,16,1152]{2,1,0:T(8,128)(2,1)S(1)}, bf16[4,16,1152]{2,1,0:T(8,128)(2,1)S(1)}, u32[]{:S(2)}, u32[]{:S(2)}) collective-permute-start(bf16[4,16,1152]{2,1,0:T(8,128)(2,1)S(1)} %bitcast.12), channel_id=1, source_target_pairs={{0,4},{1,5},{2,6},{3,7},{4,8},{5,9},{6,10},{7,11},{8,12},{9,13},{1... | collective-permute-start | bytes 442376 | tf_op jit(solution)/shard_map/ppermute | solution.py:429
  20.7 1.6 %copy-done.1 = bf16[1,128,2,16,256]{4,3,2,1,0:T(8,128)(2,1)S(1)} copy-done((bf16[1,128,2,16,256]{4,3,2,1,0:T(8,128)(2,1)S(1)}, bf16[1,128,2,16,256]{4,3,2,1,0:T(8,128)(2,1)}, u32[]{:S(2)}) %copy-start.1) | copy-done | bytes 2097176
  22.3 1.5 %copy-done.2 = bf16[3,3,3,128,256]{4,3,2,1,0:T(8,128)(2,1)S(1)} copy-done((bf16[3,3,3,128,256]{4,3,2,1,0:T(8,128)(2,1)S(1)}, bf16[3,3,3,128,256]{4,3,2,1,0:T(8,128)(2,1)}, u32[]{:S(2)}) %copy-start.2) | copy-done | bytes 1769496
  23.8 3.6 %shard_map.59 = (bf16[4,256,256]{2,1,0:T(8,128)(2,1)S(1)}, f32[4,256,256]{2,1,0:T(8,128)S(1)}) custom-call(bf16[3456,256]{1,0:T(8,128)(2,1)S(1)} %bitcast.19, bf16[128,32,256]{2,1,0:T(8,128)(2,1)S(1)} %bitcast.18), custom_call_target="tpu_custom_call" | custom-call | flops 1811939328 | bytes 3538944 | tf_op jit(solution)/shard_map/pallas_call | solution.py:112
  27.4 2.8 %collective-permute-start = (bf16[4,256,256]{2,1,0:T(8,128)(2,1)S(1)}, bf16[4,256,256]{2,1,0:T(8,128)(2,1)S(1)}, u32[]{:S(2)}, u32[]{:S(2)}) collective-permute-start(bf16[4,256,256]{2,1,0:T(8,128)(2,1)S(1)} %get-tuple-element.9), channel_id=1, source_target_pairs={{0,1},{1,2},{2,3},{3,4},{4,5},{5,6},{6,7},{7,8},{8,9},{9,10},{10,1... | collective-permute-start | bytes 1572872 | tf_op jit(solution)/shard_map/ppermute | solution.py:21
  30.2 0.8 collective-permute-start.7
  31.0 2.8 %collective-permute-start.3 = (bf16[4,16,1152]{2,1,0:T(8,128)(2,1)S(1)}, bf16[4,16,1152]{2,1,0:T(8,128)(2,1)S(1)}, u32[]{:S(2)}, u32[]{:S(2)}) collective-permute-start(bf16[4,16,1152]{2,1,0:T(8,128)(2,1)S(1)} %collective-permute-done.2.refs_2_), channel_id=1, source_target_pairs={{0,14},{1,15},{2,0},{3,1},{4,2},{5,3},{6,4},{7,5},{8,6},{9,7},{10,... | collective-permute-start | bytes 442376 | tf_op jit(solution)/shard_map/ppermute | solution.py:429
  33.8 1.8 %collective-permute-start.4 = (bf16[4,16,1152]{2,1,0:T(8,128)(2,1)S(1)}, bf16[4,16,1152]{2,1,0:T(8,128)(2,1)S(1)}, u32[]{:S(2)}, u32[]{:S(2)}) collective-permute-start(bf16[4,16,1152]{2,1,0:T(8,128)(2,1)S(1)} %collective-permute-done.2.refs_2_), channel_id=1, source_target_pairs={{0,12},{1,13},{2,14},{3,15},{4,0},{5,1},{6,2},{7,3},{8,4},{9,5},{1... | collective-permute-start | bytes 442376 | tf_op jit(solution)/shard_map/ppermute | solution.py:429
  35.6 0.7 collective-permute-start.6
  36.3 8.5 %collective-permute-done.7.refs_7_ = bf16[4,16,1152]{2,1,0:T(8,128)(2,1)S(1)} collective-permute-done((bf16[4,16,1152]{2,1,0:T(8,128)(2,1)S(1)}, bf16[4,16,1152]{2,1,0:T(8,128)(2,1)S(1)}, u32[]{:S(2)}, u32[]{:S(2)}) %collective-permute-start.7) | collective-permute-done | bytes 147488 | tf_op jit(solution)/shard_map/ppermute | solution.py:429
  44.9 1.6 %collective-permute-done.6.refs_5_ = bf16[4,16,1152]{2,1,0:T(8,128)(2,1)S(1)} collective-permute-done((bf16[4,16,1152]{2,1,0:T(8,128)(2,1)S(1)}, bf16[4,16,1152]{2,1,0:T(8,128)(2,1)S(1)}, u32[]{:S(2)}, u32[]{:S(2)}) %collective-permute-start.6) | collective-permute-done | bytes 147488 | tf_op jit(solution)/shard_map/ppermute | solution.py:429
  46.5 2.6 %shard_map.62 = bf16[8,4,16,1152]{3,2,1,0:T(8,128)(2,1)} custom-call(bf16[4,16,1152]{2,1,0:T(8,128)(2,1)S(1)} %bitcast.14, bf16[4,16,1152]{2,1,0:T(8,128)(2,1)S(1)} %collective-permute-done.1.refs_1_, bf16[4,16,1152]{2,1,0:T(8,128)(2,1)S(1)} %collective-permute-done.2.refs_2_, bf16[4,16,1152]{2,1,0:T(8,128)(2,1)S(1)} %collective-permute-done.3.refs_3_, ...), custom_call_target="tpu_custom_call" | custom-call | bytes 2359296 | tf_op jit(solution)/shard_map/pallas_call | solution.py:177
  49.1 0.1 collective-permute-start.8
  49.2 1.2 %shard_map.60 = bf16[16,64,256]{2,1,0:T(8,128)(2,1)} custom-call(f32[4,256,256]{2,1,0:T(8,128)S(1)} %get-tuple-element.8.part_ref, bf16[4,256,256]{2,1,0:T(8,128)(2,1)S(1)} %collective-permute-done.behind_ref), custom_call_target="tpu_custom_call" | custom-call | flops 2621440 | bytes 2097152 | tf_op jit(solution)/shard_map/pallas_call | solution.py:152
  50.3 4.0 %all-to-all-start = ((bf16[16,64,256]{2,1,0:T(8,128)(2,1)}), bf16[16,64,256]{2,1,0:T(8,128)(2,1)S(1)}, u32[]{:S(2)}, u32[]{:S(2)}) async-start(bf16[16,64,256]{2,1,0:T(8,128)(2,1)} %shard_map.60), calls=%async_computation | async-start | bytes 1048576 | tf_op jit(solution)/shard_map/all_to_all | solution.py:449
  54.4 1.0 collective-permute-start.15
  55.4 1.2 %collective-permute-start.16 = (bf16[108,512]{1,0:T(8,128)(2,1)S(1)}, bf16[108,512]{1,0:T(8,128)(2,1)}, u32[]{:S(2)}, u32[]{:S(2)}) collective-permute-start(bf16[108,512]{1,0:T(8,128)(2,1)S(1)} %reshape.25.refs_0_), channel_id=1, source_target_pairs={{0,32},{1,33},{2,34},{3,35},{4,36},{5,37},{6,38},{7,39},{8,40},{9,... | collective-permute-start | bytes 331784 | tf_op jit(solution)/shard_map/ppermute | solution.py:429
  56.5 0.1 pad_add_fusion.place_ref
  56.6 2.5 %collective-permute-done.15.refs_1_ = bf16[108,512]{1,0:T(8,128)(2,1)S(1)} collective-permute-done((bf16[108,512]{1,0:T(8,128)(2,1)S(1)}, bf16[108,512]{1,0:T(8,128)(2,1)S(1)}, u32[]{:S(2)}, u32[]{:S(2)}) %collective-permute-start.15) | collective-permute-done | bytes 110624 | tf_op jit(solution)/shard_map/ppermute | solution.py:429
  59.1 2.2 %collective-permute-done.16.refs_2_ = bf16[108,512]{1,0:T(8,128)(2,1)} collective-permute-done((bf16[108,512]{1,0:T(8,128)(2,1)S(1)}, bf16[108,512]{1,0:T(8,128)(2,1)}, u32[]{:S(2)}, u32[]{:S(2)}) %collective-permute-start.16) | collective-permute-done | bytes 110624 | tf_op jit(solution)/shard_map/ppermute | solution.py:429
  61.3 3.1 %collective-permute-done.17.refs_3_ = bf16[108,512]{1,0:T(8,128)(2,1)} collective-permute-done((bf16[108,512]{1,0:T(8,128)(2,1)S(1)}, bf16[108,512]{1,0:T(8,128)(2,1)}, u32[]{:S(2)}, u32[]{:S(2)}) %collective-permute-start.17) | collective-permute-done | bytes 110624 | tf_op jit(solution)/shard_map/ppermute | solution.py:429
  64.4 1.2 %shard_map.65.moves_ref = bf16[768,512]{1,0:T(8,128)(2,1)S(1)} custom-call(s32[3]{0:T(128)S(1)} %pad_add_fusion.place_ref, bf16[108,512]{1,0:T(8,128)(2,1)S(1)} %reshape.25.refs_0_, bf16[108,512]{1,0:T(8,128)(2,1)S(1)} %collective-permute-done.15.refs_1_, bf16[108,512]{1,0:T(8,128)(2,1)} %collective-permute-done.16.refs_2_, ...), custom_call_target="tpu_custom_call" | custom-call | bytes 1048576 | tf_op jit(solution)/shard_map/pallas_call | solution.py:313
  65.6 4.8 %shard_map.66 = bf16[16,64,256]{2,1,0:T(8,128)(2,1)} custom-call(s32[3]{0:T(128)S(1)} %pad_add_fusion.place_ref, bf16[768,512]{1,0:T(8,128)(2,1)S(1)} %shard_map.65.moves_ref, bf16[4,16,1152]{2,1,0:T(8,128)(2,1)S(1)} %bitcast.15, bf16[4,16,1152]{2,1,0:T(8,128)(2,1)S(1)} %collective-permute-done.1.refs_1_, ...), custom_call_target="tpu_custom_call" | custom-call | flops 1610612736 | bytes 4194304 | tf_op jit(solution)/shard_map/pallas_call | solution.py:353
  70.4 1.1 %all-to-all-done.hidden_ref = bf16[16,64,256]{2,1,0:T(8,128)(2,1)S(1)} async-done(((bf16[16,64,256]{2,1,0:T(8,128)(2,1)}), bf16[16,64,256]{2,1,0:T(8,128)(2,1)S(1)}, u32[]{:S(2)}, u32[]{:S(2)}) %all-to-all-start) | async-done | bytes 524320 | tf_op jit(solution)/shard_map/all_to_all | solution.py:449
  71.6 6.3 %all-to-all-start.2 = ((bf16[16,64,256]{2,1,0:T(8,128)(2,1)}), bf16[16,64,256]{2,1,0:T(8,128)(2,1)}, u32[]{:S(2)}, u32[]{:S(2)}) async-start(bf16[16,64,256]{2,1,0:T(8,128)(2,1)} %shard_map.66), calls=%async_computation.2 | async-start | bytes 1048576 | tf_op jit(solution)/shard_map/all_to_all | solution.py:449
  77.9 4.0 %shard_map.63 = (f32[108,512]{1,0:T(8,128)S(1)}, bf16[108,512]{1,0:T(8,128)(2,1)S(1)}, bf16[108,512]{1,0:T(8,128)(2,1)S(1)}, bf16[108,512]{1,0:T(8,128)(2,1)S(1)}) custom-call(s32[3]{0:T(128)S(1)} %pad_add_fusion.place_ref, bf16[16,64,256]{2,1,0:T(8,128)(2,1)S(1)} %all-to-all-done.hidden_ref, bf16[4,16,1152]{2,1,0:T(8,128)(2,1)S(1)} %bitcast.16, ...), custom_call_target="tpu_custom_call" | custom-call | flops 1610612736 | bytes 4194304 | tf_op jit(solution)/shard_map/pallas_call | solution.py:273
  81.9 0.4 collective-permute-start.11
  82.3 1.2 %collective-permute-start.10 = (bf16[108,512]{1,0:T(8,128)(2,1)S(1)}, bf16[108,512]{1,0:T(8,128)(2,1)S(1)}, u32[]{:S(2)}, u32[]{:S(2)}) collective-permute-start(bf16[108,512]{1,0:T(8,128)(2,1)S(1)} %get-tuple-element.12), channel_id=1, source_target_pairs={{0,32},{1,33},{2,34},{3,35},{4,36},{5,37},{6,38},{7,39},{8,40},{9,... | collective-permute-start | bytes 331784 | tf_op jit(solution)/shard_map/ppermute | solution.py:429
  83.4 0.6 collective-permute-start.9
  84.0 2.6 %collective-permute-done.11 = bf16[108,512]{1,0:T(8,128)(2,1)S(1)} collective-permute-done((bf16[108,512]{1,0:T(8,128)(2,1)S(1)}, bf16[108,512]{1,0:T(8,128)(2,1)S(1)}, u32[]{:S(2)}, u32[]{:S(2)}) %collective-permute-start.11) | collective-permute-done | bytes 110624 | tf_op jit(solution)/shard_map/ppermute | solution.py:429
  86.6 1.5 %collective-permute-done.10 = bf16[108,512]{1,0:T(8,128)(2,1)S(1)} collective-permute-done((bf16[108,512]{1,0:T(8,128)(2,1)S(1)}, bf16[108,512]{1,0:T(8,128)(2,1)S(1)}, u32[]{:S(2)}, u32[]{:S(2)}) %collective-permute-start.10) | collective-permute-done | bytes 110624 | tf_op jit(solution)/shard_map/ppermute | solution.py:429
  88.1 3.1 %collective-permute-done.9 = bf16[108,512]{1,0:T(8,128)(2,1)S(1)} collective-permute-done((bf16[108,512]{1,0:T(8,128)(2,1)S(1)}, bf16[108,512]{1,0:T(8,128)(2,1)S(1)}, u32[]{:S(2)}, u32[]{:S(2)}) %collective-permute-start.9) | collective-permute-done | bytes 110624 | tf_op jit(solution)/shard_map/ppermute | solution.py:429
  91.2 0.1 add_convert_fusion.own_ref
  91.3 1.3 %collective-permute-start.12 = (bf16[108,512]{1,0:T(8,128)(2,1)S(1)}, bf16[108,512]{1,0:T(8,128)(2,1)S(1)}, u32[]{:S(2)}, u32[]{:S(2)}) collective-permute-start(bf16[108,512]{1,0:T(8,128)(2,1)S(1)} %add_convert_fusion.own_ref), channel_id=1, source_target_pairs={{0,64},{64,128},{128,192},{192,0},{1,65},{65,129},{129,193},{193,1... | collective-permute-start | bytes 331784 | tf_op jit(solution)/shard_map/ppermute | solution.py:26
  92.6 2.4 %collective-permute-start.13 = (bf16[108,512]{1,0:T(8,128)(2,1)S(1)}, bf16[108,512]{1,0:T(8,128)(2,1)S(1)}, u32[]{:S(2)}, u32[]{:S(2)}) collective-permute-start(bf16[108,512]{1,0:T(8,128)(2,1)S(1)} %add_convert_fusion.own_ref), channel_id=1, source_target_pairs={{0,128},{64,192},{128,0},{192,64},{1,129},{65,193},{129,1},{193,65... | collective-permute-start | bytes 331784 | tf_op jit(solution)/shard_map/ppermute | solution.py:26
  95.0 1.2 %collective-permute-start.14 = (bf16[108,512]{1,0:T(8,128)(2,1)S(1)}, bf16[108,512]{1,0:T(8,128)(2,1)S(1)}, u32[]{:S(2)}, u32[]{:S(2)}) collective-permute-start(bf16[108,512]{1,0:T(8,128)(2,1)S(1)} %add_convert_fusion.own_ref), channel_id=1, source_target_pairs={{0,192},{64,0},{128,64},{192,128},{1,193},{65,1},{129,65},{193,129... | collective-permute-start | bytes 331784 | tf_op jit(solution)/shard_map/ppermute | solution.py:26
  96.2 0.4 shard_map.67
  96.6 0.2 collective-permute-done.12.left_ref
  96.8 3.4 %collective-permute-done.13.opposite_ref = bf16[108,512]{1,0:T(8,128)(2,1)S(1)} collective-permute-done((bf16[108,512]{1,0:T(8,128)(2,1)S(1)}, bf16[108,512]{1,0:T(8,128)(2,1)S(1)}, u32[]{:S(2)}, u32[]{:S(2)}) %collective-permute-start.13) | collective-permute-done | bytes 110624 | tf_op jit(solution)/shard_map/ppermute | solution.py:26
  100.2 0.7 shard_map.64
  100.9 1.2 %multiply_convert_fusion = bf16[16,64,256]{2,1,0:T(8,128)(2,1)S(1)} fusion(f32[16,64,256]{2,1,0:T(8,128)S(1)} %shard_map.67, bf16[16,64,256]{2,1,0:T(8,128)(2,1)} %all-to-all-done.2), kind=kLoop, calls=%fused_computation | loop fusion | flops 786432 | bytes 2097152 | tf_op jit(solution)/shard_map/convert_element_type | solution.py:502
  102.1 0.1 reshape.26
  102.3 1.1 %copy.6 = bf16[4,16,4,4,256]{4,3,2,1,0:T(4,128)(2,1)} copy(bf16[4,16,4,4,256]{4,2,0,3,1:T(4,128)(2,1)S(1)} %bitcast.20) | data formatting | bytes 1048576 | tf_op jit(solution)/shard_map/transpose | solution.py:503
  (16 shorter events, 0.1 us)
Async XLA Ops:
  0.6 0.9 copy-start
  12.8 21.0 %collective-permute-start.1 = (bf16[4,16,1152]{2,1,0:T(8,128)(2,1)S(1)}, bf16[4,16,1152]{2,1,0:T(8,128)(2,1)S(1)}, u32[]{:S(2)}, u32[]{:S(2)}) collective-permute-start(bf16[4,16,1152]{2,1,0:T(8,128)(2,1)S(1)} %bitcast.10), channel_id=1, source_target_pairs={{0,14},{1,15},{2,0},{3,1},{4,2},{5,3},{6,4},{7,5},{8,6},{9,7},{10,... | collective-permute-start | bytes 442376 | tf_op jit(solution)/shard_map/ppermute | solution.py:429
  18.3 12.7 %collective-permute-start.2 = (bf16[4,16,1152]{2,1,0:T(8,128)(2,1)S(1)}, bf16[4,16,1152]{2,1,0:T(8,128)(2,1)S(1)}, u32[]{:S(2)}, u32[]{:S(2)}) collective-permute-start(bf16[4,16,1152]{2,1,0:T(8,128)(2,1)S(1)} %bitcast.11), channel_id=1, source_target_pairs={{0,12},{1,13},{2,14},{3,15},{4,0},{5,1},{6,2},{7,3},{8,4},{9,5},{1... | collective-permute-start | bytes 442376 | tf_op jit(solution)/shard_map/ppermute | solution.py:429
  19.5 16.1 %collective-permute-start.5 = (bf16[4,16,1152]{2,1,0:T(8,128)(2,1)S(1)}, bf16[4,16,1152]{2,1,0:T(8,128)(2,1)S(1)}, u32[]{:S(2)}, u32[]{:S(2)}) collective-permute-start(bf16[4,16,1152]{2,1,0:T(8,128)(2,1)S(1)} %bitcast.12), channel_id=1, source_target_pairs={{0,4},{1,5},{2,6},{3,7},{4,8},{5,9},{6,10},{7,11},{8,12},{9,13},{1... | collective-permute-start | bytes 442376 | tf_op jit(solution)/shard_map/ppermute | solution.py:429
  20.7 1.6 %copy-start.1 = (bf16[1,128,2,16,256]{4,3,2,1,0:T(8,128)(2,1)S(1)}, bf16[1,128,2,16,256]{4,3,2,1,0:T(8,128)(2,1)}, u32[]{:S(2)}) copy-start(bf16[1,128,2,16,256]{4,3,2,1,0:T(8,128)(2,1)} %param.4) | copy-start | bytes 6291460
  22.3 1.5 %copy-start.2 = (bf16[3,3,3,128,256]{4,3,2,1,0:T(8,128)(2,1)S(1)}, bf16[3,3,3,128,256]{4,3,2,1,0:T(8,128)(2,1)}, u32[]{:S(2)}) copy-start(bf16[3,3,3,128,256]{4,3,2,1,0:T(8,128)(2,1)} %param.5) | copy-start | bytes 5308420
  27.4 21.8 %collective-permute-start = (bf16[4,256,256]{2,1,0:T(8,128)(2,1)S(1)}, bf16[4,256,256]{2,1,0:T(8,128)(2,1)S(1)}, u32[]{:S(2)}, u32[]{:S(2)}) collective-permute-start(bf16[4,256,256]{2,1,0:T(8,128)(2,1)S(1)} %get-tuple-element.9), channel_id=1, source_target_pairs={{0,1},{1,2},{2,3},{3,4},{4,5},{5,6},{6,7},{7,8},{8,9},{9,10},{10,1... | collective-permute-start | bytes 1572872 | tf_op jit(solution)/shard_map/ppermute | solution.py:21
  30.2 14.7 %collective-permute-start.7 = (bf16[4,16,1152]{2,1,0:T(8,128)(2,1)S(1)}, bf16[4,16,1152]{2,1,0:T(8,128)(2,1)S(1)}, u32[]{:S(2)}, u32[]{:S(2)}) collective-permute-start(bf16[4,16,1152]{2,1,0:T(8,128)(2,1)S(1)} %bitcast.13), channel_id=1, source_target_pairs={{0,2},{1,3},{2,4},{3,5},{4,6},{5,7},{6,8},{7,9},{8,10},{9,11},{10,... | collective-permute-start | bytes 442376 | tf_op jit(solution)/shard_map/ppermute | solution.py:429
  31.0 13.9 %collective-permute-start.3 = (bf16[4,16,1152]{2,1,0:T(8,128)(2,1)S(1)}, bf16[4,16,1152]{2,1,0:T(8,128)(2,1)S(1)}, u32[]{:S(2)}, u32[]{:S(2)}) collective-permute-start(bf16[4,16,1152]{2,1,0:T(8,128)(2,1)S(1)} %collective-permute-done.2.refs_2_), channel_id=1, source_target_pairs={{0,14},{1,15},{2,0},{3,1},{4,2},{5,3},{6,4},{7,5},{8,6},{9,7},{10,... | collective-permute-start | bytes 442376 | tf_op jit(solution)/shard_map/ppermute | solution.py:429
  33.8 11.1 %collective-permute-start.4 = (bf16[4,16,1152]{2,1,0:T(8,128)(2,1)S(1)}, bf16[4,16,1152]{2,1,0:T(8,128)(2,1)S(1)}, u32[]{:S(2)}, u32[]{:S(2)}) collective-permute-start(bf16[4,16,1152]{2,1,0:T(8,128)(2,1)S(1)} %collective-permute-done.2.refs_2_), channel_id=1, source_target_pairs={{0,12},{1,13},{2,14},{3,15},{4,0},{5,1},{6,2},{7,3},{8,4},{9,5},{1... | collective-permute-start | bytes 442376 | tf_op jit(solution)/shard_map/ppermute | solution.py:429
  35.6 10.9 %collective-permute-start.6 = (bf16[4,16,1152]{2,1,0:T(8,128)(2,1)S(1)}, bf16[4,16,1152]{2,1,0:T(8,128)(2,1)S(1)}, u32[]{:S(2)}, u32[]{:S(2)}) collective-permute-start(bf16[4,16,1152]{2,1,0:T(8,128)(2,1)S(1)} %collective-permute-done.5.refs_6_), channel_id=1, source_target_pairs={{0,2},{1,3},{2,4},{3,5},{4,6},{5,7},{6,8},{7,9},{8,10},{9,11},{10,... | collective-permute-start | bytes 442376 | tf_op jit(solution)/shard_map/ppermute | solution.py:429
  49.1 5.3 %copy-start.3 = (bf16[3,3,3,4,512]{4,3,2,1,0:T(4,128)(2,1)S(1)}, bf16[3,3,3,4,512]{4,3,2,1,0:T(4,128)(2,1)}, u32[]{:S(2)}) copy-start(bf16[3,3,3,4,512]{4,3,2,1,0:T(4,128)(2,1)} %param.6) | copy-start | bytes 331780
  49.1 16.5 %collective-permute-start.8 = (bf16[8,4,16,1152]{3,2,1,0:T(8,128)(2,1)}, bf16[8,4,16,1152]{3,2,1,0:T(8,128)(2,1)}, u32[]{:S(2)}, u32[]{:S(2)}) collective-permute-start(bf16[8,4,16,1152]{3,2,1,0:T(8,128)(2,1)} %shard_map.62), channel_id=1, source_target_pairs={{0,1},{1,0},{2,3},{3,2},{4,5},{5,4},{6,7},{7,6},{8,9},{9,8},{10,11... | collective-permute-start | bytes 3538952 | tf_op jit(solution)/shard_map/ppermute | solution.py:429
  50.3 21.2 %all-to-all-start = ((bf16[16,64,256]{2,1,0:T(8,128)(2,1)}), bf16[16,64,256]{2,1,0:T(8,128)(2,1)S(1)}, u32[]{:S(2)}, u32[]{:S(2)}) async-start(bf16[16,64,256]{2,1,0:T(8,128)(2,1)} %shard_map.60), calls=%async_computation | async-start | bytes 1048576 | tf_op jit(solution)/shard_map/all_to_all | solution.py:449
  54.4 4.7 %collective-permute-start.15 = (bf16[108,512]{1,0:T(8,128)(2,1)S(1)}, bf16[108,512]{1,0:T(8,128)(2,1)S(1)}, u32[]{:S(2)}, u32[]{:S(2)}) collective-permute-start(bf16[108,512]{1,0:T(8,128)(2,1)S(1)} %reshape.25.refs_0_), channel_id=1, source_target_pairs={{0,48},{1,49},{2,50},{3,51},{4,52},{5,53},{6,54},{7,55},{8,56},{9,... | collective-permute-start | bytes 331784 | tf_op jit(solution)/shard_map/ppermute | solution.py:429
  55.4 5.9 %collective-permute-start.16 = (bf16[108,512]{1,0:T(8,128)(2,1)S(1)}, bf16[108,512]{1,0:T(8,128)(2,1)}, u32[]{:S(2)}, u32[]{:S(2)}) collective-permute-start(bf16[108,512]{1,0:T(8,128)(2,1)S(1)} %reshape.25.refs_0_), channel_id=1, source_target_pairs={{0,32},{1,33},{2,34},{3,35},{4,36},{5,37},{6,38},{7,39},{8,40},{9,... | collective-permute-start | bytes 331784 | tf_op jit(solution)/shard_map/ppermute | solution.py:429
  56.5 7.9 %collective-permute-start.17 = (bf16[108,512]{1,0:T(8,128)(2,1)S(1)}, bf16[108,512]{1,0:T(8,128)(2,1)}, u32[]{:S(2)}, u32[]{:S(2)}) collective-permute-start(bf16[108,512]{1,0:T(8,128)(2,1)S(1)} %reshape.25.refs_0_), channel_id=1, source_target_pairs={{0,16},{1,17},{2,18},{3,19},{4,20},{5,21},{6,22},{7,23},{8,24},{9,... | collective-permute-start | bytes 331784 | tf_op jit(solution)/shard_map/ppermute | solution.py:429
  71.6 29.4 %all-to-all-start.2 = ((bf16[16,64,256]{2,1,0:T(8,128)(2,1)}), bf16[16,64,256]{2,1,0:T(8,128)(2,1)}, u32[]{:S(2)}, u32[]{:S(2)}) async-start(bf16[16,64,256]{2,1,0:T(8,128)(2,1)} %shard_map.66), calls=%async_computation.2 | async-start | bytes 1048576 | tf_op jit(solution)/shard_map/all_to_all | solution.py:449
  81.9 4.7 %collective-permute-start.11 = (bf16[108,512]{1,0:T(8,128)(2,1)S(1)}, bf16[108,512]{1,0:T(8,128)(2,1)S(1)}, u32[]{:S(2)}, u32[]{:S(2)}) collective-permute-start(bf16[108,512]{1,0:T(8,128)(2,1)S(1)} %get-tuple-element.13), channel_id=1, source_target_pairs={{0,48},{1,49},{2,50},{3,51},{4,52},{5,53},{6,54},{7,55},{8,56},{9,... | collective-permute-start | bytes 331784 | tf_op jit(solution)/shard_map/ppermute | solution.py:429
  82.3 5.9 %collective-permute-start.10 = (bf16[108,512]{1,0:T(8,128)(2,1)S(1)}, bf16[108,512]{1,0:T(8,128)(2,1)S(1)}, u32[]{:S(2)}, u32[]{:S(2)}) collective-permute-start(bf16[108,512]{1,0:T(8,128)(2,1)S(1)} %get-tuple-element.12), channel_id=1, source_target_pairs={{0,32},{1,33},{2,34},{3,35},{4,36},{5,37},{6,38},{7,39},{8,40},{9,... | collective-permute-start | bytes 331784 | tf_op jit(solution)/shard_map/ppermute | solution.py:429
  83.4 7.8 %collective-permute-start.9 = (bf16[108,512]{1,0:T(8,128)(2,1)S(1)}, bf16[108,512]{1,0:T(8,128)(2,1)S(1)}, u32[]{:S(2)}, u32[]{:S(2)}) collective-permute-start(bf16[108,512]{1,0:T(8,128)(2,1)S(1)} %get-tuple-element.11), channel_id=1, source_target_pairs={{0,16},{1,17},{2,18},{3,19},{4,20},{5,21},{6,22},{7,23},{8,24},{9,... | collective-permute-start | bytes 331784 | tf_op jit(solution)/shard_map/ppermute | solution.py:429
  91.3 5.5 %collective-permute-start.12 = (bf16[108,512]{1,0:T(8,128)(2,1)S(1)}, bf16[108,512]{1,0:T(8,128)(2,1)S(1)}, u32[]{:S(2)}, u32[]{:S(2)}) collective-permute-start(bf16[108,512]{1,0:T(8,128)(2,1)S(1)} %add_convert_fusion.own_ref), channel_id=1, source_target_pairs={{0,64},{64,128},{128,192},{192,0},{1,65},{65,129},{129,193},{193,1... | collective-permute-start | bytes 331784 | tf_op jit(solution)/shard_map/ppermute | solution.py:26
  92.6 7.6 %collective-permute-start.13 = (bf16[108,512]{1,0:T(8,128)(2,1)S(1)}, bf16[108,512]{1,0:T(8,128)(2,1)S(1)}, u32[]{:S(2)}, u32[]{:S(2)}) collective-permute-start(bf16[108,512]{1,0:T(8,128)(2,1)S(1)} %add_convert_fusion.own_ref), channel_id=1, source_target_pairs={{0,128},{64,192},{128,0},{192,64},{1,129},{65,193},{129,1},{193,65... | collective-permute-start | bytes 331784 | tf_op jit(solution)/shard_map/ppermute | solution.py:26
  95.0 5.2 %collective-permute-start.14 = (bf16[108,512]{1,0:T(8,128)(2,1)S(1)}, bf16[108,512]{1,0:T(8,128)(2,1)S(1)}, u32[]{:S(2)}, u32[]{:S(2)}) collective-permute-start(bf16[108,512]{1,0:T(8,128)(2,1)S(1)} %add_convert_fusion.own_ref), channel_id=1, source_target_pairs={{0,192},{64,0},{128,64},{192,128},{1,193},{65,1},{129,65},{193,129... | collective-permute-start | bytes 331784 | tf_op jit(solution)/shard_map/ppermute | solution.py:26

commit v11 on v10

--- a/solution.py
+++ b/solution.py
@@ -40,6 +40,7 @@
 ROWS, RING, CORES = 4, 8, 2
 IN_VMEM = pl.BlockSpec(memory_space=pltpu.VMEM)
 IN_HBM = pl.BlockSpec(memory_space=pltpu.HBM)
+WIDE = pltpu.CompilerParams(vmem_limit_bytes=64900000)
 GRANT = pltpu.CompilerParams(vmem_limit_bytes=16 * 2**20)
 
 
@@ -124,7 +125,7 @@
             pltpu.VMEM((2, 16 * channels, cells), jnp.bfloat16),
             pltpu.SemaphoreType.DMA((3,)),
         ],
-        compiler_params=GRANT,
+        compiler_params=WIDE,
         cost_estimate=pl.CostEstimate(
             flops=8 * outs * depth * cells, bytes_accessed=4 * depth * cells, transcendentals=0
         ),
@@ -137,10 +138,17 @@
     return jnp.concatenate([values[start : start + own] for start in starts], 0)
 
 
-def pointwise_kernel(rule, part_ref, behind_ref, result_ref):
+def pointwise_kernel(rule, part_from, behind_ref, result_ref, part_ref, sems):
     groups, rows, _ = result_ref.shape
     unit = rows // 4
+    copies = [
+        pltpu.make_async_copy(part_from.at[phase], part_ref.at[phase], sems.at[phase])
+        for phase in range(4)
+    ]
+    for copy in copies:
+        copy.start()
     for phase in range(4):
+        copies[phase].wait()
         values = rule(part_ref[phase] + behind_ref[phase].astype(jnp.float32))
         for at in range(groups):
             block = regrouped(values, unit // ROWS, at)
@@ -152,9 +160,10 @@
     return pl.pallas_call(
         functools.partial(pointwise_kernel, rule),
         out_shape=jax.ShapeDtypeStruct((groups, phases * outs // groups, cells), dtype),
-        in_specs=[IN_VMEM] * 2,
+        in_specs=[IN_HBM, IN_VMEM],
         out_specs=IN_VMEM,
-        compiler_params=GRANT,
+        scratch_shapes=[pltpu.VMEM(part.shape, part.dtype), pltpu.SemaphoreType.DMA((4,))],
+        compiler_params=pltpu.CompilerParams(vmem_limit_bytes=65_800_000),
         cost_estimate=pl.CostEstimate(
             flops=10 * part.size, bytes_accessed=8 * part.size, transcendentals=part.size
         ),

time: 104 us -> 105 us (level)
  Pallas kernels: 18.6 us -> 23.9 us
  waiting for transfers between devices: 29.9 us -> 26.4 us
  local copies, waits for them, and re-layouts: 5.19 us -> 3.87 us
    pallas_call x2, Pallas kernels: 1.57 us -> 6.67 us  [pointwise(): pl.pallas_call(functools.partial(pointwise_kernel, rule), out_shape=jax.S...]
    ppermute x3, waiting for transfers between devices: 3.58 us -> 0.57 us  [from_side(): lax.ppermute(block, axis, [(i, (i + distance) % size) for i in range(size)])]
    unnamed x8 -> x36, local copies, waits for them, and re-layouts: 3.97 us -> 1.75 us
    pallas_call x1, Pallas kernels: 3.63 us -> 5.29 us  [conv(): pl.pallas_call(functools.partial(conv_kernel, row_len), out_shape=(jax.Sh...]
  transfers between devices with their start and end apart: 20 -> 20, of which waited for: 11 -> 10; matrix products, arithmetic and copies ran while one was open for 0% -> 1% of each run, Pallas kernels for 18% -> 23%
where the time goes in v11:
time: 105 us
  starting transfers between devices  37 us (35%)
  waiting for transfers between devices  26.4 us (25%)
  Pallas kernels  23.9 us (23%)
  blocking collectives  11.2 us (11%)
  local copies, waits for them, and re-layouts  3.87 us (4%)
  other arithmetic  1.52 us (1%)
    ppermute x14, waiting for transfers between devices, on_space(): return lax.ppermute(block, 'space', route)  25.1 us
    ppermute x14, starting transfers between devices, on_space(): return lax.ppermute(block, 'space', route)  18.5 us
    all_to_all x1, blocking collectives, exchange(): lax.all_to_all(blocks, 'space', split_axis=0, concat_axis=0, axis_index_g...  11.2 us
    all_to_all x2, starting transfers between devices, exchange(): lax.all_to_all(blocks, 'space', split_axis=0, concat_axis=0, axis_index_g...  10.8 us
    pallas_call x2, Pallas kernels, pointwise(): pl.pallas_call(functools.partial(pointwise_kernel, rule), out_shape=jax.S...  6.67 us
    pallas_call x1, Pallas kernels, conv(): pl.pallas_call(functools.partial(conv_kernel, row_len), out_shape=(jax.Sh...  5.29 us
    ppermute x3, starting transfers between devices, from_side(): lax.ppermute(block, axis, [(i, (i + distance) % size) for i in range(size)])  4.9 us
    pallas_call x1, Pallas kernels, back(): pl.pallas_call(functools.partial(back_kernel, row_len), out_shape=jax.Sha...  4.84 us
  transfers between devices with their start and end apart: 20, of which 10 were waited for; matrix products, arithmetic and copies ran while one was open for 1% of the time, Pallas kernels for 23%

profile of v11, /device:TPU:1, one launch (start us, length us, event | category | flops | bytes accessed | tf_op | source)
XLA Modules:
  0.0 104.8 jit_solution(921518827933008703)
XLA Ops:
  0.6 0.9 copy-done.16
  1.5 0.1 shard_map.61
  1.6 11.2 %all_to_all.15 = bf16[8,8,1152]{2,1,0:T(8,128)(2,1)S(1)} all-to-all(bf16[8,8,1152]{2,1,0:T(8,128)(2,1)S(1)} %shard_map.61), channel_id=1, replica_groups={{0,1,16,17,32,33,48,49},{2,3,18,19,34,35,50,51},{4,5,20,21,36,37,52,53}..., dimensions={0} | all-to-all | bytes 294912 | tf_op jit(solution)/shard_map/all_to_all | solution.py:458
  12.8 5.6 %collective-permute-start.1 = (bf16[4,16,1152]{2,1,0:T(8,128)(2,1)S(1)}, bf16[4,16,1152]{2,1,0:T(8,128)(2,1)S(1)}, u32[]{:S(2)}, u32[]{:S(2)}) collective-permute-start(bf16[4,16,1152]{2,1,0:T(8,128)(2,1)S(1)} %bitcast.10), channel_id=1, source_target_pairs={{0,14},{1,15},{2,0},{3,1},{4,2},{5,3},{6,4},{7,5},{8,6},{9,7},{10,... | collective-permute-start | bytes 442376 | tf_op jit(solution)/shard_map/ppermute | solution.py:438
  18.3 1.2 %collective-permute-start.2 = (bf16[4,16,1152]{2,1,0:T(8,128)(2,1)S(1)}, bf16[4,16,1152]{2,1,0:T(8,128)(2,1)S(1)}, u32[]{:S(2)}, u32[]{:S(2)}) collective-permute-start(bf16[4,16,1152]{2,1,0:T(8,128)(2,1)S(1)} %bitcast.11), channel_id=1, source_target_pairs={{0,12},{1,13},{2,14},{3,15},{4,0},{5,1},{6,2},{7,3},{8,4},{9,5},{1... | collective-permute-start | bytes 442376 | tf_op jit(solution)/shard_map/ppermute | solution.py:438
  19.5 1.2 %collective-permute-start.5 = (bf16[4,16,1152]{2,1,0:T(8,128)(2,1)S(1)}, bf16[4,16,1152]{2,1,0:T(8,128)(2,1)S(1)}, u32[]{:S(2)}, u32[]{:S(2)}) collective-permute-start(bf16[4,16,1152]{2,1,0:T(8,128)(2,1)S(1)} %bitcast.12), channel_id=1, source_target_pairs={{0,4},{1,5},{2,6},{3,7},{4,8},{5,9},{6,10},{7,11},{8,12},{9,13},{1... | collective-permute-start | bytes 442376 | tf_op jit(solution)/shard_map/ppermute | solution.py:438
  20.7 5.3 %shard_map.59 = (bf16[4,256,256]{2,1,0:T(8,128)(2,1)}, f32[4,256,256]{2,1,0:T(8,128)}) custom-call(bf16[3456,256]{1,0:T(8,128)(2,1)} %bitcast.22, bf16[128,32,256]{2,1,0:T(8,128)(2,1)} %bitcast.21), custom_call_target="tpu_custom_call" | custom-call | flops 1811939328 | bytes 3538944 | tf_op jit(solution)/shard_map/pallas_call | solution.py:113
  26.0 2.8 %collective-permute-start = (bf16[4,256,256]{2,1,0:T(8,128)(2,1)}, bf16[4,256,256]{2,1,0:T(8,128)(2,1)S(1)}, u32[]{:S(2)}, u32[]{:S(2)}) collective-permute-start(bf16[4,256,256]{2,1,0:T(8,128)(2,1)} %get-tuple-element.9), channel_id=1, source_target_pairs={{0,1},{1,2},{2,3},{3,4},{4,5},{5,6},{6,7},{7,8},{8,9},{9,10},{10,1... | collective-permute-start | bytes 1572872 | tf_op jit(solution)/shard_map/ppermute | solution.py:21
  28.8 0.8 collective-permute-start.7
  29.6 2.8 %collective-permute-start.3 = (bf16[4,16,1152]{2,1,0:T(8,128)(2,1)S(1)}, bf16[4,16,1152]{2,1,0:T(8,128)(2,1)S(1)}, u32[]{:S(2)}, u32[]{:S(2)}) collective-permute-start(bf16[4,16,1152]{2,1,0:T(8,128)(2,1)S(1)} %collective-permute-done.2.refs_2_), channel_id=1, source_target_pairs={{0,14},{1,15},{2,0},{3,1},{4,2},{5,3},{6,4},{7,5},{8,6},{9,7},{10,... | collective-permute-start | bytes 442376 | tf_op jit(solution)/shard_map/ppermute | solution.py:438
  32.4 1.8 %collective-permute-start.4 = (bf16[4,16,1152]{2,1,0:T(8,128)(2,1)S(1)}, bf16[4,16,1152]{2,1,0:T(8,128)(2,1)S(1)}, u32[]{:S(2)}, u32[]{:S(2)}) collective-permute-start(bf16[4,16,1152]{2,1,0:T(8,128)(2,1)S(1)} %collective-permute-done.2.refs_2_), channel_id=1, source_target_pairs={{0,12},{1,13},{2,14},{3,15},{4,0},{5,1},{6,2},{7,3},{8,4},{9,5},{1... | collective-permute-start | bytes 442376 | tf_op jit(solution)/shard_map/ppermute | solution.py:438
  34.2 0.7 collective-permute-start.6
  34.9 8.6 %collective-permute-done.7.refs_7_ = bf16[4,16,1152]{2,1,0:T(8,128)(2,1)S(1)} collective-permute-done((bf16[4,16,1152]{2,1,0:T(8,128)(2,1)S(1)}, bf16[4,16,1152]{2,1,0:T(8,128)(2,1)S(1)}, u32[]{:S(2)}, u32[]{:S(2)}) %collective-permute-start.7) | collective-permute-done | bytes 147488 | tf_op jit(solution)/shard_map/ppermute | solution.py:438
  43.6 1.6 %collective-permute-done.6.refs_5_ = bf16[4,16,1152]{2,1,0:T(8,128)(2,1)S(1)} collective-permute-done((bf16[4,16,1152]{2,1,0:T(8,128)(2,1)S(1)}, bf16[4,16,1152]{2,1,0:T(8,128)(2,1)S(1)}, u32[]{:S(2)}, u32[]{:S(2)}) %collective-permute-start.6) | collective-permute-done | bytes 147488 | tf_op jit(solution)/shard_map/ppermute | solution.py:438
  45.2 1.6 %shard_map.62 = bf16[8,4,16,1152]{3,2,1,0:T(8,128)(2,1)S(1)} custom-call(bf16[4,16,1152]{2,1,0:T(8,128)(2,1)S(1)} %bitcast.14, bf16[4,16,1152]{2,1,0:T(8,128)(2,1)S(1)} %collective-permute-done.1.refs_1_, bf16[4,16,1152]{2,1,0:T(8,128)(2,1)S(1)} %collective-permute-done.2.refs_2_, bf16[4,16,1152]{2,1,0:T(8,128)(2,1)S(1)} %collective-permute-done.3.refs_3_, ...), custom_call_target="tpu_custom_call" | custom-call | bytes 2359296 | tf_op jit(solution)/shard_map/pallas_call | solution.py:186
  46.8 0.1 collective-permute-start.8
  46.9 0.0 copy-start.17
  46.9 0.8 copy-done.17
  47.7 3.2 %shard_map.60 = bf16[16,64,256]{2,1,0:T(8,128)(2,1)} custom-call(f32[4,256,256]{2,1,0:T(8,128)} %get-tuple-element.8.part_from, bf16[4,256,256]{2,1,0:T(8,128)(2,1)} %copy-done.17), custom_call_target="tpu_custom_call" | custom-call | flops 2621440 | bytes 2097152 | tf_op jit(solution)/shard_map/pallas_call | solution.py:160
  51.0 4.1 %all-to-all-start = ((bf16[16,64,256]{2,1,0:T(8,128)(2,1)}), bf16[16,64,256]{2,1,0:T(8,128)(2,1)S(1)}, u32[]{:S(2)}, u32[]{:S(2)}) async-start(bf16[16,64,256]{2,1,0:T(8,128)(2,1)} %shard_map.60), calls=%async_computation | async-start | bytes 1048576 | tf_op jit(solution)/shard_map/all_to_all | solution.py:458
  55.1 0.9 reshape.25.refs_0_
  56.0 1.0 collective-permute-start.15
  57.0 1.2 %collective-permute-start.16 = (bf16[108,512]{1,0:T(8,128)(2,1)S(1)}, bf16[108,512]{1,0:T(8,128)(2,1)S(1)}, u32[]{:S(2)}, u32[]{:S(2)}) collective-permute-start(bf16[108,512]{1,0:T(8,128)(2,1)S(1)} %reshape.25.refs_0_), channel_id=1, source_target_pairs={{0,32},{1,33},{2,34},{3,35},{4,36},{5,37},{6,38},{7,39},{8,40},{9,... | collective-permute-start | bytes 331784 | tf_op jit(solution)/shard_map/ppermute | solution.py:438
  58.2 0.1 pad_add_fusion.place_ref
  58.3 2.4 %collective-permute-done.15.refs_1_ = bf16[108,512]{1,0:T(8,128)(2,1)S(1)} collective-permute-done((bf16[108,512]{1,0:T(8,128)(2,1)S(1)}, bf16[108,512]{1,0:T(8,128)(2,1)S(1)}, u32[]{:S(2)}, u32[]{:S(2)}) %collective-permute-start.15) | collective-permute-done | bytes 110624 | tf_op jit(solution)/shard_map/ppermute | solution.py:438
  60.7 2.1 %collective-permute-done.16.refs_2_ = bf16[108,512]{1,0:T(8,128)(2,1)S(1)} collective-permute-done((bf16[108,512]{1,0:T(8,128)(2,1)S(1)}, bf16[108,512]{1,0:T(8,128)(2,1)S(1)}, u32[]{:S(2)}, u32[]{:S(2)}) %collective-permute-start.16) | collective-permute-done | bytes 110624 | tf_op jit(solution)/shard_map/ppermute | solution.py:438
  62.8 3.1 %collective-permute-done.17.refs_3_ = bf16[108,512]{1,0:T(8,128)(2,1)S(1)} collective-permute-done((bf16[108,512]{1,0:T(8,128)(2,1)S(1)}, bf16[108,512]{1,0:T(8,128)(2,1)S(1)}, u32[]{:S(2)}, u32[]{:S(2)}) %collective-permute-start.17) | collective-permute-done | bytes 110624 | tf_op jit(solution)/shard_map/ppermute | solution.py:438
  65.9 0.7 shard_map.65.moves_ref
  66.8 4.8 %shard_map.66 = bf16[16,64,256]{2,1,0:T(8,128)(2,1)} custom-call(s32[3]{0:T(128)S(1)} %pad_add_fusion.place_ref, bf16[768,512]{1,0:T(8,128)(2,1)S(1)} %shard_map.65.moves_ref, bf16[4,16,1152]{2,1,0:T(8,128)(2,1)S(1)} %bitcast.15, bf16[4,16,1152]{2,1,0:T(8,128)(2,1)S(1)} %copy-done.3, bf16[4,16,1152]{2,1,0:T(8,128)(2,1)S(1)} %copy-done.5, ...), custom_call_target="tpu_custom_call" | custom-call | flops 1610612736 | bytes 4194304 | tf_op jit(solution)/shard_map/pallas_call | solution.py:362
  71.6 0.7 all-to-all-done.hidden_ref
  72.3 6.7 %all-to-all-start.2 = ((bf16[16,64,256]{2,1,0:T(8,128)(2,1)}), bf16[16,64,256]{2,1,0:T(8,128)(2,1)S(1)}, u32[]{:S(2)}, u32[]{:S(2)}) async-start(bf16[16,64,256]{2,1,0:T(8,128)(2,1)} %shard_map.66), calls=%async_computation.2 | async-start | bytes 1048576 | tf_op jit(solution)/shard_map/all_to_all | solution.py:458
  79.1 4.0 %shard_map.63 = (f32[108,512]{1,0:T(8,128)S(1)}, bf16[108,512]{1,0:T(8,128)(2,1)S(1)}, bf16[108,512]{1,0:T(8,128)(2,1)S(1)}, bf16[108,512]{1,0:T(8,128)(2,1)S(1)}) custom-call(s32[3]{0:T(128)S(1)} %pad_add_fusion.place_ref, bf16[16,64,256]{2,1,0:T(8,128)(2,1)S(1)} %all-to-all-done.hidden_ref, bf16[4,16,1152]{2,1,0:T(8,128)(2,1)S(1)} %bitcast.16, ...), custom_call_target="tpu_custom_call" | custom-call | flops 1610612736 | bytes 4194304 | tf_op jit(solution)/shard_map/pallas_call | solution.py:282
  83.1 0.4 collective-permute-start.11
  83.4 1.2 %collective-permute-start.10 = (bf16[108,512]{1,0:T(8,128)(2,1)S(1)}, bf16[108,512]{1,0:T(8,128)(2,1)S(1)}, u32[]{:S(2)}, u32[]{:S(2)}) collective-permute-start(bf16[108,512]{1,0:T(8,128)(2,1)S(1)} %get-tuple-element.12), channel_id=1, source_target_pairs={{0,32},{1,33},{2,34},{3,35},{4,36},{5,37},{6,38},{7,39},{8,40},{9,... | collective-permute-start | bytes 331784 | tf_op jit(solution)/shard_map/ppermute | solution.py:438
  84.6 0.6 collective-permute-start.9
  85.2 2.5 %collective-permute-done.11 = bf16[108,512]{1,0:T(8,128)(2,1)S(1)} collective-permute-done((bf16[108,512]{1,0:T(8,128)(2,1)S(1)}, bf16[108,512]{1,0:T(8,128)(2,1)S(1)}, u32[]{:S(2)}, u32[]{:S(2)}) %collective-permute-start.11) | collective-permute-done | bytes 110624 | tf_op jit(solution)/shard_map/ppermute | solution.py:438
  87.7 1.5 %collective-permute-done.10 = bf16[108,512]{1,0:T(8,128)(2,1)S(1)} collective-permute-done((bf16[108,512]{1,0:T(8,128)(2,1)S(1)}, bf16[108,512]{1,0:T(8,128)(2,1)S(1)}, u32[]{:S(2)}, u32[]{:S(2)}) %collective-permute-start.10) | collective-permute-done | bytes 110624 | tf_op jit(solution)/shard_map/ppermute | solution.py:438
  89.3 3.2 %collective-permute-done.9 = bf16[108,512]{1,0:T(8,128)(2,1)S(1)} collective-permute-done((bf16[108,512]{1,0:T(8,128)(2,1)S(1)}, bf16[108,512]{1,0:T(8,128)(2,1)S(1)}, u32[]{:S(2)}, u32[]{:S(2)}) %collective-permute-start.9) | collective-permute-done | bytes 110624 | tf_op jit(solution)/shard_map/ppermute | solution.py:438
  92.4 0.1 add_convert_fusion.own_ref
  92.5 1.3 %collective-permute-start.12 = (bf16[108,512]{1,0:T(8,128)(2,1)S(1)}, bf16[108,512]{1,0:T(8,128)(2,1)S(1)}, u32[]{:S(2)}, u32[]{:S(2)}) collective-permute-start(bf16[108,512]{1,0:T(8,128)(2,1)S(1)} %add_convert_fusion.own_ref), channel_id=1, source_target_pairs={{0,64},{64,128},{128,192},{192,0},{1,65},{65,129},{129,193},{193,1... | collective-permute-start | bytes 331784 | tf_op jit(solution)/shard_map/ppermute | solution.py:26
  93.8 2.5 %collective-permute-start.13 = (bf16[108,512]{1,0:T(8,128)(2,1)S(1)}, bf16[108,512]{1,0:T(8,128)(2,1)S(1)}, u32[]{:S(2)}, u32[]{:S(2)}) collective-permute-start(bf16[108,512]{1,0:T(8,128)(2,1)S(1)} %add_convert_fusion.own_ref), channel_id=1, source_target_pairs={{0,128},{64,192},{128,0},{192,64},{1,129},{65,193},{129,1},{193,65... | collective-permute-start | bytes 331784 | tf_op jit(solution)/shard_map/ppermute | solution.py:26
  96.3 1.1 %collective-permute-start.14 = (bf16[108,512]{1,0:T(8,128)(2,1)S(1)}, bf16[108,512]{1,0:T(8,128)(2,1)S(1)}, u32[]{:S(2)}, u32[]{:S(2)}) collective-permute-start(bf16[108,512]{1,0:T(8,128)(2,1)S(1)} %add_convert_fusion.own_ref), channel_id=1, source_target_pairs={{0,192},{64,0},{128,64},{192,128},{1,193},{65,1},{129,65},{193,129... | collective-permute-start | bytes 331784 | tf_op jit(solution)/shard_map/ppermute | solution.py:26
  97.4 3.5 %shard_map.67 = f32[16,64,256]{2,1,0:T(8,128)} custom-call(f32[4,256,256]{2,1,0:T(8,128)} %get-tuple-element.8.part_from, bf16[4,256,256]{2,1,0:T(8,128)(2,1)} %copy-done.17), custom_call_target="tpu_custom_call" | custom-call | flops 2621440 | bytes 2097152 | tf_op jit(solution)/shard_map/pallas_call | solution.py:160
  100.9 0.6 collective-permute-done.13.opposite_ref
  101.4 0.7 shard_map.64
  102.2 1.4 %multiply_convert_fusion = bf16[16,64,256]{2,1,0:T(8,128)(2,1)S(1)} fusion(f32[16,64,256]{2,1,0:T(8,128)} %shard_map.67, bf16[16,64,256]{2,1,0:T(8,128)(2,1)S(1)} %all-to-all-done.2), kind=kLoop, calls=%fused_computation | loop fusion | flops 786432 | bytes 2097152 | tf_op jit(solution)/shard_map/convert_element_type | solution.py:511
  103.6 0.1 reshape.26
  103.7 1.1 %copy.6 = bf16[4,16,4,4,256]{4,3,2,1,0:T(4,128)(2,1)} copy(bf16[4,16,4,4,256]{4,2,0,3,1:T(4,128)(2,1)S(1)} %bitcast.18) | data formatting | bytes 1048576 | tf_op jit(solution)/shard_map/transpose | solution.py:512
  (44 shorter events, 0.1 us)
Async XLA Ops:
  0.6 0.9 copy-start.16
  12.8 32.4 %copy-start = (bf16[8,8,1152]{2,1,0:T(8,128)(2,1)}, bf16[8,8,1152]{2,1,0:T(8,128)(2,1)S(1)}, u32[]{:S(2)}) copy-start(bf16[8,8,1152]{2,1,0:T(8,128)(2,1)S(1)} %all_to_all.15) | copy-start | bytes 442372
  12.8 19.6 %collective-permute-start.1 = (bf16[4,16,1152]{2,1,0:T(8,128)(2,1)S(1)}, bf16[4,16,1152]{2,1,0:T(8,128)(2,1)S(1)}, u32[]{:S(2)}, u32[]{:S(2)}) collective-permute-start(bf16[4,16,1152]{2,1,0:T(8,128)(2,1)S(1)} %bitcast.10), channel_id=1, source_target_pairs={{0,14},{1,15},{2,0},{3,1},{4,2},{5,3},{6,4},{7,5},{8,6},{9,7},{10,... | collective-permute-start | bytes 442376 | tf_op jit(solution)/shard_map/ppermute | solution.py:438
  18.3 11.3 %collective-permute-start.2 = (bf16[4,16,1152]{2,1,0:T(8,128)(2,1)S(1)}, bf16[4,16,1152]{2,1,0:T(8,128)(2,1)S(1)}, u32[]{:S(2)}, u32[]{:S(2)}) collective-permute-start(bf16[4,16,1152]{2,1,0:T(8,128)(2,1)S(1)} %bitcast.11), channel_id=1, source_target_pairs={{0,12},{1,13},{2,14},{3,15},{4,0},{5,1},{6,2},{7,3},{8,4},{9,5},{1... | collective-permute-start | bytes 442376 | tf_op jit(solution)/shard_map/ppermute | solution.py:438
  19.5 14.7 %collective-permute-start.5 = (bf16[4,16,1152]{2,1,0:T(8,128)(2,1)S(1)}, bf16[4,16,1152]{2,1,0:T(8,128)(2,1)S(1)}, u32[]{:S(2)}, u32[]{:S(2)}) collective-permute-start(bf16[4,16,1152]{2,1,0:T(8,128)(2,1)S(1)} %bitcast.12), channel_id=1, source_target_pairs={{0,4},{1,5},{2,6},{3,7},{4,8},{5,9},{6,10},{7,11},{8,12},{9,13},{1... | collective-permute-start | bytes 442376 | tf_op jit(solution)/shard_map/ppermute | solution.py:438
  26.0 20.9 %collective-permute-start = (bf16[4,256,256]{2,1,0:T(8,128)(2,1)}, bf16[4,256,256]{2,1,0:T(8,128)(2,1)S(1)}, u32[]{:S(2)}, u32[]{:S(2)}) collective-permute-start(bf16[4,256,256]{2,1,0:T(8,128)(2,1)} %get-tuple-element.9), channel_id=1, source_target_pairs={{0,1},{1,2},{2,3},{3,4},{4,5},{5,6},{6,7},{7,8},{8,9},{9,10},{10,1... | collective-permute-start | bytes 1572872 | tf_op jit(solution)/shard_map/ppermute | solution.py:21
  28.8 14.8 %collective-permute-start.7 = (bf16[4,16,1152]{2,1,0:T(8,128)(2,1)S(1)}, bf16[4,16,1152]{2,1,0:T(8,128)(2,1)S(1)}, u32[]{:S(2)}, u32[]{:S(2)}) collective-permute-start(bf16[4,16,1152]{2,1,0:T(8,128)(2,1)S(1)} %bitcast.13), channel_id=1, source_target_pairs={{0,2},{1,3},{2,4},{3,5},{4,6},{5,7},{6,8},{7,9},{8,10},{9,11},{10,... | collective-permute-start | bytes 442376 | tf_op jit(solution)/shard_map/ppermute | solution.py:438
  29.6 17.3 %copy-start.4 = (bf16[4,16,1152]{2,1,0:T(8,128)(2,1)}, bf16[4,16,1152]{2,1,0:T(8,128)(2,1)S(1)}, u32[]{:S(2)}) copy-start(bf16[4,16,1152]{2,1,0:T(8,128)(2,1)S(1)} %collective-permute-done.2.refs_2_) | copy-start | bytes 442372
  29.6 14.0 %collective-permute-start.3 = (bf16[4,16,1152]{2,1,0:T(8,128)(2,1)S(1)}, bf16[4,16,1152]{2,1,0:T(8,128)(2,1)S(1)}, u32[]{:S(2)}, u32[]{:S(2)}) collective-permute-start(bf16[4,16,1152]{2,1,0:T(8,128)(2,1)S(1)} %collective-permute-done.2.refs_2_), channel_id=1, source_target_pairs={{0,14},{1,15},{2,0},{3,1},{4,2},{5,3},{6,4},{7,5},{8,6},{9,7},{10,... | collective-permute-start | bytes 442376 | tf_op jit(solution)/shard_map/ppermute | solution.py:438
  32.4 14.5 %copy-start.2 = (bf16[4,16,1152]{2,1,0:T(8,128)(2,1)}, bf16[4,16,1152]{2,1,0:T(8,128)(2,1)S(1)}, u32[]{:S(2)}) copy-start(bf16[4,16,1152]{2,1,0:T(8,128)(2,1)S(1)} %collective-permute-done.1.refs_1_) | copy-start | bytes 442372
  32.4 11.2 %collective-permute-start.4 = (bf16[4,16,1152]{2,1,0:T(8,128)(2,1)S(1)}, bf16[4,16,1152]{2,1,0:T(8,128)(2,1)S(1)}, u32[]{:S(2)}, u32[]{:S(2)}) collective-permute-start(bf16[4,16,1152]{2,1,0:T(8,128)(2,1)S(1)} %collective-permute-done.2.refs_2_), channel_id=1, source_target_pairs={{0,12},{1,13},{2,14},{3,15},{4,0},{5,1},{6,2},{7,3},{8,4},{9,5},{1... | collective-permute-start | bytes 442376 | tf_op jit(solution)/shard_map/ppermute | solution.py:438
  34.2 12.7 %copy-start.6 = (bf16[4,16,1152]{2,1,0:T(8,128)(2,1)}, bf16[4,16,1152]{2,1,0:T(8,128)(2,1)S(1)}, u32[]{:S(2)}) copy-start(bf16[4,16,1152]{2,1,0:T(8,128)(2,1)S(1)} %collective-permute-done.5.refs_6_) | copy-start | bytes 442372
  34.2 10.9 %collective-permute-start.6 = (bf16[4,16,1152]{2,1,0:T(8,128)(2,1)S(1)}, bf16[4,16,1152]{2,1,0:T(8,128)(2,1)S(1)}, u32[]{:S(2)}, u32[]{:S(2)}) collective-permute-start(bf16[4,16,1152]{2,1,0:T(8,128)(2,1)S(1)} %collective-permute-done.5.refs_6_), channel_id=1, source_target_pairs={{0,2},{1,3},{2,4},{3,5},{4,6},{5,7},{6,8},{7,9},{8,10},{9,11},{10,... | collective-permute-start | bytes 442376 | tf_op jit(solution)/shard_map/ppermute | solution.py:438
  43.6 3.3 %copy-start.8 = (bf16[4,16,1152]{2,1,0:T(8,128)(2,1)}, bf16[4,16,1152]{2,1,0:T(8,128)(2,1)S(1)}, u32[]{:S(2)}) copy-start(bf16[4,16,1152]{2,1,0:T(8,128)(2,1)S(1)} %collective-permute-done.7.refs_7_) | copy-start | bytes 442372
  43.6 3.3 %copy-start.10 = (bf16[4,16,1152]{2,1,0:T(8,128)(2,1)}, bf16[4,16,1152]{2,1,0:T(8,128)(2,1)S(1)}, u32[]{:S(2)}) copy-start(bf16[4,16,1152]{2,1,0:T(8,128)(2,1)S(1)} %collective-permute-done.3.refs_3_) | copy-start | bytes 442372
  43.6 3.3 %copy-start.12 = (bf16[4,16,1152]{2,1,0:T(8,128)(2,1)}, bf16[4,16,1152]{2,1,0:T(8,128)(2,1)S(1)}, u32[]{:S(2)}) copy-start(bf16[4,16,1152]{2,1,0:T(8,128)(2,1)S(1)} %collective-permute-done.4.refs_4_) | copy-start | bytes 442372
  45.2 1.8 %copy-start.14 = (bf16[4,16,1152]{2,1,0:T(8,128)(2,1)}, bf16[4,16,1152]{2,1,0:T(8,128)(2,1)S(1)}, u32[]{:S(2)}) copy-start(bf16[4,16,1152]{2,1,0:T(8,128)(2,1)S(1)} %collective-permute-done.6.refs_5_) | copy-start | bytes 442372
  46.8 19.9 %collective-permute-start.8 = (bf16[8,4,16,1152]{3,2,1,0:T(8,128)(2,1)S(1)}, bf16[8,4,16,1152]{3,2,1,0:T(8,128)(2,1)}, u32[]{:S(2)}, u32[]{:S(2)}) collective-permute-start(bf16[8,4,16,1152]{3,2,1,0:T(8,128)(2,1)S(1)} %shard_map.62), channel_id=1, source_target_pairs={{0,1},{1,0},{2,3},{3,2},{4,5},{5,4},{6,7},{7,6},{8,9},{9,8},{10,11... | collective-permute-start | bytes 3538952 | tf_op jit(solution)/shard_map/ppermute | solution.py:438
  46.9 0.8 copy-start.17
  51.0 15.7 %copy-start.1 = (bf16[8,8,1152]{2,1,0:T(8,128)(2,1)S(1)}, bf16[8,8,1152]{2,1,0:T(8,128)(2,1)}, u32[]{:S(2)}) copy-start(bf16[8,8,1152]{2,1,0:T(8,128)(2,1)} %copy-done) | copy-start | bytes 442372
  51.0 15.7 %copy-start.3 = (bf16[4,16,1152]{2,1,0:T(8,128)(2,1)S(1)}, bf16[4,16,1152]{2,1,0:T(8,128)(2,1)}, u32[]{:S(2)}) copy-start(bf16[4,16,1152]{2,1,0:T(8,128)(2,1)} %copy-done.2) | copy-start | bytes 442372
  51.0 15.7 %copy-start.5 = (bf16[4,16,1152]{2,1,0:T(8,128)(2,1)S(1)}, bf16[4,16,1152]{2,1,0:T(8,128)(2,1)}, u32[]{:S(2)}) copy-start(bf16[4,16,1152]{2,1,0:T(8,128)(2,1)} %copy-done.4) | copy-start | bytes 442372
  51.0 15.7 %copy-start.7 = (bf16[4,16,1152]{2,1,0:T(8,128)(2,1)S(1)}, bf16[4,16,1152]{2,1,0:T(8,128)(2,1)}, u32[]{:S(2)}) copy-start(bf16[4,16,1152]{2,1,0:T(8,128)(2,1)} %copy-done.6) | copy-start | bytes 442372
  51.0 15.7 %copy-start.9 = (bf16[4,16,1152]{2,1,0:T(8,128)(2,1)S(1)}, bf16[4,16,1152]{2,1,0:T(8,128)(2,1)}, u32[]{:S(2)}) copy-start(bf16[4,16,1152]{2,1,0:T(8,128)(2,1)} %copy-done.8) | copy-start | bytes 442372
  51.0 15.7 %copy-start.11 = (bf16[4,16,1152]{2,1,0:T(8,128)(2,1)S(1)}, bf16[4,16,1152]{2,1,0:T(8,128)(2,1)}, u32[]{:S(2)}) copy-start(bf16[4,16,1152]{2,1,0:T(8,128)(2,1)} %copy-done.10) | copy-start | bytes 442372
  51.0 15.7 %copy-start.13 = (bf16[4,16,1152]{2,1,0:T(8,128)(2,1)S(1)}, bf16[4,16,1152]{2,1,0:T(8,128)(2,1)}, u32[]{:S(2)}) copy-start(bf16[4,16,1152]{2,1,0:T(8,128)(2,1)} %copy-done.12) | copy-start | bytes 442372
  51.0 15.7 %copy-start.15 = (bf16[4,16,1152]{2,1,0:T(8,128)(2,1)S(1)}, bf16[4,16,1152]{2,1,0:T(8,128)(2,1)}, u32[]{:S(2)}) copy-start(bf16[4,16,1152]{2,1,0:T(8,128)(2,1)} %copy-done.14) | copy-start | bytes 442372
  51.0 21.3 %all-to-all-start = ((bf16[16,64,256]{2,1,0:T(8,128)(2,1)}), bf16[16,64,256]{2,1,0:T(8,128)(2,1)S(1)}, u32[]{:S(2)}, u32[]{:S(2)}) async-start(bf16[16,64,256]{2,1,0:T(8,128)(2,1)} %shard_map.60), calls=%async_computation | async-start | bytes 1048576 | tf_op jit(solution)/shard_map/all_to_all | solution.py:458
  56.0 4.6 %collective-permute-start.15 = (bf16[108,512]{1,0:T(8,128)(2,1)S(1)}, bf16[108,512]{1,0:T(8,128)(2,1)S(1)}, u32[]{:S(2)}, u32[]{:S(2)}) collective-permute-start(bf16[108,512]{1,0:T(8,128)(2,1)S(1)} %reshape.25.refs_0_), channel_id=1, source_target_pairs={{0,48},{1,49},{2,50},{3,51},{4,52},{5,53},{6,54},{7,55},{8,56},{9,... | collective-permute-start | bytes 331784 | tf_op jit(solution)/shard_map/ppermute | solution.py:438
  57.0 5.8 %collective-permute-start.16 = (bf16[108,512]{1,0:T(8,128)(2,1)S(1)}, bf16[108,512]{1,0:T(8,128)(2,1)S(1)}, u32[]{:S(2)}, u32[]{:S(2)}) collective-permute-start(bf16[108,512]{1,0:T(8,128)(2,1)S(1)} %reshape.25.refs_0_), channel_id=1, source_target_pairs={{0,32},{1,33},{2,34},{3,35},{4,36},{5,37},{6,38},{7,39},{8,40},{9,... | collective-permute-start | bytes 331784 | tf_op jit(solution)/shard_map/ppermute | solution.py:438
  58.2 7.7 %collective-permute-start.17 = (bf16[108,512]{1,0:T(8,128)(2,1)S(1)}, bf16[108,512]{1,0:T(8,128)(2,1)S(1)}, u32[]{:S(2)}, u32[]{:S(2)}) collective-permute-start(bf16[108,512]{1,0:T(8,128)(2,1)S(1)} %reshape.25.refs_0_), channel_id=1, source_target_pairs={{0,16},{1,17},{2,18},{3,19},{4,20},{5,21},{6,22},{7,23},{8,24},{9,... | collective-permute-start | bytes 331784 | tf_op jit(solution)/shard_map/ppermute | solution.py:438
  72.3 29.9 %all-to-all-start.2 = ((bf16[16,64,256]{2,1,0:T(8,128)(2,1)}), bf16[16,64,256]{2,1,0:T(8,128)(2,1)S(1)}, u32[]{:S(2)}, u32[]{:S(2)}) async-start(bf16[16,64,256]{2,1,0:T(8,128)(2,1)} %shard_map.66), calls=%async_computation.2 | async-start | bytes 1048576 | tf_op jit(solution)/shard_map/all_to_all | solution.py:458
  83.1 4.7 %collective-permute-start.11 = (bf16[108,512]{1,0:T(8,128)(2,1)S(1)}, bf16[108,512]{1,0:T(8,128)(2,1)S(1)}, u32[]{:S(2)}, u32[]{:S(2)}) collective-permute-start(bf16[108,512]{1,0:T(8,128)(2,1)S(1)} %get-tuple-element.13), channel_id=1, source_target_pairs={{0,48},{1,49},{2,50},{3,51},{4,52},{5,53},{6,54},{7,55},{8,56},{9,... | collective-permute-start | bytes 331784 | tf_op jit(solution)/shard_map/ppermute | solution.py:438
  83.4 5.8 %collective-permute-start.10 = (bf16[108,512]{1,0:T(8,128)(2,1)S(1)}, bf16[108,512]{1,0:T(8,128)(2,1)S(1)}, u32[]{:S(2)}, u32[]{:S(2)}) collective-permute-start(bf16[108,512]{1,0:T(8,128)(2,1)S(1)} %get-tuple-element.12), channel_id=1, source_target_pairs={{0,32},{1,33},{2,34},{3,35},{4,36},{5,37},{6,38},{7,39},{8,40},{9,... | collective-permute-start | bytes 331784 | tf_op jit(solution)/shard_map/ppermute | solution.py:438
  84.6 7.8 %collective-permute-start.9 = (bf16[108,512]{1,0:T(8,128)(2,1)S(1)}, bf16[108,512]{1,0:T(8,128)(2,1)S(1)}, u32[]{:S(2)}, u32[]{:S(2)}) collective-permute-start(bf16[108,512]{1,0:T(8,128)(2,1)S(1)} %get-tuple-element.11), channel_id=1, source_target_pairs={{0,16},{1,17},{2,18},{3,19},{4,20},{5,21},{6,22},{7,23},{8,24},{9,... | collective-permute-start | bytes 331784 | tf_op jit(solution)/shard_map/ppermute | solution.py:438
  92.5 8.4 %collective-permute-start.12 = (bf16[108,512]{1,0:T(8,128)(2,1)S(1)}, bf16[108,512]{1,0:T(8,128)(2,1)S(1)}, u32[]{:S(2)}, u32[]{:S(2)}) collective-permute-start(bf16[108,512]{1,0:T(8,128)(2,1)S(1)} %add_convert_fusion.own_ref), channel_id=1, source_target_pairs={{0,64},{64,128},{128,192},{192,0},{1,65},{65,129},{129,193},{193,1... | collective-permute-start | bytes 331784 | tf_op jit(solution)/shard_map/ppermute | solution.py:26
  93.8 7.6 %collective-permute-start.13 = (bf16[108,512]{1,0:T(8,128)(2,1)S(1)}, bf16[108,512]{1,0:T(8,128)(2,1)S(1)}, u32[]{:S(2)}, u32[]{:S(2)}) collective-permute-start(bf16[108,512]{1,0:T(8,128)(2,1)S(1)} %add_convert_fusion.own_ref), channel_id=1, source_target_pairs={{0,128},{64,192},{128,0},{192,64},{1,129},{65,193},{129,1},{193,65... | collective-permute-start | bytes 331784 | tf_op jit(solution)/shard_map/ppermute | solution.py:26
  96.3 5.2 %collective-permute-start.14 = (bf16[108,512]{1,0:T(8,128)(2,1)S(1)}, bf16[108,512]{1,0:T(8,128)(2,1)S(1)}, u32[]{:S(2)}, u32[]{:S(2)}) collective-permute-start(bf16[108,512]{1,0:T(8,128)(2,1)S(1)} %add_convert_fusion.own_ref), channel_id=1, source_target_pairs={{0,192},{64,0},{128,64},{192,128},{1,193},{65,1},{129,65},{193,129... | collective-permute-start | bytes 331784 | tf_op jit(solution)/shard_map/ppermute | solution.py:26

commit v12 on v10

--- a/solution.py
+++ b/solution.py
@@ -56,23 +56,9 @@
     return jnp.where(keep, moved, 0.0).astype(block.dtype)
 
 
-def conv_kernel(row_len, w_from, volume_from, ahead_ref, part_ref, *scratch):
-    cols_ref, w_ref, volume_ref, planes_ref, sems = scratch
-    moves = [
-        pltpu.make_async_copy(volume_from.at[:, at * 16 : at * 16 + 16], volume_ref.at[at], sems.at[at])
-        for at in range(2)
-    ]
-    copy = pltpu.make_async_copy(w_from, w_ref, sems.at[2])
-    for move in moves:
-        move.start()
+def conv_kernel(row_len, w_from, planes_ref, ahead_ref, part_ref, cols_ref, w_ref, sem):
+    copy = pltpu.make_async_copy(w_from, w_ref, sem)
     copy.start()
-    for at in range(2):
-        moves[at].wait()
-        for first in range(0, volume_ref.shape[1], 16):
-            turned = jnp.swapaxes(volume_ref[at, first : first + 16], 0, 1)
-            for phase in range(16):
-                row = phase * volume_ref.shape[1] + first
-                planes_ref[at, row : row + 16, :] = turned[phase]
     cells = planes_ref.shape[2]
     channels = planes_ref.shape[1] // 16
     tap_rows = 9 * channels
@@ -106,29 +92,27 @@
             out_ref[phase] = total[:, phase * cells : (phase + 1) * cells].astype(out_ref.dtype)
 
 
-def conv(w_rows, volume, row_len):
+def conv(w_rows, planes, row_len):
     depth, outs = w_rows.shape
-    channels, _, cells = volume.shape
+    cells = planes.shape[2]
     return pl.pallas_call(
         functools.partial(conv_kernel, row_len),
         out_shape=(
             jax.ShapeDtypeStruct((4, outs, cells), jnp.bfloat16),
             jax.ShapeDtypeStruct((4, outs, cells), jnp.float32),
         ),
-        in_specs=[IN_HBM] * 2,
+        in_specs=[IN_HBM, IN_VMEM],
         out_specs=(IN_VMEM,) * 2,
         scratch_shapes=[
             pltpu.VMEM((2 * depth // 3, 4 * cells), jnp.bfloat16),
             pltpu.VMEM(w_rows.shape, jnp.bfloat16),
-            pltpu.VMEM((2, channels, 16, cells), jnp.bfloat16),
-            pltpu.VMEM((2, 16 * channels, cells), jnp.bfloat16),
-            pltpu.SemaphoreType.DMA((3,)),
+            pltpu.SemaphoreType.DMA(()),
         ],
         compiler_params=GRANT,
         cost_estimate=pl.CostEstimate(
             flops=8 * outs * depth * cells, bytes_accessed=4 * depth * cells, transcendentals=0
         ),
-    )(w_rows, volume)
+    )(w_rows, planes)
 
 
 def regrouped(values, own, at):
@@ -478,8 +462,9 @@
     for step in range(1, ROWS):
         w_rel.append(on_space(w_rel[0], y_by=-step))
 
+    planes = volume[0].transpose(1, 2, 0, 3).reshape(2, 16 * channels, cells)
     w_rows = w_first.reshape(27 * channels, outs)
-    ahead, part = conv(w_rows, volume[0].reshape(channels, 32, cells), row_len)
+    ahead, part = conv(w_rows, planes, row_len)
     behind = from_behind(ahead, "space", 1)
     hidden = pointwise(activate, part, behind, group, jnp.bfloat16)
     slopes = pointwise(slope_of, part, behind, group, jnp.float32)

time: 104 us -> 103 us (level)
  blocking collectives: 11.2 us -> 0 us
  starting transfers between devices: 36.4 us -> 42.6 us
  waiting for transfers between devices: 29.9 us -> 32.4 us
  local copies, waits for them, and re-layouts: 5.19 us -> 6.38 us
    all_to_all x1 -> x0, blocking collectives: 11.2 us -> none  [exchange(): lax.all_to_all(blocks, 'space', split_axis=0, concat_axis=0, axis_index_g...]
    all_to_all x2 -> x3, starting transfers between devices: 10.3 us -> 17 us  [exchange(): lax.all_to_all(blocks, 'space', split_axis=0, concat_axis=0, axis_index_g...]
    transpose x0 -> x1, local copies, waits for them, and re-layouts: none -> 2.76 us  [section(): planes = volume[0].transpose(1, 2, 0, 3).reshape(2, 16 * channels, cells)]
    all_to_all x2 -> x3, waiting for transfers between devices: 1.13 us -> 3.75 us  [exchange(): lax.all_to_all(blocks, 'space', split_axis=0, concat_axis=0, axis_index_g...]
    unnamed x8 -> x14, local copies, waits for them, and re-layouts: 3.97 us -> 2.39 us
  transfers between devices with their start and end apart: 20 -> 21, of which waited for: 11 -> 12; matrix products, arithmetic and copies ran while one was open for 0% -> 3% of each run, Pallas kernels for 18% -> 18%
where the time goes in v12:
time: 103 us; the launch traced here: 102 us
  starting transfers between devices  42.6 us (41%)
  waiting for transfers between devices  32.4 us (31%)
  Pallas kernels  18.6 us (18%)
  local copies, waits for them, and re-layouts  6.38 us (6%)
  other arithmetic  1.32 us (1%)
    ppermute x14, waiting for transfers between devices, on_space(): return lax.ppermute(block, 'space', route)  25.1 us
    ppermute x14, starting transfers between devices, on_space(): return lax.ppermute(block, 'space', route)  17.9 us
    all_to_all x3, starting transfers between devices, exchange(): lax.all_to_all(blocks, 'space', split_axis=0, concat_axis=0, axis_index_g...  17 us
    ppermute x3, starting transfers between devices, from_side(): lax.ppermute(block, axis, [(i, (i + distance) % size) for i in range(size)])  4.89 us
    pallas_call x1, Pallas kernels, back(): pl.pallas_call(functools.partial(back_kernel, row_len), out_shape=jax.Sha...  4.86 us
    pallas_call x1, Pallas kernels, grad(): pl.pallas_call(functools.partial(grad_kernel, row_len), out_shape=[jax.Sh...  4.01 us
    all_to_all x3, waiting for transfers between devices, exchange(): lax.all_to_all(blocks, 'space', split_axis=0, concat_axis=0, axis_index_g...  3.75 us
    ppermute x3, waiting for transfers between devices, from_side(): lax.ppermute(block, axis, [(i, (i + distance) % size) for i in range(size)])  3.57 us
  transfers between devices with their start and end apart: 21, of which 12 were waited for; matrix products, arithmetic and copies ran while one was open for 3% of the time, Pallas kernels for 18%

profile of v12, /device:TPU:1, one launch (start us, length us, event | category | flops | bytes accessed | tf_op | source)
XLA Modules:
  0.0 102.1 jit_solution(2853753094347263033)
XLA Ops:
  0.6 0.9 copy-done.4
  1.5 0.7 shard_map.61
  2.3 6.5 %all-to-all-start.1 = ((bf16[8,8,1152]{2,1,0:T(8,128)(2,1)}), bf16[8,8,1152]{2,1,0:T(8,128)(2,1)S(1)}, u32[]{:S(2)}, u32[]{:S(2)}) async-start(bf16[8,8,1152]{2,1,0:T(8,128)(2,1)} %shard_map.61), calls=%async_computation.1 | async-start | bytes 294912 | tf_op jit(solution)/shard_map/all_to_all | solution.py:433
  8.7 2.8 %copy.6 = bf16[2,16,128,256]{3,2,1,0:T(8,128)(2,1)S(1)} copy(bf16[2,16,128,256]{3,1,0,2:T(8,128)(2,1)} %bitcast.23) | data formatting | bytes 4194304 | tf_op jit(solution)/shard_map/transpose | solution.py:465
  11.5 2.7 %all-to-all-done.1 = bf16[8,8,1152]{2,1,0:T(8,128)(2,1)S(1)} async-done(((bf16[8,8,1152]{2,1,0:T(8,128)(2,1)}), bf16[8,8,1152]{2,1,0:T(8,128)(2,1)S(1)}, u32[]{:S(2)}, u32[]{:S(2)}) %all-to-all-start.1) | async-done | bytes 147488 | tf_op jit(solution)/shard_map/all_to_all | solution.py:433
  14.2 5.0 %collective-permute-start.1 = (bf16[4,16,1152]{2,1,0:T(8,128)(2,1)S(1)}, bf16[4,16,1152]{2,1,0:T(8,128)(2,1)S(1)}, u32[]{:S(2)}, u32[]{:S(2)}) collective-permute-start(bf16[4,16,1152]{2,1,0:T(8,128)(2,1)S(1)} %bitcast.14), channel_id=1, source_target_pairs={{0,14},{1,15},{2,0},{3,1},{4,2},{5,3},{6,4},{7,5},{8,6},{9,7},{10,... | collective-permute-start | bytes 442376 | tf_op jit(solution)/shard_map/ppermute | solution.py:413
  19.2 1.2 %collective-permute-start.2 = (bf16[4,16,1152]{2,1,0:T(8,128)(2,1)S(1)}, bf16[4,16,1152]{2,1,0:T(8,128)(2,1)S(1)}, u32[]{:S(2)}, u32[]{:S(2)}) collective-permute-start(bf16[4,16,1152]{2,1,0:T(8,128)(2,1)S(1)} %bitcast.15), channel_id=1, source_target_pairs={{0,12},{1,13},{2,14},{3,15},{4,0},{5,1},{6,2},{7,3},{8,4},{9,5},{1... | collective-permute-start | bytes 442376 | tf_op jit(solution)/shard_map/ppermute | solution.py:413
  20.4 1.2 %collective-permute-start.5 = (bf16[4,16,1152]{2,1,0:T(8,128)(2,1)S(1)}, bf16[4,16,1152]{2,1,0:T(8,128)(2,1)S(1)}, u32[]{:S(2)}, u32[]{:S(2)}) collective-permute-start(bf16[4,16,1152]{2,1,0:T(8,128)(2,1)S(1)} %bitcast.16), channel_id=1, source_target_pairs={{0,4},{1,5},{2,6},{3,7},{4,8},{5,9},{6,10},{7,11},{8,12},{9,13},{1... | collective-permute-start | bytes 442376 | tf_op jit(solution)/shard_map/ppermute | solution.py:413
  21.6 1.5 %copy-done.5 = bf16[3,3,3,128,256]{4,3,2,1,0:T(8,128)(2,1)S(1)} copy-done((bf16[3,3,3,128,256]{4,3,2,1,0:T(8,128)(2,1)S(1)}, bf16[3,3,3,128,256]{4,3,2,1,0:T(8,128)(2,1)}, u32[]{:S(2)}) %copy-start.5) | copy-done | bytes 1769496
  23.0 3.0 %shard_map.59 = (bf16[4,256,256]{2,1,0:T(8,128)(2,1)S(1)}, f32[4,256,256]{2,1,0:T(8,128)S(1)}) custom-call(bf16[3456,256]{1,0:T(8,128)(2,1)S(1)} %bitcast.22, bf16[2,2048,256]{2,1,0:T(8,128)(2,1)S(1)} %bitcast.13), custom_call_target="tpu_custom_call" | custom-call | flops 1811939328 | bytes 3538944 | tf_op jit(solution)/shard_map/pallas_call | solution.py:98
  26.0 2.8 %collective-permute-start = (bf16[4,256,256]{2,1,0:T(8,128)(2,1)S(1)}, bf16[4,256,256]{2,1,0:T(8,128)(2,1)S(1)}, u32[]{:S(2)}, u32[]{:S(2)}) collective-permute-start(bf16[4,256,256]{2,1,0:T(8,128)(2,1)S(1)} %get-tuple-element.9), channel_id=1, source_target_pairs={{0,1},{1,2},{2,3},{3,4},{4,5},{5,6},{6,7},{7,8},{8,9},{9,10},{10,1... | collective-permute-start | bytes 1572872 | tf_op jit(solution)/shard_map/ppermute | solution.py:21
  28.8 0.8 collective-permute-start.7
  29.6 2.8 %collective-permute-start.3 = (bf16[4,16,1152]{2,1,0:T(8,128)(2,1)S(1)}, bf16[4,16,1152]{2,1,0:T(8,128)(2,1)S(1)}, u32[]{:S(2)}, u32[]{:S(2)}) collective-permute-start(bf16[4,16,1152]{2,1,0:T(8,128)(2,1)S(1)} %collective-permute-done.2.refs_2_), channel_id=1, source_target_pairs={{0,14},{1,15},{2,0},{3,1},{4,2},{5,3},{6,4},{7,5},{8,6},{9,7},{10,... | collective-permute-start | bytes 442376 | tf_op jit(solution)/shard_map/ppermute | solution.py:413
  32.4 1.8 %collective-permute-start.4 = (bf16[4,16,1152]{2,1,0:T(8,128)(2,1)S(1)}, bf16[4,16,1152]{2,1,0:T(8,128)(2,1)S(1)}, u32[]{:S(2)}, u32[]{:S(2)}) collective-permute-start(bf16[4,16,1152]{2,1,0:T(8,128)(2,1)S(1)} %collective-permute-done.2.refs_2_), channel_id=1, source_target_pairs={{0,12},{1,13},{2,14},{3,15},{4,0},{5,1},{6,2},{7,3},{8,4},{9,5},{1... | collective-permute-start | bytes 442376 | tf_op jit(solution)/shard_map/ppermute | solution.py:413
  34.2 0.7 collective-permute-start.6
  34.9 8.5 %collective-permute-done.7.refs_7_ = bf16[4,16,1152]{2,1,0:T(8,128)(2,1)S(1)} collective-permute-done((bf16[4,16,1152]{2,1,0:T(8,128)(2,1)S(1)}, bf16[4,16,1152]{2,1,0:T(8,128)(2,1)S(1)}, u32[]{:S(2)}, u32[]{:S(2)}) %collective-permute-start.7) | collective-permute-done | bytes 147488 | tf_op jit(solution)/shard_map/ppermute | solution.py:413
  43.5 1.6 %collective-permute-done.6.refs_5_ = bf16[4,16,1152]{2,1,0:T(8,128)(2,1)S(1)} collective-permute-done((bf16[4,16,1152]{2,1,0:T(8,128)(2,1)S(1)}, bf16[4,16,1152]{2,1,0:T(8,128)(2,1)S(1)}, u32[]{:S(2)}, u32[]{:S(2)}) %collective-permute-start.6) | collective-permute-done | bytes 147488 | tf_op jit(solution)/shard_map/ppermute | solution.py:413
  45.1 2.6 %shard_map.62 = bf16[8,4,16,1152]{3,2,1,0:T(8,128)(2,1)} custom-call(bf16[4,16,1152]{2,1,0:T(8,128)(2,1)S(1)} %bitcast.18, bf16[4,16,1152]{2,1,0:T(8,128)(2,1)S(1)} %collective-permute-done.1.refs_1_, bf16[4,16,1152]{2,1,0:T(8,128)(2,1)S(1)} %collective-permute-done.2.refs_2_, bf16[4,16,1152]{2,1,0:T(8,128)(2,1)S(1)} %collective-permute-done.3.refs_3_, ...), custom_call_target="tpu_custom_call" | custom-call | bytes 2359296 | tf_op jit(solution)/shard_map/pallas_call | solution.py:161
  47.7 0.1 collective-permute-start.8
  47.8 1.2 %shard_map.60 = bf16[16,64,256]{2,1,0:T(8,128)(2,1)} custom-call(f32[4,256,256]{2,1,0:T(8,128)S(1)} %get-tuple-element.8.part_ref, bf16[4,256,256]{2,1,0:T(8,128)(2,1)S(1)} %collective-permute-done.behind_ref), custom_call_target="tpu_custom_call" | custom-call | flops 2621440 | bytes 2097152 | tf_op jit(solution)/shard_map/pallas_call | solution.py:136
  49.0 4.1 %all-to-all-start = ((bf16[16,64,256]{2,1,0:T(8,128)(2,1)}), bf16[16,64,256]{2,1,0:T(8,128)(2,1)S(1)}, u32[]{:S(2)}, u32[]{:S(2)}) async-start(bf16[16,64,256]{2,1,0:T(8,128)(2,1)} %shard_map.60), calls=%async_computation | async-start | bytes 1048576 | tf_op jit(solution)/shard_map/all_to_all | solution.py:433
  53.2 1.0 collective-permute-start.15
  54.1 1.2 %collective-permute-start.16 = (bf16[108,512]{1,0:T(8,128)(2,1)S(1)}, bf16[108,512]{1,0:T(8,128)(2,1)}, u32[]{:S(2)}, u32[]{:S(2)}) collective-permute-start(bf16[108,512]{1,0:T(8,128)(2,1)S(1)} %reshape.29.refs_0_), channel_id=1, source_target_pairs={{0,32},{1,33},{2,34},{3,35},{4,36},{5,37},{6,38},{7,39},{8,40},{9,... | collective-permute-start | bytes 331784 | tf_op jit(solution)/shard_map/ppermute | solution.py:413
  55.3 0.1 pad_add_fusion.place_ref
  55.4 2.4 %collective-permute-done.15.refs_1_ = bf16[108,512]{1,0:T(8,128)(2,1)S(1)} collective-permute-done((bf16[108,512]{1,0:T(8,128)(2,1)S(1)}, bf16[108,512]{1,0:T(8,128)(2,1)S(1)}, u32[]{:S(2)}, u32[]{:S(2)}) %collective-permute-start.15) | collective-permute-done | bytes 110624 | tf_op jit(solution)/shard_map/ppermute | solution.py:413
  57.8 2.2 %collective-permute-done.16.refs_2_ = bf16[108,512]{1,0:T(8,128)(2,1)} collective-permute-done((bf16[108,512]{1,0:T(8,128)(2,1)S(1)}, bf16[108,512]{1,0:T(8,128)(2,1)}, u32[]{:S(2)}, u32[]{:S(2)}) %collective-permute-start.16) | collective-permute-done | bytes 110624 | tf_op jit(solution)/shard_map/ppermute | solution.py:413
  60.1 3.1 %collective-permute-done.17.refs_3_ = bf16[108,512]{1,0:T(8,128)(2,1)} collective-permute-done((bf16[108,512]{1,0:T(8,128)(2,1)S(1)}, bf16[108,512]{1,0:T(8,128)(2,1)}, u32[]{:S(2)}, u32[]{:S(2)}) %collective-permute-start.17) | collective-permute-done | bytes 110624 | tf_op jit(solution)/shard_map/ppermute | solution.py:413
  63.2 1.2 %shard_map.65.moves_ref = bf16[768,512]{1,0:T(8,128)(2,1)S(1)} custom-call(s32[3]{0:T(128)S(1)} %pad_add_fusion.place_ref, bf16[108,512]{1,0:T(8,128)(2,1)S(1)} %reshape.29.refs_0_, bf16[108,512]{1,0:T(8,128)(2,1)S(1)} %collective-permute-done.15.refs_1_, bf16[108,512]{1,0:T(8,128)(2,1)} %collective-permute-done.16.refs_2_, ...), custom_call_target="tpu_custom_call" | custom-call | bytes 1048576 | tf_op jit(solution)/shard_map/pallas_call | solution.py:297
  64.4 4.9 %shard_map.66 = bf16[16,64,256]{2,1,0:T(8,128)(2,1)} custom-call(s32[3]{0:T(128)S(1)} %pad_add_fusion.place_ref, bf16[768,512]{1,0:T(8,128)(2,1)S(1)} %shard_map.65.moves_ref, bf16[4,16,1152]{2,1,0:T(8,128)(2,1)S(1)} %bitcast.19, bf16[4,16,1152]{2,1,0:T(8,128)(2,1)S(1)} %collective-permute-done.1.refs_1_, bf16[4,16,1152]{2,1,0:T(8,128)(2,1)S(1)} %copy-done.1, ...), custom_call_target="tpu_custom_call" | custom-call | flops 1610612736 | bytes 4194304 | tf_op jit(solution)/shard_map/pallas_call | solution.py:337
  69.2 1.1 %all-to-all-done.hidden_ref = bf16[16,64,256]{2,1,0:T(8,128)(2,1)S(1)} async-done(((bf16[16,64,256]{2,1,0:T(8,128)(2,1)}), bf16[16,64,256]{2,1,0:T(8,128)(2,1)S(1)}, u32[]{:S(2)}, u32[]{:S(2)}) %all-to-all-start) | async-done | bytes 524320 | tf_op jit(solution)/shard_map/all_to_all | solution.py:433
  70.3 6.4 %all-to-all-start.2 = ((bf16[16,64,256]{2,1,0:T(8,128)(2,1)}), bf16[16,64,256]{2,1,0:T(8,128)(2,1)}, u32[]{:S(2)}, u32[]{:S(2)}) async-start(bf16[16,64,256]{2,1,0:T(8,128)(2,1)} %shard_map.66), calls=%async_computation.2 | async-start | bytes 1048576 | tf_op jit(solution)/shard_map/all_to_all | solution.py:433
  76.7 4.0 %shard_map.63 = (f32[108,512]{1,0:T(8,128)S(1)}, bf16[108,512]{1,0:T(8,128)(2,1)S(1)}, bf16[108,512]{1,0:T(8,128)(2,1)S(1)}, bf16[108,512]{1,0:T(8,128)(2,1)S(1)}) custom-call(s32[3]{0:T(128)S(1)} %pad_add_fusion.place_ref, bf16[16,64,256]{2,1,0:T(8,128)(2,1)S(1)} %all-to-all-done.hidden_ref, bf16[4,16,1152]{2,1,0:T(8,128)(2,1)S(1)} %bitcast.20, ...), custom_call_target="tpu_custom_call" | custom-call | flops 1610612736 | bytes 4194304 | tf_op jit(solution)/shard_map/pallas_call | solution.py:257
  80.7 0.4 collective-permute-start.11
  81.1 1.2 %collective-permute-start.10 = (bf16[108,512]{1,0:T(8,128)(2,1)S(1)}, bf16[108,512]{1,0:T(8,128)(2,1)S(1)}, u32[]{:S(2)}, u32[]{:S(2)}) collective-permute-start(bf16[108,512]{1,0:T(8,128)(2,1)S(1)} %get-tuple-element.12), channel_id=1, source_target_pairs={{0,32},{1,33},{2,34},{3,35},{4,36},{5,37},{6,38},{7,39},{8,40},{9,... | collective-permute-start | bytes 331784 | tf_op jit(solution)/shard_map/ppermute | solution.py:413
  82.2 0.6 collective-permute-start.9
  82.8 2.6 %collective-permute-done.11 = bf16[108,512]{1,0:T(8,128)(2,1)S(1)} collective-permute-done((bf16[108,512]{1,0:T(8,128)(2,1)S(1)}, bf16[108,512]{1,0:T(8,128)(2,1)S(1)}, u32[]{:S(2)}, u32[]{:S(2)}) %collective-permute-start.11) | collective-permute-done | bytes 110624 | tf_op jit(solution)/shard_map/ppermute | solution.py:413
  85.4 1.5 %collective-permute-done.10 = bf16[108,512]{1,0:T(8,128)(2,1)S(1)} collective-permute-done((bf16[108,512]{1,0:T(8,128)(2,1)S(1)}, bf16[108,512]{1,0:T(8,128)(2,1)S(1)}, u32[]{:S(2)}, u32[]{:S(2)}) %collective-permute-start.10) | collective-permute-done | bytes 110624 | tf_op jit(solution)/shard_map/ppermute | solution.py:413
  86.9 3.1 %collective-permute-done.9 = bf16[108,512]{1,0:T(8,128)(2,1)S(1)} collective-permute-done((bf16[108,512]{1,0:T(8,128)(2,1)S(1)}, bf16[108,512]{1,0:T(8,128)(2,1)S(1)}, u32[]{:S(2)}, u32[]{:S(2)}) %collective-permute-start.9) | collective-permute-done | bytes 110624 | tf_op jit(solution)/shard_map/ppermute | solution.py:413
  90.1 1.3 %collective-permute-start.12 = (bf16[108,512]{1,0:T(8,128)(2,1)S(1)}, bf16[108,512]{1,0:T(8,128)(2,1)S(1)}, u32[]{:S(2)}, u32[]{:S(2)}) collective-permute-start(bf16[108,512]{1,0:T(8,128)(2,1)S(1)} %add_convert_fusion.own_ref), channel_id=1, source_target_pairs={{0,64},{64,128},{128,192},{192,0},{1,65},{65,129},{129,193},{193,1... | collective-permute-start | bytes 331784 | tf_op jit(solution)/shard_map/ppermute | solution.py:26
  91.4 2.4 %collective-permute-start.13 = (bf16[108,512]{1,0:T(8,128)(2,1)S(1)}, bf16[108,512]{1,0:T(8,128)(2,1)S(1)}, u32[]{:S(2)}, u32[]{:S(2)}) collective-permute-start(bf16[108,512]{1,0:T(8,128)(2,1)S(1)} %add_convert_fusion.own_ref), channel_id=1, source_target_pairs={{0,128},{64,192},{128,0},{192,64},{1,129},{65,193},{129,1},{193,65... | collective-permute-start | bytes 331784 | tf_op jit(solution)/shard_map/ppermute | solution.py:26
  93.8 1.2 %collective-permute-start.14 = (bf16[108,512]{1,0:T(8,128)(2,1)S(1)}, bf16[108,512]{1,0:T(8,128)(2,1)S(1)}, u32[]{:S(2)}, u32[]{:S(2)}) collective-permute-start(bf16[108,512]{1,0:T(8,128)(2,1)S(1)} %add_convert_fusion.own_ref), channel_id=1, source_target_pairs={{0,192},{64,0},{128,64},{192,128},{1,193},{65,1},{129,65},{193,129... | collective-permute-start | bytes 331784 | tf_op jit(solution)/shard_map/ppermute | solution.py:26
  95.0 0.4 shard_map.67
  95.4 0.1 collective-permute-done.12.left_ref
  95.6 3.4 %collective-permute-done.13.opposite_ref = bf16[108,512]{1,0:T(8,128)(2,1)S(1)} collective-permute-done((bf16[108,512]{1,0:T(8,128)(2,1)S(1)}, bf16[108,512]{1,0:T(8,128)(2,1)S(1)}, u32[]{:S(2)}, u32[]{:S(2)}) %collective-permute-start.13) | collective-permute-done | bytes 110624 | tf_op jit(solution)/shard_map/ppermute | solution.py:26
  99.0 0.7 shard_map.64
  99.7 1.2 %multiply_convert_fusion = bf16[16,64,256]{2,1,0:T(8,128)(2,1)S(1)} fusion(f32[16,64,256]{2,1,0:T(8,128)S(1)} %shard_map.67, bf16[16,64,256]{2,1,0:T(8,128)(2,1)} %all-to-all-done.2), kind=kLoop, calls=%fused_computation | loop fusion | flops 786432 | bytes 2097152 | tf_op jit(solution)/shard_map/convert_element_type | solution.py:487
  100.9 0.1 reshape.30
  101.1 1.1 %copy.7 = bf16[4,16,4,4,256]{4,3,2,1,0:T(4,128)(2,1)} copy(bf16[4,16,4,4,256]{4,2,0,3,1:T(4,128)(2,1)S(1)} %bitcast.24) | data formatting | bytes 1048576 | tf_op jit(solution)/shard_map/transpose | solution.py:488
  (24 shorter events, 0.1 us)
Async XLA Ops:
  0.6 0.9 copy-start.4
  2.3 11.9 %all-to-all-start.1 = ((bf16[8,8,1152]{2,1,0:T(8,128)(2,1)}), bf16[8,8,1152]{2,1,0:T(8,128)(2,1)S(1)}, u32[]{:S(2)}, u32[]{:S(2)}) async-start(bf16[8,8,1152]{2,1,0:T(8,128)(2,1)} %shard_map.61), calls=%async_computation.1 | async-start | bytes 294912 | tf_op jit(solution)/shard_map/all_to_all | solution.py:433
  14.2 18.2 %collective-permute-start.1 = (bf16[4,16,1152]{2,1,0:T(8,128)(2,1)S(1)}, bf16[4,16,1152]{2,1,0:T(8,128)(2,1)S(1)}, u32[]{:S(2)}, u32[]{:S(2)}) collective-permute-start(bf16[4,16,1152]{2,1,0:T(8,128)(2,1)S(1)} %bitcast.14), channel_id=1, source_target_pairs={{0,14},{1,15},{2,0},{3,1},{4,2},{5,3},{6,4},{7,5},{8,6},{9,7},{10,... | collective-permute-start | bytes 442376 | tf_op jit(solution)/shard_map/ppermute | solution.py:413
  19.2 10.4 %collective-permute-start.2 = (bf16[4,16,1152]{2,1,0:T(8,128)(2,1)S(1)}, bf16[4,16,1152]{2,1,0:T(8,128)(2,1)S(1)}, u32[]{:S(2)}, u32[]{:S(2)}) collective-permute-start(bf16[4,16,1152]{2,1,0:T(8,128)(2,1)S(1)} %bitcast.15), channel_id=1, source_target_pairs={{0,12},{1,13},{2,14},{3,15},{4,0},{5,1},{6,2},{7,3},{8,4},{9,5},{1... | collective-permute-start | bytes 442376 | tf_op jit(solution)/shard_map/ppermute | solution.py:413
  20.4 13.8 %collective-permute-start.5 = (bf16[4,16,1152]{2,1,0:T(8,128)(2,1)S(1)}, bf16[4,16,1152]{2,1,0:T(8,128)(2,1)S(1)}, u32[]{:S(2)}, u32[]{:S(2)}) collective-permute-start(bf16[4,16,1152]{2,1,0:T(8,128)(2,1)S(1)} %bitcast.16), channel_id=1, source_target_pairs={{0,4},{1,5},{2,6},{3,7},{4,8},{5,9},{6,10},{7,11},{8,12},{9,13},{1... | collective-permute-start | bytes 442376 | tf_op jit(solution)/shard_map/ppermute | solution.py:413
  21.6 1.5 %copy-start.5 = (bf16[3,3,3,128,256]{4,3,2,1,0:T(8,128)(2,1)S(1)}, bf16[3,3,3,128,256]{4,3,2,1,0:T(8,128)(2,1)}, u32[]{:S(2)}) copy-start(bf16[3,3,3,128,256]{4,3,2,1,0:T(8,128)(2,1)} %param.5) | copy-start | bytes 5308420
  26.0 21.8 %collective-permute-start = (bf16[4,256,256]{2,1,0:T(8,128)(2,1)S(1)}, bf16[4,256,256]{2,1,0:T(8,128)(2,1)S(1)}, u32[]{:S(2)}, u32[]{:S(2)}) collective-permute-start(bf16[4,256,256]{2,1,0:T(8,128)(2,1)S(1)} %get-tuple-element.9), channel_id=1, source_target_pairs={{0,1},{1,2},{2,3},{3,4},{4,5},{5,6},{6,7},{7,8},{8,9},{9,10},{10,1... | collective-permute-start | bytes 1572872 | tf_op jit(solution)/shard_map/ppermute | solution.py:21
  28.8 14.7 %collective-permute-start.7 = (bf16[4,16,1152]{2,1,0:T(8,128)(2,1)S(1)}, bf16[4,16,1152]{2,1,0:T(8,128)(2,1)S(1)}, u32[]{:S(2)}, u32[]{:S(2)}) collective-permute-start(bf16[4,16,1152]{2,1,0:T(8,128)(2,1)S(1)} %bitcast.17), channel_id=1, source_target_pairs={{0,2},{1,3},{2,4},{3,5},{4,6},{5,7},{6,8},{7,9},{8,10},{9,11},{10,... | collective-permute-start | bytes 442376 | tf_op jit(solution)/shard_map/ppermute | solution.py:413
  29.6 18.2 %copy-start = (bf16[4,16,1152]{2,1,0:T(8,128)(2,1)}, bf16[4,16,1152]{2,1,0:T(8,128)(2,1)S(1)}, u32[]{:S(2)}) copy-start(bf16[4,16,1152]{2,1,0:T(8,128)(2,1)S(1)} %collective-permute-done.2.refs_2_) | copy-start | bytes 442372
  29.6 13.9 %collective-permute-start.3 = (bf16[4,16,1152]{2,1,0:T(8,128)(2,1)S(1)}, bf16[4,16,1152]{2,1,0:T(8,128)(2,1)S(1)}, u32[]{:S(2)}, u32[]{:S(2)}) collective-permute-start(bf16[4,16,1152]{2,1,0:T(8,128)(2,1)S(1)} %collective-permute-done.2.refs_2_), channel_id=1, source_target_pairs={{0,14},{1,15},{2,0},{3,1},{4,2},{5,3},{6,4},{7,5},{8,6},{9,7},{10,... | collective-permute-start | bytes 442376 | tf_op jit(solution)/shard_map/ppermute | solution.py:413
  32.4 11.1 %collective-permute-start.4 = (bf16[4,16,1152]{2,1,0:T(8,128)(2,1)S(1)}, bf16[4,16,1152]{2,1,0:T(8,128)(2,1)S(1)}, u32[]{:S(2)}, u32[]{:S(2)}) collective-permute-start(bf16[4,16,1152]{2,1,0:T(8,128)(2,1)S(1)} %collective-permute-done.2.refs_2_), channel_id=1, source_target_pairs={{0,12},{1,13},{2,14},{3,15},{4,0},{5,1},{6,2},{7,3},{8,4},{9,5},{1... | collective-permute-start | bytes 442376 | tf_op jit(solution)/shard_map/ppermute | solution.py:413
  34.2 13.6 %copy-start.2 = (bf16[4,16,1152]{2,1,0:T(8,128)(2,1)}, bf16[4,16,1152]{2,1,0:T(8,128)(2,1)S(1)}, u32[]{:S(2)}) copy-start(bf16[4,16,1152]{2,1,0:T(8,128)(2,1)S(1)} %collective-permute-done.5.refs_6_) | copy-start | bytes 442372
  34.2 10.9 %collective-permute-start.6 = (bf16[4,16,1152]{2,1,0:T(8,128)(2,1)S(1)}, bf16[4,16,1152]{2,1,0:T(8,128)(2,1)S(1)}, u32[]{:S(2)}, u32[]{:S(2)}) collective-permute-start(bf16[4,16,1152]{2,1,0:T(8,128)(2,1)S(1)} %collective-permute-done.5.refs_6_), channel_id=1, source_target_pairs={{0,2},{1,3},{2,4},{3,5},{4,6},{5,7},{6,8},{7,9},{8,10},{9,11},{10,... | collective-permute-start | bytes 442376 | tf_op jit(solution)/shard_map/ppermute | solution.py:413
  47.7 5.4 %copy-start.6 = (bf16[3,3,3,4,512]{4,3,2,1,0:T(4,128)(2,1)S(1)}, bf16[3,3,3,4,512]{4,3,2,1,0:T(4,128)(2,1)}, u32[]{:S(2)}) copy-start(bf16[3,3,3,4,512]{4,3,2,1,0:T(4,128)(2,1)} %param.6) | copy-start | bytes 331780
  47.7 16.6 %collective-permute-start.8 = (bf16[8,4,16,1152]{3,2,1,0:T(8,128)(2,1)}, bf16[8,4,16,1152]{3,2,1,0:T(8,128)(2,1)}, u32[]{:S(2)}, u32[]{:S(2)}) collective-permute-start(bf16[8,4,16,1152]{3,2,1,0:T(8,128)(2,1)} %shard_map.62), channel_id=1, source_target_pairs={{0,1},{1,0},{2,3},{3,2},{4,5},{5,4},{6,7},{7,6},{8,9},{9,8},{10,11... | collective-permute-start | bytes 3538952 | tf_op jit(solution)/shard_map/ppermute | solution.py:413
  49.0 15.4 %copy-start.1 = (bf16[4,16,1152]{2,1,0:T(8,128)(2,1)S(1)}, bf16[4,16,1152]{2,1,0:T(8,128)(2,1)}, u32[]{:S(2)}) copy-start(bf16[4,16,1152]{2,1,0:T(8,128)(2,1)} %copy-done) | copy-start | bytes 442372
  49.0 15.4 %copy-start.3 = (bf16[4,16,1152]{2,1,0:T(8,128)(2,1)S(1)}, bf16[4,16,1152]{2,1,0:T(8,128)(2,1)}, u32[]{:S(2)}) copy-start(bf16[4,16,1152]{2,1,0:T(8,128)(2,1)} %copy-done.2) | copy-start | bytes 442372
  49.0 21.3 %all-to-all-start = ((bf16[16,64,256]{2,1,0:T(8,128)(2,1)}), bf16[16,64,256]{2,1,0:T(8,128)(2,1)S(1)}, u32[]{:S(2)}, u32[]{:S(2)}) async-start(bf16[16,64,256]{2,1,0:T(8,128)(2,1)} %shard_map.60), calls=%async_computation | async-start | bytes 1048576 | tf_op jit(solution)/shard_map/all_to_all | solution.py:433
  53.2 4.7 %collective-permute-start.15 = (bf16[108,512]{1,0:T(8,128)(2,1)S(1)}, bf16[108,512]{1,0:T(8,128)(2,1)S(1)}, u32[]{:S(2)}, u32[]{:S(2)}) collective-permute-start(bf16[108,512]{1,0:T(8,128)(2,1)S(1)} %reshape.29.refs_0_), channel_id=1, source_target_pairs={{0,48},{1,49},{2,50},{3,51},{4,52},{5,53},{6,54},{7,55},{8,56},{9,... | collective-permute-start | bytes 331784 | tf_op jit(solution)/shard_map/ppermute | solution.py:413
  54.1 5.9 %collective-permute-start.16 = (bf16[108,512]{1,0:T(8,128)(2,1)S(1)}, bf16[108,512]{1,0:T(8,128)(2,1)}, u32[]{:S(2)}, u32[]{:S(2)}) collective-permute-start(bf16[108,512]{1,0:T(8,128)(2,1)S(1)} %reshape.29.refs_0_), channel_id=1, source_target_pairs={{0,32},{1,33},{2,34},{3,35},{4,36},{5,37},{6,38},{7,39},{8,40},{9,... | collective-permute-start | bytes 331784 | tf_op jit(solution)/shard_map/ppermute | solution.py:413
  55.3 7.8 %collective-permute-start.17 = (bf16[108,512]{1,0:T(8,128)(2,1)S(1)}, bf16[108,512]{1,0:T(8,128)(2,1)}, u32[]{:S(2)}, u32[]{:S(2)}) collective-permute-start(bf16[108,512]{1,0:T(8,128)(2,1)S(1)} %reshape.29.refs_0_), channel_id=1, source_target_pairs={{0,16},{1,17},{2,18},{3,19},{4,20},{5,21},{6,22},{7,23},{8,24},{9,... | collective-permute-start | bytes 331784 | tf_op jit(solution)/shard_map/ppermute | solution.py:413
  70.3 29.4 %all-to-all-start.2 = ((bf16[16,64,256]{2,1,0:T(8,128)(2,1)}), bf16[16,64,256]{2,1,0:T(8,128)(2,1)}, u32[]{:S(2)}, u32[]{:S(2)}) async-start(bf16[16,64,256]{2,1,0:T(8,128)(2,1)} %shard_map.66), calls=%async_computation.2 | async-start | bytes 1048576 | tf_op jit(solution)/shard_map/all_to_all | solution.py:433
  80.7 4.7 %collective-permute-start.11 = (bf16[108,512]{1,0:T(8,128)(2,1)S(1)}, bf16[108,512]{1,0:T(8,128)(2,1)S(1)}, u32[]{:S(2)}, u32[]{:S(2)}) collective-permute-start(bf16[108,512]{1,0:T(8,128)(2,1)S(1)} %get-tuple-element.13), channel_id=1, source_target_pairs={{0,48},{1,49},{2,50},{3,51},{4,52},{5,53},{6,54},{7,55},{8,56},{9,... | collective-permute-start | bytes 331784 | tf_op jit(solution)/shard_map/ppermute | solution.py:413
  81.1 5.9 %collective-permute-start.10 = (bf16[108,512]{1,0:T(8,128)(2,1)S(1)}, bf16[108,512]{1,0:T(8,128)(2,1)S(1)}, u32[]{:S(2)}, u32[]{:S(2)}) collective-permute-start(bf16[108,512]{1,0:T(8,128)(2,1)S(1)} %get-tuple-element.12), channel_id=1, source_target_pairs={{0,32},{1,33},{2,34},{3,35},{4,36},{5,37},{6,38},{7,39},{8,40},{9,... | collective-permute-start | bytes 331784 | tf_op jit(solution)/shard_map/ppermute | solution.py:413
  82.2 7.8 %collective-permute-start.9 = (bf16[108,512]{1,0:T(8,128)(2,1)S(1)}, bf16[108,512]{1,0:T(8,128)(2,1)S(1)}, u32[]{:S(2)}, u32[]{:S(2)}) collective-permute-start(bf16[108,512]{1,0:T(8,128)(2,1)S(1)} %get-tuple-element.11), channel_id=1, source_target_pairs={{0,16},{1,17},{2,18},{3,19},{4,20},{5,21},{6,22},{7,23},{8,24},{9,... | collective-permute-start | bytes 331784 | tf_op jit(solution)/shard_map/ppermute | solution.py:413
  90.1 5.5 %collective-permute-start.12 = (bf16[108,512]{1,0:T(8,128)(2,1)S(1)}, bf16[108,512]{1,0:T(8,128)(2,1)S(1)}, u32[]{:S(2)}, u32[]{:S(2)}) collective-permute-start(bf16[108,512]{1,0:T(8,128)(2,1)S(1)} %add_convert_fusion.own_ref), channel_id=1, source_target_pairs={{0,64},{64,128},{128,192},{192,0},{1,65},{65,129},{129,193},{193,1... | collective-permute-start | bytes 331784 | tf_op jit(solution)/shard_map/ppermute | solution.py:26
  91.4 7.6 %collective-permute-start.13 = (bf16[108,512]{1,0:T(8,128)(2,1)S(1)}, bf16[108,512]{1,0:T(8,128)(2,1)S(1)}, u32[]{:S(2)}, u32[]{:S(2)}) collective-permute-start(bf16[108,512]{1,0:T(8,128)(2,1)S(1)} %add_convert_fusion.own_ref), channel_id=1, source_target_pairs={{0,128},{64,192},{128,0},{192,64},{1,129},{65,193},{129,1},{193,65... | collective-permute-start | bytes 331784 | tf_op jit(solution)/shard_map/ppermute | solution.py:26
  93.8 5.2 %collective-permute-start.14 = (bf16[108,512]{1,0:T(8,128)(2,1)S(1)}, bf16[108,512]{1,0:T(8,128)(2,1)S(1)}, u32[]{:S(2)}, u32[]{:S(2)}) collective-permute-start(bf16[108,512]{1,0:T(8,128)(2,1)S(1)} %add_convert_fusion.own_ref), channel_id=1, source_target_pairs={{0,192},{64,0},{128,64},{192,128},{1,193},{65,1},{129,65},{193,129... | collective-permute-start | bytes 331784 | tf_op jit(solution)/shard_map/ppermute | solution.py:26
